TPU v7x, 32 devices: a whole 2x2x4 slice. The times are simulated.
32 devices in a mesh: sample: 4 (over y, x), tile: 8 (over z, core).
Axes of the slice: x: 2, y: 2, z: 4, core: 2. Of those that a mesh axis runs over, the one named last changes fastest.
Arguments:
- points: bfloat16 [4, 8192, 64], P('sample', 'tile'), may hold values from -6 to 6
- slot: int32 [4, 8192], P('sample', 'tile'), may hold values from 0 to 2047, as said below
- voxel: int32 [4, 8192], P('sample', 'tile'), may hold values from 0 to 1023
- conv_weight: bfloat16 [1728, 128], replicated, may hold values from -0.15625 to 0.15625
- down_weight: bfloat16 [1024, 256], replicated, may hold values from -0.1875 to 0.1875
- cotangent: bfloat16 [4, 16, 16, 4, 256], P('sample', 'tile'), may hold values from -0.09375 to 0.09375
Outputs:
- down_features: bfloat16 [4, 16, 16, 4, 256], P('sample', 'tile')
- conv_grad: float32 [1728, 128], P('sample')
- down_grad: float32 [1024, 256], P('sample')
Inputs may be any that keep to these rules, and one draw needn't show every extreme that they name: Within one scene, the 1024 points held by one device have distinct slots; slot // 256 names the slab owner, so at most 256 points go from one device to one owner; in every scene one owner receives exactly 256 points from every device.
All inputs are finite; a program needn't handle non-finite values.
Results may differ from a plain program's by a relative error of at most 0.0056.
Values may be sent and summed in bfloat16 or wider, within the bound.
No kernel may reach another device: no remote copies, remote signals or barrier semaphores. Data moves between devices by JAX's collectives and lax.ppermute only.
A program may use at most 64 MiB of HBM per device.

v0:
```python
import jax
import jax.numpy as jnp
from jax import lax
from jax.sharding import PartitionSpec as P

CIN = 64
C1 = 128
C2 = 256
SX = 4
SY = 32
SZ = 8
PTS_DEV = 1024


def extended(block, sides, width):
    for axis, dim in sides:
        count = lax.axis_size(axis)
        forward = [(i, i + 1) for i in range(count - 1)]
        backward = [(target, source) for source, target in forward]
        low = lax.ppermute(
            lax.slice_in_dim(block, block.shape[dim] - width, None, axis=dim), axis, forward
        )
        high = lax.ppermute(lax.slice_in_dim(block, 0, width, axis=dim), axis, backward)
        block = jnp.concatenate([low, block, high], axis=dim)
    return block


def silu_slope(value):
    sigmoid = jax.nn.sigmoid(value)
    return sigmoid * (1.0 + value * (1.0 - sigmoid))


def stack_taps(padded):
    pieces = []
    for shift_x in range(3):
        for shift_y in range(3):
            for shift_z in range(3):
                pieces.append(
                    padded[
                        shift_x : shift_x + SX, shift_y : shift_y + SY, shift_z : shift_z + SZ, :
                    ]
                )
    return jnp.concatenate(pieces, axis=-1).reshape(-1, 27 * CIN)


def regroup(values):
    shaped = values.reshape(SX // 2, 2, SY // 2, 2, SZ // 2, 2, C1)
    return shaped.transpose(0, 2, 4, 1, 3, 5, 6).reshape(-1, 8 * C1)


def ungroup(values):
    shaped = values.reshape(SX // 2, SY // 2, SZ // 2, 2, 2, 2, C1)
    return shaped.transpose(0, 3, 1, 4, 2, 5, 6).reshape(-1, C1)


def local(points, slot, voxel, conv_weight, down_weight, cotangent):
    tile_count = lax.axis_size("tile")
    capacity = 2 * (PTS_DEV // tile_count)
    slab_size = SX * SY * SZ
    slot_ids = slot[0]
    send_rows = jnp.zeros((tile_count * capacity, CIN), jnp.bfloat16).at[slot_ids].set(points[0])
    send_voxels = (
        jnp.full((tile_count * capacity,), slab_size, jnp.int32).at[slot_ids].set(voxel[0])
    )
    send_rows = send_rows.reshape(tile_count, capacity // 2, 2 * CIN)
    send_voxels = send_voxels.reshape(tile_count, capacity)
    recv_rows, recv_voxels = (
        lax.all_to_all(send_rows, "tile", split_axis=0, concat_axis=0, tiled=True),
        lax.all_to_all(send_voxels, "tile", split_axis=0, concat_axis=0, tiled=True),
    )
    arrived = recv_rows.reshape(-1, CIN).astype(jnp.float32)
    targets = recv_voxels.reshape(-1)
    summed = jnp.zeros((slab_size + 1, CIN), jnp.float32).at[targets].add(arrived)
    counts = jnp.zeros((slab_size + 1,), jnp.int32).at[targets].add(1)
    grid = summed[:slab_size].astype(jnp.bfloat16).reshape(SX, SY, SZ * CIN)
    active = (counts[:slab_size] > 0)[:, None]
    widened = extended(grid, (("tile", 0),), 1)
    widened = widened.reshape(SX + 2, SY, SZ, CIN)
    padded = jnp.pad(widened, ((0, 0), (1, 1), (1, 1), (0, 0)))
    columns = stack_taps(padded)
    pre = jnp.dot(columns, conv_weight, preferred_element_type=jnp.float32)
    activated = jnp.where(active, jax.nn.silu(pre), 0.0).astype(jnp.bfloat16)
    grouped = regroup(activated)
    output_rows = jnp.dot(grouped, down_weight, preferred_element_type=jnp.float32).astype(
        jnp.bfloat16
    )
    cot_rows = cotangent.reshape(-1, C2)
    grad_down = jnp.dot(grouped.T, cot_rows, preferred_element_type=jnp.float32)
    back = ungroup(jnp.dot(cot_rows, down_weight.T, preferred_element_type=jnp.float32))
    pre_grad = jnp.where(active, back * silu_slope(pre), 0.0).astype(jnp.bfloat16)
    grad_conv = jnp.dot(columns.T, pre_grad, preferred_element_type=jnp.float32)
    total_conv, total_down = lax.psum((grad_conv, grad_down), "tile")
    share_conv, share_down = (
        lax.psum_scatter(total_conv, "sample", scatter_dimension=0, tiled=True),
        lax.psum_scatter(total_down, "sample", scatter_dimension=0, tiled=True),
    )
    down_features = output_rows.reshape(1, SX // 2, SY // 2, SZ // 2, C2)
    return (down_features, share_conv, share_down)


def solution(mesh):
    placed = (
        P("sample", "tile", None),
        P("sample", "tile"),
        P("sample", "tile"),
        P(),
        P(),
        P("sample", "tile", None, None, None),
    )
    return jax.shard_map(
        local,
        mesh=mesh,
        in_specs=placed,
        out_specs=(P("sample", "tile", None, None, None), P("sample", None), P("sample", None)),
        check_vma=False,
    )
```

profile of v0, /device:TPU:0, one launch (start us, length us, event | category | flops | bytes accessed | tf_op | source)
XLA Modules:
  0.0 209.1 jit_solution(11818611916392953577)
XLA Ops:
  7.2 0.0 copy-start
  7.2 0.0 copy-start.3
  7.2 0.8 compare_select_fusion.1
  7.9 5.0 %scatter_custom_fusion = s32[2048]{0:T(1024)} fusion(s32[1024]{0:T(1024)S(1)} %bitcast.96, s32[1024]{0:T(1024)} %bitcast.98, s32[]{:T(128)} %constant.9.clone.1), kind=kCustom, calls=%fused_computation.36 | custom fusion | bytes 8704 | tf_op jit(solution)/shard_map/scatter | solution.py:63
  13.0 6.3 %all-to-all-start = ((s32[8,1,256]{2,1,0:T(1,128)}), s32[8,1,256]{2,1,0:T(1,128)S(1)}, u32[]{:S(2)}, u32[]{:S(2)}) async-start(s32[8,1,256]{2,1,0:T(1,128)} %bitcast.3), calls=%async_computation | async-start | bytes 16384 | tf_op jit(solution)/shard_map/all_to_all | solution.py:69
  19.3 1.1 copy.15
  20.4 3.3 %scatter_custom_fusion.2 = bf16[2048,64]{1,0:T(8,128)(2,1)S(1)} fusion(s32[1024]{0:T(1024)S(1)} %bitcast.97, bf16[1024,64]{1,0:T(8,128)(2,1)S(1)} %copy.15, bf16[]{:T(256)} %constant.3.clone.1), kind=kCustom, calls=%fused_computation.29 | custom fusion | bytes 262146 | tf_op jit(solution)/shard_map/scatter | solution.py:61
  23.7 1.0 reshape.134
  24.7 0.2 all-to-all-done
  24.9 4.9 %all-to-all-start.1 = ((bf16[8,128,128]{2,1,0:T(8,128)(2,1)}), bf16[8,128,128]{2,1,0:T(8,128)(2,1)S(1)}, u32[]{:S(2)}, u32[]{:S(2)}) async-start(bf16[8,128,128]{2,1,0:T(8,128)(2,1)} %reshape.134), calls=%async_computation.1 | async-start | bytes 524288 | tf_op jit(solution)/shard_map/all_to_all | solution.py:68
  29.8 0.0 reduce-scatter.7.cloned.1.call-start
  29.8 0.0 copy-done
  29.8 0.3 convolution_bitcast_fusion
  30.2 1.1 copy.18
  31.2 11.3 %scatter_custom_fusion.1 = s32[1025]{0:T(1024)S(1)} fusion(s32[2048]{0:T(1024)S(1)} %bitcast.94, s32[2048]{0:T(1024)S(1)} %broadcast.53, s32[]{:T(128)} %constant.8.clone.1), kind=kCustom, calls=%fused_computation.38 | custom fusion | flops 2048 | bytes 4104 | tf_op jit(solution)/shard_map/scatter-add | solution.py:74
  42.6 0.0 all-to-all-done.1
  42.6 0.2 reshape.169
  42.8 11.6 %scatter_custom_fusion.3 = f32[1025,64]{1,0:T(8,128)S(1)} fusion(s32[2048]{0:T(1024)S(1)} %bitcast.95, f32[2048,64]{1,0:T(8,128)S(1)} %reshape.169, f32[]{:T(128)} %constant.2.clone.1), kind=kCustom, calls=%fused_computation.21 | custom fusion | flops 131072 | bytes 262404 | tf_op jit(solution)/shard_map/scatter-add | solution.py:73
  54.4 0.1 slice.110
  54.5 1.3 collective-permute-start.1
  55.8 0.1 slice.107
  55.9 3.0 %collective-permute-start = (bf16[1,32,512]{2,1,0:T(8,128)(2,1)S(1)}, bf16[1,32,512]{2,1,0:T(8,128)(2,1)S(1)}, u32[]{:S(2)}, u32[]{:S(2)}) collective-permute-start(bf16[1,32,512]{2,1,0:T(8,128)(2,1)S(1)} %slice.107), channel_id=1, source_target_pairs={{0,1},{1,2},{2,3},{3,4},{4,5},{5,6},{6,7},{8,9},{9,10},{10,11},{11... | collective-permute-start | bytes 98312 | tf_op jit(solution)/shard_map/ppermute | solution.py:20
  59.0 0.0 collective-permute-done.1
  59.0 0.1 concatenate.74
  59.1 0.7 collective-permute-done
  59.8 0.1 concatenate.72
  59.9 0.4 select_maximum_fusion
  60.3 0.1 pad_maximum_fusion
  60.4 0.2 fusion.22
  60.6 2.3 %fusion.21 = (bf16[4,32,8,64]{3,2,1,0:T(8,128)(2,1)S(1)}, bf16[4,32,8,64]{3,2,1,0:T(8,128)(2,1)S(1)}, bf16[4,32,8,64]{3,2,1,0:T(8,128)(2,1)S(1)}, bf16[4,32,8,64...) fusion(bf16[6,34,10,64]{3,2,1,0:T(8,128)(2,1)S(1)} %select_maxi, ...), kind=kLoop, calls=%fused_computation.42 | loop fusion | bytes 4980736 | tf_op jit(solution)/shard_map/slice | solution.py:39
  62.9 8.9 %concatenate.104 = bf16[1024,1728]{1,0:T(8,128)(2,1)} concatenate(bf16[1024,64]{1,0:T(8,128)(2,1)S(1)} %bitcast.69, bf16[1024,64]{1,0:T(8,128)(2,1)S(1)} %bitcast.68, bf16[1024,64]{1,0:T(8,128)(2,1)S(1)} %bitcast.67, bf16[1024,64]{1,0:T(8,128)(2,1)S(1)} %bitcast.66, bf16[1024,64]{1,0:T(8,128)(2,1)S(1)} %bitcast.64, bf16[1024,64]{1,0:T(8,128)(2,1)S(1)} %bitcast.65, ...), dimensions={1} | concatenate | bytes 7077888 | tf_op jit(solution)/shard_map/concatenate | solution.py:43
  71.8 3.4 %select_convert_fusion.1 = (bf16[1024,128]{1,0:T(8,128)(2,1)S(1)}, f32[1024,128]{1,0:T(8,128)S(1)}) fusion(pred[1024]{0:T(1024)(128)(4,1)S(1)} %slice_compare_fusion, bf16[1024,1728]{1,0:T(8,128)(2,1)} %concatenate.104, bf16[1728,128]{1,0:T(8,128)(2,1)} %param.9), kind=kOutput, calls=%fused_computation.19 | convolution fusion | flops 453771264 | bytes 4768768 | tf_op jit(solution)/shard_map/dot_general | solution.py:81
  75.2 2.3 %fusion.8 = f32[1728,128]{1,0:T(8,128)} fusion(bf16[1024,1728]{1,0:T(8,128)(2,1)S(1)} %copy-done.1, f32[1024,128]{1,0:T(8,128)S(1)} %bitcast.89, f32[1024,128]{1,0:T(8,128)S(1)} %get-tuple-element.34, pred[1024]{0:T(1024)(128)(4,1)S(1)} %slice_compare_fusion), kind=kOutput, calls=%fused_computation.23 | convolution fusion | flops 454295552 | bytes 5473280 | tf_op jit(solution)/shard_map/dot_general | solution.py:91
  77.5 0.0 reduce-scatter.7.cloned.1.call-update
  77.6 0.0 reduce-scatter.5.cloned.1.call-start
  77.6 0.2 copy.26
  77.8 0.2 reshape.136
  78.0 1.3 fusion.24
  79.3 0.0 reduce-scatter.5.cloned.1.call-update
  79.3 0.0 all-reduce.5.cloned.1.call-start
  79.4 32.1 %reduce-scatter.7.cloned.1.call-done = f32[432,128]{1,0:T(8,128)} async-done(((f32[1728,128]{1,0:T(8,128)}), f32[432,128]{1,0:T(8,128)}) %reduce-scatter.7.cloned.1.call-update) | async-done | bytes 221200
  111.4 30.6 %reduce-scatter.5.cloned.1.call-done = f32[256,256]{1,0:T(8,128)} async-done(((f32[1024,256]{1,0:T(8,128)}), f32[256,256]{1,0:T(8,128)}) %reduce-scatter.5.cloned.1.call-update) | async-done | bytes 262160 | tf_op jit(solution)/shard_map/reduce_scatter | solution.py:95
  142.1 0.0 all-reduce.5.cloned.1.call-update
  142.1 0.2 convolution_convert_fusion
  142.4 0.7 reshape.137
  143.0 56.2 %all-reduce.5.cloned.1.call-done = (f32[432,128]{1,0:T(8,128)}, f32[256,256]{1,0:T(8,128)}) async-done(((f32[432,128]{1,0:T(8,128)}, f32[256,256]{1,0:T(8,128)}), (f32[432,128]{1,0:T(8,128)}, f32[256,256]{1,0:T(8,128)})) %all-reduce.5.cloned.1.call-update) | async-done | bytes 483344 | tf_op jit(solution)/shard_map/psum | solution.py:92
  199.2 1.6 copy.29
  200.9 1.7 copy.30
  (12 shorter events, 0.1 us)
Async XLA Ops:
  7.2 22.7 %copy-start = (bf16[1024,256]{1,0:T(8,128)(2,1)S(1)}, bf16[1024,256]{1,0:T(8,128)(2,1)}, u32[]{:S(2)}) copy-start(bf16[1024,256]{1,0:T(8,128)(2,1)} %param.10) | copy-start | bytes 1572868
  7.2 22.7 %copy-start.3 = (bf16[1,2,16,4,256]{4,3,2,1,0:T(4,128)(2,1)S(1)}, bf16[1,2,16,4,256]{4,3,2,1,0:T(4,128)(2,1)}, u32[]{:S(2)}) copy-start(bf16[1,2,16,4,256]{4,3,2,1,0:T(4,128)(2,1)} %param.11) | copy-start | bytes 196612
  13.0 11.9 %all-to-all-start = ((s32[8,1,256]{2,1,0:T(1,128)}), s32[8,1,256]{2,1,0:T(1,128)S(1)}, u32[]{:S(2)}, u32[]{:S(2)}) async-start(s32[8,1,256]{2,1,0:T(1,128)} %bitcast.3), calls=%async_computation | async-start | bytes 16384 | tf_op jit(solution)/shard_map/all_to_all | solution.py:69
  24.9 17.7 %all-to-all-start.1 = ((bf16[8,128,128]{2,1,0:T(8,128)(2,1)}), bf16[8,128,128]{2,1,0:T(8,128)(2,1)S(1)}, u32[]{:S(2)}, u32[]{:S(2)}) async-start(bf16[8,128,128]{2,1,0:T(8,128)(2,1)} %reshape.134), calls=%async_computation.1 | async-start | bytes 524288 | tf_op jit(solution)/shard_map/all_to_all | solution.py:68
  29.8 81.7 %reduce-scatter.7.cloned.1.call-start = ((), (), s32[]{:S(2)}) async-start(), calls=%async_computation.5 | async-start | bytes 1105920
  54.5 4.5 %collective-permute-start.1 = (bf16[1,32,512]{2,1,0:T(8,128)(2,1)S(1)}, bf16[1,32,512]{2,1,0:T(8,128)(2,1)S(1)}, u32[]{:S(2)}, u32[]{:S(2)}) collective-permute-start(bf16[1,32,512]{2,1,0:T(8,128)(2,1)S(1)} %slice.110), channel_id=1, source_target_pairs={{1,0},{2,1},{3,2},{4,3},{5,4},{6,5},{7,6},{9,8},{10,9},{11,10},{12... | collective-permute-start | bytes 98312 | tf_op jit(solution)/shard_map/ppermute | solution.py:23
  55.9 3.9 %collective-permute-start = (bf16[1,32,512]{2,1,0:T(8,128)(2,1)S(1)}, bf16[1,32,512]{2,1,0:T(8,128)(2,1)S(1)}, u32[]{:S(2)}, u32[]{:S(2)}) collective-permute-start(bf16[1,32,512]{2,1,0:T(8,128)(2,1)S(1)} %slice.107), channel_id=1, source_target_pairs={{0,1},{1,2},{2,3},{3,4},{4,5},{5,6},{6,7},{8,9},{9,10},{10,11},{11... | collective-permute-start | bytes 98312 | tf_op jit(solution)/shard_map/ppermute | solution.py:20
  71.8 3.4 %copy-start.1 = (bf16[1024,1728]{1,0:T(8,128)(2,1)S(1)}, bf16[1024,1728]{1,0:T(8,128)(2,1)}, u32[]{:S(2)}) copy-start(bf16[1024,1728]{1,0:T(8,128)(2,1)} %concatenate.104) | copy-start | bytes 10616836
  71.8 3.4 %copy-start.2 = (f32[2,2,16,2,4,2,128]{6,5,4,3,2,1,0:T(2,128)S(1)}, f32[2,2,16,2,4,2,128]{6,5,4,3,2,1,0:T(2,128)}, u32[]{:S(2)}) copy-start(f32[2,2,16,2,4,2,128]{6,5,4,3,2,1,0:T(2,128)} %copy.18) | copy-start | bytes 1572868
  77.6 64.5 %reduce-scatter.5.cloned.1.call-start = ((), (), s32[]{:S(2)}) async-start(), calls=%async_computation.4 | async-start | bytes 1310720 | tf_op jit(solution)/shard_map/reduce_scatter | solution.py:95
  79.3 119.9 %all-reduce.5.cloned.1.call-start = ((), (), s32[]{:S(2)}) async-start(), calls=%async_computation.6 | async-start | bytes 966656 | tf_op jit(solution)/shard_map/psum | solution.py:92
Sparse Core Ops, SparseCore 0:
  77.7 33.7 reduce-scatter.6
  114.3 27.7 reduce-scatter.4
  144.7 54.5 all-reduce.4
where the time goes:
time: 210 us; the launch traced here: 209 us
  waiting for transfers between devices  120 us (57%)
  local copies, waits for them, and re-layouts  27.8 us (13%)
  other arithmetic  24.2 us (12%)
  starting transfers between devices  15.6 us (7%)
  between operations  14 us (7%)
  matrix products  7.56 us (4%)
    psum x1, waiting for transfers between devices, local(): total_conv, total_down = lax.psum((grad_conv, grad_down), 'tile')  56.2 us
    unnamed x4, waiting for transfers between devices  32.1 us
    reduce_scatter x1, waiting for transfers between devices, local(): lax.psum_scatter(total_down, 'sample', scatter_dimension=0, tiled=True)  30.6 us
    scatter-add x1, other arithmetic, local(): jnp.zeros((slab_size + 1, CIN), jnp.float32).at[targets].add(arrived)  11.6 us
    scatter-add x1, other arithmetic, local(): counts = jnp.zeros((slab_size + 1,), jnp.int32).at[targets].add(1)  11.3 us
    concatenate x1, local copies, waits for them, and re-layouts, stack_taps(): return jnp.concatenate(pieces, axis=-1).reshape(-1, 27 * CIN)  8.87 us
    all_to_all x1, starting transfers between devices, local(): lax.all_to_all(send_voxels, 'tile', split_axis=0, concat_axis=0, tiled=True)  6.33 us
    scatter x1, local copies, waits for them, and re-layouts, local(): jnp.full((tile_count * capacity,), slab_size, jnp.int32).at[slot_ids]  5.04 us
  transfers between devices with their start and end apart: 7, of which 5 were waited for; matrix products, arithmetic and copies ran while one was open for 10% of the time, Pallas kernels for 0%

commit v1 on v0

v1 whole, which is shorter than its diff:
```python
import functools

import jax
import jax.numpy as jnp
from jax import lax
from jax.experimental import pallas as pl
from jax.experimental.pallas import tpu as pltpu
from jax.sharding import PartitionSpec as P

CIN = 64
C1 = 128
C2 = 256
SX = 4
SY = 32
SZ = 8
PTS_DEV = 1024
TAPS = 27
CODED = CIN + 8
LAYER = SZ * SY // 2
BF16 = jnp.bfloat16
F32 = jnp.float32
I32 = jnp.int32
NT = (((1,), (1,)), ((), ()))
TN = (((0,), (0,)), ((), ()))
VMEM_LIMIT = 56 * 1024 * 1024


def in_vmem(count):
    return [pl.BlockSpec(memory_space=pltpu.VMEM)] * count


def call(body, outs, scratch=(), inputs=0):
    single = not isinstance(outs, (list, tuple))
    return pl.pallas_call(
        body,
        out_shape=outs,
        in_specs=in_vmem(inputs),
        out_specs=in_vmem(1)[0] if single else in_vmem(len(outs)),
        scratch_shapes=list(scratch),
        compiler_params=pltpu.CompilerParams(vmem_limit_bytes=VMEM_LIMIT),
    )


def target(index, k, count):
    if count & (count - 1) == 0:
        return index ^ k
    return (index + k) % count


def origin(index, k, count):
    if count & (count - 1) == 0:
        return index ^ k
    return (index - k + count) % count


def swap_core(value, tiles):
    return lax.ppermute(value, "tile", [(i, i ^ 1) for i in range(tiles)])


def send_column(value, k, tiles):
    chips = tiles // 2
    pairs = [(2 * i + c, 2 * target(i, k, chips) + c) for i in range(chips) for c in range(2)]
    return lax.ppermute(value, "tile", pairs)


def send_sample(value, k, samples):
    return lax.ppermute(value, "sample", [(i, target(i, k, samples)) for i in range(samples)])


def encode_kernel(capacity, points_ref, slot_ref, voxel_ref, out_ref):
    slot = slot_ref[...]
    voxel = voxel_ref[...]
    if capacity & (capacity - 1) == 0:
        owner = slot >> (capacity.bit_length() - 1)
    else:
        owner = jnp.floor((slot.astype(F32) + 0.5) * (1.0 / capacity)).astype(I32)
    layer = owner * SX + (voxel >> 8) + 1
    z = voxel & 7
    y = (voxel >> 3) & 31
    place = ((z * 16 + (y >> 1)) << 1) + (y & 1)
    row = lax.broadcasted_iota(I32, (8, slot.shape[1]), 0)
    codes = jnp.where(row == 0, layer, jnp.where(row == 1, place, 0))
    out_ref[0:CIN, :] = points_ref[...]
    out_ref[CIN:CODED, :] = codes.astype(F32).astype(BF16)


def scene_kernel(sources, samples, half_rows, *refs):
    coded = refs[:sources]
    conv_ref, down_ref, cot_ref, out_ref, mine_ref, other_ref, es_ref, pg_ref, wide_ref, tall_ref = refs[sources:]
    tile = lax.axis_index("tile")
    rows = 3 * LAYER
    row_iota = lax.broadcasted_iota(I32, (rows, PTS_DEV), 0)
    small_iota = lax.broadcasted_iota(I32, (32, PTS_DEV), 0)

    grid = jnp.zeros((rows, 4 * CIN), F32)
    counts = jnp.zeros((32, 32), F32)
    for ref in coded:
        codes = ref[CIN:CODED, :].astype(F32).astype(I32)
        layer = codes[0:1, :]
        place = codes[1:2, :]
        pair = (layer >> 1) - 2 * tile
        odd = layer & 1
        spot = place >> 1
        side = place & 1
        hot = (row_iota == pair * LAYER + spot).astype(F32).astype(BF16)
        group = odd * 2 + side
        features = ref[0:CIN, :]
        spread = jnp.concatenate(
            [features * (group == g).astype(F32).astype(BF16) for g in range(4)], axis=0
        )
        grid = grid + lax.dot_general(hot, spread, NT, preferred_element_type=F32)
        plane = (2 * pair + odd - 1) * SZ + (spot >> 4)
        hot_plane = (small_iota == plane).astype(F32).astype(BF16)
        hot_line = (small_iota == (spot & 15) * 2 + side).astype(F32).astype(BF16)
        counts = counts + lax.dot_general(hot_plane, hot_line, NT, preferred_element_type=F32)

    es_ref[...] = jnp.zeros_like(es_ref)
    pg_ref[...] = jnp.zeros_like(pg_ref)
    line = lax.broadcasted_iota(I32, (LAYER, 2 * CIN), 0) & 15
    lane = lax.broadcasted_iota(I32, (LAYER, 2 * CIN), 1)
    for x in range(SX + 2):
        both = grid[(x // 2) * LAYER : (x // 2 + 1) * LAYER, (x % 2) * 128 : (x % 2 + 1) * 128]
        turned = pltpu.roll(both, CIN, 1)
        before = jnp.where(line == 0, 0.0, pltpu.roll(turned, 1, 0))
        after = jnp.where(line == 15, 0.0, pltpu.roll(turned, LAYER - 1, 0))
        sides = jnp.where(lane < CIN, before, after)
        es_ref[x, 1 : SZ + 1, :, 0:128] = both.astype(BF16).reshape(SZ, 16, 128)
        es_ref[x, 1 : SZ + 1, :, 128:256] = sides.astype(BF16).reshape(SZ, 16, 128)

    full = SX * LAYER
    flags = (counts > 0.5).astype(F32).astype(BF16)
    row_plane = lax.broadcasted_iota(I32, (full, 32), 0) >> 4
    pick = (row_plane == lax.broadcasted_iota(I32, (full, 32), 1)).astype(F32).astype(BF16)
    lines = jnp.dot(pick, flags, preferred_element_type=F32)
    row_line = lax.broadcasted_iota(I32, (full, 32), 0) & 15
    lines = jnp.where(row_line == (lax.broadcasted_iota(I32, (full, 32), 1) >> 1), lines, 0.0).astype(BF16)
    expand = (
        (lax.broadcasted_iota(I32, (32, 256), 0) & 1) == (lax.broadcasted_iota(I32, (32, 256), 1) >> 7)
    ).astype(F32).astype(BF16)
    active = jnp.dot(lines, expand, preferred_element_type=F32) > 0.5

    zero_tap = jnp.zeros((CIN, C1), BF16)

    def tap(dx, dy, dz):
        start = ((dx * 3 + dy) * 3 + dz) * CIN
        return conv_ref[start : start + CIN, :]

    pre = jnp.zeros((full, 2 * C1), F32)
    for dx in range(3):
        for dz in range(3):
            weight = jnp.concatenate(
                [
                    jnp.concatenate([tap(dx, 1, dz), tap(dx, 0, dz)], axis=1),
                    jnp.concatenate([tap(dx, 2, dz), tap(dx, 1, dz)], axis=1),
                    jnp.concatenate([tap(dx, 0, dz), zero_tap], axis=1),
                    jnp.concatenate([zero_tap, tap(dx, 2, dz)], axis=1),
                ],
                axis=0,
            )
            part = es_ref[dx : dx + SX, dz : dz + SZ].reshape(full, 4 * CIN)
            pre = pre + jnp.dot(part, weight, preferred_element_type=F32)

    sigmoid = 1.0 / (1.0 + jnp.exp(-pre))
    act = jnp.where(active, pre * sigmoid, 0.0).astype(BF16)
    slope = jnp.where(active, sigmoid * (1.0 + pre * (1.0 - sigmoid)), 0.0)

    act = act.reshape(2, 2, 4, 2, 16, 2 * C1)
    slope = slope.reshape(2, 2, 4, 2, 16, 2 * C1)
    here = lax.broadcasted_iota(I32, (128, 128), 0)
    there = lax.broadcasted_iota(I32, (128, 128), 1)
    turn = ((here >> 6) * 64 + (here & 3) * 16 + ((here >> 2) & 15) == there).astype(F32).astype(BF16)
    cot = lax.dot_general(turn, cot_ref[...], TN, preferred_element_type=F32).astype(BF16)
    down = jnp.zeros((128, C2), F32)
    for ox in range(2):
        for oz in range(2):
            block = act[:, ox, :, oz].reshape(128, 2 * C1)
            first = (ox * 4 + oz) * C1
            second = first + 2 * C1
            weight = jnp.concatenate(
                [down_ref[first : first + C1, :], down_ref[second : second + C1, :]], axis=0
            )
            down = down + jnp.dot(block, weight, preferred_element_type=F32)
            grad = lax.dot_general(block, cot, TN, preferred_element_type=F32)
            wide_ref[first : first + C1, :] = grad[0:C1]
            wide_ref[second : second + C1, :] = grad[C1:]
            back = lax.dot_general(cot, weight, NT, preferred_element_type=F32)
            part = (back * slope[:, ox, :, oz].reshape(128, 2 * C1)).astype(BF16).reshape(2, 4, 16, 2 * C1)
            for u in range(2):
                for w in range(4):
                    pg_ref[2 * u + ox, 1 + 2 * w + oz] = part[u, w]
    out_ref[...] = jnp.dot(turn, down.astype(BF16), preferred_element_type=F32).astype(BF16)

    flipped = es_ref[:, 1 : SZ + 1].reshape((SX + 2) * LAYER, 4 * CIN).T
    for dz in range(3):
        part = pg_ref[:, 2 - dz : 2 - dz + SZ].reshape(full, 2 * C1)
        for dx in range(3):
            grad = jnp.dot(
                flipped[:, dx * LAYER : dx * LAYER + full], part, preferred_element_type=F32
            )
            sums = (
                grad[0:64, 128:256] + grad[128:192, 0:128],
                grad[0:64, 0:128] + grad[64:128, 128:256],
                grad[64:128, 0:128] + grad[192:256, 128:256],
            )
            for dy in range(3):
                start = ((dx * 3 + dy) * 3 + dz) * CIN
                tall_ref[start : start + CIN, :] = sums[dy]

    conv_rows = TAPS * CIN // samples
    down_rows = 8 * C1 // samples
    filler = 2 * half_rows - conv_rows - 2 * down_rows

    def leave(low_ref, high_ref):
        for s in range(samples):
            pieces = [
                tall_ref[s * conv_rows : (s + 1) * conv_rows, :],
                wide_ref[s * down_rows : (s + 1) * down_rows, 0:128],
                wide_ref[s * down_rows : (s + 1) * down_rows, 128:256],
            ]
            if filler:
                pieces.append(jnp.zeros((filler, 128), F32))
            chunk = jnp.concatenate(pieces, axis=0).astype(BF16)
            low_ref[s] = chunk[:half_rows]
            high_ref[s] = chunk[half_rows:]

    core = tile & 1

    @pl.when(core == 0)
    def _():
        leave(mine_ref, other_ref)

    @pl.when(core == 1)
    def _():
        leave(other_ref, mine_ref)


def share_samples_kernel(samples, mine_ref, got_ref, keep_ref, *send_refs):
    me = lax.axis_index("sample")
    keep_ref[...] = mine_ref[me].astype(F32) + got_ref[me].astype(F32)
    for k, ref in enumerate(send_refs, 1):
        to = target(me, k, samples)
        ref[...] = (mine_ref[to].astype(F32) + got_ref[to].astype(F32)).astype(BF16)


def share_column_kernel(samples, chips, rows, keep_ref, *refs):
    got = refs[: samples - 1]
    own_ref = refs[samples - 1]
    sends = refs[samples : samples + chips - 1]
    total_ref = refs[-1]
    total = keep_ref[...]
    for ref in got:
        total = total + ref[...].astype(F32)
    for i in range(chips):
        total_ref[i] = total[i * rows : (i + 1) * rows]
    me = lax.axis_index("tile") >> 1
    own_ref[...] = total_ref[me]
    for k, ref in enumerate(sends, 1):
        ref[...] = total_ref[target(me, k, chips)].astype(BF16)


def sum_kernel(own_ref, *refs):
    total = own_ref[...]
    for ref in refs[:-1]:
        total = total + ref[...].astype(F32)
    refs[-1][...] = total.astype(BF16)


def finish_kernel(chips, rows, conv_rows, down_rows, own_ref, got_ref, conv_ref, down_ref, hold_ref):
    tile = lax.axis_index("tile")
    core = tile & 1
    me = tile >> 1
    for k in range(chips):
        place = origin(me, k, chips)
        hold_ref[core * chips + place] = own_ref[k].astype(F32)
        hold_ref[(1 - core) * chips + place] = got_ref[k].astype(F32)
    whole = jnp.concatenate([hold_ref[i] for i in range(2 * chips)], axis=0)
    conv_ref[...] = whole[:conv_rows]
    down_ref[:, 0:128] = whole[conv_rows : conv_rows + down_rows]
    down_ref[:, 128:256] = whole[conv_rows + down_rows : conv_rows + 2 * down_rows]


def local(points, slot, voxel, conv_weight, down_weight, cotangent):
    tiles = lax.axis_size("tile")
    samples = lax.axis_size("sample")
    chips = tiles // 2
    capacity = 2 * (PTS_DEV // tiles)
    conv_rows = TAPS * CIN // samples
    down_rows = 8 * C1 // samples
    unit = 16 * chips
    total_rows = -(-(conv_rows + 2 * down_rows) // unit) * unit
    half_rows = total_rows // 2
    piece_rows = half_rows // chips

    shape = jax.ShapeDtypeStruct
    coded = call(functools.partial(encode_kernel, capacity), shape((CODED, PTS_DEV), BF16), inputs=3)(
        points[0].T, slot, voxel
    )
    near = [coded] + [send_column(coded, k, tiles) for k in range(1, chips)]
    gathered = near + [swap_core(value, tiles) for value in near]

    down, mine, other = call(
        functools.partial(scene_kernel, tiles, samples, half_rows),
        (
            shape((128, C2), BF16),
            shape((samples, half_rows, 128), BF16),
            shape((samples, half_rows, 128), BF16),
        ),
        scratch=(
            pltpu.VMEM((SX + 2, SZ + 2, 16, 4 * CIN), BF16),
            pltpu.VMEM((SX, SZ + 2, 16, 2 * C1), BF16),
            pltpu.VMEM((8 * C1, C2), F32),
            pltpu.VMEM((TAPS * CIN, C1), F32),
        ),
        inputs=tiles + 3,
    )(*gathered, conv_weight, down_weight, cotangent.reshape(128, C2))

    got = swap_core(other, tiles)
    keep, *sends = call(
        functools.partial(share_samples_kernel, samples),
        [shape((half_rows, 128), F32)] + [shape((half_rows, 128), BF16)] * (samples - 1),
        inputs=2,
    )(mine, got)
    got = [send_sample(value, k, samples) for k, value in enumerate(sends, 1)]
    own, *sends = call(
        functools.partial(share_column_kernel, samples, chips, piece_rows),
        [shape((piece_rows, 128), F32)] + [shape((piece_rows, 128), BF16)] * (chips - 1),
        scratch=(pltpu.VMEM((chips, piece_rows, 128), F32),),
        inputs=samples,
    )(keep, *got)
    got = [send_column(value, k, tiles) for k, value in enumerate(sends, 1)]
    piece = call(sum_kernel, shape((piece_rows, 128), BF16), inputs=chips)(own, *got)
    pieces = jnp.stack([piece] + [send_column(piece, k, tiles) for k in range(1, chips)])
    got = swap_core(pieces, tiles)
    conv_grad, down_grad = call(
        functools.partial(finish_kernel, chips, piece_rows, conv_rows, down_rows),
        (shape((conv_rows, C1), F32), shape((down_rows, C2), F32)),
        scratch=(pltpu.VMEM((tiles, piece_rows, 128), F32),),
        inputs=2,
    )(pieces, got)
    return (down.reshape(1, SX // 2, SY // 2, SZ // 2, C2), conv_grad, down_grad)


def solution(mesh):
    placed = (
        P("sample", "tile", None),
        P("sample", "tile"),
        P("sample", "tile"),
        P(),
        P(),
        P("sample", "tile", None, None, None),
    )
    return jax.shard_map(
        local,
        mesh=mesh,
        in_specs=placed,
        out_specs=(P("sample", "tile", None, None, None), P("sample", None), P("sample", None)),
        check_vma=False,
    )
```

time: 210 us -> 72 us (0.34)
  waiting for transfers between devices: 120 us -> 28 us
  other arithmetic: 24.2 us -> 0.8 us
  local copies, waits for them, and re-layouts: 27.8 us -> 5.18 us
  Pallas kernels: 0 us -> 18.3 us
  between operations: 14 us -> 0.73 us
  matrix products: 7.56 us -> 0 us
  starting transfers between devices: 15.6 us -> 18.6 us
    psum x1 -> x0, waiting for transfers between devices: 56.2 us -> none  [local(): total_conv, total_down = lax.psum((grad_conv, grad_down), 'tile')]
    unnamed x4 -> x0, waiting for transfers between devices: 32.1 us -> none
    reduce_scatter x1 -> x0, waiting for transfers between devices: 30.6 us -> none  [local(): lax.psum_scatter(total_down, 'sample', scatter_dimension=0, tiled=True)]
    ppermute x2 -> x18, waiting for transfers between devices: 0.69 us -> 28 us  [the longest x9 19.1 us: send_column(): return lax.ppermute(value, 'tile', pairs)]
    scatter-add x2 -> x0, other arithmetic: 22.9 us -> none  [the longest x1 11.6 us: local(): jnp.zeros((slab_size + 1, CIN), jnp.float32).at[targets].add(arrived)]
    pallas_call x0 -> x6, Pallas kernels: none -> 18.3 us  [the longest x1 9.54 us: local(): call(functools.partial(scene_kernel, tiles, samples, half_rows), (shape((...]
    ppermute x2 -> x18, starting transfers between devices: 4.32 us -> 18.6 us  [the longest x9 14.4 us: send_column(): return lax.ppermute(value, 'tile', pairs)]
    all_to_all x2 -> x0, starting transfers between devices: 11.2 us -> none  [the longest x1 6.33 us: local(): lax.all_to_all(send_voxels, 'tile', split_axis=0, concat_axis=0, tiled=True)]
  transfers between devices with their start and end apart: 7 -> 18, of which waited for: 5 -> 13; matrix products, arithmetic and copies ran while one was open for 10% -> 2% of each run, Pallas kernels for 0% -> 0%
where the time goes in v1:
time: 72 us; the launch traced here: 71.7 us
  waiting for transfers between devices  28 us (39%)
  starting transfers between devices  18.6 us (26%)
  Pallas kernels  18.3 us (25%)
  local copies, waits for them, and re-layouts  5.18 us (7%)
  other arithmetic  0.8 us (1%)
  between operations  0.73 us (1%)
    ppermute x9, waiting for transfers between devices, send_column(): return lax.ppermute(value, 'tile', pairs)  19.1 us
    ppermute x9, starting transfers between devices, send_column(): return lax.ppermute(value, 'tile', pairs)  14.4 us
    pallas_call x1, Pallas kernels, local(): call(functools.partial(scene_kernel, tiles, samples, half_rows), (shape((...  9.54 us
    ppermute x3, waiting for transfers between devices, send_sample(): lax.ppermute(value, 'sample', [(i, target(i, k, samples)) for i in range(...  5.96 us
    unnamed x36, local copies, waits for them, and re-layouts  3.88 us
    ppermute x3, starting transfers between devices, send_sample(): lax.ppermute(value, 'sample', [(i, target(i, k, samples)) for i in range(...  3.49 us
    ppermute x6, waiting for transfers between devices, swap_core(): return lax.ppermute(value, 'tile', [(i, i ^ 1) for i in range(tiles)])  2.97 us
    pallas_call x1, Pallas kernels, local(): call(functools.partial(share_samples_kernel, samples), [shape((half_rows,...  2.02 us
  transfers between devices with their start and end apart: 18, of which 13 were waited for; matrix products, arithmetic and copies ran while one was open for 2% of the time, Pallas kernels for 0%

profile of v1, /device:TPU:0, one launch (start us, length us, event | category | flops | bytes accessed | tf_op | source)
XLA Modules:
  0.0 71.7 jit_solution(14661826180786787803)
XLA Ops:
  0.6 1.6 %shard_map.85.refs_0_ = bf16[72,1024]{1,0:T(8,128)(2,1)} custom-call(bf16[64,1024]{1,0:T(8,128)(2,1)} %bitcast.7, s32[1,1024]{1,0:T(1,128)} %slot_ref.1, s32[1,1024]{1,0:T(1,128)} %voxel_ref.1), custom_call_target="tpu_custom_call" | custom-call | tf_op jit(solution)/shard_map/pallas_call | solution.py:295
  2.3 5.0 %collective-permute-start.2 = (bf16[72,1024]{1,0:T(8,128)(2,1)}, bf16[72,1024]{1,0:T(8,128)(2,1)S(1)}, u32[]{:S(2)}, u32[]{:S(2)}) collective-permute-start(bf16[72,1024]{1,0:T(8,128)(2,1)} %shard_map.85.refs_0_), channel_id=1, source_target_pairs={{0,6},{1,7},{2,4},{3,5},{4,2},{5,3},{6,0},{7,1},{8,14},{9,15},{10,... | collective-permute-start | bytes 442376 | tf_op jit(solution)/shard_map/ppermute | solution.py:63
  7.3 0.0 collective-permute-start.1
  7.3 0.6 collective-permute-start
  7.9 4.4 %collective-permute-done.2.refs_3_ = bf16[72,1024]{1,0:T(8,128)(2,1)S(1)} collective-permute-done((bf16[72,1024]{1,0:T(8,128)(2,1)}, bf16[72,1024]{1,0:T(8,128)(2,1)S(1)}, u32[]{:S(2)}, u32[]{:S(2)}) %collective-permute-start.2) | collective-permute-done | bytes 147488 | tf_op jit(solution)/shard_map/ppermute | solution.py:63
  12.3 0.0 collective-permute-start.6
  12.3 7.7 %collective-permute-done.1.refs_2_ = bf16[72,1024]{1,0:T(8,128)(2,1)S(1)} collective-permute-done((bf16[72,1024]{1,0:T(8,128)(2,1)}, bf16[72,1024]{1,0:T(8,128)(2,1)S(1)}, u32[]{:S(2)}, u32[]{:S(2)}) %collective-permute-start.1) | collective-permute-done | bytes 147488 | tf_op jit(solution)/shard_map/ppermute | solution.py:63
  20.0 0.0 collective-permute-start.5
  20.0 0.0 collective-permute-done.refs_1_
  20.0 0.0 copy-start.4
  20.0 0.5 collective-permute-start.4
  20.5 0.6 reshape.12.refs_10_
  21.2 0.2 collective-permute-done.5.refs_6_
  21.4 0.2 collective-permute-done.4.refs_5_
  21.6 0.3 copy-done.5
  21.9 0.1 copy-done.6
  21.9 0.1 copy-done.7
  22.1 0.7 copy-done.8
  22.7 9.5 %shard_map.86 = (bf16[128,256]{1,0:T(8,128)(2,1)}, bf16[4,480,128]{2,1,0:T(8,128)(2,1)}, bf16[4,480,128]{2,1,0:T(8,128)(2,1)}) custom-call(bf16[72,1024]{1,0:T(8,128)(2,1)} %shard_map.85.refs_0_, bf16[72,1024]{1,0:T(8,128)(2,1)} %copy-done.4, bf16[72,1024]{1,0:T(8,128)(2,1)} %copy-done.3, bf16[72,1024]{1,0:T(8,128)(2,1)} %copy-done.2, ...), custom_call_target="tpu_custom_call" | custom-call | tf_op jit(solution)/shard_map/pallas_call | solution.py:301
  32.3 0.2 collective-permute-start.7
  32.4 1.9 %collective-permute-done.7.got_ref = bf16[4,480,128]{2,1,0:T(8,128)(2,1)S(1)} collective-permute-done((bf16[4,480,128]{2,1,0:T(8,128)(2,1)}, bf16[4,480,128]{2,1,0:T(8,128)(2,1)S(1)}, u32[]{:S(2)}, u32[]{:S(2)}) %collective-permute-start.7) | collective-permute-done | bytes 491552 | tf_op jit(solution)/shard_map/ppermute | solution.py:57
  34.3 0.8 %copy-done = bf16[4,480,128]{2,1,0:T(8,128)(2,1)} copy-done((bf16[4,480,128]{2,1,0:T(8,128)(2,1)}, bf16[4,480,128]{2,1,0:T(8,128)(2,1)S(1)}, u32[]{:S(2)}) %copy-start) | copy-done | bytes 491544
  35.1 2.0 %shard_map.87 = (f32[480,128]{1,0:T(8,128)}, bf16[480,128]{1,0:T(8,128)(2,1)}, bf16[480,128]{1,0:T(8,128)(2,1)}, bf16[480,128]{1,0:T(8,128)(2,1)}) custom-call(bf16[4,480,128]{2,1,0:T(8,128)(2,1)} %get-tuple-element.17.mine_ref, bf16[4,480,128]{2,1,0:T(8,128)(2,1)} %copy-done), custom_call_target="tpu_custom_call" | custom-call | tf_op jit(solution)/shard_map/pallas_call | solution.py:318
  37.2 1.5 %collective-permute-start.8 = (bf16[480,128]{1,0:T(8,128)(2,1)}, bf16[480,128]{1,0:T(8,128)(2,1)S(1)}, u32[]{:S(2)}, u32[]{:S(2)}) collective-permute-start(bf16[480,128]{1,0:T(8,128)(2,1)} %get-tuple-element.20), channel_id=1, source_target_pairs={{0,8},{8,0},{16,24},{24,16},{1,9},{9,1},{17,25},{25,17},{2,10},{10... | collective-permute-start | bytes 368648 | tf_op jit(solution)/shard_map/ppermute | solution.py:67
  38.6 1.5 %collective-permute-start.9 = (bf16[480,128]{1,0:T(8,128)(2,1)}, bf16[480,128]{1,0:T(8,128)(2,1)S(1)}, u32[]{:S(2)}, u32[]{:S(2)}) collective-permute-start(bf16[480,128]{1,0:T(8,128)(2,1)} %get-tuple-element.21), channel_id=1, source_target_pairs={{0,16},{8,24},{16,0},{24,8},{1,17},{9,25},{17,1},{25,9},{2,18},{10... | collective-permute-start | bytes 368648 | tf_op jit(solution)/shard_map/ppermute | solution.py:67
  40.2 0.5 collective-permute-start.10
  40.6 2.3 %collective-permute-done.8.refs_0_ = bf16[480,128]{1,0:T(8,128)(2,1)S(1)} collective-permute-done((bf16[480,128]{1,0:T(8,128)(2,1)}, bf16[480,128]{1,0:T(8,128)(2,1)S(1)}, u32[]{:S(2)}, u32[]{:S(2)}) %collective-permute-start.8) | collective-permute-done | bytes 122912 | tf_op jit(solution)/shard_map/ppermute | solution.py:67
  42.9 3.7 %collective-permute-done.9.refs_1_ = bf16[480,128]{1,0:T(8,128)(2,1)S(1)} collective-permute-done((bf16[480,128]{1,0:T(8,128)(2,1)}, bf16[480,128]{1,0:T(8,128)(2,1)S(1)}, u32[]{:S(2)}, u32[]{:S(2)}) %collective-permute-start.9) | collective-permute-done | bytes 122912 | tf_op jit(solution)/shard_map/ppermute | solution.py:67
  46.6 0.6 copy-done.10
  47.2 0.1 copy-done.11
  47.3 1.8 %shard_map.88 = (f32[120,128]{1,0:T(8,128)}, bf16[120,128]{1,0:T(8,128)(2,1)}, bf16[120,128]{1,0:T(8,128)(2,1)}, bf16[120,128]{1,0:T(8,128)(2,1)}) custom-call(f32[480,128]{1,0:T(8,128)} %get-tuple-element.19.keep_ref, bf16[480,128]{1,0:T(8,128)(2,1)} %copy-done.9, bf16[480,128]{1,0:T(8,128)(2,1)} %copy-done.10, bf16[480,128]{1,0:T(8,128)(2,1)} %copy-done.11), custom_call_target="tpu_custom_call" | custom-call | tf_op jit(solution)/shard_map/pallas_call | solution.py:324
  49.2 3.1 %collective-permute-start.12 = (bf16[120,128]{1,0:T(8,128)(2,1)}, bf16[120,128]{1,0:T(8,128)(2,1)S(1)}, u32[]{:S(2)}, u32[]{:S(2)}) collective-permute-start(bf16[120,128]{1,0:T(8,128)(2,1)} %get-tuple-element.25), channel_id=1, source_target_pairs={{0,4},{1,5},{2,6},{3,7},{4,0},{5,1},{6,2},{7,3},{8,12},{9,13},{10,... | collective-permute-start | bytes 92168 | tf_op jit(solution)/shard_map/ppermute | solution.py:63
  52.2 1.3 %collective-permute-start.13 = (bf16[120,128]{1,0:T(8,128)(2,1)}, bf16[120,128]{1,0:T(8,128)(2,1)S(1)}, u32[]{:S(2)}, u32[]{:S(2)}) collective-permute-start(bf16[120,128]{1,0:T(8,128)(2,1)} %get-tuple-element.26), channel_id=1, source_target_pairs={{0,6},{1,7},{2,4},{3,5},{4,2},{5,3},{6,0},{7,1},{8,14},{9,15},{10,... | collective-permute-start | bytes 92168 | tf_op jit(solution)/shard_map/ppermute | solution.py:63
  53.5 0.8 %collective-permute-done.12.refs_1_ = bf16[120,128]{1,0:T(8,128)(2,1)S(1)} collective-permute-done((bf16[120,128]{1,0:T(8,128)(2,1)}, bf16[120,128]{1,0:T(8,128)(2,1)S(1)}, u32[]{:S(2)}, u32[]{:S(2)}) %collective-permute-start.12) | collective-permute-done | bytes 30752 | tf_op jit(solution)/shard_map/ppermute | solution.py:63
  54.3 3.8 %collective-permute-done.13.refs_2_ = bf16[120,128]{1,0:T(8,128)(2,1)S(1)} collective-permute-done((bf16[120,128]{1,0:T(8,128)(2,1)}, bf16[120,128]{1,0:T(8,128)(2,1)S(1)}, u32[]{:S(2)}, u32[]{:S(2)}) %collective-permute-start.13) | collective-permute-done | bytes 30752 | tf_op jit(solution)/shard_map/ppermute | solution.py:63
  58.1 0.6 copy-done.17
  58.7 1.5 %shard_map.89 = bf16[120,128]{1,0:T(8,128)(2,1)} custom-call(f32[120,128]{1,0:T(8,128)} %get-tuple-element.23.own_ref, bf16[120,128]{1,0:T(8,128)(2,1)} %copy-done.15, bf16[120,128]{1,0:T(8,128)(2,1)} %copy-done.16, bf16[120,128]{1,0:T(8,128)(2,1)} %copy-done.17), custom_call_target="tpu_custom_call" | custom-call | tf_op jit(solution)/shard_map/pallas_call | solution.py:331
  60.2 1.3 %collective-permute-start.16 = (bf16[120,128]{1,0:T(8,128)(2,1)}, bf16[120,128]{1,0:T(8,128)(2,1)S(1)}, u32[]{:S(2)}, u32[]{:S(2)}) collective-permute-start(bf16[120,128]{1,0:T(8,128)(2,1)} %shard_map.89), channel_id=1, source_target_pairs={{0,6},{1,7},{2,4},{3,5},{4,2},{5,3},{6,0},{7,1},{8,14},{9,15},{10,... | collective-permute-start | bytes 92168 | tf_op jit(solution)/shard_map/ppermute | solution.py:63
  61.5 3.1 %collective-permute-start.14 = (bf16[120,128]{1,0:T(8,128)(2,1)}, bf16[120,128]{1,0:T(8,128)(2,1)S(1)}, u32[]{:S(2)}, u32[]{:S(2)}) collective-permute-start(bf16[120,128]{1,0:T(8,128)(2,1)} %shard_map.89), channel_id=1, source_target_pairs={{0,2},{1,3},{2,0},{3,1},{4,6},{5,7},{6,4},{7,5},{8,10},{9,11},{10,... | collective-permute-start | bytes 92168 | tf_op jit(solution)/shard_map/ppermute | solution.py:63
  64.6 1.5 %collective-permute-done.16 = bf16[120,128]{1,0:T(8,128)(2,1)S(1)} collective-permute-done((bf16[120,128]{1,0:T(8,128)(2,1)}, bf16[120,128]{1,0:T(8,128)(2,1)S(1)}, u32[]{:S(2)}, u32[]{:S(2)}) %collective-permute-start.16) | collective-permute-done | bytes 30752 | tf_op jit(solution)/shard_map/ppermute | solution.py:63
  66.1 0.8 %collective-permute-done.15 = bf16[120,128]{1,0:T(8,128)(2,1)S(1)} collective-permute-done((bf16[120,128]{1,0:T(8,128)(2,1)}, bf16[120,128]{1,0:T(8,128)(2,1)S(1)}, u32[]{:S(2)}, u32[]{:S(2)}) %collective-permute-start.15) | collective-permute-done | bytes 30752 | tf_op jit(solution)/shard_map/ppermute | solution.py:63
  66.9 0.1 collective-permute-done.14
  67.0 0.8 %pad_maximum_fusion.own_ref = bf16[4,120,128]{2,1,0:T(8,128)(2,1)S(1)} fusion(bf16[1,120,128]{2,1,0:T(8,128)(2,1)S(1)} %bitcast.9, bf16[1,120,128]{2,1,0:T(8,128)(2,1)S(1)} %bitcast.10, bf16[1,120,128]{2,1,0:T(8,128)(2,1)S(1)} %bitcast.11, bf16[1,120,128]{2,1,0:T(8,128)(2,1)} %bitcast.8), kind=kLoop, calls=%fused_computation | loop fusion | flops 184320 | bytes 245760 | tf_op jit(solution)/shard_map/stack | solution.py:332
  67.8 0.1 collective-permute-start.17
  67.9 0.7 reshape.13
  68.6 0.7 collective-permute-done.17.got_ref
  69.2 0.6 copy-done.12
  69.9 1.8 %shard_map.90 = (f32[432,128]{1,0:T(8,128)}, f32[256,256]{1,0:T(8,128)}) custom-call(bf16[4,120,128]{2,1,0:T(8,128)(2,1)} %copy-done.1, bf16[4,120,128]{2,1,0:T(8,128)(2,1)} %copy-done.12), custom_call_target="tpu_custom_call" | custom-call | tf_op jit(solution)/shard_map/pallas_call | solution.py:334
  (33 shorter events, 0.1 us)
Async XLA Ops:
  0.6 19.9 %copy-start.13 = (bf16[1,2,16,4,256]{4,3,2,1,0:T(4,128)(2,1)S(1)}, bf16[1,2,16,4,256]{4,3,2,1,0:T(4,128)(2,1)}, u32[]{:S(2)}) copy-start(bf16[1,2,16,4,256]{4,3,2,1,0:T(4,128)(2,1)} %param.11) | copy-start | bytes 196612
  2.3 10.0 %collective-permute-start.2 = (bf16[72,1024]{1,0:T(8,128)(2,1)}, bf16[72,1024]{1,0:T(8,128)(2,1)S(1)}, u32[]{:S(2)}, u32[]{:S(2)}) collective-permute-start(bf16[72,1024]{1,0:T(8,128)(2,1)} %shard_map.85.refs_0_), channel_id=1, source_target_pairs={{0,6},{1,7},{2,4},{3,5},{4,2},{5,3},{6,0},{7,1},{8,14},{9,15},{10,... | collective-permute-start | bytes 442376 | tf_op jit(solution)/shard_map/ppermute | solution.py:63
  7.3 12.7 %collective-permute-start.1 = (bf16[72,1024]{1,0:T(8,128)(2,1)}, bf16[72,1024]{1,0:T(8,128)(2,1)S(1)}, u32[]{:S(2)}, u32[]{:S(2)}) collective-permute-start(bf16[72,1024]{1,0:T(8,128)(2,1)} %shard_map.85.refs_0_), channel_id=1, source_target_pairs={{0,4},{1,5},{2,6},{3,7},{4,0},{5,1},{6,2},{7,3},{8,12},{9,13},{10,... | collective-permute-start | bytes 442376 | tf_op jit(solution)/shard_map/ppermute | solution.py:63
  7.3 12.7 %collective-permute-start = (bf16[72,1024]{1,0:T(8,128)(2,1)}, bf16[72,1024]{1,0:T(8,128)(2,1)S(1)}, u32[]{:S(2)}, u32[]{:S(2)}) collective-permute-start(bf16[72,1024]{1,0:T(8,128)(2,1)} %shard_map.85.refs_0_), channel_id=1, source_target_pairs={{0,2},{1,3},{2,0},{3,1},{4,6},{5,7},{6,4},{7,5},{8,10},{9,11},{10,... | collective-permute-start | bytes 442376 | tf_op jit(solution)/shard_map/ppermute | solution.py:63
  7.9 13.3 %collective-permute-start.3 = (bf16[72,1024]{1,0:T(8,128)(2,1)}, bf16[72,1024]{1,0:T(8,128)(2,1)S(1)}, u32[]{:S(2)}, u32[]{:S(2)}) collective-permute-start(bf16[72,1024]{1,0:T(8,128)(2,1)} %shard_map.85.refs_0_), channel_id=1, source_target_pairs={{0,1},{1,0},{2,3},{3,2},{4,5},{5,4},{6,7},{7,6},{8,9},{9,8},{10,11... | collective-permute-start | bytes 442376 | tf_op jit(solution)/shard_map/ppermute | solution.py:57
  12.3 9.3 %copy-start.2 = (bf16[72,1024]{1,0:T(8,128)(2,1)}, bf16[72,1024]{1,0:T(8,128)(2,1)S(1)}, u32[]{:S(2)}) copy-start(bf16[72,1024]{1,0:T(8,128)(2,1)S(1)} %collective-permute-done.2.refs_3_) | copy-start | bytes 442372
  12.3 8.9 %collective-permute-start.6 = (bf16[72,1024]{1,0:T(8,128)(2,1)S(1)}, bf16[72,1024]{1,0:T(8,128)(2,1)S(1)}, u32[]{:S(2)}, u32[]{:S(2)}) collective-permute-start(bf16[72,1024]{1,0:T(8,128)(2,1)S(1)} %collective-permute-done.2.refs_3_), channel_id=1, source_target_pairs={{0,1},{1,0},{2,3},{3,2},{4,5},{5,4},{6,7},{7,6},{8,9},{9,8},{10,11... | collective-permute-start | bytes 442376 | tf_op jit(solution)/shard_map/ppermute | solution.py:57
  20.0 1.6 %copy-start.3 = (bf16[72,1024]{1,0:T(8,128)(2,1)}, bf16[72,1024]{1,0:T(8,128)(2,1)S(1)}, u32[]{:S(2)}) copy-start(bf16[72,1024]{1,0:T(8,128)(2,1)S(1)} %collective-permute-done.1.refs_2_) | copy-start | bytes 442372
  20.0 1.4 %collective-permute-start.5 = (bf16[72,1024]{1,0:T(8,128)(2,1)S(1)}, bf16[72,1024]{1,0:T(8,128)(2,1)S(1)}, u32[]{:S(2)}, u32[]{:S(2)}) collective-permute-start(bf16[72,1024]{1,0:T(8,128)(2,1)S(1)} %collective-permute-done.1.refs_2_), channel_id=1, source_target_pairs={{0,1},{1,0},{2,3},{3,2},{4,5},{5,4},{6,7},{7,6},{8,9},{9,8},{10,11... | collective-permute-start | bytes 442376 | tf_op jit(solution)/shard_map/ppermute | solution.py:57
  20.0 1.6 %copy-start.4 = (bf16[72,1024]{1,0:T(8,128)(2,1)}, bf16[72,1024]{1,0:T(8,128)(2,1)S(1)}, u32[]{:S(2)}) copy-start(bf16[72,1024]{1,0:T(8,128)(2,1)S(1)} %collective-permute-done.refs_1_) | copy-start | bytes 442372
  20.0 1.6 %collective-permute-start.4 = (bf16[72,1024]{1,0:T(8,128)(2,1)S(1)}, bf16[72,1024]{1,0:T(8,128)(2,1)S(1)}, u32[]{:S(2)}, u32[]{:S(2)}) collective-permute-start(bf16[72,1024]{1,0:T(8,128)(2,1)S(1)} %collective-permute-done.refs_1_), channel_id=1, source_target_pairs={{0,1},{1,0},{2,3},{3,2},{4,5},{5,4},{6,7},{7,6},{8,9},{9,8},{10,11... | collective-permute-start | bytes 442376 | tf_op jit(solution)/shard_map/ppermute | solution.py:57
  21.2 0.7 copy-start.5
  21.2 0.7 copy-start.6
  21.4 0.7 copy-start.7
  22.1 0.7 copy-start.8
  32.3 2.1 %collective-permute-start.7 = (bf16[4,480,128]{2,1,0:T(8,128)(2,1)}, bf16[4,480,128]{2,1,0:T(8,128)(2,1)S(1)}, u32[]{:S(2)}, u32[]{:S(2)}) collective-permute-start(bf16[4,480,128]{2,1,0:T(8,128)(2,1)} %get-tuple-element.18), channel_id=1, source_target_pairs={{0,1},{1,0},{2,3},{3,2},{4,5},{5,4},{6,7},{7,6},{8,9},{9,8},{10,11... | collective-permute-start | bytes 1474568 | tf_op jit(solution)/shard_map/ppermute | solution.py:57
  34.3 0.8 %copy-start = (bf16[4,480,128]{2,1,0:T(8,128)(2,1)}, bf16[4,480,128]{2,1,0:T(8,128)(2,1)S(1)}, u32[]{:S(2)}) copy-start(bf16[4,480,128]{2,1,0:T(8,128)(2,1)S(1)} %collective-permute-done.7.got_ref) | copy-start | bytes 1474564
  37.2 5.8 %collective-permute-start.8 = (bf16[480,128]{1,0:T(8,128)(2,1)}, bf16[480,128]{1,0:T(8,128)(2,1)S(1)}, u32[]{:S(2)}, u32[]{:S(2)}) collective-permute-start(bf16[480,128]{1,0:T(8,128)(2,1)} %get-tuple-element.20), channel_id=1, source_target_pairs={{0,8},{8,0},{16,24},{24,16},{1,9},{9,1},{17,25},{25,17},{2,10},{10... | collective-permute-start | bytes 368648 | tf_op jit(solution)/shard_map/ppermute | solution.py:67
  38.6 8.0 %collective-permute-start.9 = (bf16[480,128]{1,0:T(8,128)(2,1)}, bf16[480,128]{1,0:T(8,128)(2,1)S(1)}, u32[]{:S(2)}, u32[]{:S(2)}) collective-permute-start(bf16[480,128]{1,0:T(8,128)(2,1)} %get-tuple-element.21), channel_id=1, source_target_pairs={{0,16},{8,24},{16,0},{24,8},{1,17},{9,25},{17,1},{25,9},{2,18},{10... | collective-permute-start | bytes 368648 | tf_op jit(solution)/shard_map/ppermute | solution.py:67
  40.2 6.4 %collective-permute-start.10 = (bf16[480,128]{1,0:T(8,128)(2,1)}, bf16[480,128]{1,0:T(8,128)(2,1)S(1)}, u32[]{:S(2)}, u32[]{:S(2)}) collective-permute-start(bf16[480,128]{1,0:T(8,128)(2,1)} %get-tuple-element.22), channel_id=1, source_target_pairs={{0,24},{8,16},{16,8},{24,0},{1,25},{9,17},{17,9},{25,1},{2,26},{10... | collective-permute-start | bytes 368648 | tf_op jit(solution)/shard_map/ppermute | solution.py:67
  42.9 3.7 %copy-start.9 = (bf16[480,128]{1,0:T(8,128)(2,1)}, bf16[480,128]{1,0:T(8,128)(2,1)S(1)}, u32[]{:S(2)}) copy-start(bf16[480,128]{1,0:T(8,128)(2,1)S(1)} %collective-permute-done.8.refs_0_) | copy-start | bytes 368644
  46.6 0.6 copy-start.10
  46.6 0.7 copy-start.11
  49.1 4.4 %collective-permute-start.11 = (bf16[120,128]{1,0:T(8,128)(2,1)}, bf16[120,128]{1,0:T(8,128)(2,1)S(1)}, u32[]{:S(2)}, u32[]{:S(2)}) collective-permute-start(bf16[120,128]{1,0:T(8,128)(2,1)} %get-tuple-element.24), channel_id=1, source_target_pairs={{0,2},{1,3},{2,0},{3,1},{4,6},{5,7},{6,4},{7,5},{8,10},{9,11},{10,... | collective-permute-start | bytes 92168 | tf_op jit(solution)/shard_map/ppermute | solution.py:63
  49.2 5.2 %collective-permute-start.12 = (bf16[120,128]{1,0:T(8,128)(2,1)}, bf16[120,128]{1,0:T(8,128)(2,1)S(1)}, u32[]{:S(2)}, u32[]{:S(2)}) collective-permute-start(bf16[120,128]{1,0:T(8,128)(2,1)} %get-tuple-element.25), channel_id=1, source_target_pairs={{0,4},{1,5},{2,6},{3,7},{4,0},{5,1},{6,2},{7,3},{8,12},{9,13},{10,... | collective-permute-start | bytes 92168 | tf_op jit(solution)/shard_map/ppermute | solution.py:63
  52.2 5.9 %collective-permute-start.13 = (bf16[120,128]{1,0:T(8,128)(2,1)}, bf16[120,128]{1,0:T(8,128)(2,1)S(1)}, u32[]{:S(2)}, u32[]{:S(2)}) collective-permute-start(bf16[120,128]{1,0:T(8,128)(2,1)} %get-tuple-element.26), channel_id=1, source_target_pairs={{0,6},{1,7},{2,4},{3,5},{4,2},{5,3},{6,0},{7,1},{8,14},{9,15},{10,... | collective-permute-start | bytes 92168 | tf_op jit(solution)/shard_map/ppermute | solution.py:63
  53.5 4.6 %copy-start.15 = (bf16[120,128]{1,0:T(8,128)(2,1)}, bf16[120,128]{1,0:T(8,128)(2,1)S(1)}, u32[]{:S(2)}) copy-start(bf16[120,128]{1,0:T(8,128)(2,1)S(1)} %collective-permute-done.11.refs_0_) | copy-start | bytes 92164
  54.3 3.8 %copy-start.16 = (bf16[120,128]{1,0:T(8,128)(2,1)}, bf16[120,128]{1,0:T(8,128)(2,1)S(1)}, u32[]{:S(2)}) copy-start(bf16[120,128]{1,0:T(8,128)(2,1)S(1)} %collective-permute-done.12.refs_1_) | copy-start | bytes 92164
  58.1 0.6 copy-start.17
  60.2 5.9 %collective-permute-start.16 = (bf16[120,128]{1,0:T(8,128)(2,1)}, bf16[120,128]{1,0:T(8,128)(2,1)S(1)}, u32[]{:S(2)}, u32[]{:S(2)}) collective-permute-start(bf16[120,128]{1,0:T(8,128)(2,1)} %shard_map.89), channel_id=1, source_target_pairs={{0,6},{1,7},{2,4},{3,5},{4,2},{5,3},{6,0},{7,1},{8,14},{9,15},{10,... | collective-permute-start | bytes 92168 | tf_op jit(solution)/shard_map/ppermute | solution.py:63
  61.5 5.4 %collective-permute-start.15 = (bf16[120,128]{1,0:T(8,128)(2,1)}, bf16[120,128]{1,0:T(8,128)(2,1)S(1)}, u32[]{:S(2)}, u32[]{:S(2)}) collective-permute-start(bf16[120,128]{1,0:T(8,128)(2,1)} %shard_map.89), channel_id=1, source_target_pairs={{0,4},{1,5},{2,6},{3,7},{4,0},{5,1},{6,2},{7,3},{8,12},{9,13},{10,... | collective-permute-start | bytes 92168 | tf_op jit(solution)/shard_map/ppermute | solution.py:63
  61.5 5.5 %collective-permute-start.14 = (bf16[120,128]{1,0:T(8,128)(2,1)}, bf16[120,128]{1,0:T(8,128)(2,1)S(1)}, u32[]{:S(2)}, u32[]{:S(2)}) collective-permute-start(bf16[120,128]{1,0:T(8,128)(2,1)} %shard_map.89), channel_id=1, source_target_pairs={{0,2},{1,3},{2,0},{3,1},{4,6},{5,7},{6,4},{7,5},{8,10},{9,11},{10,... | collective-permute-start | bytes 92168 | tf_op jit(solution)/shard_map/ppermute | solution.py:63
  67.0 0.9 %copy-start.14 = (bf16[128,256]{1,0:T(8,128)(2,1)S(1)}, bf16[128,256]{1,0:T(8,128)(2,1)}, u32[]{:S(2)}) copy-start(bf16[128,256]{1,0:T(8,128)(2,1)} %get-tuple-element.16) | copy-start | bytes 196612
  67.8 1.4 %copy-start.1 = (bf16[4,120,128]{2,1,0:T(8,128)(2,1)}, bf16[4,120,128]{2,1,0:T(8,128)(2,1)S(1)}, u32[]{:S(2)}) copy-start(bf16[4,120,128]{2,1,0:T(8,128)(2,1)S(1)} %pad_maximum_fusion.own_ref) | copy-start | bytes 368644
  67.8 1.4 %collective-permute-start.17 = (bf16[4,120,128]{2,1,0:T(8,128)(2,1)S(1)}, bf16[4,120,128]{2,1,0:T(8,128)(2,1)S(1)}, u32[]{:S(2)}, u32[]{:S(2)}) collective-permute-start(bf16[4,120,128]{2,1,0:T(8,128)(2,1)S(1)} %pad_maximum_fusion.own_ref), channel_id=1, source_target_pairs={{0,1},{1,0},{2,3},{3,2},{4,5},{5,4},{6,7},{7,6},{8,9},{9,8},{10,11... | collective-permute-start | bytes 368648 | tf_op jit(solution)/shard_map/ppermute | solution.py:57
  69.2 0.7 copy-start.12

commit v2 on v1

--- a/solution.py
+++ b/solution.py
@@ -22,7 +22,7 @@
 I32 = jnp.int32
 NT = (((1,), (1,)), ((), ()))
 TN = (((0,), (0,)), ((), ()))
-VMEM_LIMIT = 56 * 1024 * 1024
+VMEM_LIMIT = 24 * 1024 * 1024
 
 
 def in_vmem(count):
@@ -31,7 +31,7 @@
 
 def call(body, outs, scratch=(), inputs=0):
     single = not isinstance(outs, (list, tuple))
-    return pl.pallas_call(
+    kernel = pl.pallas_call(
         body,
         out_shape=outs,
         in_specs=in_vmem(inputs),
@@ -39,6 +39,7 @@
         scratch_shapes=list(scratch),
         compiler_params=pltpu.CompilerParams(vmem_limit_bytes=VMEM_LIMIT),
     )
+    return lambda *args: kernel(*[pltpu.with_memory_space_constraint(a, pltpu.VMEM) for a in args])
 
 
 def target(index, k, count):
@@ -291,7 +292,7 @@
     half_rows = total_rows // 2
     piece_rows = half_rows // chips
 
-    shape = jax.ShapeDtypeStruct
+    shape = pltpu.VMEM
     coded = call(functools.partial(encode_kernel, capacity), shape((CODED, PTS_DEV), BF16), inputs=3)(
         points[0].T, slot, voxel
     )
@@ -333,7 +334,10 @@
     got = swap_core(pieces, tiles)
     conv_grad, down_grad = call(
         functools.partial(finish_kernel, chips, piece_rows, conv_rows, down_rows),
-        (shape((conv_rows, C1), F32), shape((down_rows, C2), F32)),
+        (
+            jax.ShapeDtypeStruct((conv_rows, C1), F32),
+            jax.ShapeDtypeStruct((down_rows, C2), F32),
+        ),
         scratch=(pltpu.VMEM((tiles, piece_rows, 128), F32),),
         inputs=2,
     )(pieces, got)

time: 72 us -> 60.7 us (0.84)
  Pallas kernels: 18.3 us -> 7.96 us
  other arithmetic: 0.8 us -> 0.02 us
    pallas_call x6, Pallas kernels: 18.3 us -> 7.96 us  [call(): kernel(*[pltpu.with_memory_space_constraint(a, pltpu.VMEM) for a in args])]
    another operation x1, other arithmetic: 0.8 us -> 0.02 us  [local(): jnp.stack([piece] + [send_column(piece, k, tiles) for k in range(1, chips)])]
    unnamed x36 -> x12, local copies, waits for them, and re-layouts: 3.88 us -> 4.33 us
  transfers between devices with their start and end apart: 18 -> 18, of which waited for: 13 -> 13; matrix products, arithmetic and copies ran while one was open for 2% -> 1% of each run, Pallas kernels for 0% -> 0%
where the time goes in v2:
time: 60.7 us; the launch traced here: 60.4 us
  waiting for transfers between devices  27.5 us (45%)
  starting transfers between devices  19.2 us (32%)
  Pallas kernels  7.96 us (13%)
  local copies, waits for them, and re-layouts  5 us (8%)
  between operations  0.72 us (1%)
    ppermute x9, waiting for transfers between devices, send_column(): return lax.ppermute(value, 'tile', pairs)  18.4 us
    ppermute x9, starting transfers between devices, send_column(): return lax.ppermute(value, 'tile', pairs)  14.7 us
    pallas_call x6, Pallas kernels, call(): kernel(*[pltpu.with_memory_space_constraint(a, pltpu.VMEM) for a in args])  7.96 us
    ppermute x3, waiting for transfers between devices, send_sample(): lax.ppermute(value, 'sample', [(i, target(i, k, samples)) for i in range(...  5.9 us
    unnamed x12, local copies, waits for them, and re-layouts  4.33 us
    ppermute x3, starting transfers between devices, send_sample(): lax.ppermute(value, 'sample', [(i, target(i, k, samples)) for i in range(...  3.55 us
    ppermute x6, waiting for transfers between devices, swap_core(): return lax.ppermute(value, 'tile', [(i, i ^ 1) for i in range(tiles)])  3.24 us
  transfers between devices with their start and end apart: 18, of which 13 were waited for; matrix products, arithmetic and copies ran while one was open for 1% of the time, Pallas kernels for 0%

profile of v2, /device:TPU:0, one launch (start us, length us, event | category | flops | bytes accessed | tf_op | source)
XLA Modules:
  0.0 60.4 jit_solution(16427889321217770810)
XLA Ops:
  0.6 0.0 copy-start.2
  0.6 0.9 %copy-done.2 = bf16[1,1024,64]{1,2,0:T(8,128)(2,1)S(1)} copy-done((bf16[1,1024,64]{1,2,0:T(8,128)(2,1)S(1)}, bf16[1,1024,64]{1,2,0:T(8,128)(2,1)}, u32[]{:S(2)}) %copy-start.2) | copy-done | bytes 131096
  1.5 0.7 %copy-done.3 = s32[1,1024]{1,0:T(1,128)S(1)} copy-done((s32[1,1024]{1,0:T(1,128)S(1)}, s32[1,1024]{1,0:T(1,128)}, u32[]{:S(2)}) %copy-start.3) | copy-done | bytes 4120
  2.2 0.7 %copy-done.4 = s32[1,1024]{1,0:T(1,128)S(1)} copy-done((s32[1,1024]{1,0:T(1,128)S(1)}, s32[1,1024]{1,0:T(1,128)}, u32[]{:S(2)}) %copy-start.4) | copy-done | bytes 4120
  2.9 5.1 %collective-permute-start.2 = (bf16[72,1024]{1,0:T(8,128)(2,1)S(1)}, bf16[72,1024]{1,0:T(8,128)(2,1)S(1)}, u32[]{:S(2)}, u32[]{:S(2)}) collective-permute-start(bf16[72,1024]{1,0:T(8,128)(2,1)S(1)} %shard_map.85.refs_0_), channel_id=1, source_target_pairs={{0,6},{1,7},{2,4},{3,5},{4,2},{5,3},{6,0},{7,1},{8,14},{9,15},{10,... | collective-permute-start | bytes 442376 | tf_op jit(solution)/shard_map/ppermute | solution.py:64
  8.1 0.0 collective-permute-start.1
  8.1 0.6 %collective-permute-start = (bf16[72,1024]{1,0:T(8,128)(2,1)S(1)}, bf16[72,1024]{1,0:T(8,128)(2,1)S(1)}, u32[]{:S(2)}, u32[]{:S(2)}) collective-permute-start(bf16[72,1024]{1,0:T(8,128)(2,1)S(1)} %shard_map.85.refs_0_), channel_id=1, source_target_pairs={{0,2},{1,3},{2,0},{3,1},{4,6},{5,7},{6,4},{7,5},{8,10},{9,11},{10,... | collective-permute-start | bytes 442376 | tf_op jit(solution)/shard_map/ppermute | solution.py:64
  8.7 0.0 collective-permute-start.3
  8.7 4.1 %collective-permute-done.2.refs_3_ = bf16[72,1024]{1,0:T(8,128)(2,1)S(1)} collective-permute-done((bf16[72,1024]{1,0:T(8,128)(2,1)S(1)}, bf16[72,1024]{1,0:T(8,128)(2,1)S(1)}, u32[]{:S(2)}, u32[]{:S(2)}) %collective-permute-start.2) | collective-permute-done | bytes 147488 | tf_op jit(solution)/shard_map/ppermute | solution.py:64
  12.8 0.0 collective-permute-start.6
  12.8 7.7 %collective-permute-done.1.refs_2_ = bf16[72,1024]{1,0:T(8,128)(2,1)S(1)} collective-permute-done((bf16[72,1024]{1,0:T(8,128)(2,1)S(1)}, bf16[72,1024]{1,0:T(8,128)(2,1)S(1)}, u32[]{:S(2)}, u32[]{:S(2)}) %collective-permute-start.1) | collective-permute-done | bytes 147488 | tf_op jit(solution)/shard_map/ppermute | solution.py:64
  20.5 0.0 collective-permute-start.5
  20.5 0.0 collective-permute-done.refs_1_
  20.5 0.5 collective-permute-start.4
  21.0 0.0 copy-done.5
  21.1 0.0 collective-permute-done.3.refs_4_
  21.1 0.0 collective-permute-done.6.refs_7_
  21.1 0.8 %collective-permute-done.5.refs_6_ = bf16[72,1024]{1,0:T(8,128)(2,1)S(1)} collective-permute-done((bf16[72,1024]{1,0:T(8,128)(2,1)S(1)}, bf16[72,1024]{1,0:T(8,128)(2,1)S(1)}, u32[]{:S(2)}, u32[]{:S(2)}) %collective-permute-start.5) | collective-permute-done | bytes 147488 | tf_op jit(solution)/shard_map/ppermute | solution.py:58
  21.9 0.2 collective-permute-done.4.refs_5_
  22.1 1.0 %copy-done = bf16[1024,256]{1,0:T(8,128)(2,1)S(1)} copy-done((bf16[1024,256]{1,0:T(8,128)(2,1)S(1)}, bf16[1024,256]{1,0:T(8,128)(2,1)}, u32[]{:S(2)}) %copy-start) | copy-done | bytes 524312
  23.2 1.0 %copy-done.1 = bf16[1728,128]{1,0:T(8,128)(2,1)S(1)} copy-done((bf16[1728,128]{1,0:T(8,128)(2,1)S(1)}, bf16[1728,128]{1,0:T(8,128)(2,1)}, u32[]{:S(2)}) %copy-start.1) | copy-done | bytes 442392
  24.2 6.9 %shard_map.86 = (bf16[128,256]{1,0:T(8,128)(2,1)S(1)}, bf16[4,480,128]{2,1,0:T(8,128)(2,1)S(1)}, bf16[4,480,128]{2,1,0:T(8,128)(2,1)S(1)}) custom-call(bf16[72,1024]{1,0:T(8,128)(2,1)S(1)} %shard_map.85.refs_0_, bf16[72,1024]{1,0:T(8,128)(2,1)S(1)} %collective-permute-done.refs_1_, bf16[72,1024]{1,0:T(8,128)(2,1)S(1)} %collective-permute-done.1.refs_2_, ...), custom_call_target="tpu_custom_call" | custom-call | tf_op jit(solution)/shard_map/pallas_call | solution.py:42
  31.1 0.4 collective-permute-start.7
  31.5 1.5 %collective-permute-done.7.got_ref = bf16[4,480,128]{2,1,0:T(8,128)(2,1)S(1)} collective-permute-done((bf16[4,480,128]{2,1,0:T(8,128)(2,1)S(1)}, bf16[4,480,128]{2,1,0:T(8,128)(2,1)S(1)}, u32[]{:S(2)}, u32[]{:S(2)}) %collective-permute-start.7) | collective-permute-done | bytes 491552 | tf_op jit(solution)/shard_map/ppermute | solution.py:58
  33.0 0.1 shard_map.87
  33.1 1.6 %collective-permute-start.8 = (bf16[480,128]{1,0:T(8,128)(2,1)S(1)}, bf16[480,128]{1,0:T(8,128)(2,1)S(1)}, u32[]{:S(2)}, u32[]{:S(2)}) collective-permute-start(bf16[480,128]{1,0:T(8,128)(2,1)S(1)} %get-tuple-element.20), channel_id=1, source_target_pairs={{0,8},{8,0},{16,24},{24,16},{1,9},{9,1},{17,25},{25,17},{2,10},{10... | collective-permute-start | bytes 368648 | tf_op jit(solution)/shard_map/ppermute | solution.py:68
  34.7 1.5 %collective-permute-start.9 = (bf16[480,128]{1,0:T(8,128)(2,1)S(1)}, bf16[480,128]{1,0:T(8,128)(2,1)S(1)}, u32[]{:S(2)}, u32[]{:S(2)}) collective-permute-start(bf16[480,128]{1,0:T(8,128)(2,1)S(1)} %get-tuple-element.21), channel_id=1, source_target_pairs={{0,16},{8,24},{16,0},{24,8},{1,17},{9,25},{17,1},{25,9},{2,18},{10... | collective-permute-start | bytes 368648 | tf_op jit(solution)/shard_map/ppermute | solution.py:68
  36.2 0.5 collective-permute-start.10
  36.7 2.2 %collective-permute-done.8.refs_0_ = bf16[480,128]{1,0:T(8,128)(2,1)S(1)} collective-permute-done((bf16[480,128]{1,0:T(8,128)(2,1)S(1)}, bf16[480,128]{1,0:T(8,128)(2,1)S(1)}, u32[]{:S(2)}, u32[]{:S(2)}) %collective-permute-start.8) | collective-permute-done | bytes 122912 | tf_op jit(solution)/shard_map/ppermute | solution.py:68
  38.9 3.7 %collective-permute-done.9.refs_1_ = bf16[480,128]{1,0:T(8,128)(2,1)S(1)} collective-permute-done((bf16[480,128]{1,0:T(8,128)(2,1)S(1)}, bf16[480,128]{1,0:T(8,128)(2,1)S(1)}, u32[]{:S(2)}, u32[]{:S(2)}) %collective-permute-start.9) | collective-permute-done | bytes 122912 | tf_op jit(solution)/shard_map/ppermute | solution.py:68
  42.6 0.0 collective-permute-done.10.refs_2_
  42.6 0.1 shard_map.88
  42.7 0.1 collective-permute-start.11
  42.7 3.1 %collective-permute-start.12 = (bf16[120,128]{1,0:T(8,128)(2,1)S(1)}, bf16[120,128]{1,0:T(8,128)(2,1)S(1)}, u32[]{:S(2)}, u32[]{:S(2)}) collective-permute-start(bf16[120,128]{1,0:T(8,128)(2,1)S(1)} %get-tuple-element.25), channel_id=1, source_target_pairs={{0,4},{1,5},{2,6},{3,7},{4,0},{5,1},{6,2},{7,3},{8,12},{9,13},{10,... | collective-permute-start | bytes 92168 | tf_op jit(solution)/shard_map/ppermute | solution.py:64
  45.8 1.3 %collective-permute-start.13 = (bf16[120,128]{1,0:T(8,128)(2,1)S(1)}, bf16[120,128]{1,0:T(8,128)(2,1)S(1)}, u32[]{:S(2)}, u32[]{:S(2)}) collective-permute-start(bf16[120,128]{1,0:T(8,128)(2,1)S(1)} %get-tuple-element.26), channel_id=1, source_target_pairs={{0,6},{1,7},{2,4},{3,5},{4,2},{5,3},{6,0},{7,1},{8,14},{9,15},{10,... | collective-permute-start | bytes 92168 | tf_op jit(solution)/shard_map/ppermute | solution.py:64
  47.1 0.0 collective-permute-done.11.refs_0_
  47.1 0.6 collective-permute-done.12.refs_1_
  47.7 3.8 %collective-permute-done.13.refs_2_ = bf16[120,128]{1,0:T(8,128)(2,1)S(1)} collective-permute-done((bf16[120,128]{1,0:T(8,128)(2,1)S(1)}, bf16[120,128]{1,0:T(8,128)(2,1)S(1)}, u32[]{:S(2)}, u32[]{:S(2)}) %collective-permute-start.13) | collective-permute-done | bytes 30752 | tf_op jit(solution)/shard_map/ppermute | solution.py:64
  51.5 1.4 %collective-permute-start.16 = (bf16[120,128]{1,0:T(8,128)(2,1)S(1)}, bf16[120,128]{1,0:T(8,128)(2,1)S(1)}, u32[]{:S(2)}, u32[]{:S(2)}) collective-permute-start(bf16[120,128]{1,0:T(8,128)(2,1)S(1)} %shard_map.89), channel_id=1, source_target_pairs={{0,6},{1,7},{2,4},{3,5},{4,2},{5,3},{6,0},{7,1},{8,14},{9,15},{10,... | collective-permute-start | bytes 92168 | tf_op jit(solution)/shard_map/ppermute | solution.py:64
  52.9 0.0 collective-permute-start.15
  52.9 3.1 %collective-permute-start.14 = (bf16[120,128]{1,0:T(8,128)(2,1)S(1)}, bf16[120,128]{1,0:T(8,128)(2,1)S(1)}, u32[]{:S(2)}, u32[]{:S(2)}) collective-permute-start(bf16[120,128]{1,0:T(8,128)(2,1)S(1)} %shard_map.89), channel_id=1, source_target_pairs={{0,2},{1,3},{2,0},{3,1},{4,6},{5,7},{6,4},{7,5},{8,10},{9,11},{10,... | collective-permute-start | bytes 92168 | tf_op jit(solution)/shard_map/ppermute | solution.py:64
  56.0 1.3 %collective-permute-done.16 = bf16[120,128]{1,0:T(8,128)(2,1)S(1)} collective-permute-done((bf16[120,128]{1,0:T(8,128)(2,1)S(1)}, bf16[120,128]{1,0:T(8,128)(2,1)S(1)}, u32[]{:S(2)}, u32[]{:S(2)}) %collective-permute-start.16) | collective-permute-done | bytes 30752 | tf_op jit(solution)/shard_map/ppermute | solution.py:64
  57.3 0.8 %collective-permute-done.15 = bf16[120,128]{1,0:T(8,128)(2,1)S(1)} collective-permute-done((bf16[120,128]{1,0:T(8,128)(2,1)S(1)}, bf16[120,128]{1,0:T(8,128)(2,1)S(1)}, u32[]{:S(2)}, u32[]{:S(2)}) %collective-permute-start.15) | collective-permute-done | bytes 30752 | tf_op jit(solution)/shard_map/ppermute | solution.py:64
  58.0 0.1 collective-permute-done.14
  58.2 0.1 collective-permute-start.17
  58.3 0.7 %reshape.13 = bf16[1,2,16,4,256]{4,3,2,1,0:T(4,128)(2,1)} reshape(bf16[128,256]{1,0:T(8,128)(2,1)S(1)} %get-tuple-element.16) | data formatting | bytes 131072 | tf_op jit(solution)/shard_map/reshape | solution.py:344
  58.9 0.7 %collective-permute-done.17.got_ref = bf16[4,120,128]{2,1,0:T(8,128)(2,1)S(1)} collective-permute-done((bf16[4,120,128]{2,1,0:T(8,128)(2,1)S(1)}, bf16[4,120,128]{2,1,0:T(8,128)(2,1)S(1)}, u32[]{:S(2)}, u32[]{:S(2)}) %collective-permute-start.17) | collective-permute-done | bytes 122912 | tf_op jit(solution)/shard_map/ppermute | solution.py:58
  59.6 0.8 %shard_map.90 = (f32[432,128]{1,0:T(8,128)}, f32[256,256]{1,0:T(8,128)}) custom-call(bf16[4,120,128]{2,1,0:T(8,128)(2,1)S(1)} %pad_maximum_fusion.own_ref, bf16[4,120,128]{2,1,0:T(8,128)(2,1)S(1)} %collective-permute-done.17.got_ref), custom_call_target="tpu_custom_call" | custom-call | tf_op jit(solution)/shard_map/pallas_call | solution.py:42
  (9 shorter events, 0.1 us)
Async XLA Ops:
  0.6 0.9 %copy-start.2 = (bf16[1,1024,64]{1,2,0:T(8,128)(2,1)S(1)}, bf16[1,1024,64]{1,2,0:T(8,128)(2,1)}, u32[]{:S(2)}) copy-start(bf16[1,1024,64]{1,2,0:T(8,128)(2,1)} %param.6) | copy-start | bytes 393220
  1.5 0.7 %copy-start.3 = (s32[1,1024]{1,0:T(1,128)S(1)}, s32[1,1024]{1,0:T(1,128)}, u32[]{:S(2)}) copy-start(s32[1,1024]{1,0:T(1,128)} %slot_ref.1) | copy-start | bytes 12292
  2.2 0.7 %copy-start.4 = (s32[1,1024]{1,0:T(1,128)S(1)}, s32[1,1024]{1,0:T(1,128)}, u32[]{:S(2)}) copy-start(s32[1,1024]{1,0:T(1,128)} %voxel_ref.1) | copy-start | bytes 12292
  2.9 18.1 %copy-start.5 = (bf16[1,2,16,4,256]{4,3,2,1,0:T(4,128)(2,1)S(1)}, bf16[1,2,16,4,256]{4,3,2,1,0:T(4,128)(2,1)}, u32[]{:S(2)}) copy-start(bf16[1,2,16,4,256]{4,3,2,1,0:T(4,128)(2,1)} %param.11) | copy-start | bytes 196612
  2.9 9.9 %collective-permute-start.2 = (bf16[72,1024]{1,0:T(8,128)(2,1)S(1)}, bf16[72,1024]{1,0:T(8,128)(2,1)S(1)}, u32[]{:S(2)}, u32[]{:S(2)}) collective-permute-start(bf16[72,1024]{1,0:T(8,128)(2,1)S(1)} %shard_map.85.refs_0_), channel_id=1, source_target_pairs={{0,6},{1,7},{2,4},{3,5},{4,2},{5,3},{6,0},{7,1},{8,14},{9,15},{10,... | collective-permute-start | bytes 442376 | tf_op jit(solution)/shard_map/ppermute | solution.py:64
  8.1 12.5 %collective-permute-start.1 = (bf16[72,1024]{1,0:T(8,128)(2,1)S(1)}, bf16[72,1024]{1,0:T(8,128)(2,1)S(1)}, u32[]{:S(2)}, u32[]{:S(2)}) collective-permute-start(bf16[72,1024]{1,0:T(8,128)(2,1)S(1)} %shard_map.85.refs_0_), channel_id=1, source_target_pairs={{0,4},{1,5},{2,6},{3,7},{4,0},{5,1},{6,2},{7,3},{8,12},{9,13},{10,... | collective-permute-start | bytes 442376 | tf_op jit(solution)/shard_map/ppermute | solution.py:64
  8.1 12.5 %collective-permute-start = (bf16[72,1024]{1,0:T(8,128)(2,1)S(1)}, bf16[72,1024]{1,0:T(8,128)(2,1)S(1)}, u32[]{:S(2)}, u32[]{:S(2)}) collective-permute-start(bf16[72,1024]{1,0:T(8,128)(2,1)S(1)} %shard_map.85.refs_0_), channel_id=1, source_target_pairs={{0,2},{1,3},{2,0},{3,1},{4,6},{5,7},{6,4},{7,5},{8,10},{9,11},{10,... | collective-permute-start | bytes 442376 | tf_op jit(solution)/shard_map/ppermute | solution.py:64
  8.7 12.4 %collective-permute-start.3 = (bf16[72,1024]{1,0:T(8,128)(2,1)S(1)}, bf16[72,1024]{1,0:T(8,128)(2,1)S(1)}, u32[]{:S(2)}, u32[]{:S(2)}) collective-permute-start(bf16[72,1024]{1,0:T(8,128)(2,1)S(1)} %shard_map.85.refs_0_), channel_id=1, source_target_pairs={{0,1},{1,0},{2,3},{3,2},{4,5},{5,4},{6,7},{7,6},{8,9},{9,8},{10,11... | collective-permute-start | bytes 442376 | tf_op jit(solution)/shard_map/ppermute | solution.py:58
  12.8 8.3 %collective-permute-start.6 = (bf16[72,1024]{1,0:T(8,128)(2,1)S(1)}, bf16[72,1024]{1,0:T(8,128)(2,1)S(1)}, u32[]{:S(2)}, u32[]{:S(2)}) collective-permute-start(bf16[72,1024]{1,0:T(8,128)(2,1)S(1)} %collective-permute-done.2.refs_3_), channel_id=1, source_target_pairs={{0,1},{1,0},{2,3},{3,2},{4,5},{5,4},{6,7},{7,6},{8,9},{9,8},{10,11... | collective-permute-start | bytes 442376 | tf_op jit(solution)/shard_map/ppermute | solution.py:58
  20.5 1.4 %collective-permute-start.5 = (bf16[72,1024]{1,0:T(8,128)(2,1)S(1)}, bf16[72,1024]{1,0:T(8,128)(2,1)S(1)}, u32[]{:S(2)}, u32[]{:S(2)}) collective-permute-start(bf16[72,1024]{1,0:T(8,128)(2,1)S(1)} %collective-permute-done.1.refs_2_), channel_id=1, source_target_pairs={{0,1},{1,0},{2,3},{3,2},{4,5},{5,4},{6,7},{7,6},{8,9},{9,8},{10,11... | collective-permute-start | bytes 442376 | tf_op jit(solution)/shard_map/ppermute | solution.py:58
  20.5 1.6 %collective-permute-start.4 = (bf16[72,1024]{1,0:T(8,128)(2,1)S(1)}, bf16[72,1024]{1,0:T(8,128)(2,1)S(1)}, u32[]{:S(2)}, u32[]{:S(2)}) collective-permute-start(bf16[72,1024]{1,0:T(8,128)(2,1)S(1)} %collective-permute-done.refs_1_), channel_id=1, source_target_pairs={{0,1},{1,0},{2,3},{3,2},{4,5},{5,4},{6,7},{7,6},{8,9},{9,8},{10,11... | collective-permute-start | bytes 442376 | tf_op jit(solution)/shard_map/ppermute | solution.py:58
  22.1 1.0 %copy-start = (bf16[1024,256]{1,0:T(8,128)(2,1)S(1)}, bf16[1024,256]{1,0:T(8,128)(2,1)}, u32[]{:S(2)}) copy-start(bf16[1024,256]{1,0:T(8,128)(2,1)} %refs_9_.1) | copy-start | bytes 1572868
  23.2 1.0 %copy-start.1 = (bf16[1728,128]{1,0:T(8,128)(2,1)S(1)}, bf16[1728,128]{1,0:T(8,128)(2,1)}, u32[]{:S(2)}) copy-start(bf16[1728,128]{1,0:T(8,128)(2,1)} %refs_8_.1) | copy-start | bytes 1327108
  31.1 1.9 %collective-permute-start.7 = (bf16[4,480,128]{2,1,0:T(8,128)(2,1)S(1)}, bf16[4,480,128]{2,1,0:T(8,128)(2,1)S(1)}, u32[]{:S(2)}, u32[]{:S(2)}) collective-permute-start(bf16[4,480,128]{2,1,0:T(8,128)(2,1)S(1)} %get-tuple-element.18), channel_id=1, source_target_pairs={{0,1},{1,0},{2,3},{3,2},{4,5},{5,4},{6,7},{7,6},{8,9},{9,8},{10,11... | collective-permute-start | bytes 1474568 | tf_op jit(solution)/shard_map/ppermute | solution.py:58
  33.1 5.8 %collective-permute-start.8 = (bf16[480,128]{1,0:T(8,128)(2,1)S(1)}, bf16[480,128]{1,0:T(8,128)(2,1)S(1)}, u32[]{:S(2)}, u32[]{:S(2)}) collective-permute-start(bf16[480,128]{1,0:T(8,128)(2,1)S(1)} %get-tuple-element.20), channel_id=1, source_target_pairs={{0,8},{8,0},{16,24},{24,16},{1,9},{9,1},{17,25},{25,17},{2,10},{10... | collective-permute-start | bytes 368648 | tf_op jit(solution)/shard_map/ppermute | solution.py:68
  34.7 7.9 %collective-permute-start.9 = (bf16[480,128]{1,0:T(8,128)(2,1)S(1)}, bf16[480,128]{1,0:T(8,128)(2,1)S(1)}, u32[]{:S(2)}, u32[]{:S(2)}) collective-permute-start(bf16[480,128]{1,0:T(8,128)(2,1)S(1)} %get-tuple-element.21), channel_id=1, source_target_pairs={{0,16},{8,24},{16,0},{24,8},{1,17},{9,25},{17,1},{25,9},{2,18},{10... | collective-permute-start | bytes 368648 | tf_op jit(solution)/shard_map/ppermute | solution.py:68
  36.2 6.4 %collective-permute-start.10 = (bf16[480,128]{1,0:T(8,128)(2,1)S(1)}, bf16[480,128]{1,0:T(8,128)(2,1)S(1)}, u32[]{:S(2)}, u32[]{:S(2)}) collective-permute-start(bf16[480,128]{1,0:T(8,128)(2,1)S(1)} %get-tuple-element.22), channel_id=1, source_target_pairs={{0,24},{8,16},{16,8},{24,0},{1,25},{9,17},{17,9},{25,1},{2,26},{10... | collective-permute-start | bytes 368648 | tf_op jit(solution)/shard_map/ppermute | solution.py:68
  42.7 4.5 %collective-permute-start.11 = (bf16[120,128]{1,0:T(8,128)(2,1)S(1)}, bf16[120,128]{1,0:T(8,128)(2,1)S(1)}, u32[]{:S(2)}, u32[]{:S(2)}) collective-permute-start(bf16[120,128]{1,0:T(8,128)(2,1)S(1)} %get-tuple-element.24), channel_id=1, source_target_pairs={{0,2},{1,3},{2,0},{3,1},{4,6},{5,7},{6,4},{7,5},{8,10},{9,11},{10,... | collective-permute-start | bytes 92168 | tf_op jit(solution)/shard_map/ppermute | solution.py:64
  42.7 4.9 %collective-permute-start.12 = (bf16[120,128]{1,0:T(8,128)(2,1)S(1)}, bf16[120,128]{1,0:T(8,128)(2,1)S(1)}, u32[]{:S(2)}, u32[]{:S(2)}) collective-permute-start(bf16[120,128]{1,0:T(8,128)(2,1)S(1)} %get-tuple-element.25), channel_id=1, source_target_pairs={{0,4},{1,5},{2,6},{3,7},{4,0},{5,1},{6,2},{7,3},{8,12},{9,13},{10,... | collective-permute-start | bytes 92168 | tf_op jit(solution)/shard_map/ppermute | solution.py:64
  45.8 5.7 %collective-permute-start.13 = (bf16[120,128]{1,0:T(8,128)(2,1)S(1)}, bf16[120,128]{1,0:T(8,128)(2,1)S(1)}, u32[]{:S(2)}, u32[]{:S(2)}) collective-permute-start(bf16[120,128]{1,0:T(8,128)(2,1)S(1)} %get-tuple-element.26), channel_id=1, source_target_pairs={{0,6},{1,7},{2,4},{3,5},{4,2},{5,3},{6,0},{7,1},{8,14},{9,15},{10,... | collective-permute-start | bytes 92168 | tf_op jit(solution)/shard_map/ppermute | solution.py:64
  51.5 5.8 %collective-permute-start.16 = (bf16[120,128]{1,0:T(8,128)(2,1)S(1)}, bf16[120,128]{1,0:T(8,128)(2,1)S(1)}, u32[]{:S(2)}, u32[]{:S(2)}) collective-permute-start(bf16[120,128]{1,0:T(8,128)(2,1)S(1)} %shard_map.89), channel_id=1, source_target_pairs={{0,6},{1,7},{2,4},{3,5},{4,2},{5,3},{6,0},{7,1},{8,14},{9,15},{10,... | collective-permute-start | bytes 92168 | tf_op jit(solution)/shard_map/ppermute | solution.py:64
  52.9 5.2 %collective-permute-start.15 = (bf16[120,128]{1,0:T(8,128)(2,1)S(1)}, bf16[120,128]{1,0:T(8,128)(2,1)S(1)}, u32[]{:S(2)}, u32[]{:S(2)}) collective-permute-start(bf16[120,128]{1,0:T(8,128)(2,1)S(1)} %shard_map.89), channel_id=1, source_target_pairs={{0,4},{1,5},{2,6},{3,7},{4,0},{5,1},{6,2},{7,3},{8,12},{9,13},{10,... | collective-permute-start | bytes 92168 | tf_op jit(solution)/shard_map/ppermute | solution.py:64
  52.9 5.3 %collective-permute-start.14 = (bf16[120,128]{1,0:T(8,128)(2,1)S(1)}, bf16[120,128]{1,0:T(8,128)(2,1)S(1)}, u32[]{:S(2)}, u32[]{:S(2)}) collective-permute-start(bf16[120,128]{1,0:T(8,128)(2,1)S(1)} %shard_map.89), channel_id=1, source_target_pairs={{0,2},{1,3},{2,0},{3,1},{4,6},{5,7},{6,4},{7,5},{8,10},{9,11},{10,... | collective-permute-start | bytes 92168 | tf_op jit(solution)/shard_map/ppermute | solution.py:64
  58.2 1.4 %collective-permute-start.17 = (bf16[4,120,128]{2,1,0:T(8,128)(2,1)S(1)}, bf16[4,120,128]{2,1,0:T(8,128)(2,1)S(1)}, u32[]{:S(2)}, u32[]{:S(2)}) collective-permute-start(bf16[4,120,128]{2,1,0:T(8,128)(2,1)S(1)} %pad_maximum_fusion.own_ref), channel_id=1, source_target_pairs={{0,1},{1,0},{2,3},{3,2},{4,5},{5,4},{6,7},{7,6},{8,9},{9,8},{10,11... | collective-permute-start | bytes 368648 | tf_op jit(solution)/shard_map/ppermute | solution.py:58

commit v3 on v2

v3 whole, which is shorter than its diff:
```python
import functools

import jax
import jax.numpy as jnp
from jax import lax
from jax.experimental import pallas as pl
from jax.experimental.pallas import tpu as pltpu
from jax.sharding import PartitionSpec as P

CIN = 64
C1 = 128
C2 = 256
SX = 4
SY = 32
SZ = 8
PTS_DEV = 1024
TAPS = 27
CODED = CIN + 8
LAYER = SZ * SY // 2
BF16 = jnp.bfloat16
F32 = jnp.float32
I32 = jnp.int32
NT = (((1,), (1,)), ((), ()))
TN = (((0,), (0,)), ((), ()))
VMEM_LIMIT = 24 * 1024 * 1024


def call(body, outs, scratch=(), pinned=0, loose=0, raw=0):
    single = not isinstance(outs, (list, tuple))
    vmem = pl.BlockSpec(memory_space=pltpu.VMEM)
    kernel = pl.pallas_call(
        body,
        out_shape=outs,
        in_specs=[vmem] * (pinned + loose) + [pl.BlockSpec(memory_space=pl.ANY)] * raw,
        out_specs=vmem if single else [vmem] * len(outs),
        scratch_shapes=list(scratch),
        compiler_params=pltpu.CompilerParams(vmem_limit_bytes=VMEM_LIMIT),
    )

    def run(*args):
        held = [pltpu.with_memory_space_constraint(a, pltpu.VMEM) for a in args[:pinned]]
        return kernel(*held, *args[pinned:])

    return run


def target(index, k, count):
    if count & (count - 1) == 0:
        return index ^ k
    return (index + k) % count


def swap_core(value, tiles):
    return lax.ppermute(value, "tile", [(i, i ^ 1) for i in range(tiles)])


def send_column_by(value, to, tiles):
    pairs = [(2 * i + c, 2 * to(i) + c) for i in range(tiles // 2) for c in range(2)]
    return lax.ppermute(value, "tile", pairs)


def send_column(value, k, tiles):
    return send_column_by(value, lambda i: target(i, k, tiles // 2), tiles)


def send_sample(value, k, samples):
    return lax.ppermute(value, "sample", [(i, target(i, k, samples)) for i in range(samples)])


def encode_kernel(capacity, points_hbm, slot_hbm, voxel_hbm, out_ref, slot_ref, voxel_ref, sems):
    copies = [
        pltpu.make_async_copy(slot_hbm, slot_ref, sems.at[0]),
        pltpu.make_async_copy(voxel_hbm, voxel_ref, sems.at[1]),
        pltpu.make_async_copy(points_hbm, out_ref.at[0:CIN], sems.at[2]),
    ]
    for copy in copies:
        copy.start()
    copies[0].wait()
    copies[1].wait()
    slot = slot_ref[...]
    voxel = voxel_ref[...]
    if capacity & (capacity - 1) == 0:
        owner = slot >> (capacity.bit_length() - 1)
    else:
        owner = jnp.floor((slot.astype(F32) + 0.5) * (1.0 / capacity)).astype(I32)
    layer = owner * SX + (voxel >> 8) + 1
    z = voxel & 7
    y = (voxel >> 3) & 31
    place = ((z * 16 + (y >> 1)) << 1) + (y & 1)
    row = lax.broadcasted_iota(I32, (8, slot.shape[1]), 0)
    codes = jnp.where(row == 0, layer, jnp.where(row == 1, place, 0))
    out_ref[CIN:CODED, :] = codes.astype(F32).astype(BF16)
    copies[2].wait()


def weights_kernel(conv_ref, down_ref, cot_ref, taps_ref, pairs_ref, cot_out_ref, back_ref):
    zero_tap = jnp.zeros((CIN, C1), BF16)

    def tap(dx, dy, dz):
        start = ((dx * 3 + dy) * 3 + dz) * CIN
        return conv_ref[start : start + CIN, :]

    for dx in range(3):
        for dz in range(3):
            taps_ref[dx * 3 + dz] = jnp.concatenate(
                [
                    jnp.concatenate([tap(dx, 1, dz), tap(dx, 0, dz)], axis=1),
                    jnp.concatenate([tap(dx, 2, dz), tap(dx, 1, dz)], axis=1),
                    jnp.concatenate([tap(dx, 0, dz), zero_tap], axis=1),
                    jnp.concatenate([zero_tap, tap(dx, 2, dz)], axis=1),
                ],
                axis=0,
            )
    cot = lax.dot_general(turn_matrix(), cot_ref[...], TN, preferred_element_type=F32).astype(BF16)
    cot_out_ref[...] = cot
    for ox in range(2):
        for oz in range(2):
            first = (ox * 4 + oz) * C1
            second = first + 2 * C1
            weight = jnp.concatenate(
                [down_ref[first : first + C1, :], down_ref[second : second + C1, :]], axis=0
            )
            pairs_ref[ox * 2 + oz] = weight
            back_ref[ox * 2 + oz] = lax.dot_general(cot, weight, NT, preferred_element_type=F32)


def turn_matrix():
    here = lax.broadcasted_iota(I32, (128, 128), 0)
    there = lax.broadcasted_iota(I32, (128, 128), 1)
    return ((here >> 6) * 64 + (here & 3) * 16 + ((here >> 2) & 15) == there).astype(F32).astype(BF16)


def voxelize(refs, grid, counts):
    tile = lax.axis_index("tile")
    row_iota = lax.broadcasted_iota(I32, (3 * LAYER, PTS_DEV), 0)
    small_iota = lax.broadcasted_iota(I32, (32, PTS_DEV), 0)
    for ref in refs:
        codes = ref[CIN:CODED, :].astype(F32).astype(I32)
        layer = codes[0:1, :]
        place = codes[1:2, :]
        pair = (layer >> 1) - 2 * tile
        odd = layer & 1
        spot = place >> 1
        side = place & 1
        hot = (row_iota == pair * LAYER + spot).astype(F32).astype(BF16)
        group = odd * 2 + side
        features = ref[0:CIN, :]
        spread = jnp.concatenate(
            [features * (group == g).astype(F32).astype(BF16) for g in range(4)], axis=0
        )
        part = lax.dot_general(hot, spread, NT, preferred_element_type=F32)
        grid = part if grid is None else grid + part
        plane = (2 * pair + odd - 1) * SZ + (spot >> 4)
        hot_plane = (small_iota == plane).astype(F32).astype(BF16)
        hot_line = (small_iota == (spot & 15) * 2 + side).astype(F32).astype(BF16)
        part = lax.dot_general(hot_plane, hot_line, NT, preferred_element_type=F32)
        counts = part if counts is None else counts + part
    return grid, counts


def first_points_kernel(*refs):
    grid_ref, counts_ref = refs[-2:]
    grid_ref[...], counts_ref[...] = voxelize(refs[:-2], None, None)


def more_points_kernel(old_grid_ref, old_counts_ref, *refs):
    grid_ref, counts_ref = refs[-2:]
    grid_ref[...], counts_ref[...] = voxelize(refs[:-2], old_grid_ref[...], old_counts_ref[...])


def scene_kernel(
    samples, half_rows,
    grid_ref, counts_ref, coded_ref, other_coded_ref, taps_ref, pairs_ref, cot_ref, back_ref,
    out_ref, mine_ref, other_ref, es_ref, pg_ref, wide_ref, tall_ref,
):
    grid, counts = voxelize((coded_ref, other_coded_ref), grid_ref[...], counts_ref[...])

    es_ref[...] = jnp.zeros_like(es_ref)
    pg_ref[...] = jnp.zeros_like(pg_ref)
    line = lax.broadcasted_iota(I32, (LAYER, 2 * CIN), 0) & 15
    lane = lax.broadcasted_iota(I32, (LAYER, 2 * CIN), 1)
    for x in range(SX + 2):
        both = grid[(x // 2) * LAYER : (x // 2 + 1) * LAYER, (x % 2) * 128 : (x % 2 + 1) * 128]
        turned = pltpu.roll(both, CIN, 1)
        before = jnp.where(line == 0, 0.0, pltpu.roll(turned, 1, 0))
        after = jnp.where(line == 15, 0.0, pltpu.roll(turned, LAYER - 1, 0))
        sides = jnp.where(lane < CIN, before, after)
        es_ref[x, 1 : SZ + 1, :, 0:128] = both.astype(BF16).reshape(SZ, 16, 128)
        es_ref[x, 1 : SZ + 1, :, 128:256] = sides.astype(BF16).reshape(SZ, 16, 128)

    full = SX * LAYER
    flags = (counts > 0.5).astype(F32).astype(BF16)
    row_plane = lax.broadcasted_iota(I32, (full, 32), 0) >> 4
    pick = (row_plane == lax.broadcasted_iota(I32, (full, 32), 1)).astype(F32).astype(BF16)
    lines = jnp.dot(pick, flags, preferred_element_type=F32)
    row_line = lax.broadcasted_iota(I32, (full, 32), 0) & 15
    lines = jnp.where(row_line == (lax.broadcasted_iota(I32, (full, 32), 1) >> 1), lines, 0.0).astype(BF16)
    expand = (
        (lax.broadcasted_iota(I32, (32, 256), 0) & 1) == (lax.broadcasted_iota(I32, (32, 256), 1) >> 7)
    ).astype(F32).astype(BF16)
    active = jnp.dot(lines, expand, preferred_element_type=F32) > 0.5

    pre = jnp.zeros((full, 2 * C1), F32)
    for dx in range(3):
        for dz in range(3):
            part = es_ref[dx : dx + SX, dz : dz + SZ].reshape(full, 4 * CIN)
            pre = pre + jnp.dot(part, taps_ref[dx * 3 + dz], preferred_element_type=F32)

    sigmoid = 1.0 / (1.0 + jnp.exp(-pre))
    act = jnp.where(active, pre * sigmoid, 0.0).astype(BF16)
    slope = jnp.where(active, sigmoid * (1.0 + pre * (1.0 - sigmoid)), 0.0)

    act = act.reshape(2, 2, 4, 2, 16, 2 * C1)
    slope = slope.reshape(2, 2, 4, 2, 16, 2 * C1)
    cot = cot_ref[...]
    down = jnp.zeros((128, C2), F32)
    for ox in range(2):
        for oz in range(2):
            block = act[:, ox, :, oz].reshape(128, 2 * C1)
            first = (ox * 4 + oz) * C1
            second = first + 2 * C1
            down = down + jnp.dot(block, pairs_ref[ox * 2 + oz], preferred_element_type=F32)
            grad = lax.dot_general(block, cot, TN, preferred_element_type=F32)
            wide_ref[first : first + C1, :] = grad[0:C1]
            wide_ref[second : second + C1, :] = grad[C1:]
            back = back_ref[ox * 2 + oz]
            part = (back * slope[:, ox, :, oz].reshape(128, 2 * C1)).astype(BF16).reshape(2, 4, 16, 2 * C1)
            for u in range(2):
                for w in range(4):
                    pg_ref[2 * u + ox, 1 + 2 * w + oz] = part[u, w]
    out_ref[...] = jnp.dot(turn_matrix(), down.astype(BF16), preferred_element_type=F32).astype(BF16)

    flipped = es_ref[:, 1 : SZ + 1].reshape((SX + 2) * LAYER, 4 * CIN).T
    for dz in range(3):
        part = pg_ref[:, 2 - dz : 2 - dz + SZ].reshape(full, 2 * C1)
        for dx in range(3):
            grad = jnp.dot(
                flipped[:, dx * LAYER : dx * LAYER + full], part, preferred_element_type=F32
            )
            sums = (
                grad[0:64, 128:256] + grad[128:192, 0:128],
                grad[0:64, 0:128] + grad[64:128, 128:256],
                grad[64:128, 0:128] + grad[192:256, 128:256],
            )
            for dy in range(3):
                start = ((dx * 3 + dy) * 3 + dz) * CIN
                tall_ref[start : start + CIN, :] = sums[dy]

    conv_rows = TAPS * CIN // samples
    down_rows = 8 * C1 // samples
    filler = 2 * half_rows - conv_rows - 2 * down_rows

    def leave(mine_first):
        for s in range(samples):
            pieces = [
                tall_ref[s * conv_rows : (s + 1) * conv_rows, :],
                wide_ref[s * down_rows : (s + 1) * down_rows, 0:128],
                wide_ref[s * down_rows : (s + 1) * down_rows, 128:256],
            ]
            if filler:
                pieces.append(jnp.zeros((filler, 128), F32))
            chunk = jnp.concatenate(pieces, axis=0)
            low, high = chunk[:half_rows], chunk[half_rows:]
            mine, other = (low, high) if mine_first else (high, low)
            mine_ref[s] = mine
            other_ref[s] = other.astype(BF16)

    core = lax.axis_index("tile") & 1

    @pl.when(core == 0)
    def _():
        leave(True)

    @pl.when(core == 1)
    def _():
        leave(False)


def share_samples_kernel(samples, mine_ref, got_ref, keep_ref, *send_refs):
    me = lax.axis_index("sample")
    keep_ref[...] = mine_ref[me] + got_ref[me].astype(F32)
    for k, ref in enumerate(send_refs, 1):
        to = target(me, k, samples)
        ref[...] = (mine_ref[to] + got_ref[to].astype(F32)).astype(BF16)


def sum_kernel(*refs):
    total = refs[0][...].astype(F32)
    for ref in refs[1:-1]:
        total = total + ref[...].astype(F32)
    refs[-1][...] = total.astype(refs[-1].dtype)


def ordered_sum_kernel(block, own_ref, *refs):
    held_ref, out_ref = refs[-1], refs[-2]
    count = len(refs) - 1
    me = (lax.axis_index("tile") >> 1) // block
    held_ref[me] = own_ref[...].astype(F32)
    for j, ref in enumerate(refs[:-2], 1):
        held_ref[(me - j + count) % count] = ref[...].astype(F32)
    total = held_ref[0]
    for i in range(1, count):
        total = total + held_ref[i]
    out_ref[...] = total


def finish_kernel(conv_rows, down_rows, own_ref, got_ref, conv_ref, down_ref):
    first = (lax.axis_index("tile") & 1) == 0
    own = own_ref[...]
    got = got_ref[...]
    whole = jnp.concatenate([jnp.where(first, own, got), jnp.where(first, got, own)], axis=0)
    conv_ref[...] = whole[:conv_rows]
    down_ref[:, 0:128] = whole[conv_rows : conv_rows + down_rows]
    down_ref[:, 128:256] = whole[conv_rows + down_rows : conv_rows + 2 * down_rows]


def local(points, slot, voxel, conv_weight, down_weight, cotangent):
    tiles = lax.axis_size("tile")
    samples = lax.axis_size("sample")
    chips = tiles // 2
    capacity = 2 * (PTS_DEV // tiles)
    conv_rows = TAPS * CIN // samples
    down_rows = 8 * C1 // samples
    half_rows = -(-(conv_rows + 2 * down_rows) // 32) * 16

    hbm = jax.ShapeDtypeStruct
    shape = pltpu.VMEM
    coded = call(
        functools.partial(encode_kernel, capacity),
        shape((CODED, PTS_DEV), BF16),
        scratch=(
            pltpu.VMEM((1, PTS_DEV), I32),
            pltpu.VMEM((1, PTS_DEV), I32),
            pltpu.SemaphoreType.DMA((3,)),
        ),
        raw=3,
    )(points[0].T, slot, voxel)
    near = {0: coded}
    for k in range(1, chips):
        near[k] = send_column(near[2], 1, tiles) if (k == 3 and chips == 4) else send_column(coded, k, tiles)
    pieces = [(value, swap_core(value, tiles)) for value in near.values()]
    taps, pairs, cot, back = call(
        weights_kernel,
        (
            shape((9, 4 * CIN, 2 * C1), BF16),
            shape((4, 2 * C1, C2), BF16),
            shape((128, C2), BF16),
            shape((4, 128, 2 * C1), F32),
        ),
        loose=3,
    )(conv_weight, down_weight, cotangent.reshape(128, C2))
    sums = (shape((3 * LAYER, 4 * CIN), F32), shape((32, 32), F32))
    grid = call(first_points_kernel, sums, pinned=2)(*pieces[0])
    for pair in pieces[1:-1]:
        grid = call(more_points_kernel, sums, pinned=4)(*grid, *pair)

    down, mine, other = call(
        functools.partial(scene_kernel, samples, half_rows),
        (
            shape((128, C2), BF16),
            shape((samples, half_rows, 128), F32),
            shape((samples, half_rows, 128), BF16),
        ),
        scratch=(
            pltpu.VMEM((SX + 2, SZ + 2, 16, 4 * CIN), BF16),
            pltpu.VMEM((SX, SZ + 2, 16, 2 * C1), BF16),
            pltpu.VMEM((8 * C1, C2), F32),
            pltpu.VMEM((TAPS * CIN, C1), F32),
        ),
        pinned=8,
    )(*grid, *pieces[-1], taps, pairs, cot, back)

    got = swap_core(other, tiles)
    keep, *sends = call(
        functools.partial(share_samples_kernel, samples),
        [shape((half_rows, 128), F32)] + [shape((half_rows, 128), BF16)] * (samples - 1),
        pinned=2,
    )(mine, got)
    got = [send_sample(value, k, samples) for k, value in enumerate(sends, 1)]
    block = chips & -chips
    parts = chips // block
    steps = [1 << i for i in range(block.bit_length() - 1)]
    terms = (keep, *got)
    for at, step in enumerate(steps + [0]):
        last = at == len(steps) and parts == 1
        total = call(sum_kernel, shape((half_rows, 128), F32 if last else BF16), pinned=len(terms))(*terms)
        if step:
            terms = (total, send_column_by(total, lambda i: i ^ step, tiles))
    if parts > 1:
        got = [send_column_by(total, lambda i: (i + j * block) % chips, tiles) for j in range(1, parts)]
        total = call(
            functools.partial(ordered_sum_kernel, block),
            shape((half_rows, 128), F32),
            scratch=(pltpu.VMEM((parts, half_rows, 128), F32),),
            pinned=parts,
        )(total, *got)
    conv_grad, down_grad = call(
        functools.partial(finish_kernel, conv_rows, down_rows),
        (hbm((conv_rows, C1), F32), hbm((down_rows, C2), F32)),
        pinned=2,
    )(total, swap_core(total, tiles))
    return (down.reshape(1, SX // 2, SY // 2, SZ // 2, C2), conv_grad, down_grad)


def solution(mesh):
    placed = (
        P("sample", "tile", None),
        P("sample", "tile"),
        P("sample", "tile"),
        P(),
        P(),
        P("sample", "tile", None, None, None),
    )
    return jax.shard_map(
        local,
        mesh=mesh,
        in_specs=placed,
        out_specs=(P("sample", "tile", None, None, None), P("sample", None), P("sample", None)),
        check_vma=False,
    )
```

time: 60.7 us -> 55.7 us (0.918)
  starting transfers between devices: 19.2 us -> 15.2 us
  waiting for transfers between devices: 27.5 us -> 25.8 us
  local copies, waits for them, and re-layouts: 5 us -> 5.83 us
    ppermute x9 -> x5, starting transfers between devices: 14.7 us -> 10.5 us  [send_column_by(): return lax.ppermute(value, 'tile', pairs)]
    ppermute x9 -> x5, waiting for transfers between devices: 18.4 us -> 17.5 us  [send_column_by(): return lax.ppermute(value, 'tile', pairs)]
    ppermute x6, waiting for transfers between devices: 3.24 us -> 2.35 us  [swap_core(): return lax.ppermute(value, 'tile', [(i, i ^ 1) for i in range(tiles)])]
    reshape x1, local copies, waits for them, and re-layouts: 0.02 us -> 0.86 us  [local(): cotangent.reshape(128, C2)]
    pallas_call x6 -> x11, Pallas kernels: 7.96 us -> 7.72 us  [run(): return kernel(*held, *args[pinned:])]
    unnamed x12 -> x10, local copies, waits for them, and re-layouts: 4.33 us -> 4.32 us
  transfers between devices with their start and end apart: 18 -> 14, of which waited for: 13 -> 8; matrix products, arithmetic and copies ran while one was open for 1% -> 3% of each run, Pallas kernels for 0% -> 5%
where the time goes in v3:
time: 55.7 us; the launch traced here: 55.4 us
  waiting for transfers between devices  25.8 us (46%)
  starting transfers between devices  15.2 us (27%)
  Pallas kernels  7.72 us (14%)
  local copies, waits for them, and re-layouts  5.83 us (10%)
  between operations  0.76 us (1%)
    ppermute x5, waiting for transfers between devices, send_column_by(): return lax.ppermute(value, 'tile', pairs)  17.5 us
    ppermute x5, starting transfers between devices, send_column_by(): return lax.ppermute(value, 'tile', pairs)  10.5 us
    pallas_call x11, Pallas kernels, run(): return kernel(*held, *args[pinned:])  7.72 us
    ppermute x3, waiting for transfers between devices, send_sample(): lax.ppermute(value, 'sample', [(i, target(i, k, samples)) for i in range(...  5.99 us
    unnamed x10, local copies, waits for them, and re-layouts  4.32 us
    ppermute x3, starting transfers between devices, send_sample(): lax.ppermute(value, 'sample', [(i, target(i, k, samples)) for i in range(...  3.57 us
    ppermute x6, waiting for transfers between devices, swap_core(): return lax.ppermute(value, 'tile', [(i, i ^ 1) for i in range(tiles)])  2.35 us
    ppermute x6, starting transfers between devices, swap_core(): return lax.ppermute(value, 'tile', [(i, i ^ 1) for i in range(tiles)])  1.19 us
  transfers between devices with their start and end apart: 14, of which 8 were waited for; matrix products, arithmetic and copies ran while one was open for 3% of the time, Pallas kernels for 5%

profile of v3, /device:TPU:0, one launch (start us, length us, event | category | flops | bytes accessed | tf_op | source)
XLA Modules:
  0.0 55.4 jit_solution(15879713219518846847)
XLA Ops:
  0.6 0.0 copy-start.2
  0.6 0.9 %copy-done.2 = bf16[1,1024,64]{1,2,0:T(8,128)(2,1)S(1)} copy-done((bf16[1,1024,64]{1,2,0:T(8,128)(2,1)S(1)}, bf16[1,1024,64]{1,2,0:T(8,128)(2,1)}, u32[]{:S(2)}) %copy-start.2) | copy-done | bytes 131096
  1.5 0.0 copy-start.3
  1.5 0.7 %copy-done.3 = s32[1,1024]{1,0:T(1,128)S(1)} copy-done((s32[1,1024]{1,0:T(1,128)S(1)}, s32[1,1024]{1,0:T(1,128)}, u32[]{:S(2)}) %copy-start.3) | copy-done | bytes 4120
  2.2 0.7 %copy-done.4 = s32[1,1024]{1,0:T(1,128)S(1)} copy-done((s32[1,1024]{1,0:T(1,128)S(1)}, s32[1,1024]{1,0:T(1,128)}, u32[]{:S(2)}) %copy-start.4) | copy-done | bytes 4120
  2.9 0.2 shard_map.85.refs_0_
  3.1 4.1 %collective-permute-start.3 = (bf16[72,1024]{1,0:T(8,128)(2,1)S(1)}, bf16[72,1024]{1,0:T(8,128)(2,1)S(1)}, u32[]{:S(2)}, u32[]{:S(2)}) collective-permute-start(bf16[72,1024]{1,0:T(8,128)(2,1)S(1)} %shard_map.85.refs_0_), channel_id=1, source_target_pairs={{0,4},{1,5},{2,6},{3,7},{4,0},{5,1},{6,2},{7,3},{8,12},{9,13},{10,... | collective-permute-start | bytes 442376 | tf_op jit(solution)/shard_map/ppermute | solution.py:59
  7.2 1.6 %collective-permute-start.1 = (bf16[72,1024]{1,0:T(8,128)(2,1)S(1)}, bf16[72,1024]{1,0:T(8,128)(2,1)S(1)}, u32[]{:S(2)}, u32[]{:S(2)}) collective-permute-start(bf16[72,1024]{1,0:T(8,128)(2,1)S(1)} %shard_map.85.refs_0_), channel_id=1, source_target_pairs={{0,2},{1,3},{2,0},{3,1},{4,6},{5,7},{6,4},{7,5},{8,10},{9,11},{10,... | collective-permute-start | bytes 442376 | tf_op jit(solution)/shard_map/ppermute | solution.py:59
  8.8 5.5 %collective-permute-done.3.refs_0_ = bf16[72,1024]{1,0:T(8,128)(2,1)S(1)} collective-permute-done((bf16[72,1024]{1,0:T(8,128)(2,1)S(1)}, bf16[72,1024]{1,0:T(8,128)(2,1)S(1)}, u32[]{:S(2)}, u32[]{:S(2)}) %collective-permute-start.3) | collective-permute-done | bytes 147488 | tf_op jit(solution)/shard_map/ppermute | solution.py:59
  14.3 0.6 %collective-permute-start.5 = (bf16[72,1024]{1,0:T(8,128)(2,1)S(1)}, bf16[72,1024]{1,0:T(8,128)(2,1)S(1)}, u32[]{:S(2)}, u32[]{:S(2)}) collective-permute-start(bf16[72,1024]{1,0:T(8,128)(2,1)S(1)} %collective-permute-done.3.refs_0_), channel_id=1, source_target_pairs={{0,2},{1,3},{2,0},{3,1},{4,6},{5,7},{6,4},{7,5},{8,10},{9,11},{10,... | collective-permute-start | bytes 442376 | tf_op jit(solution)/shard_map/ppermute | solution.py:59
  14.9 0.0 collective-permute-start
  14.9 0.0 collective-permute-done.1.refs_0_
  15.0 0.5 collective-permute-start.2
  15.5 0.0 collective-permute-start.4
  15.5 4.0 %collective-permute-done.5.coded_ref = bf16[72,1024]{1,0:T(8,128)(2,1)S(1)} collective-permute-done((bf16[72,1024]{1,0:T(8,128)(2,1)S(1)}, bf16[72,1024]{1,0:T(8,128)(2,1)S(1)}, u32[]{:S(2)}, u32[]{:S(2)}) %collective-permute-start.5) | collective-permute-done | bytes 147488 | tf_op jit(solution)/shard_map/ppermute | solution.py:59
  19.5 0.0 collective-permute-start.6
  19.5 0.9 %reshape.12.cot_ref = bf16[128,256]{1,0:T(8,128)(2,1)S(1)} reshape(bf16[1,2,16,4,256]{4,3,2,1,0:T(4,128)(2,1)} %param.11) | data formatting | bytes 131072 | tf_op jit(solution)/shard_map/reshape | solution.py:351
  20.3 0.0 copy-start
  20.3 1.0 %copy-done = bf16[1024,256]{1,0:T(8,128)(2,1)S(1)} copy-done((bf16[1024,256]{1,0:T(8,128)(2,1)S(1)}, bf16[1024,256]{1,0:T(8,128)(2,1)}, u32[]{:S(2)}) %copy-start) | copy-done | bytes 524312
  21.4 0.0 copy-start.1
  21.4 1.0 %copy-done.1 = bf16[1728,128]{1,0:T(8,128)(2,1)S(1)} copy-done((bf16[1728,128]{1,0:T(8,128)(2,1)S(1)}, bf16[1728,128]{1,0:T(8,128)(2,1)}, u32[]{:S(2)}) %copy-start.1) | copy-done | bytes 442392
  22.4 0.5 shard_map.89
  22.9 0.0 collective-permute-done.refs_1_
  22.9 0.7 %shard_map.86 = (f32[384,256]{1,0:T(8,128)S(1)}, f32[32,32]{1,0:T(8,128)S(1)}) custom-call(bf16[72,1024]{1,0:T(8,128)(2,1)S(1)} %shard_map.85.refs_0_, bf16[72,1024]{1,0:T(8,128)(2,1)S(1)} %collective-permute-done.refs_1_), custom_call_target="tpu_custom_call" | custom-call | tf_op jit(solution)/shard_map/pallas_call | solution.py:42
  23.5 0.0 collective-permute-done.2.refs_1_
  23.5 0.7 %shard_map.87 = (f32[384,256]{1,0:T(8,128)S(1)}, f32[32,32]{1,0:T(8,128)S(1)}) custom-call(f32[384,256]{1,0:T(8,128)S(1)} %get-tuple-element.22.old_grid_ref, f32[32,32]{1,0:T(8,128)S(1)} %get-tuple-element.23.old_counts_ref, bf16[72,1024]{1,0:T(8,128)(2,1)S(1)} %collective-permute-done.1.refs_0_, bf16[72,1024]{1,0:T(8,128)(2,1)S(1)} %collective-permute-done.2.refs_1_), custom_call_target="tpu_custom_call" | custom-call | tf_op jit(solution)/shard_map/pallas_call | solution.py:42
  24.2 0.0 collective-permute-done.4.refs_1_
  24.3 0.7 %shard_map.88 = (f32[384,256]{1,0:T(8,128)S(1)}, f32[32,32]{1,0:T(8,128)S(1)}) custom-call(f32[384,256]{1,0:T(8,128)S(1)} %get-tuple-element.24.old_grid_ref, f32[32,32]{1,0:T(8,128)S(1)} %get-tuple-element.25.old_counts_ref, bf16[72,1024]{1,0:T(8,128)(2,1)S(1)} %collective-permute-done.3.refs_0_, bf16[72,1024]{1,0:T(8,128)(2,1)S(1)} %collective-permute-done.4.refs_1_), custom_call_target="tpu_custom_call" | custom-call | tf_op jit(solution)/shard_map/pallas_call | solution.py:42
  25.0 0.0 collective-permute-done.6.other_coded_ref
  25.0 4.0 %shard_map.90 = (bf16[128,256]{1,0:T(8,128)(2,1)S(1)}, f32[4,480,128]{2,1,0:T(8,128)S(1)}, bf16[4,480,128]{2,1,0:T(8,128)(2,1)S(1)}) custom-call(f32[384,256]{1,0:T(8,128)S(1)} %get-tuple-element.26.grid_ref, f32[32,32]{1,0:T(8,128)S(1)} %get-tuple-element.27.counts_ref, bf16[72,1024]{1,0:T(8,128)(2,1)S(1)} %collective-permute-done.5.coded_ref, ...), custom_call_target="tpu_custom_call" | custom-call | tf_op jit(solution)/shard_map/pallas_call | solution.py:42
  29.0 0.6 %collective-permute-start.7 = (bf16[4,480,128]{2,1,0:T(8,128)(2,1)S(1)}, bf16[4,480,128]{2,1,0:T(8,128)(2,1)S(1)}, u32[]{:S(2)}, u32[]{:S(2)}) collective-permute-start(bf16[4,480,128]{2,1,0:T(8,128)(2,1)S(1)} %get-tuple-element.34), channel_id=1, source_target_pairs={{0,1},{1,0},{2,3},{3,2},{4,5},{5,4},{6,7},{7,6},{8,9},{9,8},{10,11... | collective-permute-start | bytes 1474568 | tf_op jit(solution)/shard_map/ppermute | solution.py:54
  29.6 1.5 %collective-permute-done.7.got_ref = bf16[4,480,128]{2,1,0:T(8,128)(2,1)S(1)} collective-permute-done((bf16[4,480,128]{2,1,0:T(8,128)(2,1)S(1)}, bf16[4,480,128]{2,1,0:T(8,128)(2,1)S(1)}, u32[]{:S(2)}, u32[]{:S(2)}) %collective-permute-start.7) | collective-permute-done | bytes 491552 | tf_op jit(solution)/shard_map/ppermute | solution.py:54
  31.1 0.1 shard_map.91
  31.2 1.6 %collective-permute-start.8 = (bf16[480,128]{1,0:T(8,128)(2,1)S(1)}, bf16[480,128]{1,0:T(8,128)(2,1)S(1)}, u32[]{:S(2)}, u32[]{:S(2)}) collective-permute-start(bf16[480,128]{1,0:T(8,128)(2,1)S(1)} %get-tuple-element.36), channel_id=1, source_target_pairs={{0,8},{8,0},{16,24},{24,16},{1,9},{9,1},{17,25},{25,17},{2,10},{10... | collective-permute-start | bytes 368648 | tf_op jit(solution)/shard_map/ppermute | solution.py:67
  32.8 1.5 %collective-permute-start.9 = (bf16[480,128]{1,0:T(8,128)(2,1)S(1)}, bf16[480,128]{1,0:T(8,128)(2,1)S(1)}, u32[]{:S(2)}, u32[]{:S(2)}) collective-permute-start(bf16[480,128]{1,0:T(8,128)(2,1)S(1)} %get-tuple-element.37), channel_id=1, source_target_pairs={{0,16},{8,24},{16,0},{24,8},{1,17},{9,25},{17,1},{25,9},{2,18},{10... | collective-permute-start | bytes 368648 | tf_op jit(solution)/shard_map/ppermute | solution.py:67
  34.3 0.4 collective-permute-start.10
  34.7 2.2 %collective-permute-done.8.refs_1_ = bf16[480,128]{1,0:T(8,128)(2,1)S(1)} collective-permute-done((bf16[480,128]{1,0:T(8,128)(2,1)S(1)}, bf16[480,128]{1,0:T(8,128)(2,1)S(1)}, u32[]{:S(2)}, u32[]{:S(2)}) %collective-permute-start.8) | collective-permute-done | bytes 122912 | tf_op jit(solution)/shard_map/ppermute | solution.py:67
  37.0 3.8 %collective-permute-done.9.refs_2_ = bf16[480,128]{1,0:T(8,128)(2,1)S(1)} collective-permute-done((bf16[480,128]{1,0:T(8,128)(2,1)S(1)}, bf16[480,128]{1,0:T(8,128)(2,1)S(1)}, u32[]{:S(2)}, u32[]{:S(2)}) %collective-permute-start.9) | collective-permute-done | bytes 122912 | tf_op jit(solution)/shard_map/ppermute | solution.py:67
  40.7 0.0 collective-permute-done.10.refs_3_
  40.7 0.1 shard_map.92.refs_0_
  40.8 1.3 %collective-permute-start.11 = (bf16[480,128]{1,0:T(8,128)(2,1)S(1)}, bf16[480,128]{1,0:T(8,128)(2,1)S(1)}, u32[]{:S(2)}, u32[]{:S(2)}) collective-permute-start(bf16[480,128]{1,0:T(8,128)(2,1)S(1)} %shard_map.92.refs_0_), channel_id=1, source_target_pairs={{0,2},{1,3},{2,0},{3,1},{4,6},{5,7},{6,4},{7,5},{8,10},{9,11},{10,... | collective-permute-start | bytes 368648 | tf_op jit(solution)/shard_map/ppermute | solution.py:59
  42.1 3.7 %collective-permute-done.11.refs_1_ = bf16[480,128]{1,0:T(8,128)(2,1)S(1)} collective-permute-done((bf16[480,128]{1,0:T(8,128)(2,1)S(1)}, bf16[480,128]{1,0:T(8,128)(2,1)S(1)}, u32[]{:S(2)}, u32[]{:S(2)}) %collective-permute-start.11) | collective-permute-done | bytes 122912 | tf_op jit(solution)/shard_map/ppermute | solution.py:59
  45.8 2.9 %collective-permute-start.12 = (bf16[480,128]{1,0:T(8,128)(2,1)S(1)}, bf16[480,128]{1,0:T(8,128)(2,1)S(1)}, u32[]{:S(2)}, u32[]{:S(2)}) collective-permute-start(bf16[480,128]{1,0:T(8,128)(2,1)S(1)} %shard_map.93.refs_0_), channel_id=1, source_target_pairs={{0,4},{1,5},{2,6},{3,7},{4,0},{5,1},{6,2},{7,3},{8,12},{9,13},{10,... | collective-permute-start | bytes 368648 | tf_op jit(solution)/shard_map/ppermute | solution.py:59
  48.7 4.3 %collective-permute-done.12.refs_1_ = bf16[480,128]{1,0:T(8,128)(2,1)S(1)} collective-permute-done((bf16[480,128]{1,0:T(8,128)(2,1)S(1)}, bf16[480,128]{1,0:T(8,128)(2,1)S(1)}, u32[]{:S(2)}, u32[]{:S(2)}) %collective-permute-start.12) | collective-permute-done | bytes 122912 | tf_op jit(solution)/shard_map/ppermute | solution.py:59
  53.0 0.1 collective-permute-start.13
  53.0 0.7 %reshape.13 = bf16[1,2,16,4,256]{4,3,2,1,0:T(4,128)(2,1)} reshape(bf16[128,256]{1,0:T(8,128)(2,1)S(1)} %get-tuple-element.32) | data formatting | bytes 131072 | tf_op jit(solution)/shard_map/reshape | solution.py:402
  53.7 0.8 %collective-permute-done.13.got_ref = f32[480,128]{1,0:T(8,128)S(1)} collective-permute-done((f32[480,128]{1,0:T(8,128)S(1)}, f32[480,128]{1,0:T(8,128)S(1)}, u32[]{:S(2)}, u32[]{:S(2)}) %collective-permute-start.13) | collective-permute-done | bytes 245792 | tf_op jit(solution)/shard_map/ppermute | solution.py:54
  54.5 0.8 %shard_map.95 = (f32[432,128]{1,0:T(8,128)}, f32[256,256]{1,0:T(8,128)}) custom-call(f32[480,128]{1,0:T(8,128)S(1)} %shard_map.94.own_ref, f32[480,128]{1,0:T(8,128)S(1)} %collective-permute-done.13.got_ref), custom_call_target="tpu_custom_call" | custom-call | tf_op jit(solution)/shard_map/pallas_call | solution.py:42
  (3 shorter events, 0.1 us)
Async XLA Ops:
  0.6 0.9 %copy-start.2 = (bf16[1,1024,64]{1,2,0:T(8,128)(2,1)S(1)}, bf16[1,1024,64]{1,2,0:T(8,128)(2,1)}, u32[]{:S(2)}) copy-start(bf16[1,1024,64]{1,2,0:T(8,128)(2,1)} %param.6) | copy-start | bytes 393220
  1.5 0.7 %copy-start.3 = (s32[1,1024]{1,0:T(1,128)S(1)}, s32[1,1024]{1,0:T(1,128)}, u32[]{:S(2)}) copy-start(s32[1,1024]{1,0:T(1,128)} %slot_hbm.1) | copy-start | bytes 12292
  2.2 0.7 %copy-start.4 = (s32[1,1024]{1,0:T(1,128)S(1)}, s32[1,1024]{1,0:T(1,128)}, u32[]{:S(2)}) copy-start(s32[1,1024]{1,0:T(1,128)} %voxel_hbm.1) | copy-start | bytes 12292
  3.1 11.2 %collective-permute-start.3 = (bf16[72,1024]{1,0:T(8,128)(2,1)S(1)}, bf16[72,1024]{1,0:T(8,128)(2,1)S(1)}, u32[]{:S(2)}, u32[]{:S(2)}) collective-permute-start(bf16[72,1024]{1,0:T(8,128)(2,1)S(1)} %shard_map.85.refs_0_), channel_id=1, source_target_pairs={{0,4},{1,5},{2,6},{3,7},{4,0},{5,1},{6,2},{7,3},{8,12},{9,13},{10,... | collective-permute-start | bytes 442376 | tf_op jit(solution)/shard_map/ppermute | solution.py:59
  7.2 7.7 %collective-permute-start.1 = (bf16[72,1024]{1,0:T(8,128)(2,1)S(1)}, bf16[72,1024]{1,0:T(8,128)(2,1)S(1)}, u32[]{:S(2)}, u32[]{:S(2)}) collective-permute-start(bf16[72,1024]{1,0:T(8,128)(2,1)S(1)} %shard_map.85.refs_0_), channel_id=1, source_target_pairs={{0,2},{1,3},{2,0},{3,1},{4,6},{5,7},{6,4},{7,5},{8,10},{9,11},{10,... | collective-permute-start | bytes 442376 | tf_op jit(solution)/shard_map/ppermute | solution.py:59
  14.3 5.1 %collective-permute-start.5 = (bf16[72,1024]{1,0:T(8,128)(2,1)S(1)}, bf16[72,1024]{1,0:T(8,128)(2,1)S(1)}, u32[]{:S(2)}, u32[]{:S(2)}) collective-permute-start(bf16[72,1024]{1,0:T(8,128)(2,1)S(1)} %collective-permute-done.3.refs_0_), channel_id=1, source_target_pairs={{0,2},{1,3},{2,0},{3,1},{4,6},{5,7},{6,4},{7,5},{8,10},{9,11},{10,... | collective-permute-start | bytes 442376 | tf_op jit(solution)/shard_map/ppermute | solution.py:59
  14.9 7.9 %collective-permute-start = (bf16[72,1024]{1,0:T(8,128)(2,1)S(1)}, bf16[72,1024]{1,0:T(8,128)(2,1)S(1)}, u32[]{:S(2)}, u32[]{:S(2)}) collective-permute-start(bf16[72,1024]{1,0:T(8,128)(2,1)S(1)} %shard_map.85.refs_0_), channel_id=1, source_target_pairs={{0,1},{1,0},{2,3},{3,2},{4,5},{5,4},{6,7},{7,6},{8,9},{9,8},{10,11... | collective-permute-start | bytes 442376 | tf_op jit(solution)/shard_map/ppermute | solution.py:54
  15.0 8.6 %collective-permute-start.2 = (bf16[72,1024]{1,0:T(8,128)(2,1)S(1)}, bf16[72,1024]{1,0:T(8,128)(2,1)S(1)}, u32[]{:S(2)}, u32[]{:S(2)}) collective-permute-start(bf16[72,1024]{1,0:T(8,128)(2,1)S(1)} %collective-permute-done.1.refs_0_), channel_id=1, source_target_pairs={{0,1},{1,0},{2,3},{3,2},{4,5},{5,4},{6,7},{7,6},{8,9},{9,8},{10,11... | collective-permute-start | bytes 442376 | tf_op jit(solution)/shard_map/ppermute | solution.py:54
  15.5 8.8 %collective-permute-start.4 = (bf16[72,1024]{1,0:T(8,128)(2,1)S(1)}, bf16[72,1024]{1,0:T(8,128)(2,1)S(1)}, u32[]{:S(2)}, u32[]{:S(2)}) collective-permute-start(bf16[72,1024]{1,0:T(8,128)(2,1)S(1)} %collective-permute-done.3.refs_0_), channel_id=1, source_target_pairs={{0,1},{1,0},{2,3},{3,2},{4,5},{5,4},{6,7},{7,6},{8,9},{9,8},{10,11... | collective-permute-start | bytes 442376 | tf_op jit(solution)/shard_map/ppermute | solution.py:54
  19.5 5.5 %collective-permute-start.6 = (bf16[72,1024]{1,0:T(8,128)(2,1)S(1)}, bf16[72,1024]{1,0:T(8,128)(2,1)S(1)}, u32[]{:S(2)}, u32[]{:S(2)}) collective-permute-start(bf16[72,1024]{1,0:T(8,128)(2,1)S(1)} %collective-permute-done.5.coded_ref), channel_id=1, source_target_pairs={{0,1},{1,0},{2,3},{3,2},{4,5},{5,4},{6,7},{7,6},{8,9},{9,8},{10,11... | collective-permute-start | bytes 442376 | tf_op jit(solution)/shard_map/ppermute | solution.py:54
  20.3 1.0 %copy-start = (bf16[1024,256]{1,0:T(8,128)(2,1)S(1)}, bf16[1024,256]{1,0:T(8,128)(2,1)}, u32[]{:S(2)}) copy-start(bf16[1024,256]{1,0:T(8,128)(2,1)} %down_ref.1) | copy-start | bytes 1572868
  21.4 1.0 %copy-start.1 = (bf16[1728,128]{1,0:T(8,128)(2,1)S(1)}, bf16[1728,128]{1,0:T(8,128)(2,1)}, u32[]{:S(2)}) copy-start(bf16[1728,128]{1,0:T(8,128)(2,1)} %conv_ref.1) | copy-start | bytes 1327108
  29.0 2.1 %collective-permute-start.7 = (bf16[4,480,128]{2,1,0:T(8,128)(2,1)S(1)}, bf16[4,480,128]{2,1,0:T(8,128)(2,1)S(1)}, u32[]{:S(2)}, u32[]{:S(2)}) collective-permute-start(bf16[4,480,128]{2,1,0:T(8,128)(2,1)S(1)} %get-tuple-element.34), channel_id=1, source_target_pairs={{0,1},{1,0},{2,3},{3,2},{4,5},{5,4},{6,7},{7,6},{8,9},{9,8},{10,11... | collective-permute-start | bytes 1474568 | tf_op jit(solution)/shard_map/ppermute | solution.py:54
  31.2 5.8 %collective-permute-start.8 = (bf16[480,128]{1,0:T(8,128)(2,1)S(1)}, bf16[480,128]{1,0:T(8,128)(2,1)S(1)}, u32[]{:S(2)}, u32[]{:S(2)}) collective-permute-start(bf16[480,128]{1,0:T(8,128)(2,1)S(1)} %get-tuple-element.36), channel_id=1, source_target_pairs={{0,8},{8,0},{16,24},{24,16},{1,9},{9,1},{17,25},{25,17},{2,10},{10... | collective-permute-start | bytes 368648 | tf_op jit(solution)/shard_map/ppermute | solution.py:67
  32.8 7.9 %collective-permute-start.9 = (bf16[480,128]{1,0:T(8,128)(2,1)S(1)}, bf16[480,128]{1,0:T(8,128)(2,1)S(1)}, u32[]{:S(2)}, u32[]{:S(2)}) collective-permute-start(bf16[480,128]{1,0:T(8,128)(2,1)S(1)} %get-tuple-element.37), channel_id=1, source_target_pairs={{0,16},{8,24},{16,0},{24,8},{1,17},{9,25},{17,1},{25,9},{2,18},{10... | collective-permute-start | bytes 368648 | tf_op jit(solution)/shard_map/ppermute | solution.py:67
  34.3 6.4 %collective-permute-start.10 = (bf16[480,128]{1,0:T(8,128)(2,1)S(1)}, bf16[480,128]{1,0:T(8,128)(2,1)S(1)}, u32[]{:S(2)}, u32[]{:S(2)}) collective-permute-start(bf16[480,128]{1,0:T(8,128)(2,1)S(1)} %get-tuple-element.38), channel_id=1, source_target_pairs={{0,24},{8,16},{16,8},{24,0},{1,25},{9,17},{17,9},{25,1},{2,26},{10... | collective-permute-start | bytes 368648 | tf_op jit(solution)/shard_map/ppermute | solution.py:67
  40.8 4.9 %collective-permute-start.11 = (bf16[480,128]{1,0:T(8,128)(2,1)S(1)}, bf16[480,128]{1,0:T(8,128)(2,1)S(1)}, u32[]{:S(2)}, u32[]{:S(2)}) collective-permute-start(bf16[480,128]{1,0:T(8,128)(2,1)S(1)} %shard_map.92.refs_0_), channel_id=1, source_target_pairs={{0,2},{1,3},{2,0},{3,1},{4,6},{5,7},{6,4},{7,5},{8,10},{9,11},{10,... | collective-permute-start | bytes 368648 | tf_op jit(solution)/shard_map/ppermute | solution.py:59
  45.8 7.2 %collective-permute-start.12 = (bf16[480,128]{1,0:T(8,128)(2,1)S(1)}, bf16[480,128]{1,0:T(8,128)(2,1)S(1)}, u32[]{:S(2)}, u32[]{:S(2)}) collective-permute-start(bf16[480,128]{1,0:T(8,128)(2,1)S(1)} %shard_map.93.refs_0_), channel_id=1, source_target_pairs={{0,4},{1,5},{2,6},{3,7},{4,0},{5,1},{6,2},{7,3},{8,12},{9,13},{10,... | collective-permute-start | bytes 368648 | tf_op jit(solution)/shard_map/ppermute | solution.py:59
  53.0 1.6 %collective-permute-start.13 = (f32[480,128]{1,0:T(8,128)S(1)}, f32[480,128]{1,0:T(8,128)S(1)}, u32[]{:S(2)}, u32[]{:S(2)}) collective-permute-start(f32[480,128]{1,0:T(8,128)S(1)} %shard_map.94.own_ref), channel_id=1, source_target_pairs={{0,1},{1,0},{2,3},{3,2},{4,5},{5,4},{6,7},{7,6},{8,9},{9,8},{10,11... | collective-permute-start | bytes 737288 | tf_op jit(solution)/shard_map/ppermute | solution.py:54

commit v4 on v3

v4 whole, which is shorter than its diff:
```python
import functools

import jax
import jax.numpy as jnp
from jax import lax
from jax.experimental import pallas as pl
from jax.experimental.pallas import tpu as pltpu
from jax.sharding import PartitionSpec as P

CIN = 64
C1 = 128
C2 = 256
SX = 4
SY = 32
SZ = 8
PTS_DEV = 1024
TAPS = 27
CODED = CIN + 8
LAYER = SZ * SY // 2
FAR = 3
BLOCK = 4
BF16 = jnp.bfloat16
F32 = jnp.float32
I32 = jnp.int32
NT = (((1,), (1,)), ((), ()))
TN = (((0,), (0,)), ((), ()))
VMEM_LIMIT = 24 * 1024 * 1024


def call(body, outs, scratch=(), pinned=0, loose=0, raw=0):
    single = not isinstance(outs, (list, tuple))
    vmem = pl.BlockSpec(memory_space=pltpu.VMEM)
    kernel = pl.pallas_call(
        body,
        out_shape=outs,
        in_specs=[vmem] * (pinned + loose) + [pl.BlockSpec(memory_space=pltpu.HBM)] * raw,
        out_specs=vmem if single else [vmem] * len(outs),
        scratch_shapes=list(scratch),
        compiler_params=pltpu.CompilerParams(vmem_limit_bytes=VMEM_LIMIT),
    )

    def run(*args):
        held = [pltpu.with_memory_space_constraint(a, pltpu.VMEM) for a in args[:pinned]]
        far = [pltpu.with_memory_space_constraint(a, pltpu.HBM) for a in args[pinned:]]
        return kernel(*held, *far)

    return run


def target(index, k, count):
    if count & (count - 1) == 0:
        return index ^ k
    return (index + k) % count


def swap_core(value, tiles):
    return lax.ppermute(value, "tile", [(i, i ^ 1) for i in range(tiles)])


def send_column(value, to, tiles):
    pairs = [(2 * i + c, 2 * to(i) + c) for i in range(tiles // 2) for c in range(2)]
    return lax.ppermute(value, "tile", pairs)


def send_sample(value, k, samples):
    return lax.ppermute(value, "sample", [(i, target(i, k, samples)) for i in range(samples)])


def encode_kernel(capacity, points_hbm, slot_hbm, voxel_hbm, out_ref, slot_ref, voxel_ref, sems):
    copies = [
        pltpu.make_async_copy(slot_hbm, slot_ref, sems.at[0]),
        pltpu.make_async_copy(voxel_hbm, voxel_ref, sems.at[1]),
        pltpu.make_async_copy(points_hbm, out_ref.at[0:CIN], sems.at[2]),
    ]
    for copy in copies:
        copy.start()
    copies[0].wait()
    copies[1].wait()
    slot = slot_ref[...]
    voxel = voxel_ref[...]
    if capacity & (capacity - 1) == 0:
        owner = slot >> (capacity.bit_length() - 1)
    else:
        owner = jnp.floor((slot.astype(F32) + 0.5) * (1.0 / capacity)).astype(I32)
    layer = owner * SX + (voxel >> 8) + 1
    z = voxel & 7
    y = (voxel >> 3) & 31
    place = ((z * 16 + (y >> 1)) << 1) + (y & 1)
    row = lax.broadcasted_iota(I32, (8, slot.shape[1]), 0)
    codes = jnp.where(row == 0, layer, jnp.where(row == 1, place, 0))
    out_ref[CIN:CODED, :] = codes.astype(F32).astype(BF16)
    copies[2].wait()


def slab_tiles():
    tile = lax.axis_index("tile")
    chip = tile >> 1
    core = tile & 1
    place = (chip >> 1) & 1
    low = jnp.where(place == 0, chip, chip ^ FAR)
    return (2 * low + core, 2 * (low ^ FAR) + core), place


def turn_matrix():
    here = lax.broadcasted_iota(I32, (128, 128), 0)
    there = lax.broadcasted_iota(I32, (128, 128), 1)
    return ((here >> 6) * 64 + (here & 3) * 16 + ((here >> 2) & 15) == there).astype(F32).astype(BF16)


def weights_kernel(conv_ref, down_ref, cot_ref, taps_ref, pairs_ref, turned_ref):
    zero_tap = jnp.zeros((CIN, C1), BF16)

    def tap(dx, dy, dz):
        start = ((dx * 3 + dy) * 3 + dz) * CIN
        return conv_ref[start : start + CIN, :]

    for dx in range(3):
        for dz in range(3):
            taps_ref[dx * 3 + dz] = jnp.concatenate(
                [
                    jnp.concatenate([tap(dx, 1, dz), tap(dx, 0, dz)], axis=1),
                    jnp.concatenate([tap(dx, 2, dz), tap(dx, 1, dz)], axis=1),
                    jnp.concatenate([tap(dx, 0, dz), zero_tap], axis=1),
                    jnp.concatenate([zero_tap, tap(dx, 2, dz)], axis=1),
                ],
                axis=0,
            )
    for ox in range(2):
        for oz in range(2):
            first = (ox * 4 + oz) * C1
            second = first + 2 * C1
            pairs_ref[ox * 2 + oz] = jnp.concatenate(
                [down_ref[first : first + C1, :], down_ref[second : second + C1, :]], axis=0
            )
    turned_ref[...] = lax.dot_general(turn_matrix(), cot_ref[...], TN, preferred_element_type=F32).astype(BF16)


def back_kernel(own_ref, got_ref, pairs_ref, cot_ref, back_ref):
    first = slab_tiles()[1] == 0
    own = own_ref[...].astype(F32)
    got = got_ref[...].astype(F32)
    cot = jnp.concatenate([jnp.where(first, own, got), jnp.where(first, got, own)], axis=0).astype(BF16)
    cot_ref[...] = cot
    for i in range(4):
        back_ref[i] = lax.dot_general(cot, pairs_ref[i], NT, preferred_element_type=F32)


def voxelize(ref):
    codes = ref[CIN:CODED, :].astype(F32).astype(I32)
    layer = codes[0:1, :]
    place = codes[1:2, :]
    odd = layer & 1
    spot = place >> 1
    side = place & 1
    row_iota = lax.broadcasted_iota(I32, (LAYER, PTS_DEV), 0).astype(F32).astype(BF16)
    small_iota = lax.broadcasted_iota(I32, (32, PTS_DEV), 0).astype(F32).astype(BF16)
    one = jnp.ones((), BF16)
    nought = jnp.zeros((), BF16)
    hot = []
    hot_plane = []
    for tile in slab_tiles()[0]:
        pair = (layer >> 1) - 2 * tile
        for p in range(3):
            code = jnp.where(pair == p, spot, 255).astype(F32).astype(BF16)
            hot.append(jnp.where(row_iota == code, one, nought))
        plane = (2 * pair + odd - 1) * SZ + (spot >> 4)
        plane = jnp.where((pair >= 0) & (pair <= 2) & (plane >= 0), plane, 255).astype(F32).astype(BF16)
        hot_plane.append(jnp.where(small_iota == plane, one, nought))
    group = odd * 2 + side
    features = ref[0:CIN, :]
    spread = jnp.concatenate(
        [features * (group == g).astype(F32).astype(BF16) for g in range(4)], axis=0
    )
    grid = lax.dot_general(jnp.concatenate(hot, axis=0), spread, NT, preferred_element_type=F32)
    line = ((spot & 15) * 2 + side).astype(F32).astype(BF16)
    hot_line = jnp.where(small_iota == line, one, nought)
    counts = lax.dot_general(
        jnp.concatenate(hot_plane, axis=0), hot_line, NT, preferred_element_type=F32
    )
    return grid, counts


def first_points_kernel(ref, grid_ref, counts_ref):
    grid_ref[...], counts_ref[...] = voxelize(ref)


def more_points_kernel(old_grid_ref, old_counts_ref, ref, grid_ref, counts_ref):
    grid, counts = voxelize(ref)
    grid_ref[...] = old_grid_ref[...] + grid
    counts_ref[...] = old_counts_ref[...] + counts


def add_grids_kernel(a_ref, a_counts_ref, b_ref, b_counts_ref, grid_ref, counts_ref):
    grid_ref[...] = a_ref[...] + b_ref[...]
    counts_ref[...] = a_counts_ref[...] + b_counts_ref[...]


def scene_kernel(
    samples, half_rows,
    grid_ref, counts_ref, more_grid_ref, more_counts_ref, taps_ref, cot_ref, back_ref,
    act_ref, mine_ref, other_ref, es_ref, pg_ref, wide_ref, tall_ref,
):
    counts = counts_ref[...] + more_counts_ref[...]

    es_ref[...] = jnp.zeros_like(es_ref)
    pg_ref[...] = jnp.zeros_like(pg_ref)
    line = lax.broadcasted_iota(I32, (LAYER, 2 * CIN), 0) & 15
    lane = lax.broadcasted_iota(I32, (LAYER, 2 * CIN), 1)
    for s in range(2):
        for x in range(SX + 2):
            rows = slice((s * 3 + x // 2) * LAYER, (s * 3 + x // 2 + 1) * LAYER)
            lanes = slice((x % 2) * 128, (x % 2 + 1) * 128)
            both = grid_ref[rows, lanes] + more_grid_ref[rows, lanes]
            turned = pltpu.roll(both, CIN, 1)
            before = jnp.where(line == 0, 0.0, pltpu.roll(turned, 1, 0))
            after = jnp.where(line == 15, 0.0, pltpu.roll(turned, LAYER - 1, 0))
            sides = jnp.where(lane < CIN, before, after)
            es_ref[s, x, 1 : SZ + 1, :, 0:128] = both.astype(BF16).reshape(SZ, 16, 128)
            es_ref[s, x, 1 : SZ + 1, :, 128:256] = sides.astype(BF16).reshape(SZ, 16, 128)

    full = 2 * SX * LAYER
    flags = (counts > 0.5).astype(F32).astype(BF16)
    row_plane = lax.broadcasted_iota(I32, (full, 64), 0) >> 4
    pick = (row_plane == lax.broadcasted_iota(I32, (full, 64), 1)).astype(F32).astype(BF16)
    lines = jnp.dot(pick, flags, preferred_element_type=F32)
    row_line = lax.broadcasted_iota(I32, (full, 32), 0) & 15
    lines = jnp.where(row_line == (lax.broadcasted_iota(I32, (full, 32), 1) >> 1), lines, 0.0).astype(BF16)
    expand = (
        (lax.broadcasted_iota(I32, (32, 256), 0) & 1) == (lax.broadcasted_iota(I32, (32, 256), 1) >> 7)
    ).astype(F32).astype(BF16)
    active = jnp.dot(lines, expand, preferred_element_type=F32) > 0.5

    pre = jnp.zeros((full, 2 * C1), F32)
    for dx in range(3):
        for dz in range(3):
            part = es_ref[:, dx : dx + SX, dz : dz + SZ].reshape(full, 4 * CIN)
            pre = pre + jnp.dot(part, taps_ref[dx * 3 + dz], preferred_element_type=F32)

    sigmoid = 1.0 / (1.0 + jnp.exp(-pre))
    act = jnp.where(active, pre * sigmoid, 0.0).astype(BF16)
    slope = jnp.where(active, sigmoid * (1.0 + pre * (1.0 - sigmoid)), 0.0)

    act = act.reshape(2, 2, 2, 4, 2, 16, 2 * C1)
    slope = slope.reshape(2, 2, 2, 4, 2, 16, 2 * C1)
    cot = cot_ref[...]
    for ox in range(2):
        for oz in range(2):
            block = act[:, :, ox, :, oz].reshape(256, 2 * C1)
            act_ref[0, ox * 2 + oz] = block[:128]
            act_ref[1, ox * 2 + oz] = block[128:]
            first = (ox * 4 + oz) * C1
            second = first + 2 * C1
            grad = lax.dot_general(block, cot, TN, preferred_element_type=F32)
            wide_ref[first : first + C1, :] = grad[0:C1]
            wide_ref[second : second + C1, :] = grad[C1:]
            back = back_ref[ox * 2 + oz]
            part = (back * slope[:, :, ox, :, oz].reshape(256, 2 * C1)).astype(BF16)
            part = part.reshape(2, 2, 4, 16, 2 * C1)
            for s in range(2):
                for u in range(2):
                    for w in range(4):
                        pg_ref[s, 2 * u + ox, 1 + 2 * w + oz] = part[s, u, w]

    flipped = es_ref[:, :, 1 : SZ + 1].reshape(2 * (SX + 2) * LAYER, 4 * CIN).T
    half = (SX + 2) * LAYER
    for dx in range(3):
        rows = jnp.concatenate(
            [flipped[:, s * half + dx * LAYER : s * half + (dx + SX) * LAYER] for s in range(2)], axis=1
        )
        for dz in range(3):
            part = pg_ref[:, :, 2 - dz : 2 - dz + SZ].reshape(full, 2 * C1)
            grad = jnp.dot(rows, part, preferred_element_type=F32)
            sums = (
                grad[0:64, 128:256] + grad[128:192, 0:128],
                grad[0:64, 0:128] + grad[64:128, 128:256],
                grad[64:128, 0:128] + grad[192:256, 128:256],
            )
            for dy in range(3):
                start = ((dx * 3 + dy) * 3 + dz) * CIN
                tall_ref[start : start + CIN, :] = sums[dy]

    conv_rows = TAPS * CIN // samples
    down_rows = 8 * C1 // samples
    filler = 2 * half_rows - conv_rows - 2 * down_rows

    def leave(mine_first):
        for s in range(samples):
            pieces = [
                tall_ref[s * conv_rows : (s + 1) * conv_rows, :],
                wide_ref[s * down_rows : (s + 1) * down_rows, 0:128],
                wide_ref[s * down_rows : (s + 1) * down_rows, 128:256],
            ]
            if filler:
                pieces.append(jnp.zeros((filler, 128), F32))
            chunk = jnp.concatenate(pieces, axis=0)
            low, high = chunk[:half_rows], chunk[half_rows:]
            mine, other = (low, high) if mine_first else (high, low)
            mine_ref[s] = mine
            other_ref[s] = other.astype(BF16)

    core = lax.axis_index("tile") & 1

    @pl.when(core == 0)
    def _():
        leave(True)

    @pl.when(core == 1)
    def _():
        leave(False)


def down_kernel(act_ref, pairs_ref, out_ref):
    place = slab_tiles()[1]
    down = jnp.zeros((128, C2), F32)
    for i in range(4):
        down = down + jnp.dot(act_ref[place, i], pairs_ref[i], preferred_element_type=F32)
    out_ref[...] = jnp.dot(turn_matrix(), down.astype(BF16), preferred_element_type=F32).astype(BF16)


def share_samples_kernel(samples, mine_ref, got_ref, keep_ref, *send_refs):
    me = lax.axis_index("sample")
    keep_ref[...] = mine_ref[me] + got_ref[me].astype(F32)
    for k, ref in enumerate(send_refs, 1):
        to = target(me, k, samples)
        ref[...] = (mine_ref[to] + got_ref[to].astype(F32)).astype(BF16)


def sum_kernel(*refs):
    total = refs[0][...].astype(F32)
    for ref in refs[1:-1]:
        total = total + ref[...].astype(F32)
    refs[-1][...] = total.astype(refs[-1].dtype)


def ordered_sum_kernel(own_ref, *refs):
    held_ref, out_ref = refs[-1], refs[-2]
    count = len(refs) - 1
    me = lax.axis_index("tile") // (2 * BLOCK)
    held_ref[me] = own_ref[...].astype(F32)
    for j, ref in enumerate(refs[:-2], 1):
        held_ref[lax.rem(me - j + count, count)] = ref[...].astype(F32)
    total = held_ref[0]
    for i in range(1, count):
        total = total + held_ref[i]
    out_ref[...] = total


def finish_kernel(conv_rows, down_rows, own_ref, got_ref, conv_ref, down_ref):
    first = (lax.axis_index("tile") & 1) == 0
    own = own_ref[...]
    got = got_ref[...]
    whole = jnp.concatenate([jnp.where(first, own, got), jnp.where(first, got, own)], axis=0)
    conv_ref[...] = whole[:conv_rows]
    down_ref[:, 0:128] = whole[conv_rows : conv_rows + down_rows]
    down_ref[:, 128:256] = whole[conv_rows + down_rows : conv_rows + 2 * down_rows]


def local(points, slot, voxel, conv_weight, down_weight, cotangent):
    tiles = lax.axis_size("tile")
    samples = lax.axis_size("sample")
    chips = tiles // 2
    capacity = 2 * (PTS_DEV // tiles)
    conv_rows = TAPS * CIN // samples
    down_rows = 8 * C1 // samples
    half_rows = -(-(conv_rows + 2 * down_rows) // 32) * 16

    hbm = jax.ShapeDtypeStruct
    shape = pltpu.VMEM
    coded = call(
        functools.partial(encode_kernel, capacity),
        shape((CODED, PTS_DEV), BF16),
        scratch=(
            pltpu.VMEM((1, PTS_DEV), I32),
            pltpu.VMEM((1, PTS_DEV), I32),
            pltpu.SemaphoreType.DMA((3,)),
        ),
        raw=3,
    )(points[0].T, slot, voxel)
    blocks = chips // BLOCK

    beyond = send_column(coded, lambda i: i ^ FAR, tiles)
    beside = send_column(coded, lambda i: i ^ 1, tiles)
    coded_swap = swap_core(coded, tiles)
    taps, pairs, cot = call(
        weights_kernel,
        (shape((9, 4 * CIN, 2 * C1), BF16), shape((4, 2 * C1, C2), BF16), shape((128, C2), BF16)),
        loose=3,
    )(conv_weight, down_weight, cotangent.reshape(128, C2))

    sums = (shape((6 * LAYER, 4 * CIN), F32), shape((64, 32), F32))

    def add(grid, piece):
        if grid is None:
            return call(first_points_kernel, sums, pinned=1)(piece)
        return call(more_points_kernel, sums, pinned=3)(*grid, piece)

    grid = add(None, coded)
    beyond, cot, pairs, grid = lax.optimization_barrier((beyond, cot, pairs, grid))
    across = send_column(beyond, lambda i: i ^ 1, tiles)
    cot_got = send_column(cot, lambda i: i ^ FAR, tiles)
    beside_swap = swap_core(beside, tiles)
    beyond_swap = swap_core(beyond, tiles)
    for piece in (coded_swap, beside, beside_swap):
        grid = add(grid, piece)
    more = add(add(None, beyond), beyond_swap)
    for j in range(1, blocks):
        got = [
            send_column(coded, lambda i: (i // BLOCK + j) % blocks * BLOCK + (i % BLOCK ^ m), tiles)
            for m in (0, 1, 3, 2)
        ]
        trees = []
        for first, second in ((got[0], got[1]), (got[2], got[3])):
            tree = None
            for piece in (first, swap_core(first, tiles), second, swap_core(second, tiles)):
                tree = add(tree, piece)
            trees.append(tree)
        both = call(add_grids_kernel, sums, pinned=4)(*trees[0], *trees[1])
        rest = both if j == 1 else call(add_grids_kernel, sums, pinned=4)(*rest, *both)
    cot, back = call(
        back_kernel, (shape((256, C2), BF16), shape((4, 256, 2 * C1), F32)), pinned=3
    )(cot, cot_got, pairs)
    across, grid, more, back = lax.optimization_barrier((across, grid, more, back))
    for piece in (across, swap_core(across, tiles)):
        more = add(more, piece)
    if blocks > 1:
        grid = call(add_grids_kernel, sums, pinned=4)(*grid, *more)
        more = rest

    act, mine, other = call(
        functools.partial(scene_kernel, samples, half_rows),
        (
            shape((2, 4, 128, 2 * C1), BF16),
            shape((samples, half_rows, 128), F32),
            shape((samples, half_rows, 128), BF16),
        ),
        scratch=(
            pltpu.VMEM((2, SX + 2, SZ + 2, 16, 4 * CIN), BF16),
            pltpu.VMEM((2, SX, SZ + 2, 16, 2 * C1), BF16),
            pltpu.VMEM((8 * C1, C2), F32),
            pltpu.VMEM((TAPS * CIN, C1), F32),
        ),
        pinned=7,
    )(*grid, *more, taps, cot, back)

    got = swap_core(other, tiles)
    keep, *sends = call(
        functools.partial(share_samples_kernel, samples),
        [shape((half_rows, 128), F32)] + [shape((half_rows, 128), BF16)] * (samples - 1),
        pinned=2,
    )(mine, got)
    down = call(down_kernel, shape((128, C2), BF16), pinned=2)(act, pairs)
    got = [send_sample(value, k, samples) for k, value in enumerate(sends, 1)]
    total = call(sum_kernel, shape((half_rows, 128), BF16), pinned=samples)(keep, *got)
    got = send_column(total, lambda i: i ^ 1, tiles)
    total = call(sum_kernel, shape((half_rows, 128), F32 if blocks == 1 else BF16), pinned=2)(total, got)
    if blocks > 1:
        got = [send_column(total, lambda i: (i + j * BLOCK) % chips, tiles) for j in range(1, blocks)]
        total = call(
            ordered_sum_kernel,
            shape((half_rows, 128), F32),
            scratch=(pltpu.VMEM((blocks, half_rows, 128), F32),),
            pinned=blocks,
        )(total, *got)
    conv_grad, down_grad = call(
        functools.partial(finish_kernel, conv_rows, down_rows),
        (hbm((conv_rows, C1), F32), hbm((down_rows, C2), F32)),
        pinned=2,
    )(total, swap_core(total, tiles))
    return (down.reshape(1, SX // 2, SY // 2, SZ // 2, C2), conv_grad, down_grad)


def solution(mesh):
    placed = (
        P("sample", "tile", None),
        P("sample", "tile"),
        P("sample", "tile"),
        P(),
        P(),
        P("sample", "tile", None, None, None),
    )
    return jax.shard_map(
        local,
        mesh=mesh,
        in_specs=placed,
        out_specs=(P("sample", "tile", None, None, None), P("sample", None), P("sample", None)),
        check_vma=False,
    )
```

time: 55.7 us -> 51.4 us (0.923)
  Pallas kernels: 7.72 us -> 15.1 us
  waiting for transfers between devices: 25.8 us -> 19.7 us
  local copies, waits for them, and re-layouts: 5.83 us -> 2.15 us
  starting transfers between devices: 15.2 us -> 13.4 us
    pallas_call x11 -> x17, Pallas kernels: 7.72 us -> 15.1 us  [run(): return kernel(*held, *far)]
    ppermute x5, waiting for transfers between devices: 17.5 us -> 11.2 us  [send_column(): return lax.ppermute(value, 'tile', pairs)]
    unnamed x10 -> x0, local copies, waits for them, and re-layouts: 4.32 us -> none
    ppermute x5, starting transfers between devices: 10.5 us -> 8.85 us  [send_column(): return lax.ppermute(value, 'tile', pairs)]
    reshape x1, local copies, waits for them, and re-layouts: 0.86 us -> 1.49 us  [local(): cotangent.reshape(128, C2)]
  transfers between devices with their start and end apart: 14 -> 14, of which waited for: 8 -> 8; matrix products, arithmetic and copies ran while one was open for 3% -> 4% of each run, Pallas kernels for 5% -> 13%
where the time goes in v4:
time: 51.4 us; the launch traced here: 51.1 us
  waiting for transfers between devices  19.7 us (38%)
  Pallas kernels  15.1 us (29%)
  starting transfers between devices  13.4 us (26%)
  local copies, waits for them, and re-layouts  2.15 us (4%)
  between operations  0.81 us (2%)
    pallas_call x17, Pallas kernels, run(): return kernel(*held, *far)  15.1 us
    ppermute x5, waiting for transfers between devices, send_column(): return lax.ppermute(value, 'tile', pairs)  11.2 us
    ppermute x5, starting transfers between devices, send_column(): return lax.ppermute(value, 'tile', pairs)  8.85 us
    ppermute x3, waiting for transfers between devices, send_sample(): lax.ppermute(value, 'sample', [(i, target(i, k, samples)) for i in range(...  5.75 us
    ppermute x3, starting transfers between devices, send_sample(): lax.ppermute(value, 'sample', [(i, target(i, k, samples)) for i in range(...  3.55 us
    ppermute x6, waiting for transfers between devices, swap_core(): return lax.ppermute(value, 'tile', [(i, i ^ 1) for i in range(tiles)])  2.82 us
    reshape x1, local copies, waits for them, and re-layouts, local(): cotangent.reshape(128, C2)  1.49 us
  transfers between devices with their start and end apart: 14, of which 8 were waited for; matrix products, arithmetic and copies ran while one was open for 4% of the time, Pallas kernels for 13%

profile of v4, /device:TPU:0, one launch (start us, length us, event | category | flops | bytes accessed | tf_op | source)
XLA Modules:
  0.0 51.1 jit_solution(13635812319239938994)
XLA Ops:
  0.6 1.0 %shard_map.85.ref = bf16[72,1024]{1,0:T(8,128)(2,1)S(1)} custom-call(bf16[64,1024]{1,0:T(8,128)(2,1)} %bitcast.3, s32[1,1024]{1,0:T(1,128)} %slot_hbm.1, s32[1,1024]{1,0:T(1,128)} %voxel_hbm.1), custom_call_target="tpu_custom_call" | custom-call | tf_op jit(solution)/shard_map/pallas_call | solution.py:45
  1.6 3.1 %collective-permute-start.3 = (bf16[72,1024]{1,0:T(8,128)(2,1)S(1)}, bf16[72,1024]{1,0:T(8,128)(2,1)S(1)}, u32[]{:S(2)}, u32[]{:S(2)}) collective-permute-start(bf16[72,1024]{1,0:T(8,128)(2,1)S(1)} %shard_map.85.ref), channel_id=1, source_target_pairs={{0,2},{1,3},{2,0},{3,1},{4,6},{5,7},{6,4},{7,5},{8,10},{9,11},{10,... | collective-permute-start | bytes 442376 | tf_op jit(solution)/shard_map/ppermute | solution.py:62
  4.7 2.5 %collective-permute-start = (bf16[72,1024]{1,0:T(8,128)(2,1)S(1)}, bf16[72,1024]{1,0:T(8,128)(2,1)S(1)}, u32[]{:S(2)}, u32[]{:S(2)}) collective-permute-start(bf16[72,1024]{1,0:T(8,128)(2,1)S(1)} %shard_map.85.ref), channel_id=1, source_target_pairs={{0,6},{1,7},{2,4},{3,5},{4,2},{5,3},{6,0},{7,1},{8,14},{9,15},{10,... | collective-permute-start | bytes 442376 | tf_op jit(solution)/shard_map/ppermute | solution.py:62
  7.2 0.0 collective-permute-start.2
  7.2 0.7 %shard_map.87 = (f32[768,256]{1,0:T(8,128)S(1)}, f32[64,32]{1,0:T(8,128)S(1)}) custom-call(bf16[72,1024]{1,0:T(8,128)(2,1)S(1)} %shard_map.85.ref), custom_call_target="tpu_custom_call" | custom-call | tf_op jit(solution)/shard_map/pallas_call | solution.py:45
  7.8 1.5 %reshape.12.cot_ref = bf16[128,256]{1,0:T(8,128)(2,1)} reshape(bf16[1,2,16,4,256]{4,3,2,1,0:T(4,128)(2,1)} %param.11) | data formatting | bytes 131072 | tf_op jit(solution)/shard_map/reshape | solution.py:388
  9.3 1.4 %shard_map.86 = (bf16[9,256,256]{2,1,0:T(8,128)(2,1)S(1)}, bf16[4,256,256]{2,1,0:T(8,128)(2,1)S(1)}, bf16[128,256]{1,0:T(8,128)(2,1)S(1)}) custom-call(bf16[1728,128]{1,0:T(8,128)(2,1)} %conv_ref.1, bf16[1024,256]{1,0:T(8,128)(2,1)} %down_ref.1, bf16[128,256]{1,0:T(8,128)(2,1)} %reshape.12.cot_ref), custom_call_target="tpu_custom_call" | custom-call | tf_op jit(solution)/shard_map/pallas_call | solution.py:45
  10.7 0.0 collective-permute-done.3.ref
  10.7 0.6 %collective-permute-start.4 = (bf16[72,1024]{1,0:T(8,128)(2,1)S(1)}, bf16[72,1024]{1,0:T(8,128)(2,1)S(1)}, u32[]{:S(2)}, u32[]{:S(2)}) collective-permute-start(bf16[72,1024]{1,0:T(8,128)(2,1)S(1)} %collective-permute-done.3.ref), channel_id=1, source_target_pairs={{0,1},{1,0},{2,3},{3,2},{4,5},{5,4},{6,7},{7,6},{8,9},{9,8},{10,11... | collective-permute-start | bytes 442376 | tf_op jit(solution)/shard_map/ppermute | solution.py:57
  11.3 2.7 %collective-permute-done.ref = bf16[72,1024]{1,0:T(8,128)(2,1)S(1)} collective-permute-done((bf16[72,1024]{1,0:T(8,128)(2,1)S(1)}, bf16[72,1024]{1,0:T(8,128)(2,1)S(1)}, u32[]{:S(2)}, u32[]{:S(2)}) %collective-permute-start) | collective-permute-done | bytes 147488 | tf_op jit(solution)/shard_map/ppermute | solution.py:62
  14.0 0.0 collective-permute-start.5
  14.0 0.6 %collective-permute-start.1 = (bf16[72,1024]{1,0:T(8,128)(2,1)S(1)}, bf16[72,1024]{1,0:T(8,128)(2,1)S(1)}, u32[]{:S(2)}, u32[]{:S(2)}) collective-permute-start(bf16[72,1024]{1,0:T(8,128)(2,1)S(1)} %collective-permute-done.ref), channel_id=1, source_target_pairs={{0,2},{1,3},{2,0},{3,1},{4,6},{5,7},{6,4},{7,5},{8,10},{9,11},{10,... | collective-permute-start | bytes 442376 | tf_op jit(solution)/shard_map/ppermute | solution.py:62
  14.6 2.6 %collective-permute-start.6 = (bf16[128,256]{1,0:T(8,128)(2,1)S(1)}, bf16[128,256]{1,0:T(8,128)(2,1)S(1)}, u32[]{:S(2)}, u32[]{:S(2)}) collective-permute-start(bf16[128,256]{1,0:T(8,128)(2,1)S(1)} %get-tuple-element.61.own_ref), channel_id=1, source_target_pairs={{0,6},{1,7},{2,4},{3,5},{4,2},{5,3},{6,0},{7,1},{8,14},{9,15},{10,... | collective-permute-start | bytes 196616 | tf_op jit(solution)/shard_map/ppermute | solution.py:62
  17.2 0.7 %shard_map.91 = (f32[768,256]{1,0:T(8,128)S(1)}, f32[64,32]{1,0:T(8,128)S(1)}) custom-call(bf16[72,1024]{1,0:T(8,128)(2,1)S(1)} %collective-permute-done.ref), custom_call_target="tpu_custom_call" | custom-call | tf_op jit(solution)/shard_map/pallas_call | solution.py:45
  17.9 0.0 collective-permute-done.2.ref
  17.9 0.7 %shard_map.88 = (f32[768,256]{1,0:T(8,128)S(1)}, f32[64,32]{1,0:T(8,128)S(1)}) custom-call(f32[768,256]{1,0:T(8,128)S(1)} %get-tuple-element.49.old_grid_ref, f32[64,32]{1,0:T(8,128)S(1)} %get-tuple-element.50.old_counts_ref, bf16[72,1024]{1,0:T(8,128)(2,1)S(1)} %collective-permute-done.2.ref), custom_call_target="tpu_custom_call" | custom-call | tf_op jit(solution)/shard_map/pallas_call | solution.py:45
  18.6 0.7 %shard_map.89 = (f32[768,256]{1,0:T(8,128)S(1)}, f32[64,32]{1,0:T(8,128)S(1)}) custom-call(f32[768,256]{1,0:T(8,128)S(1)} %get-tuple-element.51.old_grid_ref, f32[64,32]{1,0:T(8,128)S(1)} %get-tuple-element.52.old_counts_ref, bf16[72,1024]{1,0:T(8,128)(2,1)S(1)} %collective-permute-done.3.ref), custom_call_target="tpu_custom_call" | custom-call | tf_op jit(solution)/shard_map/pallas_call | solution.py:45
  19.2 3.6 %collective-permute-done.6.got_ref = bf16[128,256]{1,0:T(8,128)(2,1)S(1)} collective-permute-done((bf16[128,256]{1,0:T(8,128)(2,1)S(1)}, bf16[128,256]{1,0:T(8,128)(2,1)S(1)}, u32[]{:S(2)}, u32[]{:S(2)}) %collective-permute-start.6) | collective-permute-done | bytes 65568 | tf_op jit(solution)/shard_map/ppermute | solution.py:62
  22.9 0.3 shard_map.93
  23.2 0.0 collective-permute-done.4.ref
  23.2 0.7 %shard_map.90 = (f32[768,256]{1,0:T(8,128)S(1)}, f32[64,32]{1,0:T(8,128)S(1)}) custom-call(f32[768,256]{1,0:T(8,128)S(1)} %get-tuple-element.53.old_grid_ref, f32[64,32]{1,0:T(8,128)S(1)} %get-tuple-element.54.old_counts_ref, bf16[72,1024]{1,0:T(8,128)(2,1)S(1)} %collective-permute-done.4.ref), custom_call_target="tpu_custom_call" | custom-call | tf_op jit(solution)/shard_map/pallas_call | solution.py:45
  23.9 0.0 collective-permute-done.5.ref
  23.9 0.7 %shard_map.92 = (f32[768,256]{1,0:T(8,128)S(1)}, f32[64,32]{1,0:T(8,128)S(1)}) custom-call(f32[768,256]{1,0:T(8,128)S(1)} %get-tuple-element.57.old_grid_ref, f32[64,32]{1,0:T(8,128)S(1)} %get-tuple-element.58.old_counts_ref, bf16[72,1024]{1,0:T(8,128)(2,1)S(1)} %collective-permute-done.5.ref), custom_call_target="tpu_custom_call" | custom-call | tf_op jit(solution)/shard_map/pallas_call | solution.py:45
  24.6 0.0 collective-permute-done.1.ref
  24.6 0.1 collective-permute-start.7
  24.6 0.7 %shard_map.94 = (f32[768,256]{1,0:T(8,128)S(1)}, f32[64,32]{1,0:T(8,128)S(1)}) custom-call(f32[768,256]{1,0:T(8,128)S(1)} %get-tuple-element.66.old_grid_ref, f32[64,32]{1,0:T(8,128)S(1)} %get-tuple-element.67.old_counts_ref, bf16[72,1024]{1,0:T(8,128)(2,1)S(1)} %collective-permute-done.1.ref), custom_call_target="tpu_custom_call" | custom-call | tf_op jit(solution)/shard_map/pallas_call | solution.py:45
  25.3 0.7 %collective-permute-done.7.ref = bf16[72,1024]{1,0:T(8,128)(2,1)S(1)} collective-permute-done((bf16[72,1024]{1,0:T(8,128)(2,1)S(1)}, bf16[72,1024]{1,0:T(8,128)(2,1)S(1)}, u32[]{:S(2)}, u32[]{:S(2)}) %collective-permute-start.7) | collective-permute-done | bytes 147488 | tf_op jit(solution)/shard_map/ppermute | solution.py:57
  26.0 0.7 %shard_map.95 = (f32[768,256]{1,0:T(8,128)S(1)}, f32[64,32]{1,0:T(8,128)S(1)}) custom-call(f32[768,256]{1,0:T(8,128)S(1)} %get-tuple-element.69.old_grid_ref, f32[64,32]{1,0:T(8,128)S(1)} %get-tuple-element.70.old_counts_ref, bf16[72,1024]{1,0:T(8,128)(2,1)S(1)} %collective-permute-done.7.ref), custom_call_target="tpu_custom_call" | custom-call | tf_op jit(solution)/shard_map/pallas_call | solution.py:45
  26.7 5.7 %shard_map.96 = (bf16[2,4,128,256]{3,2,1,0:T(8,128)(2,1)S(1)}, f32[4,480,128]{2,1,0:T(8,128)S(1)}, bf16[4,480,128]{2,1,0:T(8,128)(2,1)S(1)}) custom-call(f32[768,256]{1,0:T(8,128)S(1)} %get-tuple-element.64.grid_ref, f32[64,32]{1,0:T(8,128)S(1)} %get-tuple-element.65.counts_ref, f32[768,256]{1,0:T(8,128)S(1)} %get-tuple-element.71.more_grid_ref, ...), custom_call_target="tpu_custom_call" | custom-call | tf_op jit(solution)/shard_map/pallas_call | solution.py:45
  32.4 0.2 collective-permute-start.8
  32.6 1.7 %collective-permute-done.8.got_ref = bf16[4,480,128]{2,1,0:T(8,128)(2,1)S(1)} collective-permute-done((bf16[4,480,128]{2,1,0:T(8,128)(2,1)S(1)}, bf16[4,480,128]{2,1,0:T(8,128)(2,1)S(1)}, u32[]{:S(2)}, u32[]{:S(2)}) %collective-permute-start.8) | collective-permute-done | bytes 491552 | tf_op jit(solution)/shard_map/ppermute | solution.py:57
  34.3 0.1 shard_map.98
  34.4 1.5 %collective-permute-start.9 = (bf16[480,128]{1,0:T(8,128)(2,1)S(1)}, bf16[480,128]{1,0:T(8,128)(2,1)S(1)}, u32[]{:S(2)}, u32[]{:S(2)}) collective-permute-start(bf16[480,128]{1,0:T(8,128)(2,1)S(1)} %get-tuple-element.80), channel_id=1, source_target_pairs={{0,8},{8,0},{16,24},{24,16},{1,9},{9,1},{17,25},{25,17},{2,10},{10... | collective-permute-start | bytes 368648 | tf_op jit(solution)/shard_map/ppermute | solution.py:66
  36.0 1.5 %collective-permute-start.10 = (bf16[480,128]{1,0:T(8,128)(2,1)S(1)}, bf16[480,128]{1,0:T(8,128)(2,1)S(1)}, u32[]{:S(2)}, u32[]{:S(2)}) collective-permute-start(bf16[480,128]{1,0:T(8,128)(2,1)S(1)} %get-tuple-element.81), channel_id=1, source_target_pairs={{0,16},{8,24},{16,0},{24,8},{1,17},{9,25},{17,1},{25,9},{2,18},{10... | collective-permute-start | bytes 368648 | tf_op jit(solution)/shard_map/ppermute | solution.py:66
  37.5 0.5 collective-permute-start.11
  38.0 2.1 %collective-permute-done.9.refs_1_ = bf16[480,128]{1,0:T(8,128)(2,1)S(1)} collective-permute-done((bf16[480,128]{1,0:T(8,128)(2,1)S(1)}, bf16[480,128]{1,0:T(8,128)(2,1)S(1)}, u32[]{:S(2)}, u32[]{:S(2)}) %collective-permute-start.9) | collective-permute-done | bytes 122912 | tf_op jit(solution)/shard_map/ppermute | solution.py:66
  40.1 3.7 %collective-permute-done.10.refs_2_ = bf16[480,128]{1,0:T(8,128)(2,1)S(1)} collective-permute-done((bf16[480,128]{1,0:T(8,128)(2,1)S(1)}, bf16[480,128]{1,0:T(8,128)(2,1)S(1)}, u32[]{:S(2)}, u32[]{:S(2)}) %collective-permute-start.10) | collective-permute-done | bytes 122912 | tf_op jit(solution)/shard_map/ppermute | solution.py:66
  43.7 0.0 collective-permute-done.11.refs_3_
  43.7 0.1 shard_map.99.refs_0_
  43.8 0.1 collective-permute-start.12
  43.9 4.9 %collective-permute-done.12.refs_1_ = bf16[480,128]{1,0:T(8,128)(2,1)S(1)} collective-permute-done((bf16[480,128]{1,0:T(8,128)(2,1)S(1)}, bf16[480,128]{1,0:T(8,128)(2,1)S(1)}, u32[]{:S(2)}, u32[]{:S(2)}) %collective-permute-start.12) | collective-permute-done | bytes 122912 | tf_op jit(solution)/shard_map/ppermute | solution.py:62
  48.8 0.1 collective-permute-start.13
  48.8 0.4 shard_map.97
  49.2 0.7 %reshape.13 = bf16[1,2,16,4,256]{4,3,2,1,0:T(4,128)(2,1)} reshape(bf16[128,256]{1,0:T(8,128)(2,1)S(1)} %shard_map.97) | data formatting | bytes 131072 | tf_op jit(solution)/shard_map/reshape | solution.py:469
  49.9 0.4 collective-permute-done.13.got_ref
  50.3 0.8 %shard_map.101 = (f32[432,128]{1,0:T(8,128)}, f32[256,256]{1,0:T(8,128)}) custom-call(f32[480,128]{1,0:T(8,128)S(1)} %shard_map.100.own_ref, f32[480,128]{1,0:T(8,128)S(1)} %collective-permute-done.13.got_ref), custom_call_target="tpu_custom_call" | custom-call | tf_op jit(solution)/shard_map/pallas_call | solution.py:45
  (1 shorter events, 0.0 us)
Async XLA Ops:
  1.6 9.1 %collective-permute-start.3 = (bf16[72,1024]{1,0:T(8,128)(2,1)S(1)}, bf16[72,1024]{1,0:T(8,128)(2,1)S(1)}, u32[]{:S(2)}, u32[]{:S(2)}) collective-permute-start(bf16[72,1024]{1,0:T(8,128)(2,1)S(1)} %shard_map.85.ref), channel_id=1, source_target_pairs={{0,2},{1,3},{2,0},{3,1},{4,6},{5,7},{6,4},{7,5},{8,10},{9,11},{10,... | collective-permute-start | bytes 442376 | tf_op jit(solution)/shard_map/ppermute | solution.py:62
  4.7 9.3 %collective-permute-start = (bf16[72,1024]{1,0:T(8,128)(2,1)S(1)}, bf16[72,1024]{1,0:T(8,128)(2,1)S(1)}, u32[]{:S(2)}, u32[]{:S(2)}) collective-permute-start(bf16[72,1024]{1,0:T(8,128)(2,1)S(1)} %shard_map.85.ref), channel_id=1, source_target_pairs={{0,6},{1,7},{2,4},{3,5},{4,2},{5,3},{6,0},{7,1},{8,14},{9,15},{10,... | collective-permute-start | bytes 442376 | tf_op jit(solution)/shard_map/ppermute | solution.py:62
  7.2 10.7 %collective-permute-start.2 = (bf16[72,1024]{1,0:T(8,128)(2,1)S(1)}, bf16[72,1024]{1,0:T(8,128)(2,1)S(1)}, u32[]{:S(2)}, u32[]{:S(2)}) collective-permute-start(bf16[72,1024]{1,0:T(8,128)(2,1)S(1)} %shard_map.85.ref), channel_id=1, source_target_pairs={{0,1},{1,0},{2,3},{3,2},{4,5},{5,4},{6,7},{7,6},{8,9},{9,8},{10,11... | collective-permute-start | bytes 442376 | tf_op jit(solution)/shard_map/ppermute | solution.py:57
  10.7 12.4 %collective-permute-start.4 = (bf16[72,1024]{1,0:T(8,128)(2,1)S(1)}, bf16[72,1024]{1,0:T(8,128)(2,1)S(1)}, u32[]{:S(2)}, u32[]{:S(2)}) collective-permute-start(bf16[72,1024]{1,0:T(8,128)(2,1)S(1)} %collective-permute-done.3.ref), channel_id=1, source_target_pairs={{0,1},{1,0},{2,3},{3,2},{4,5},{5,4},{6,7},{7,6},{8,9},{9,8},{10,11... | collective-permute-start | bytes 442376 | tf_op jit(solution)/shard_map/ppermute | solution.py:57
  14.0 9.9 %collective-permute-start.5 = (bf16[72,1024]{1,0:T(8,128)(2,1)S(1)}, bf16[72,1024]{1,0:T(8,128)(2,1)S(1)}, u32[]{:S(2)}, u32[]{:S(2)}) collective-permute-start(bf16[72,1024]{1,0:T(8,128)(2,1)S(1)} %collective-permute-done.ref), channel_id=1, source_target_pairs={{0,1},{1,0},{2,3},{3,2},{4,5},{5,4},{6,7},{7,6},{8,9},{9,8},{10,11... | collective-permute-start | bytes 442376 | tf_op jit(solution)/shard_map/ppermute | solution.py:57
  14.0 10.6 %collective-permute-start.1 = (bf16[72,1024]{1,0:T(8,128)(2,1)S(1)}, bf16[72,1024]{1,0:T(8,128)(2,1)S(1)}, u32[]{:S(2)}, u32[]{:S(2)}) collective-permute-start(bf16[72,1024]{1,0:T(8,128)(2,1)S(1)} %collective-permute-done.ref), channel_id=1, source_target_pairs={{0,2},{1,3},{2,0},{3,1},{4,6},{5,7},{6,4},{7,5},{8,10},{9,11},{10,... | collective-permute-start | bytes 442376 | tf_op jit(solution)/shard_map/ppermute | solution.py:62
  14.6 8.3 %collective-permute-start.6 = (bf16[128,256]{1,0:T(8,128)(2,1)S(1)}, bf16[128,256]{1,0:T(8,128)(2,1)S(1)}, u32[]{:S(2)}, u32[]{:S(2)}) collective-permute-start(bf16[128,256]{1,0:T(8,128)(2,1)S(1)} %get-tuple-element.61.own_ref), channel_id=1, source_target_pairs={{0,6},{1,7},{2,4},{3,5},{4,2},{5,3},{6,0},{7,1},{8,14},{9,15},{10,... | collective-permute-start | bytes 196616 | tf_op jit(solution)/shard_map/ppermute | solution.py:62
  24.6 1.4 %collective-permute-start.7 = (bf16[72,1024]{1,0:T(8,128)(2,1)S(1)}, bf16[72,1024]{1,0:T(8,128)(2,1)S(1)}, u32[]{:S(2)}, u32[]{:S(2)}) collective-permute-start(bf16[72,1024]{1,0:T(8,128)(2,1)S(1)} %collective-permute-done.1.ref), channel_id=1, source_target_pairs={{0,1},{1,0},{2,3},{3,2},{4,5},{5,4},{6,7},{7,6},{8,9},{9,8},{10,11... | collective-permute-start | bytes 442376 | tf_op jit(solution)/shard_map/ppermute | solution.py:57
  32.4 1.9 %collective-permute-start.8 = (bf16[4,480,128]{2,1,0:T(8,128)(2,1)S(1)}, bf16[4,480,128]{2,1,0:T(8,128)(2,1)S(1)}, u32[]{:S(2)}, u32[]{:S(2)}) collective-permute-start(bf16[4,480,128]{2,1,0:T(8,128)(2,1)S(1)} %get-tuple-element.78), channel_id=1, source_target_pairs={{0,1},{1,0},{2,3},{3,2},{4,5},{5,4},{6,7},{7,6},{8,9},{9,8},{10,11... | collective-permute-start | bytes 1474568 | tf_op jit(solution)/shard_map/ppermute | solution.py:57
  34.4 5.6 %collective-permute-start.9 = (bf16[480,128]{1,0:T(8,128)(2,1)S(1)}, bf16[480,128]{1,0:T(8,128)(2,1)S(1)}, u32[]{:S(2)}, u32[]{:S(2)}) collective-permute-start(bf16[480,128]{1,0:T(8,128)(2,1)S(1)} %get-tuple-element.80), channel_id=1, source_target_pairs={{0,8},{8,0},{16,24},{24,16},{1,9},{9,1},{17,25},{25,17},{2,10},{10... | collective-permute-start | bytes 368648 | tf_op jit(solution)/shard_map/ppermute | solution.py:66
  36.0 7.8 %collective-permute-start.10 = (bf16[480,128]{1,0:T(8,128)(2,1)S(1)}, bf16[480,128]{1,0:T(8,128)(2,1)S(1)}, u32[]{:S(2)}, u32[]{:S(2)}) collective-permute-start(bf16[480,128]{1,0:T(8,128)(2,1)S(1)} %get-tuple-element.81), channel_id=1, source_target_pairs={{0,16},{8,24},{16,0},{24,8},{1,17},{9,25},{17,1},{25,9},{2,18},{10... | collective-permute-start | bytes 368648 | tf_op jit(solution)/shard_map/ppermute | solution.py:66
  37.5 6.2 %collective-permute-start.11 = (bf16[480,128]{1,0:T(8,128)(2,1)S(1)}, bf16[480,128]{1,0:T(8,128)(2,1)S(1)}, u32[]{:S(2)}, u32[]{:S(2)}) collective-permute-start(bf16[480,128]{1,0:T(8,128)(2,1)S(1)} %get-tuple-element.82), channel_id=1, source_target_pairs={{0,24},{8,16},{16,8},{24,0},{1,25},{9,17},{17,9},{25,1},{2,26},{10... | collective-permute-start | bytes 368648 | tf_op jit(solution)/shard_map/ppermute | solution.py:66
  43.8 4.9 %collective-permute-start.12 = (bf16[480,128]{1,0:T(8,128)(2,1)S(1)}, bf16[480,128]{1,0:T(8,128)(2,1)S(1)}, u32[]{:S(2)}, u32[]{:S(2)}) collective-permute-start(bf16[480,128]{1,0:T(8,128)(2,1)S(1)} %shard_map.99.refs_0_), channel_id=1, source_target_pairs={{0,2},{1,3},{2,0},{3,1},{4,6},{5,7},{6,4},{7,5},{8,10},{9,11},{10,... | collective-permute-start | bytes 368648 | tf_op jit(solution)/shard_map/ppermute | solution.py:62
  48.8 1.6 %collective-permute-start.13 = (f32[480,128]{1,0:T(8,128)S(1)}, f32[480,128]{1,0:T(8,128)S(1)}, u32[]{:S(2)}, u32[]{:S(2)}) collective-permute-start(f32[480,128]{1,0:T(8,128)S(1)} %shard_map.100.own_ref), channel_id=1, source_target_pairs={{0,1},{1,0},{2,3},{3,2},{4,5},{5,4},{6,7},{7,6},{8,9},{9,8},{10,11... | collective-permute-start | bytes 737288 | tf_op jit(solution)/shard_map/ppermute | solution.py:57

commit v5 on v4

--- a/solution.py
+++ b/solution.py
@@ -180,27 +180,38 @@
     return grid, counts
 
 
-def first_points_kernel(ref, grid_ref, counts_ref):
-    grid_ref[...], counts_ref[...] = voxelize(ref)
-
-
-def more_points_kernel(old_grid_ref, old_counts_ref, ref, grid_ref, counts_ref):
-    grid, counts = voxelize(ref)
+def first_points_kernel(at, ref, grid_ref, counts_ref):
+    grid_ref[...], counts_ref[...] = voxelize(ref if at is None else ref.at[at])
+
+
+def more_points_kernel(at, old_grid_ref, old_counts_ref, ref, grid_ref, counts_ref):
+    grid, counts = voxelize(ref if at is None else ref.at[at])
     grid_ref[...] = old_grid_ref[...] + grid
     counts_ref[...] = old_counts_ref[...] + counts
 
 
-def add_grids_kernel(a_ref, a_counts_ref, b_ref, b_counts_ref, grid_ref, counts_ref):
+def stack_kernel(*refs):
+    for i, ref in enumerate(refs[:-1]):
+        refs[-1][i] = ref[...]
+
+
+def add_grids_kernel(*refs):
+    grid_ref, counts_ref = refs[-2:]
+    grid_ref[...] = (refs[0][...] + refs[2][...]) + (refs[4][...] + refs[6][...])
+    counts_ref[...] = (refs[1][...] + refs[3][...]) + (refs[5][...] + refs[7][...])
+
+
+def add_two_kernel(a_ref, a_counts_ref, b_ref, b_counts_ref, grid_ref, counts_ref):
     grid_ref[...] = a_ref[...] + b_ref[...]
     counts_ref[...] = a_counts_ref[...] + b_counts_ref[...]
 
 
 def scene_kernel(
     samples, half_rows,
-    grid_ref, counts_ref, more_grid_ref, more_counts_ref, taps_ref, cot_ref, back_ref,
+    grid0, counts0, grid1, counts1, grid2, counts2, grid3, counts3, taps_ref, cot_ref, back_ref,
     act_ref, mine_ref, other_ref, es_ref, pg_ref, wide_ref, tall_ref,
 ):
-    counts = counts_ref[...] + more_counts_ref[...]
+    counts = counts0[...] + counts1[...] + counts2[...] + counts3[...]
 
     es_ref[...] = jnp.zeros_like(es_ref)
     pg_ref[...] = jnp.zeros_like(pg_ref)
@@ -210,7 +221,7 @@
         for x in range(SX + 2):
             rows = slice((s * 3 + x // 2) * LAYER, (s * 3 + x // 2 + 1) * LAYER)
             lanes = slice((x % 2) * 128, (x % 2 + 1) * 128)
-            both = grid_ref[rows, lanes] + more_grid_ref[rows, lanes]
+            both = (grid0[rows, lanes] + grid1[rows, lanes]) + (grid2[rows, lanes] + grid3[rows, lanes])
             turned = pltpu.roll(both, CIN, 1)
             before = jnp.where(line == 0, 0.0, pltpu.roll(turned, 1, 0))
             after = jnp.where(line == 15, 0.0, pltpu.roll(turned, LAYER - 1, 0))
@@ -378,53 +389,58 @@
     )(points[0].T, slot, voxel)
     blocks = chips // BLOCK
 
+    sums = (shape((6 * LAYER, 4 * CIN), F32), shape((64, 32), F32))
+
+    def add(grid, piece, at=None):
+        if grid is None:
+            return call(functools.partial(first_points_kernel, at), sums, pinned=1)(piece)
+        return call(functools.partial(more_points_kernel, at), sums, pinned=3)(*grid, piece)
+
     beyond = send_column(coded, lambda i: i ^ FAR, tiles)
+    own = add(None, coded)
+    coded, own = lax.optimization_barrier((coded, own))
     beside = send_column(coded, lambda i: i ^ 1, tiles)
-    coded_swap = swap_core(coded, tiles)
     taps, pairs, cot = call(
         weights_kernel,
         (shape((9, 4 * CIN, 2 * C1), BF16), shape((4, 2 * C1, C2), BF16), shape((128, C2), BF16)),
         loose=3,
     )(conv_weight, down_weight, cotangent.reshape(128, C2))
-
-    sums = (shape((6 * LAYER, 4 * CIN), F32), shape((64, 32), F32))
-
-    def add(grid, piece):
-        if grid is None:
-            return call(first_points_kernel, sums, pinned=1)(piece)
-        return call(more_points_kernel, sums, pinned=3)(*grid, piece)
-
-    grid = add(None, coded)
-    beyond, cot, pairs, grid = lax.optimization_barrier((beyond, cot, pairs, grid))
+    beyond, taps, pairs, cot = lax.optimization_barrier((beyond, taps, pairs, cot))
     across = send_column(beyond, lambda i: i ^ 1, tiles)
+    far = add(None, beyond)
+    coded, beside, beyond, far, cot = lax.optimization_barrier((coded, beside, beyond, far, cot))
+    near_swap = swap_core(
+        call(stack_kernel, shape((3, CODED, PTS_DEV), BF16), pinned=3)(coded, beside, beyond), tiles
+    )
     cot_got = send_column(cot, lambda i: i ^ FAR, tiles)
-    beside_swap = swap_core(beside, tiles)
-    beyond_swap = swap_core(beyond, tiles)
-    for piece in (coded_swap, beside, beside_swap):
-        grid = add(grid, piece)
-    more = add(add(None, beyond), beyond_swap)
-    for j in range(1, blocks):
-        got = [
-            send_column(coded, lambda i: (i // BLOCK + j) % blocks * BLOCK + (i % BLOCK ^ m), tiles)
-            for m in (0, 1, 3, 2)
-        ]
-        trees = []
-        for first, second in ((got[0], got[1]), (got[2], got[3])):
-            tree = None
-            for piece in (first, swap_core(first, tiles), second, swap_core(second, tiles)):
-                tree = add(tree, piece)
-            trees.append(tree)
-        both = call(add_grids_kernel, sums, pinned=4)(*trees[0], *trees[1])
-        rest = both if j == 1 else call(add_grids_kernel, sums, pinned=4)(*rest, *both)
+    own = add(own, beside)
+    own_swap = add(add(None, near_swap, 0), near_swap, 1)
+    far_swap = add(None, near_swap, 2)
+    across, own, own_swap, far_swap, cot_got = lax.optimization_barrier((across, own, own_swap, far_swap, cot_got))
+    across_swap = swap_core(across, tiles)
+    far = add(far, across)
     cot, back = call(
         back_kernel, (shape((256, C2), BF16), shape((4, 256, 2 * C1), F32)), pinned=3
     )(cot, cot_got, pairs)
-    across, grid, more, back = lax.optimization_barrier((across, grid, more, back))
-    for piece in (across, swap_core(across, tiles)):
-        more = add(more, piece)
+    across_swap, far, cot, back = lax.optimization_barrier((across_swap, far, cot, back))
+    far_swap = add(far_swap, across_swap)
+    grids = [own, own_swap, far, far_swap]
     if blocks > 1:
-        grid = call(add_grids_kernel, sums, pinned=4)(*grid, *more)
-        more = rest
+        rest = call(add_grids_kernel, sums, pinned=8)(*grids[0], *grids[1], *grids[2], *grids[3])
+        for j in range(1, blocks):
+            got = [
+                send_column(coded, lambda i: (i // BLOCK + j) % blocks * BLOCK + (i % BLOCK ^ m), tiles)
+                for m in (0, 1, FAR, FAR ^ 1)
+            ]
+            swapped = [swap_core(piece, tiles) for piece in got]
+            trees = [
+                add(add(None, first), second)
+                for first, second in (got[:2], swapped[:2], got[2:], swapped[2:])
+            ]
+            both = call(add_grids_kernel, sums, pinned=8)(*trees[0], *trees[1], *trees[2], *trees[3])
+            parts = both if j == 1 else call(add_two_kernel, sums, pinned=4)(*parts, *both)
+        nothing = (jnp.zeros((6 * LAYER, 4 * CIN), F32), jnp.zeros((64, 32), F32))
+        grids = [rest, nothing, parts, nothing]
 
     act, mine, other = call(
         functools.partial(scene_kernel, samples, half_rows),
@@ -439,8 +455,8 @@
             pltpu.VMEM((8 * C1, C2), F32),
             pltpu.VMEM((TAPS * CIN, C1), F32),
         ),
-        pinned=7,
-    )(*grid, *more, taps, cot, back)
+        pinned=11,
+    )(*grids[0], *grids[1], *grids[2], *grids[3], taps, cot, back)
 
     got = swap_core(other, tiles)
     keep, *sends = call(
@@ -449,7 +465,9 @@
         pinned=2,
     )(mine, got)
     down = call(down_kernel, shape((128, C2), BF16), pinned=2)(act, pairs)
+    down = down.reshape(1, SX // 2, SY // 2, SZ // 2, C2)
     got = [send_sample(value, k, samples) for k, value in enumerate(sends, 1)]
+    *got, down = lax.optimization_barrier((*got, down))
     total = call(sum_kernel, shape((half_rows, 128), BF16), pinned=samples)(keep, *got)
     got = send_column(total, lambda i: i ^ 1, tiles)
     total = call(sum_kernel, shape((half_rows, 128), F32 if blocks == 1 else BF16), pinned=2)(total, got)
@@ -466,7 +484,7 @@
         (hbm((conv_rows, C1), F32), hbm((down_rows, C2), F32)),
         pinned=2,
     )(total, swap_core(total, tiles))
-    return (down.reshape(1, SX // 2, SY // 2, SZ // 2, C2), conv_grad, down_grad)
+    return (down, conv_grad, down_grad)
 
 
 def solution(mesh):

time: 51.4 us -> 49.1 us (0.955)
  starting transfers between devices: 13.4 us -> 12 us
  waiting for transfers between devices: 19.7 us -> 18.8 us
    ppermute x3, waiting for transfers between devices: 5.75 us -> 4.71 us  [send_sample(): lax.ppermute(value, 'sample', [(i, target(i, k, samples)) for i in range(...]
    ppermute x5, starting transfers between devices: 8.85 us -> 8.09 us  [send_column(): return lax.ppermute(value, 'tile', pairs)]
    ppermute x6 -> x4, waiting for transfers between devices: 2.82 us -> 3.54 us  [swap_core(): return lax.ppermute(value, 'tile', [(i, i ^ 1) for i in range(tiles)])]
    ppermute x5, waiting for transfers between devices: 11.2 us -> 10.6 us  [send_column(): return lax.ppermute(value, 'tile', pairs)]
    ppermute x6 -> x4, starting transfers between devices: 0.97 us -> 0.39 us  [swap_core(): return lax.ppermute(value, 'tile', [(i, i ^ 1) for i in range(tiles)])]
    pallas_call x17 -> x18, Pallas kernels: 15.1 us -> 15.1 us  [run(): return kernel(*held, *far)]
  transfers between devices with their start and end apart: 14 -> 12, of which waited for: 8 -> 9; matrix products, arithmetic and copies ran while one was open for 4% -> 4% of each run, Pallas kernels for 13% -> 14%
where the time goes in v5:
time: 49.1 us; the launch traced here: 48.9 us
  waiting for transfers between devices  18.8 us (38%)
  Pallas kernels  15.1 us (31%)
  starting transfers between devices  12 us (24%)
  local copies, waits for them, and re-layouts  2.15 us (4%)
  between operations  0.79 us (2%)
    pallas_call x18, Pallas kernels, run(): return kernel(*held, *far)  15.1 us
    ppermute x5, waiting for transfers between devices, send_column(): return lax.ppermute(value, 'tile', pairs)  10.6 us
    ppermute x5, starting transfers between devices, send_column(): return lax.ppermute(value, 'tile', pairs)  8.09 us
    ppermute x3, waiting for transfers between devices, send_sample(): lax.ppermute(value, 'sample', [(i, target(i, k, samples)) for i in range(...  4.71 us
    ppermute x3, starting transfers between devices, send_sample(): lax.ppermute(value, 'sample', [(i, target(i, k, samples)) for i in range(...  3.55 us
    ppermute x4, waiting for transfers between devices, swap_core(): return lax.ppermute(value, 'tile', [(i, i ^ 1) for i in range(tiles)])  3.54 us
    reshape x1, local copies, waits for them, and re-layouts, local(): cotangent.reshape(128, C2)  1.49 us
  transfers between devices with their start and end apart: 12, of which 9 were waited for; matrix products, arithmetic and copies ran while one was open for 4% of the time, Pallas kernels for 14%

profile of v5, /device:TPU:0, one launch (start us, length us, event | category | flops | bytes accessed | tf_op | source)
XLA Modules:
  0.0 48.9 jit_solution(3751504014468871653)
XLA Ops:
  0.6 1.0 %shard_map.85.ref.refs_0_ = bf16[72,1024]{1,0:T(8,128)(2,1)S(1)} custom-call(bf16[64,1024]{1,0:T(8,128)(2,1)} %bitcast.3, s32[1,1024]{1,0:T(1,128)} %slot_hbm.1, s32[1,1024]{1,0:T(1,128)} %voxel_hbm.1), custom_call_target="tpu_custom_call" | custom-call | tf_op jit(solution)/shard_map/pallas_call | solution.py:45
  1.6 5.1 %collective-permute-start = (bf16[72,1024]{1,0:T(8,128)(2,1)S(1)}, bf16[72,1024]{1,0:T(8,128)(2,1)S(1)}, u32[]{:S(2)}, u32[]{:S(2)}) collective-permute-start(bf16[72,1024]{1,0:T(8,128)(2,1)S(1)} %shard_map.85.ref.refs_0_), channel_id=1, source_target_pairs={{0,6},{1,7},{2,4},{3,5},{4,2},{5,3},{6,0},{7,1},{8,14},{9,15},{10,... | collective-permute-start | bytes 442376 | tf_op jit(solution)/shard_map/ppermute | solution.py:62
  6.7 0.7 %shard_map.87 = (f32[768,256]{1,0:T(8,128)S(1)}, f32[64,32]{1,0:T(8,128)S(1)}) custom-call(bf16[72,1024]{1,0:T(8,128)(2,1)S(1)} %shard_map.85.ref.refs_0_), custom_call_target="tpu_custom_call" | custom-call | tf_op jit(solution)/shard_map/pallas_call | solution.py:45
  7.4 0.1 collective-permute-start.2
  7.5 1.5 %reshape.12.cot_ref = bf16[128,256]{1,0:T(8,128)(2,1)} reshape(bf16[1,2,16,4,256]{4,3,2,1,0:T(4,128)(2,1)} %param.11) | data formatting | bytes 131072 | tf_op jit(solution)/shard_map/reshape | solution.py:407
  8.9 1.4 %shard_map.86 = (bf16[9,256,256]{2,1,0:T(8,128)(2,1)S(1)}, bf16[4,256,256]{2,1,0:T(8,128)(2,1)S(1)}, bf16[128,256]{1,0:T(8,128)(2,1)S(1)}) custom-call(bf16[1728,128]{1,0:T(8,128)(2,1)} %conv_ref.1, bf16[1024,256]{1,0:T(8,128)(2,1)} %down_ref.1, bf16[128,256]{1,0:T(8,128)(2,1)} %reshape.12.cot_ref), custom_call_target="tpu_custom_call" | custom-call | tf_op jit(solution)/shard_map/pallas_call | solution.py:45
  10.4 1.1 %collective-permute-done.ref.refs_2_ = bf16[72,1024]{1,0:T(8,128)(2,1)S(1)} collective-permute-done((bf16[72,1024]{1,0:T(8,128)(2,1)S(1)}, bf16[72,1024]{1,0:T(8,128)(2,1)S(1)}, u32[]{:S(2)}, u32[]{:S(2)}) %collective-permute-start) | collective-permute-done | bytes 147488 | tf_op jit(solution)/shard_map/ppermute | solution.py:62
  11.4 0.7 %shard_map.88 = (f32[768,256]{1,0:T(8,128)S(1)}, f32[64,32]{1,0:T(8,128)S(1)}) custom-call(bf16[72,1024]{1,0:T(8,128)(2,1)S(1)} %collective-permute-done.ref.refs_2_), custom_call_target="tpu_custom_call" | custom-call | tf_op jit(solution)/shard_map/pallas_call | solution.py:45
  12.1 1.7 %collective-permute-done.2.ref.refs_1_ = bf16[72,1024]{1,0:T(8,128)(2,1)S(1)} collective-permute-done((bf16[72,1024]{1,0:T(8,128)(2,1)S(1)}, bf16[72,1024]{1,0:T(8,128)(2,1)S(1)}, u32[]{:S(2)}, u32[]{:S(2)}) %collective-permute-start.2) | collective-permute-done | bytes 147488 | tf_op jit(solution)/shard_map/ppermute | solution.py:62
  13.9 0.1 collective-permute-start.3
  13.9 1.8 %collective-permute-start.1 = (bf16[72,1024]{1,0:T(8,128)(2,1)S(1)}, bf16[72,1024]{1,0:T(8,128)(2,1)S(1)}, u32[]{:S(2)}, u32[]{:S(2)}) collective-permute-start(bf16[72,1024]{1,0:T(8,128)(2,1)S(1)} %collective-permute-done.ref.refs_2_), channel_id=1, source_target_pairs={{0,2},{1,3},{2,0},{3,1},{4,6},{5,7},{6,4},{7,5},{8,10},{9,11},{10,... | collective-permute-start | bytes 442376 | tf_op jit(solution)/shard_map/ppermute | solution.py:62
  15.7 1.1 %collective-permute-start.4 = (bf16[128,256]{1,0:T(8,128)(2,1)S(1)}, bf16[128,256]{1,0:T(8,128)(2,1)S(1)}, u32[]{:S(2)}, u32[]{:S(2)}) collective-permute-start(bf16[128,256]{1,0:T(8,128)(2,1)S(1)} %get-tuple-element.86.own_ref), channel_id=1, source_target_pairs={{0,6},{1,7},{2,4},{3,5},{4,2},{5,3},{6,0},{7,1},{8,14},{9,15},{10,... | collective-permute-start | bytes 196616 | tf_op jit(solution)/shard_map/ppermute | solution.py:62
  16.8 0.7 %shard_map.89 = (f32[768,256]{1,0:T(8,128)S(1)}, f32[64,32]{1,0:T(8,128)S(1)}) custom-call(f32[768,256]{1,0:T(8,128)S(1)} %get-tuple-element.69.old_grid_ref, f32[64,32]{1,0:T(8,128)S(1)} %get-tuple-element.70.old_counts_ref, bf16[72,1024]{1,0:T(8,128)(2,1)S(1)} %collective-permute-done.2.ref.refs_1_), custom_call_target="tpu_custom_call" | custom-call | tf_op jit(solution)/shard_map/pallas_call | solution.py:45
  17.4 0.0 collective-permute-done.3.ref
  17.4 0.7 %shard_map.93 = (f32[768,256]{1,0:T(8,128)S(1)}, f32[64,32]{1,0:T(8,128)S(1)}) custom-call(bf16[3,72,1024]{2,1,0:T(8,128)(2,1)S(1)} %collective-permute-done.3.ref), custom_call_target="tpu_custom_call" | custom-call | tf_op jit(solution)/shard_map/pallas_call | solution.py:45
  18.1 0.7 %shard_map.91 = (f32[768,256]{1,0:T(8,128)S(1)}, f32[64,32]{1,0:T(8,128)S(1)}) custom-call(bf16[3,72,1024]{2,1,0:T(8,128)(2,1)S(1)} %collective-permute-done.3.ref), custom_call_target="tpu_custom_call" | custom-call | tf_op jit(solution)/shard_map/pallas_call | solution.py:45
  18.8 0.7 %shard_map.92 = (f32[768,256]{1,0:T(8,128)S(1)}, f32[64,32]{1,0:T(8,128)S(1)}) custom-call(f32[768,256]{1,0:T(8,128)S(1)} %get-tuple-element.80.old_grid_ref, f32[64,32]{1,0:T(8,128)S(1)} %get-tuple-element.81.old_counts_ref, bf16[3,72,1024]{2,1,0:T(8,128)(2,1)S(1)} %collective-permute-done.3.ref), custom_call_target="tpu_custom_call" | custom-call | tf_op jit(solution)/shard_map/pallas_call | solution.py:45
  19.4 2.9 %collective-permute-done.4.got_ref = bf16[128,256]{1,0:T(8,128)(2,1)S(1)} collective-permute-done((bf16[128,256]{1,0:T(8,128)(2,1)S(1)}, bf16[128,256]{1,0:T(8,128)(2,1)S(1)}, u32[]{:S(2)}, u32[]{:S(2)}) %collective-permute-start.4) | collective-permute-done | bytes 65568 | tf_op jit(solution)/shard_map/ppermute | solution.py:62
  22.3 0.0 collective-permute-done.1.ref
  22.4 0.0 collective-permute-start.5
  22.4 0.7 %shard_map.94 = (f32[768,256]{1,0:T(8,128)S(1)}, f32[64,32]{1,0:T(8,128)S(1)}) custom-call(f32[768,256]{1,0:T(8,128)S(1)} %get-tuple-element.92.old_grid_ref, f32[64,32]{1,0:T(8,128)S(1)} %get-tuple-element.93.old_counts_ref, bf16[72,1024]{1,0:T(8,128)(2,1)S(1)} %collective-permute-done.1.ref), custom_call_target="tpu_custom_call" | custom-call | tf_op jit(solution)/shard_map/pallas_call | solution.py:45
  23.0 0.3 shard_map.95
  23.4 0.4 collective-permute-done.5.ref
  23.7 0.7 %shard_map.96 = (f32[768,256]{1,0:T(8,128)S(1)}, f32[64,32]{1,0:T(8,128)S(1)}) custom-call(f32[768,256]{1,0:T(8,128)S(1)} %get-tuple-element.102.old_grid_ref, f32[64,32]{1,0:T(8,128)S(1)} %get-tuple-element.103.old_counts_ref, bf16[72,1024]{1,0:T(8,128)(2,1)S(1)} %collective-permute-done.5.ref), custom_call_target="tpu_custom_call" | custom-call | tf_op jit(solution)/shard_map/pallas_call | solution.py:45
  24.4 5.7 %shard_map.97 = (bf16[2,4,128,256]{3,2,1,0:T(8,128)(2,1)S(1)}, f32[4,480,128]{2,1,0:T(8,128)S(1)}, bf16[4,480,128]{2,1,0:T(8,128)(2,1)S(1)}) custom-call(f32[768,256]{1,0:T(8,128)S(1)} %get-tuple-element.87.grid0, f32[64,32]{1,0:T(8,128)S(1)} %get-tuple-element.88.counts0, f32[768,256]{1,0:T(8,128)S(1)} %get-tuple-element.89.grid1, ...), custom_call_target="tpu_custom_call" | custom-call | tf_op jit(solution)/shard_map/pallas_call | solution.py:45
  30.1 0.2 collective-permute-start.6
  30.4 1.7 %collective-permute-done.6.got_ref = bf16[4,480,128]{2,1,0:T(8,128)(2,1)S(1)} collective-permute-done((bf16[4,480,128]{2,1,0:T(8,128)(2,1)S(1)}, bf16[4,480,128]{2,1,0:T(8,128)(2,1)S(1)}, u32[]{:S(2)}, u32[]{:S(2)}) %collective-permute-start.6) | collective-permute-done | bytes 491552 | tf_op jit(solution)/shard_map/ppermute | solution.py:57
  32.1 0.1 shard_map.98
  32.2 1.6 %collective-permute-start.7 = (bf16[480,128]{1,0:T(8,128)(2,1)S(1)}, bf16[480,128]{1,0:T(8,128)(2,1)S(1)}, u32[]{:S(2)}, u32[]{:S(2)}) collective-permute-start(bf16[480,128]{1,0:T(8,128)(2,1)S(1)} %get-tuple-element.112), channel_id=1, source_target_pairs={{0,8},{8,0},{16,24},{24,16},{1,9},{9,1},{17,25},{25,17},{2,10},{10... | collective-permute-start | bytes 368648 | tf_op jit(solution)/shard_map/ppermute | solution.py:66
  33.7 1.5 %collective-permute-start.8 = (bf16[480,128]{1,0:T(8,128)(2,1)S(1)}, bf16[480,128]{1,0:T(8,128)(2,1)S(1)}, u32[]{:S(2)}, u32[]{:S(2)}) collective-permute-start(bf16[480,128]{1,0:T(8,128)(2,1)S(1)} %get-tuple-element.113), channel_id=1, source_target_pairs={{0,16},{8,24},{16,0},{24,8},{1,17},{9,25},{17,1},{25,9},{2,18},{10... | collective-permute-start | bytes 368648 | tf_op jit(solution)/shard_map/ppermute | solution.py:66
  35.2 0.5 collective-permute-start.9
  35.7 0.4 shard_map.99
  36.1 0.7 %reshape.13 = bf16[1,2,16,4,256]{4,3,2,1,0:T(4,128)(2,1)} reshape(bf16[128,256]{1,0:T(8,128)(2,1)S(1)} %shard_map.99) | data formatting | bytes 131072 | tf_op jit(solution)/shard_map/reshape | solution.py:468
  36.8 1.0 %collective-permute-done.7.refs_1_ = bf16[480,128]{1,0:T(8,128)(2,1)S(1)} collective-permute-done((bf16[480,128]{1,0:T(8,128)(2,1)S(1)}, bf16[480,128]{1,0:T(8,128)(2,1)S(1)}, u32[]{:S(2)}, u32[]{:S(2)}) %collective-permute-start.7) | collective-permute-done | bytes 122912 | tf_op jit(solution)/shard_map/ppermute | solution.py:66
  37.8 3.7 %collective-permute-done.8.refs_2_ = bf16[480,128]{1,0:T(8,128)(2,1)S(1)} collective-permute-done((bf16[480,128]{1,0:T(8,128)(2,1)S(1)}, bf16[480,128]{1,0:T(8,128)(2,1)S(1)}, u32[]{:S(2)}, u32[]{:S(2)}) %collective-permute-start.8) | collective-permute-done | bytes 122912 | tf_op jit(solution)/shard_map/ppermute | solution.py:66
  41.5 0.0 collective-permute-done.9.refs_3_
  41.5 0.1 shard_map.100.refs_0_
  41.6 0.1 collective-permute-start.10
  41.6 4.9 %collective-permute-done.10.refs_1_ = bf16[480,128]{1,0:T(8,128)(2,1)S(1)} collective-permute-done((bf16[480,128]{1,0:T(8,128)(2,1)S(1)}, bf16[480,128]{1,0:T(8,128)(2,1)S(1)}, u32[]{:S(2)}, u32[]{:S(2)}) %collective-permute-start.10) | collective-permute-done | bytes 122912 | tf_op jit(solution)/shard_map/ppermute | solution.py:62
  46.5 0.1 collective-permute-start.11
  46.6 1.5 %collective-permute-done.11.got_ref = f32[480,128]{1,0:T(8,128)S(1)} collective-permute-done((f32[480,128]{1,0:T(8,128)S(1)}, f32[480,128]{1,0:T(8,128)S(1)}, u32[]{:S(2)}, u32[]{:S(2)}) %collective-permute-start.11) | collective-permute-done | bytes 245792 | tf_op jit(solution)/shard_map/ppermute | solution.py:57
  48.1 0.8 %shard_map.102 = (f32[432,128]{1,0:T(8,128)}, f32[256,256]{1,0:T(8,128)}) custom-call(f32[480,128]{1,0:T(8,128)S(1)} %shard_map.101.own_ref, f32[480,128]{1,0:T(8,128)S(1)} %collective-permute-done.11.got_ref), custom_call_target="tpu_custom_call" | custom-call | tf_op jit(solution)/shard_map/pallas_call | solution.py:45
  (2 shorter events, 0.1 us)
Async XLA Ops:
  1.6 9.8 %collective-permute-start = (bf16[72,1024]{1,0:T(8,128)(2,1)S(1)}, bf16[72,1024]{1,0:T(8,128)(2,1)S(1)}, u32[]{:S(2)}, u32[]{:S(2)}) collective-permute-start(bf16[72,1024]{1,0:T(8,128)(2,1)S(1)} %shard_map.85.ref.refs_0_), channel_id=1, source_target_pairs={{0,6},{1,7},{2,4},{3,5},{4,2},{5,3},{6,0},{7,1},{8,14},{9,15},{10,... | collective-permute-start | bytes 442376 | tf_op jit(solution)/shard_map/ppermute | solution.py:62
  7.4 6.4 %collective-permute-start.2 = (bf16[72,1024]{1,0:T(8,128)(2,1)S(1)}, bf16[72,1024]{1,0:T(8,128)(2,1)S(1)}, u32[]{:S(2)}, u32[]{:S(2)}) collective-permute-start(bf16[72,1024]{1,0:T(8,128)(2,1)S(1)} %shard_map.85.ref.refs_0_), channel_id=1, source_target_pairs={{0,2},{1,3},{2,0},{3,1},{4,6},{5,7},{6,4},{7,5},{8,10},{9,11},{10,... | collective-permute-start | bytes 442376 | tf_op jit(solution)/shard_map/ppermute | solution.py:62
  13.9 3.6 %collective-permute-start.3 = (bf16[3,72,1024]{2,1,0:T(8,128)(2,1)S(1)}, bf16[3,72,1024]{2,1,0:T(8,128)(2,1)S(1)}, u32[]{:S(2)}, u32[]{:S(2)}) collective-permute-start(bf16[3,72,1024]{2,1,0:T(8,128)(2,1)S(1)} %shard_map.90), channel_id=1, source_target_pairs={{0,1},{1,0},{2,3},{3,2},{4,5},{5,4},{6,7},{7,6},{8,9},{9,8},{10,11... | collective-permute-start | bytes 1327112 | tf_op jit(solution)/shard_map/ppermute | solution.py:57
  13.9 8.4 %collective-permute-start.1 = (bf16[72,1024]{1,0:T(8,128)(2,1)S(1)}, bf16[72,1024]{1,0:T(8,128)(2,1)S(1)}, u32[]{:S(2)}, u32[]{:S(2)}) collective-permute-start(bf16[72,1024]{1,0:T(8,128)(2,1)S(1)} %collective-permute-done.ref.refs_2_), channel_id=1, source_target_pairs={{0,2},{1,3},{2,0},{3,1},{4,6},{5,7},{6,4},{7,5},{8,10},{9,11},{10,... | collective-permute-start | bytes 442376 | tf_op jit(solution)/shard_map/ppermute | solution.py:62
  15.7 6.7 %collective-permute-start.4 = (bf16[128,256]{1,0:T(8,128)(2,1)S(1)}, bf16[128,256]{1,0:T(8,128)(2,1)S(1)}, u32[]{:S(2)}, u32[]{:S(2)}) collective-permute-start(bf16[128,256]{1,0:T(8,128)(2,1)S(1)} %get-tuple-element.86.own_ref), channel_id=1, source_target_pairs={{0,6},{1,7},{2,4},{3,5},{4,2},{5,3},{6,0},{7,1},{8,14},{9,15},{10,... | collective-permute-start | bytes 196616 | tf_op jit(solution)/shard_map/ppermute | solution.py:62
  22.4 1.4 %collective-permute-start.5 = (bf16[72,1024]{1,0:T(8,128)(2,1)S(1)}, bf16[72,1024]{1,0:T(8,128)(2,1)S(1)}, u32[]{:S(2)}, u32[]{:S(2)}) collective-permute-start(bf16[72,1024]{1,0:T(8,128)(2,1)S(1)} %collective-permute-done.1.ref), channel_id=1, source_target_pairs={{0,1},{1,0},{2,3},{3,2},{4,5},{5,4},{6,7},{7,6},{8,9},{9,8},{10,11... | collective-permute-start | bytes 442376 | tf_op jit(solution)/shard_map/ppermute | solution.py:57
  30.1 1.9 %collective-permute-start.6 = (bf16[4,480,128]{2,1,0:T(8,128)(2,1)S(1)}, bf16[4,480,128]{2,1,0:T(8,128)(2,1)S(1)}, u32[]{:S(2)}, u32[]{:S(2)}) collective-permute-start(bf16[4,480,128]{2,1,0:T(8,128)(2,1)S(1)} %get-tuple-element.111), channel_id=1, source_target_pairs={{0,1},{1,0},{2,3},{3,2},{4,5},{5,4},{6,7},{7,6},{8,9},{9,8},{10,11... | collective-permute-start | bytes 1474568 | tf_op jit(solution)/shard_map/ppermute | solution.py:57
  32.2 5.6 %collective-permute-start.7 = (bf16[480,128]{1,0:T(8,128)(2,1)S(1)}, bf16[480,128]{1,0:T(8,128)(2,1)S(1)}, u32[]{:S(2)}, u32[]{:S(2)}) collective-permute-start(bf16[480,128]{1,0:T(8,128)(2,1)S(1)} %get-tuple-element.112), channel_id=1, source_target_pairs={{0,8},{8,0},{16,24},{24,16},{1,9},{9,1},{17,25},{25,17},{2,10},{10... | collective-permute-start | bytes 368648 | tf_op jit(solution)/shard_map/ppermute | solution.py:66
  33.7 7.8 %collective-permute-start.8 = (bf16[480,128]{1,0:T(8,128)(2,1)S(1)}, bf16[480,128]{1,0:T(8,128)(2,1)S(1)}, u32[]{:S(2)}, u32[]{:S(2)}) collective-permute-start(bf16[480,128]{1,0:T(8,128)(2,1)S(1)} %get-tuple-element.113), channel_id=1, source_target_pairs={{0,16},{8,24},{16,0},{24,8},{1,17},{9,25},{17,1},{25,9},{2,18},{10... | collective-permute-start | bytes 368648 | tf_op jit(solution)/shard_map/ppermute | solution.py:66
  35.2 6.3 %collective-permute-start.9 = (bf16[480,128]{1,0:T(8,128)(2,1)S(1)}, bf16[480,128]{1,0:T(8,128)(2,1)S(1)}, u32[]{:S(2)}, u32[]{:S(2)}) collective-permute-start(bf16[480,128]{1,0:T(8,128)(2,1)S(1)} %get-tuple-element.114), channel_id=1, source_target_pairs={{0,24},{8,16},{16,8},{24,0},{1,25},{9,17},{17,9},{25,1},{2,26},{10... | collective-permute-start | bytes 368648 | tf_op jit(solution)/shard_map/ppermute | solution.py:66
  41.6 4.9 %collective-permute-start.10 = (bf16[480,128]{1,0:T(8,128)(2,1)S(1)}, bf16[480,128]{1,0:T(8,128)(2,1)S(1)}, u32[]{:S(2)}, u32[]{:S(2)}) collective-permute-start(bf16[480,128]{1,0:T(8,128)(2,1)S(1)} %shard_map.100.refs_0_), channel_id=1, source_target_pairs={{0,2},{1,3},{2,0},{3,1},{4,6},{5,7},{6,4},{7,5},{8,10},{9,11},{10,... | collective-permute-start | bytes 368648 | tf_op jit(solution)/shard_map/ppermute | solution.py:62
  46.5 1.6 %collective-permute-start.11 = (f32[480,128]{1,0:T(8,128)S(1)}, f32[480,128]{1,0:T(8,128)S(1)}, u32[]{:S(2)}, u32[]{:S(2)}) collective-permute-start(f32[480,128]{1,0:T(8,128)S(1)} %shard_map.101.own_ref), channel_id=1, source_target_pairs={{0,1},{1,0},{2,3},{3,2},{4,5},{5,4},{6,7},{7,6},{8,9},{9,8},{10,11... | collective-permute-start | bytes 737288 | tf_op jit(solution)/shard_map/ppermute | solution.py:57

commit v6 on v5

--- a/solution.py
+++ b/solution.py
@@ -207,9 +207,9 @@
 
 
 def scene_kernel(
-    samples, half_rows,
+    samples,
     grid0, counts0, grid1, counts1, grid2, counts2, grid3, counts3, taps_ref, cot_ref, back_ref,
-    act_ref, mine_ref, other_ref, es_ref, pg_ref, wide_ref, tall_ref,
+    act_ref, es_ref, pg_ref, mine_ref, other_ref,
 ):
     counts = counts0[...] + counts1[...] + counts2[...] + counts3[...]
 
@@ -254,16 +254,22 @@
     act = act.reshape(2, 2, 2, 4, 2, 16, 2 * C1)
     slope = slope.reshape(2, 2, 2, 4, 2, 16, 2 * C1)
     cot = cot_ref[...]
+    low = (lax.axis_index("tile") & 1) == 0
+    down_rows = 8 * C1 // samples
+    step = min(C1, down_rows)
     for ox in range(2):
         for oz in range(2):
             block = act[:, :, ox, :, oz].reshape(256, 2 * C1)
             act_ref[0, ox * 2 + oz] = block[:128]
             act_ref[1, ox * 2 + oz] = block[128:]
-            first = (ox * 4 + oz) * C1
-            second = first + 2 * C1
             grad = lax.dot_general(block, cot, TN, preferred_element_type=F32)
-            wide_ref[first : first + C1, :] = grad[0:C1]
-            wide_ref[second : second + C1, :] = grad[C1:]
+            for p in range(2):
+                for i in range(0, C1, step):
+                    chunk, row = divmod((ox * 4 + p * 2 + oz) * C1 + i, down_rows)
+                    left = grad[p * C1 + i : p * C1 + i + step, 0:128]
+                    right = grad[p * C1 + i : p * C1 + i + step, 128:256]
+                    mine_ref[chunk, row : row + step, :] = jnp.where(low, left, right)
+                    other_ref[chunk, row : row + step, :] = jnp.where(low, right, left).astype(BF16)
             back = back_ref[ox * 2 + oz]
             part = (back * slope[:, :, ox, :, oz].reshape(256, 2 * C1)).astype(BF16)
             part = part.reshape(2, 2, 4, 16, 2 * C1)
@@ -272,6 +278,9 @@
                     for w in range(4):
                         pg_ref[s, 2 * u + ox, 1 + 2 * w + oz] = part[s, u, w]
 
+
+def conv_grad_kernel(samples, half_rows, es_ref, pg_ref, mine_ref, other_ref, tall_ref):
+    full = 2 * SX * LAYER
     flipped = es_ref[:, :, 1 : SZ + 1].reshape(2 * (SX + 2) * LAYER, 4 * CIN).T
     half = (SX + 2) * LAYER
     for dx in range(3):
@@ -291,33 +300,15 @@
                 tall_ref[start : start + CIN, :] = sums[dy]
 
     conv_rows = TAPS * CIN // samples
-    down_rows = 8 * C1 // samples
-    filler = 2 * half_rows - conv_rows - 2 * down_rows
-
-    def leave(mine_first):
-        for s in range(samples):
-            pieces = [
-                tall_ref[s * conv_rows : (s + 1) * conv_rows, :],
-                wide_ref[s * down_rows : (s + 1) * down_rows, 0:128],
-                wide_ref[s * down_rows : (s + 1) * down_rows, 128:256],
-            ]
-            if filler:
-                pieces.append(jnp.zeros((filler, 128), F32))
-            chunk = jnp.concatenate(pieces, axis=0)
-            low, high = chunk[:half_rows], chunk[half_rows:]
-            mine, other = (low, high) if mine_first else (high, low)
-            mine_ref[s] = mine
-            other_ref[s] = other.astype(BF16)
-
-    core = lax.axis_index("tile") & 1
-
-    @pl.when(core == 0)
-    def _():
-        leave(True)
-
-    @pl.when(core == 1)
-    def _():
-        leave(False)
+    filler = 2 * half_rows - conv_rows
+    low = (lax.axis_index("tile") & 1) == 0
+    for s in range(samples):
+        first = tall_ref[s * conv_rows : s * conv_rows + half_rows, :]
+        second = tall_ref[s * conv_rows + half_rows : (s + 1) * conv_rows, :]
+        if filler:
+            second = jnp.concatenate([second, jnp.zeros((filler, C1), F32)], axis=0)
+        mine_ref[s] = jnp.where(low, first, second)
+        other_ref[s] = jnp.where(low, second, first).astype(BF16)
 
 
 def down_kernel(act_ref, pairs_ref, out_ref):
@@ -328,12 +319,13 @@
     out_ref[...] = jnp.dot(turn_matrix(), down.astype(BF16), preferred_element_type=F32).astype(BF16)
 
 
-def share_samples_kernel(samples, mine_ref, got_ref, keep_ref, *send_refs):
+def share_samples_kernel(samples, mine_ref, got_ref, mine_conv_ref, got_conv_ref, keep_ref, *send_refs):
     me = lax.axis_index("sample")
-    keep_ref[...] = mine_ref[me] + got_ref[me].astype(F32)
-    for k, ref in enumerate(send_refs, 1):
-        to = target(me, k, samples)
-        ref[...] = (mine_ref[to] + got_ref[to].astype(F32)).astype(BF16)
+    rows = mine_ref.shape[1]
+    for k, ref in enumerate((keep_ref, *send_refs)):
+        to = target(me, k, samples) if k else me
+        ref[:rows] = (mine_ref[to] + got_ref[to].astype(F32)).astype(ref.dtype)
+        ref[rows:] = (mine_conv_ref[to] + got_conv_ref[to].astype(F32)).astype(ref.dtype)
 
 
 def sum_kernel(*refs):
@@ -356,14 +348,17 @@
     out_ref[...] = total
 
 
-def finish_kernel(conv_rows, down_rows, own_ref, got_ref, conv_ref, down_ref):
-    first = (lax.axis_index("tile") & 1) == 0
+def finish_kernel(down_rows, own_ref, got_ref, conv_ref, down_ref):
+    low = (lax.axis_index("tile") & 1) == 0
     own = own_ref[...]
     got = got_ref[...]
-    whole = jnp.concatenate([jnp.where(first, own, got), jnp.where(first, got, own)], axis=0)
-    conv_ref[...] = whole[:conv_rows]
-    down_ref[:, 0:128] = whole[conv_rows : conv_rows + down_rows]
-    down_ref[:, 128:256] = whole[conv_rows + down_rows : conv_rows + 2 * down_rows]
+    first = jnp.where(low, own, got)
+    second = jnp.where(low, got, own)
+    half_rows = first.shape[0] - down_rows
+    down_ref[:, 0:128] = first[:down_rows]
+    down_ref[:, 128:256] = second[:down_rows]
+    conv_ref[0:half_rows, :] = first[down_rows:]
+    conv_ref[half_rows:, :] = second[down_rows : down_rows + conv_ref.shape[0] - half_rows]
 
 
 def local(points, slot, voxel, conv_weight, down_weight, cotangent):
@@ -373,7 +368,7 @@
     capacity = 2 * (PTS_DEV // tiles)
     conv_rows = TAPS * CIN // samples
     down_rows = 8 * C1 // samples
-    half_rows = -(-(conv_rows + 2 * down_rows) // 32) * 16
+    half_rows = -(-conv_rows // 32) * 16
 
     hbm = jax.ShapeDtypeStruct
     shape = pltpu.VMEM
@@ -442,45 +437,49 @@
         nothing = (jnp.zeros((6 * LAYER, 4 * CIN), F32), jnp.zeros((64, 32), F32))
         grids = [rest, nothing, parts, nothing]
 
-    act, mine, other = call(
-        functools.partial(scene_kernel, samples, half_rows),
+    act, es, pg, mine, other = call(
+        functools.partial(scene_kernel, samples),
         (
             shape((2, 4, 128, 2 * C1), BF16),
-            shape((samples, half_rows, 128), F32),
-            shape((samples, half_rows, 128), BF16),
-        ),
-        scratch=(
-            pltpu.VMEM((2, SX + 2, SZ + 2, 16, 4 * CIN), BF16),
-            pltpu.VMEM((2, SX, SZ + 2, 16, 2 * C1), BF16),
-            pltpu.VMEM((8 * C1, C2), F32),
-            pltpu.VMEM((TAPS * CIN, C1), F32),
+            shape((2, SX + 2, SZ + 2, 16, 4 * CIN), BF16),
+            shape((2, SX, SZ + 2, 16, 2 * C1), BF16),
+            shape((samples, down_rows, 128), F32),
+            shape((samples, down_rows, 128), BF16),
         ),
         pinned=11,
     )(*grids[0], *grids[1], *grids[2], *grids[3], taps, cot, back)
 
     got = swap_core(other, tiles)
+    mine_conv, other_conv = call(
+        functools.partial(conv_grad_kernel, samples, half_rows),
+        (shape((samples, half_rows, C1), F32), shape((samples, half_rows, C1), BF16)),
+        scratch=(pltpu.VMEM((TAPS * CIN, C1), F32),),
+        pinned=2,
+    )(es, pg)
+    got, mine_conv, other_conv = lax.optimization_barrier((got, mine_conv, other_conv))
+    sum_rows = down_rows + half_rows
     keep, *sends = call(
         functools.partial(share_samples_kernel, samples),
-        [shape((half_rows, 128), F32)] + [shape((half_rows, 128), BF16)] * (samples - 1),
-        pinned=2,
-    )(mine, got)
+        [shape((sum_rows, 128), F32)] + [shape((sum_rows, 128), BF16)] * (samples - 1),
+        pinned=4,
+    )(mine, got, mine_conv, swap_core(other_conv, tiles))
+    terms = [keep] + [send_sample(value, k, samples) for k, value in enumerate(sends, 1)]
     down = call(down_kernel, shape((128, C2), BF16), pinned=2)(act, pairs)
     down = down.reshape(1, SX // 2, SY // 2, SZ // 2, C2)
-    got = [send_sample(value, k, samples) for k, value in enumerate(sends, 1)]
-    *got, down = lax.optimization_barrier((*got, down))
-    total = call(sum_kernel, shape((half_rows, 128), BF16), pinned=samples)(keep, *got)
+    *terms, down = lax.optimization_barrier((*terms, down))
+    total = call(sum_kernel, shape((sum_rows, 128), BF16), pinned=samples)(*terms)
     got = send_column(total, lambda i: i ^ 1, tiles)
-    total = call(sum_kernel, shape((half_rows, 128), F32 if blocks == 1 else BF16), pinned=2)(total, got)
+    total = call(sum_kernel, shape((sum_rows, 128), F32 if blocks == 1 else BF16), pinned=2)(total, got)
     if blocks > 1:
         got = [send_column(total, lambda i: (i + j * BLOCK) % chips, tiles) for j in range(1, blocks)]
         total = call(
             ordered_sum_kernel,
-            shape((half_rows, 128), F32),
-            scratch=(pltpu.VMEM((blocks, half_rows, 128), F32),),
+            shape((sum_rows, 128), F32),
+            scratch=(pltpu.VMEM((blocks, sum_rows, 128), F32),),
             pinned=blocks,
         )(total, *got)
     conv_grad, down_grad = call(
-        functools.partial(finish_kernel, conv_rows, down_rows),
+        functools.partial(finish_kernel, down_rows),
         (hbm((conv_rows, C1), F32), hbm((down_rows, C2), F32)),
         pinned=2,
     )(total, swap_core(total, tiles))

time: 49.1 us -> 47.3 us (0.963)
  Pallas kernels: 15.1 us -> 13.3 us
    pallas_call x18 -> x19, Pallas kernels: 15.1 us -> 13.3 us  [run(): return kernel(*held, *far)]
    ppermute x4 -> x5, waiting for transfers between devices: 3.54 us -> 2.99 us  [swap_core(): return lax.ppermute(value, 'tile', [(i, i ^ 1) for i in range(tiles)])]
  transfers between devices with their start and end apart: 12 -> 13, of which waited for: 9 -> 9; matrix products, arithmetic and copies ran while one was open for 4% -> 5% of each run, Pallas kernels for 14% -> 17%
where the time goes in v6:
time: 47.3 us; the launch traced here: 47.1 us
  waiting for transfers between devices  18.4 us (39%)
  Pallas kernels  13.3 us (28%)
  starting transfers between devices  12.4 us (26%)
  local copies, waits for them, and re-layouts  2.15 us (5%)
  between operations  0.81 us (2%)
    pallas_call x19, Pallas kernels, run(): return kernel(*held, *far)  13.3 us
    ppermute x5, waiting for transfers between devices, send_column(): return lax.ppermute(value, 'tile', pairs)  10.6 us
    ppermute x5, starting transfers between devices, send_column(): return lax.ppermute(value, 'tile', pairs)  8.09 us
    ppermute x3, waiting for transfers between devices, send_sample(): lax.ppermute(value, 'sample', [(i, target(i, k, samples)) for i in range(...  4.86 us
    ppermute x3, starting transfers between devices, send_sample(): lax.ppermute(value, 'sample', [(i, target(i, k, samples)) for i in range(...  3.57 us
    ppermute x5, waiting for transfers between devices, swap_core(): return lax.ppermute(value, 'tile', [(i, i ^ 1) for i in range(tiles)])  2.99 us
    reshape x1, local copies, waits for them, and re-layouts, local(): cotangent.reshape(128, C2)  1.49 us
  transfers between devices with their start and end apart: 13, of which 9 were waited for; matrix products, arithmetic and copies ran while one was open for 5% of the time, Pallas kernels for 17%

profile of v6, /device:TPU:0, one launch (start us, length us, event | category | flops | bytes accessed | tf_op | source)
XLA Modules:
  0.0 47.1 jit_solution(16858063242283188805)
XLA Ops:
  0.6 1.0 %shard_map.85.ref.refs_0_ = bf16[72,1024]{1,0:T(8,128)(2,1)S(1)} custom-call(bf16[64,1024]{1,0:T(8,128)(2,1)} %bitcast.3, s32[1,1024]{1,0:T(1,128)} %slot_hbm.1, s32[1,1024]{1,0:T(1,128)} %voxel_hbm.1), custom_call_target="tpu_custom_call" | custom-call | tf_op jit(solution)/shard_map/pallas_call | solution.py:45
  1.6 5.1 %collective-permute-start = (bf16[72,1024]{1,0:T(8,128)(2,1)S(1)}, bf16[72,1024]{1,0:T(8,128)(2,1)S(1)}, u32[]{:S(2)}, u32[]{:S(2)}) collective-permute-start(bf16[72,1024]{1,0:T(8,128)(2,1)S(1)} %shard_map.85.ref.refs_0_), channel_id=1, source_target_pairs={{0,6},{1,7},{2,4},{3,5},{4,2},{5,3},{6,0},{7,1},{8,14},{9,15},{10,... | collective-permute-start | bytes 442376 | tf_op jit(solution)/shard_map/ppermute | solution.py:62
  6.7 0.7 %shard_map.87 = (f32[768,256]{1,0:T(8,128)S(1)}, f32[64,32]{1,0:T(8,128)S(1)}) custom-call(bf16[72,1024]{1,0:T(8,128)(2,1)S(1)} %shard_map.85.ref.refs_0_), custom_call_target="tpu_custom_call" | custom-call | tf_op jit(solution)/shard_map/pallas_call | solution.py:45
  7.4 0.1 collective-permute-start.2
  7.5 1.5 %reshape.12.cot_ref = bf16[128,256]{1,0:T(8,128)(2,1)} reshape(bf16[1,2,16,4,256]{4,3,2,1,0:T(4,128)(2,1)} %param.11) | data formatting | bytes 131072 | tf_op jit(solution)/shard_map/reshape | solution.py:402
  8.9 1.4 %shard_map.86 = (bf16[9,256,256]{2,1,0:T(8,128)(2,1)S(1)}, bf16[4,256,256]{2,1,0:T(8,128)(2,1)S(1)}, bf16[128,256]{1,0:T(8,128)(2,1)S(1)}) custom-call(bf16[1728,128]{1,0:T(8,128)(2,1)} %conv_ref.1, bf16[1024,256]{1,0:T(8,128)(2,1)} %down_ref.1, bf16[128,256]{1,0:T(8,128)(2,1)} %reshape.12.cot_ref), custom_call_target="tpu_custom_call" | custom-call | tf_op jit(solution)/shard_map/pallas_call | solution.py:45
  10.4 1.1 %collective-permute-done.ref.refs_2_ = bf16[72,1024]{1,0:T(8,128)(2,1)S(1)} collective-permute-done((bf16[72,1024]{1,0:T(8,128)(2,1)S(1)}, bf16[72,1024]{1,0:T(8,128)(2,1)S(1)}, u32[]{:S(2)}, u32[]{:S(2)}) %collective-permute-start) | collective-permute-done | bytes 147488 | tf_op jit(solution)/shard_map/ppermute | solution.py:62
  11.4 0.7 %shard_map.88 = (f32[768,256]{1,0:T(8,128)S(1)}, f32[64,32]{1,0:T(8,128)S(1)}) custom-call(bf16[72,1024]{1,0:T(8,128)(2,1)S(1)} %collective-permute-done.ref.refs_2_), custom_call_target="tpu_custom_call" | custom-call | tf_op jit(solution)/shard_map/pallas_call | solution.py:45
  12.1 1.7 %collective-permute-done.2.ref.refs_1_ = bf16[72,1024]{1,0:T(8,128)(2,1)S(1)} collective-permute-done((bf16[72,1024]{1,0:T(8,128)(2,1)S(1)}, bf16[72,1024]{1,0:T(8,128)(2,1)S(1)}, u32[]{:S(2)}, u32[]{:S(2)}) %collective-permute-start.2) | collective-permute-done | bytes 147488 | tf_op jit(solution)/shard_map/ppermute | solution.py:62
  13.9 0.1 collective-permute-start.3
  13.9 1.8 %collective-permute-start.1 = (bf16[72,1024]{1,0:T(8,128)(2,1)S(1)}, bf16[72,1024]{1,0:T(8,128)(2,1)S(1)}, u32[]{:S(2)}, u32[]{:S(2)}) collective-permute-start(bf16[72,1024]{1,0:T(8,128)(2,1)S(1)} %collective-permute-done.ref.refs_2_), channel_id=1, source_target_pairs={{0,2},{1,3},{2,0},{3,1},{4,6},{5,7},{6,4},{7,5},{8,10},{9,11},{10,... | collective-permute-start | bytes 442376 | tf_op jit(solution)/shard_map/ppermute | solution.py:62
  15.7 1.1 %collective-permute-start.4 = (bf16[128,256]{1,0:T(8,128)(2,1)S(1)}, bf16[128,256]{1,0:T(8,128)(2,1)S(1)}, u32[]{:S(2)}, u32[]{:S(2)}) collective-permute-start(bf16[128,256]{1,0:T(8,128)(2,1)S(1)} %get-tuple-element.94.own_ref), channel_id=1, source_target_pairs={{0,6},{1,7},{2,4},{3,5},{4,2},{5,3},{6,0},{7,1},{8,14},{9,15},{10,... | collective-permute-start | bytes 196616 | tf_op jit(solution)/shard_map/ppermute | solution.py:62
  16.8 0.7 %shard_map.89 = (f32[768,256]{1,0:T(8,128)S(1)}, f32[64,32]{1,0:T(8,128)S(1)}) custom-call(f32[768,256]{1,0:T(8,128)S(1)} %get-tuple-element.77.old_grid_ref, f32[64,32]{1,0:T(8,128)S(1)} %get-tuple-element.78.old_counts_ref, bf16[72,1024]{1,0:T(8,128)(2,1)S(1)} %collective-permute-done.2.ref.refs_1_), custom_call_target="tpu_custom_call" | custom-call | tf_op jit(solution)/shard_map/pallas_call | solution.py:45
  17.4 0.0 collective-permute-done.3.ref
  17.4 0.7 %shard_map.93 = (f32[768,256]{1,0:T(8,128)S(1)}, f32[64,32]{1,0:T(8,128)S(1)}) custom-call(bf16[3,72,1024]{2,1,0:T(8,128)(2,1)S(1)} %collective-permute-done.3.ref), custom_call_target="tpu_custom_call" | custom-call | tf_op jit(solution)/shard_map/pallas_call | solution.py:45
  18.1 0.7 %shard_map.91 = (f32[768,256]{1,0:T(8,128)S(1)}, f32[64,32]{1,0:T(8,128)S(1)}) custom-call(bf16[3,72,1024]{2,1,0:T(8,128)(2,1)S(1)} %collective-permute-done.3.ref), custom_call_target="tpu_custom_call" | custom-call | tf_op jit(solution)/shard_map/pallas_call | solution.py:45
  18.8 0.7 %shard_map.92 = (f32[768,256]{1,0:T(8,128)S(1)}, f32[64,32]{1,0:T(8,128)S(1)}) custom-call(f32[768,256]{1,0:T(8,128)S(1)} %get-tuple-element.88.old_grid_ref, f32[64,32]{1,0:T(8,128)S(1)} %get-tuple-element.89.old_counts_ref, bf16[3,72,1024]{2,1,0:T(8,128)(2,1)S(1)} %collective-permute-done.3.ref), custom_call_target="tpu_custom_call" | custom-call | tf_op jit(solution)/shard_map/pallas_call | solution.py:45
  19.4 2.9 %collective-permute-done.4.got_ref = bf16[128,256]{1,0:T(8,128)(2,1)S(1)} collective-permute-done((bf16[128,256]{1,0:T(8,128)(2,1)S(1)}, bf16[128,256]{1,0:T(8,128)(2,1)S(1)}, u32[]{:S(2)}, u32[]{:S(2)}) %collective-permute-start.4) | collective-permute-done | bytes 65568 | tf_op jit(solution)/shard_map/ppermute | solution.py:62
  22.3 0.0 collective-permute-done.1.ref
  22.4 0.0 collective-permute-start.5
  22.4 0.7 %shard_map.94 = (f32[768,256]{1,0:T(8,128)S(1)}, f32[64,32]{1,0:T(8,128)S(1)}) custom-call(f32[768,256]{1,0:T(8,128)S(1)} %get-tuple-element.100.old_grid_ref, f32[64,32]{1,0:T(8,128)S(1)} %get-tuple-element.101.old_counts_ref, bf16[72,1024]{1,0:T(8,128)(2,1)S(1)} %collective-permute-done.1.ref), custom_call_target="tpu_custom_call" | custom-call | tf_op jit(solution)/shard_map/pallas_call | solution.py:45
  23.0 0.3 shard_map.95
  23.4 0.4 collective-permute-done.5.ref
  23.7 0.7 %shard_map.96 = (f32[768,256]{1,0:T(8,128)S(1)}, f32[64,32]{1,0:T(8,128)S(1)}) custom-call(f32[768,256]{1,0:T(8,128)S(1)} %get-tuple-element.110.old_grid_ref, f32[64,32]{1,0:T(8,128)S(1)} %get-tuple-element.111.old_counts_ref, bf16[72,1024]{1,0:T(8,128)(2,1)S(1)} %collective-permute-done.5.ref), custom_call_target="tpu_custom_call" | custom-call | tf_op jit(solution)/shard_map/pallas_call | solution.py:45
  24.4 2.4 %shard_map.97 = (bf16[2,4,128,256]{3,2,1,0:T(8,128)(2,1)S(1)}, bf16[2,6,10,16,256]{4,3,2,1,0:T(8,128)(2,1)S(1)}, bf16[2,4,10,16,256]{4,3,2,1,0:T(8,128)(2,1)S(1)...) custom-call(f32[768,256]{1,0:T(8,128)S(1)} %get-tuple-element.95.grid0, f32[64,32]{1,0:T(8,128)S(1)} %get-tuple-element.96.counts0, ...), custom_call_target="tpu_custom_call" | custom-call | tf_op jit(solution)/shard_map/pallas_call | solution.py:45
  26.8 0.2 collective-permute-start.6
  27.1 1.4 %shard_map.98 = (f32[4,224,128]{2,1,0:T(8,128)S(1)}, bf16[4,224,128]{2,1,0:T(8,128)(2,1)S(1)}) custom-call(bf16[2,6,10,16,256]{4,3,2,1,0:T(8,128)(2,1)S(1)} %get-tuple-element.120.es_ref, bf16[2,4,10,16,256]{4,3,2,1,0:T(8,128)(2,1)S(1)} %get-tuple-element.121.pg_ref), custom_call_target="tpu_custom_call" | custom-call | tf_op jit(solution)/shard_map/pallas_call | solution.py:45
  28.5 0.0 collective-permute-done.6.got_ref
  28.5 0.4 collective-permute-start.7
  28.9 1.1 %collective-permute-done.7.got_conv_ref = bf16[4,224,128]{2,1,0:T(8,128)(2,1)S(1)} collective-permute-done((bf16[4,224,128]{2,1,0:T(8,128)(2,1)S(1)}, bf16[4,224,128]{2,1,0:T(8,128)(2,1)S(1)}, u32[]{:S(2)}, u32[]{:S(2)}) %collective-permute-start.7) | collective-permute-done | bytes 229408 | tf_op jit(solution)/shard_map/ppermute | solution.py:57
  30.1 0.1 shard_map.99
  30.2 1.6 %collective-permute-start.8 = (bf16[480,128]{1,0:T(8,128)(2,1)S(1)}, bf16[480,128]{1,0:T(8,128)(2,1)S(1)}, u32[]{:S(2)}, u32[]{:S(2)}) collective-permute-start(bf16[480,128]{1,0:T(8,128)(2,1)S(1)} %get-tuple-element.128), channel_id=1, source_target_pairs={{0,8},{8,0},{16,24},{24,16},{1,9},{9,1},{17,25},{25,17},{2,10},{10... | collective-permute-start | bytes 368648 | tf_op jit(solution)/shard_map/ppermute | solution.py:66
  31.7 1.5 %collective-permute-start.9 = (bf16[480,128]{1,0:T(8,128)(2,1)S(1)}, bf16[480,128]{1,0:T(8,128)(2,1)S(1)}, u32[]{:S(2)}, u32[]{:S(2)}) collective-permute-start(bf16[480,128]{1,0:T(8,128)(2,1)S(1)} %get-tuple-element.129), channel_id=1, source_target_pairs={{0,16},{8,24},{16,0},{24,8},{1,17},{9,25},{17,1},{25,9},{2,18},{10... | collective-permute-start | bytes 368648 | tf_op jit(solution)/shard_map/ppermute | solution.py:66
  33.2 0.5 %collective-permute-start.10 = (bf16[480,128]{1,0:T(8,128)(2,1)S(1)}, bf16[480,128]{1,0:T(8,128)(2,1)S(1)}, u32[]{:S(2)}, u32[]{:S(2)}) collective-permute-start(bf16[480,128]{1,0:T(8,128)(2,1)S(1)} %get-tuple-element.130), channel_id=1, source_target_pairs={{0,24},{8,16},{16,8},{24,0},{1,25},{9,17},{17,9},{25,1},{2,26},{10... | collective-permute-start | bytes 368648 | tf_op jit(solution)/shard_map/ppermute | solution.py:66
  33.7 0.4 shard_map.100
  34.1 0.7 %reshape.13 = bf16[1,2,16,4,256]{4,3,2,1,0:T(4,128)(2,1)} reshape(bf16[128,256]{1,0:T(8,128)(2,1)S(1)} %shard_map.100) | data formatting | bytes 131072 | tf_op jit(solution)/shard_map/reshape | solution.py:468
  34.8 1.2 %collective-permute-done.8.refs_1_ = bf16[480,128]{1,0:T(8,128)(2,1)S(1)} collective-permute-done((bf16[480,128]{1,0:T(8,128)(2,1)S(1)}, bf16[480,128]{1,0:T(8,128)(2,1)S(1)}, u32[]{:S(2)}, u32[]{:S(2)}) %collective-permute-start.8) | collective-permute-done | bytes 122912 | tf_op jit(solution)/shard_map/ppermute | solution.py:66
  36.0 3.7 %collective-permute-done.9.refs_2_ = bf16[480,128]{1,0:T(8,128)(2,1)S(1)} collective-permute-done((bf16[480,128]{1,0:T(8,128)(2,1)S(1)}, bf16[480,128]{1,0:T(8,128)(2,1)S(1)}, u32[]{:S(2)}, u32[]{:S(2)}) %collective-permute-start.9) | collective-permute-done | bytes 122912 | tf_op jit(solution)/shard_map/ppermute | solution.py:66
  39.7 0.0 collective-permute-done.10.refs_3_
  39.7 0.1 shard_map.101.refs_0_
  39.7 0.1 collective-permute-start.11
  39.8 4.9 %collective-permute-done.11.refs_1_ = bf16[480,128]{1,0:T(8,128)(2,1)S(1)} collective-permute-done((bf16[480,128]{1,0:T(8,128)(2,1)S(1)}, bf16[480,128]{1,0:T(8,128)(2,1)S(1)}, u32[]{:S(2)}, u32[]{:S(2)}) %collective-permute-start.11) | collective-permute-done | bytes 122912 | tf_op jit(solution)/shard_map/ppermute | solution.py:62
  44.7 0.1 collective-permute-start.12
  44.8 1.5 %collective-permute-done.12.got_ref = f32[480,128]{1,0:T(8,128)S(1)} collective-permute-done((f32[480,128]{1,0:T(8,128)S(1)}, f32[480,128]{1,0:T(8,128)S(1)}, u32[]{:S(2)}, u32[]{:S(2)}) %collective-permute-start.12) | collective-permute-done | bytes 245792 | tf_op jit(solution)/shard_map/ppermute | solution.py:57
  46.3 0.8 %shard_map.103 = (f32[432,128]{1,0:T(8,128)}, f32[256,256]{1,0:T(8,128)}) custom-call(f32[480,128]{1,0:T(8,128)S(1)} %shard_map.102.own_ref, f32[480,128]{1,0:T(8,128)S(1)} %collective-permute-done.12.got_ref), custom_call_target="tpu_custom_call" | custom-call | tf_op jit(solution)/shard_map/pallas_call | solution.py:45
  (2 shorter events, 0.1 us)
Async XLA Ops:
  1.6 9.8 %collective-permute-start = (bf16[72,1024]{1,0:T(8,128)(2,1)S(1)}, bf16[72,1024]{1,0:T(8,128)(2,1)S(1)}, u32[]{:S(2)}, u32[]{:S(2)}) collective-permute-start(bf16[72,1024]{1,0:T(8,128)(2,1)S(1)} %shard_map.85.ref.refs_0_), channel_id=1, source_target_pairs={{0,6},{1,7},{2,4},{3,5},{4,2},{5,3},{6,0},{7,1},{8,14},{9,15},{10,... | collective-permute-start | bytes 442376 | tf_op jit(solution)/shard_map/ppermute | solution.py:62
  7.4 6.4 %collective-permute-start.2 = (bf16[72,1024]{1,0:T(8,128)(2,1)S(1)}, bf16[72,1024]{1,0:T(8,128)(2,1)S(1)}, u32[]{:S(2)}, u32[]{:S(2)}) collective-permute-start(bf16[72,1024]{1,0:T(8,128)(2,1)S(1)} %shard_map.85.ref.refs_0_), channel_id=1, source_target_pairs={{0,2},{1,3},{2,0},{3,1},{4,6},{5,7},{6,4},{7,5},{8,10},{9,11},{10,... | collective-permute-start | bytes 442376 | tf_op jit(solution)/shard_map/ppermute | solution.py:62
  13.9 3.6 %collective-permute-start.3 = (bf16[3,72,1024]{2,1,0:T(8,128)(2,1)S(1)}, bf16[3,72,1024]{2,1,0:T(8,128)(2,1)S(1)}, u32[]{:S(2)}, u32[]{:S(2)}) collective-permute-start(bf16[3,72,1024]{2,1,0:T(8,128)(2,1)S(1)} %shard_map.90), channel_id=1, source_target_pairs={{0,1},{1,0},{2,3},{3,2},{4,5},{5,4},{6,7},{7,6},{8,9},{9,8},{10,11... | collective-permute-start | bytes 1327112 | tf_op jit(solution)/shard_map/ppermute | solution.py:57
  13.9 8.4 %collective-permute-start.1 = (bf16[72,1024]{1,0:T(8,128)(2,1)S(1)}, bf16[72,1024]{1,0:T(8,128)(2,1)S(1)}, u32[]{:S(2)}, u32[]{:S(2)}) collective-permute-start(bf16[72,1024]{1,0:T(8,128)(2,1)S(1)} %collective-permute-done.ref.refs_2_), channel_id=1, source_target_pairs={{0,2},{1,3},{2,0},{3,1},{4,6},{5,7},{6,4},{7,5},{8,10},{9,11},{10,... | collective-permute-start | bytes 442376 | tf_op jit(solution)/shard_map/ppermute | solution.py:62
  15.7 6.7 %collective-permute-start.4 = (bf16[128,256]{1,0:T(8,128)(2,1)S(1)}, bf16[128,256]{1,0:T(8,128)(2,1)S(1)}, u32[]{:S(2)}, u32[]{:S(2)}) collective-permute-start(bf16[128,256]{1,0:T(8,128)(2,1)S(1)} %get-tuple-element.94.own_ref), channel_id=1, source_target_pairs={{0,6},{1,7},{2,4},{3,5},{4,2},{5,3},{6,0},{7,1},{8,14},{9,15},{10,... | collective-permute-start | bytes 196616 | tf_op jit(solution)/shard_map/ppermute | solution.py:62
  22.4 1.4 %collective-permute-start.5 = (bf16[72,1024]{1,0:T(8,128)(2,1)S(1)}, bf16[72,1024]{1,0:T(8,128)(2,1)S(1)}, u32[]{:S(2)}, u32[]{:S(2)}) collective-permute-start(bf16[72,1024]{1,0:T(8,128)(2,1)S(1)} %collective-permute-done.1.ref), channel_id=1, source_target_pairs={{0,1},{1,0},{2,3},{3,2},{4,5},{5,4},{6,7},{7,6},{8,9},{9,8},{10,11... | collective-permute-start | bytes 442376 | tf_op jit(solution)/shard_map/ppermute | solution.py:57
  26.8 1.7 %collective-permute-start.6 = (bf16[4,256,128]{2,1,0:T(8,128)(2,1)S(1)}, bf16[4,256,128]{2,1,0:T(8,128)(2,1)S(1)}, u32[]{:S(2)}, u32[]{:S(2)}) collective-permute-start(bf16[4,256,128]{2,1,0:T(8,128)(2,1)S(1)} %get-tuple-element.119), channel_id=1, source_target_pairs={{0,1},{1,0},{2,3},{3,2},{4,5},{5,4},{6,7},{7,6},{8,9},{9,8},{10,11... | collective-permute-start | bytes 786440 | tf_op jit(solution)/shard_map/ppermute | solution.py:57
  28.5 1.6 %collective-permute-start.7 = (bf16[4,224,128]{2,1,0:T(8,128)(2,1)S(1)}, bf16[4,224,128]{2,1,0:T(8,128)(2,1)S(1)}, u32[]{:S(2)}, u32[]{:S(2)}) collective-permute-start(bf16[4,224,128]{2,1,0:T(8,128)(2,1)S(1)} %get-tuple-element.126), channel_id=1, source_target_pairs={{0,1},{1,0},{2,3},{3,2},{4,5},{5,4},{6,7},{7,6},{8,9},{9,8},{10,11... | collective-permute-start | bytes 688136 | tf_op jit(solution)/shard_map/ppermute | solution.py:57
  30.2 5.8 %collective-permute-start.8 = (bf16[480,128]{1,0:T(8,128)(2,1)S(1)}, bf16[480,128]{1,0:T(8,128)(2,1)S(1)}, u32[]{:S(2)}, u32[]{:S(2)}) collective-permute-start(bf16[480,128]{1,0:T(8,128)(2,1)S(1)} %get-tuple-element.128), channel_id=1, source_target_pairs={{0,8},{8,0},{16,24},{24,16},{1,9},{9,1},{17,25},{25,17},{2,10},{10... | collective-permute-start | bytes 368648 | tf_op jit(solution)/shard_map/ppermute | solution.py:66
  31.7 7.9 %collective-permute-start.9 = (bf16[480,128]{1,0:T(8,128)(2,1)S(1)}, bf16[480,128]{1,0:T(8,128)(2,1)S(1)}, u32[]{:S(2)}, u32[]{:S(2)}) collective-permute-start(bf16[480,128]{1,0:T(8,128)(2,1)S(1)} %get-tuple-element.129), channel_id=1, source_target_pairs={{0,16},{8,24},{16,0},{24,8},{1,17},{9,25},{17,1},{25,9},{2,18},{10... | collective-permute-start | bytes 368648 | tf_op jit(solution)/shard_map/ppermute | solution.py:66
  33.2 6.4 %collective-permute-start.10 = (bf16[480,128]{1,0:T(8,128)(2,1)S(1)}, bf16[480,128]{1,0:T(8,128)(2,1)S(1)}, u32[]{:S(2)}, u32[]{:S(2)}) collective-permute-start(bf16[480,128]{1,0:T(8,128)(2,1)S(1)} %get-tuple-element.130), channel_id=1, source_target_pairs={{0,24},{8,16},{16,8},{24,0},{1,25},{9,17},{17,9},{25,1},{2,26},{10... | collective-permute-start | bytes 368648 | tf_op jit(solution)/shard_map/ppermute | solution.py:66
  39.7 4.9 %collective-permute-start.11 = (bf16[480,128]{1,0:T(8,128)(2,1)S(1)}, bf16[480,128]{1,0:T(8,128)(2,1)S(1)}, u32[]{:S(2)}, u32[]{:S(2)}) collective-permute-start(bf16[480,128]{1,0:T(8,128)(2,1)S(1)} %shard_map.101.refs_0_), channel_id=1, source_target_pairs={{0,2},{1,3},{2,0},{3,1},{4,6},{5,7},{6,4},{7,5},{8,10},{9,11},{10,... | collective-permute-start | bytes 368648 | tf_op jit(solution)/shard_map/ppermute | solution.py:62
  44.7 1.6 %collective-permute-start.12 = (f32[480,128]{1,0:T(8,128)S(1)}, f32[480,128]{1,0:T(8,128)S(1)}, u32[]{:S(2)}, u32[]{:S(2)}) collective-permute-start(f32[480,128]{1,0:T(8,128)S(1)} %shard_map.102.own_ref), channel_id=1, source_target_pairs={{0,1},{1,0},{2,3},{3,2},{4,5},{5,4},{6,7},{7,6},{8,9},{9,8},{10,11... | collective-permute-start | bytes 737288 | tf_op jit(solution)/shard_map/ppermute | solution.py:57

commit v7 on v6

--- a/solution.py
+++ b/solution.py
@@ -133,16 +133,6 @@
                 [down_ref[first : first + C1, :], down_ref[second : second + C1, :]], axis=0
             )
     turned_ref[...] = lax.dot_general(turn_matrix(), cot_ref[...], TN, preferred_element_type=F32).astype(BF16)
-
-
-def back_kernel(own_ref, got_ref, pairs_ref, cot_ref, back_ref):
-    first = slab_tiles()[1] == 0
-    own = own_ref[...].astype(F32)
-    got = got_ref[...].astype(F32)
-    cot = jnp.concatenate([jnp.where(first, own, got), jnp.where(first, got, own)], axis=0).astype(BF16)
-    cot_ref[...] = cot
-    for i in range(4):
-        back_ref[i] = lax.dot_general(cot, pairs_ref[i], NT, preferred_element_type=F32)
 
 
 def voxelize(ref):
@@ -207,14 +197,14 @@
 
 
 def scene_kernel(
-    samples,
-    grid0, counts0, grid1, counts1, grid2, counts2, grid3, counts3, taps_ref, cot_ref, back_ref,
-    act_ref, es_ref, pg_ref, mine_ref, other_ref,
+    grid0, counts0, grid1, counts1, grid2, counts2, grid3, counts3, taps_ref,
+    act_ref, slope_ref, es_ref,
 ):
     counts = counts0[...] + counts1[...] + counts2[...] + counts3[...]
 
-    es_ref[...] = jnp.zeros_like(es_ref)
-    pg_ref[...] = jnp.zeros_like(pg_ref)
+    edge = jnp.zeros((2, SX + 2, 1, 16, 4 * CIN), BF16)
+    es_ref[:, :, 0:1] = edge
+    es_ref[:, :, SZ + 1 : SZ + 2] = edge
     line = lax.broadcasted_iota(I32, (LAYER, 2 * CIN), 0) & 15
     lane = lax.broadcasted_iota(I32, (LAYER, 2 * CIN), 1)
     for s in range(2):
@@ -241,11 +231,15 @@
     ).astype(F32).astype(BF16)
     active = jnp.dot(lines, expand, preferred_element_type=F32) > 0.5
 
-    pre = jnp.zeros((full, 2 * C1), F32)
-    for dx in range(3):
-        for dz in range(3):
-            part = es_ref[:, dx : dx + SX, dz : dz + SZ].reshape(full, 4 * CIN)
-            pre = pre + jnp.dot(part, taps_ref[dx * 3 + dz], preferred_element_type=F32)
+    part = jnp.concatenate(
+        [
+            es_ref[:, dx : dx + SX, dz : dz + SZ].reshape(full, 4 * CIN)
+            for dx in range(3)
+            for dz in range(3)
+        ],
+        axis=1,
+    )
+    pre = jnp.dot(part, taps_ref[...].reshape(36 * CIN, 2 * C1), preferred_element_type=F32)
 
     sigmoid = 1.0 / (1.0 + jnp.exp(-pre))
     act = jnp.where(active, pre * sigmoid, 0.0).astype(BF16)
@@ -253,16 +247,33 @@
 
     act = act.reshape(2, 2, 2, 4, 2, 16, 2 * C1)
     slope = slope.reshape(2, 2, 2, 4, 2, 16, 2 * C1)
-    cot = cot_ref[...]
+    for ox in range(2):
+        for oz in range(2):
+            act_ref[ox * 2 + oz] = act[:, :, ox, :, oz].reshape(256, 2 * C1)
+            slope_ref[ox * 2 + oz] = slope[:, :, ox, :, oz].reshape(256, 2 * C1)
+
+
+def down_grad_kernel(samples, act_ref, slope_ref, own_ref, got_ref, pairs_ref, pg_ref, mine_ref, other_ref):
+    first = slab_tiles()[1] == 0
+    own = own_ref[...].astype(F32)
+    got = got_ref[...].astype(F32)
+    cot = jnp.concatenate([jnp.where(first, own, got), jnp.where(first, got, own)], axis=0).astype(BF16)
+    edge = jnp.zeros((2, SX, 1, 16, 2 * C1), BF16)
+    pg_ref[:, :, 0:1] = edge
+    pg_ref[:, :, SZ + 1 : SZ + 2] = edge
     low = (lax.axis_index("tile") & 1) == 0
     down_rows = 8 * C1 // samples
     step = min(C1, down_rows)
     for ox in range(2):
         for oz in range(2):
-            block = act[:, :, ox, :, oz].reshape(256, 2 * C1)
-            act_ref[0, ox * 2 + oz] = block[:128]
-            act_ref[1, ox * 2 + oz] = block[128:]
-            grad = lax.dot_general(block, cot, TN, preferred_element_type=F32)
+            back = lax.dot_general(cot, pairs_ref[ox * 2 + oz], NT, preferred_element_type=F32)
+            part = (back * slope_ref[ox * 2 + oz]).astype(BF16)
+            part = part.reshape(2, 2, 4, 16, 2 * C1)
+            for s in range(2):
+                for u in range(2):
+                    for w in range(4):
+                        pg_ref[s, 2 * u + ox, 1 + 2 * w + oz] = part[s, u, w]
+            grad = lax.dot_general(act_ref[ox * 2 + oz], cot, TN, preferred_element_type=F32)
             for p in range(2):
                 for i in range(0, C1, step):
                     chunk, row = divmod((ox * 4 + p * 2 + oz) * C1 + i, down_rows)
@@ -270,26 +281,22 @@
                     right = grad[p * C1 + i : p * C1 + i + step, 128:256]
                     mine_ref[chunk, row : row + step, :] = jnp.where(low, left, right)
                     other_ref[chunk, row : row + step, :] = jnp.where(low, right, left).astype(BF16)
-            back = back_ref[ox * 2 + oz]
-            part = (back * slope[:, :, ox, :, oz].reshape(256, 2 * C1)).astype(BF16)
-            part = part.reshape(2, 2, 4, 16, 2 * C1)
-            for s in range(2):
-                for u in range(2):
-                    for w in range(4):
-                        pg_ref[s, 2 * u + ox, 1 + 2 * w + oz] = part[s, u, w]
 
 
 def conv_grad_kernel(samples, half_rows, es_ref, pg_ref, mine_ref, other_ref, tall_ref):
     full = 2 * SX * LAYER
     flipped = es_ref[:, :, 1 : SZ + 1].reshape(2 * (SX + 2) * LAYER, 4 * CIN).T
     half = (SX + 2) * LAYER
+    part = jnp.concatenate(
+        [pg_ref[:, :, 2 - dz : 2 - dz + SZ].reshape(full, 2 * C1) for dz in range(3)], axis=1
+    )
     for dx in range(3):
         rows = jnp.concatenate(
             [flipped[:, s * half + dx * LAYER : s * half + (dx + SX) * LAYER] for s in range(2)], axis=1
         )
+        grads = jnp.dot(rows, part, preferred_element_type=F32)
         for dz in range(3):
-            part = pg_ref[:, :, 2 - dz : 2 - dz + SZ].reshape(full, 2 * C1)
-            grad = jnp.dot(rows, part, preferred_element_type=F32)
+            grad = grads[:, dz * 256 : (dz + 1) * 256]
             sums = (
                 grad[0:64, 128:256] + grad[128:192, 0:128],
                 grad[0:64, 0:128] + grad[64:128, 128:256],
@@ -315,7 +322,8 @@
     place = slab_tiles()[1]
     down = jnp.zeros((128, C2), F32)
     for i in range(4):
-        down = down + jnp.dot(act_ref[place, i], pairs_ref[i], preferred_element_type=F32)
+        rows = act_ref[i, pl.ds(pl.multiple_of(place * 128, 128), 128)]
+        down = down + jnp.dot(rows, pairs_ref[i], preferred_element_type=F32)
     out_ref[...] = jnp.dot(turn_matrix(), down.astype(BF16), preferred_element_type=F32).astype(BF16)
 
 
@@ -392,32 +400,29 @@
         return call(functools.partial(more_points_kernel, at), sums, pinned=3)(*grid, piece)
 
     beyond = send_column(coded, lambda i: i ^ FAR, tiles)
-    own = add(None, coded)
-    coded, own = lax.optimization_barrier((coded, own))
     beside = send_column(coded, lambda i: i ^ 1, tiles)
     taps, pairs, cot = call(
         weights_kernel,
         (shape((9, 4 * CIN, 2 * C1), BF16), shape((4, 2 * C1, C2), BF16), shape((128, C2), BF16)),
         loose=3,
     )(conv_weight, down_weight, cotangent.reshape(128, C2))
-    beyond, taps, pairs, cot = lax.optimization_barrier((beyond, taps, pairs, cot))
+    beyond, taps, pairs, cot, coded = lax.optimization_barrier((beyond, taps, pairs, cot, coded))
     across = send_column(beyond, lambda i: i ^ 1, tiles)
     far = add(None, beyond)
-    coded, beside, beyond, far, cot = lax.optimization_barrier((coded, beside, beyond, far, cot))
-    near_swap = swap_core(
-        call(stack_kernel, shape((3, CODED, PTS_DEV), BF16), pinned=3)(coded, beside, beyond), tiles
-    )
+    coded, beyond, far, cot = lax.optimization_barrier((coded, beyond, far, cot))
+    own = add(None, coded)
+    coded_swap = swap_core(coded, tiles)
+    beyond_swap = swap_core(beyond, tiles)
     cot_got = send_column(cot, lambda i: i ^ FAR, tiles)
     own = add(own, beside)
-    own_swap = add(add(None, near_swap, 0), near_swap, 1)
-    far_swap = add(None, near_swap, 2)
-    across, own, own_swap, far_swap, cot_got = lax.optimization_barrier((across, own, own_swap, far_swap, cot_got))
+    beside, own = lax.optimization_barrier((beside, own))
+    beside_swap = swap_core(beside, tiles)
+    across, own, far, cot_got = lax.optimization_barrier((across, own, far, cot_got))
     across_swap = swap_core(across, tiles)
     far = add(far, across)
-    cot, back = call(
-        back_kernel, (shape((256, C2), BF16), shape((4, 256, 2 * C1), F32)), pinned=3
-    )(cot, cot_got, pairs)
-    across_swap, far, cot, back = lax.optimization_barrier((across_swap, far, cot, back))
+    own_swap = add(add(None, coded_swap), beside_swap)
+    far_swap = add(None, beyond_swap)
+    across_swap, far = lax.optimization_barrier((across_swap, far))
     far_swap = add(far_swap, across_swap)
     grids = [own, own_swap, far, far_swap]
     if blocks > 1:
@@ -437,17 +442,24 @@
         nothing = (jnp.zeros((6 * LAYER, 4 * CIN), F32), jnp.zeros((64, 32), F32))
         grids = [rest, nothing, parts, nothing]
 
-    act, es, pg, mine, other = call(
-        functools.partial(scene_kernel, samples),
+    act, slope, es = call(
+        scene_kernel,
         (
-            shape((2, 4, 128, 2 * C1), BF16),
+            shape((4, 256, 2 * C1), BF16),
+            shape((4, 256, 2 * C1), F32),
             shape((2, SX + 2, SZ + 2, 16, 4 * CIN), BF16),
+        ),
+        pinned=9,
+    )(*grids[0], *grids[1], *grids[2], *grids[3], taps)
+    pg, mine, other = call(
+        functools.partial(down_grad_kernel, samples),
+        (
             shape((2, SX, SZ + 2, 16, 2 * C1), BF16),
             shape((samples, down_rows, 128), F32),
             shape((samples, down_rows, 128), BF16),
         ),
-        pinned=11,
-    )(*grids[0], *grids[1], *grids[2], *grids[3], taps, cot, back)
+        pinned=5,
+    )(act, slope, cot, cot_got, pairs)
 
     got = swap_core(other, tiles)
     mine_conv, other_conv = call(

time: 47.3 us -> 46.9 us (level)
  starting transfers between devices: 12.4 us -> 14.7 us
  waiting for transfers between devices: 18.4 us -> 16.1 us
    ppermute x5, waiting for transfers between devices: 10.6 us -> 8.46 us  [send_column(): return lax.ppermute(value, 'tile', pairs)]
    ppermute x5, starting transfers between devices: 8.09 us -> 9.73 us  [send_column(): return lax.ppermute(value, 'tile', pairs)]
    ppermute x5 -> x7, starting transfers between devices: 0.79 us -> 1.39 us  [swap_core(): return lax.ppermute(value, 'tile', [(i, i ^ 1) for i in range(tiles)])]
    pallas_call x19 -> x18, Pallas kernels: 13.3 us -> 13 us  [run(): return kernel(*held, *far)]
    ppermute x5 -> x7, waiting for transfers between devices: 2.99 us -> 2.98 us  [swap_core(): return lax.ppermute(value, 'tile', [(i, i ^ 1) for i in range(tiles)])]
  transfers between devices with their start and end apart: 13 -> 15, of which waited for: 9 -> 7; matrix products, arithmetic and copies ran while one was open for 5% -> 5% of each run, Pallas kernels for 17% -> 17%
where the time goes in v7:
time: 46.9 us; the launch traced here: 46.7 us
  waiting for transfers between devices  16.1 us (34%)
  starting transfers between devices  14.7 us (31%)
  Pallas kernels  13 us (28%)
  local copies, waits for them, and re-layouts  2.14 us (5%)
  between operations  0.81 us (2%)
    pallas_call x18, Pallas kernels, run(): return kernel(*held, *far)  13 us
    ppermute x5, starting transfers between devices, send_column(): return lax.ppermute(value, 'tile', pairs)  9.73 us
    ppermute x5, waiting for transfers between devices, send_column(): return lax.ppermute(value, 'tile', pairs)  8.46 us
    ppermute x3, waiting for transfers between devices, send_sample(): lax.ppermute(value, 'sample', [(i, target(i, k, samples)) for i in range(...  4.66 us
    ppermute x3, starting transfers between devices, send_sample(): lax.ppermute(value, 'sample', [(i, target(i, k, samples)) for i in range(...  3.55 us
    ppermute x7, waiting for transfers between devices, swap_core(): return lax.ppermute(value, 'tile', [(i, i ^ 1) for i in range(tiles)])  2.98 us
    reshape x1, local copies, waits for them, and re-layouts, local(): cotangent.reshape(128, C2)  1.49 us
    ppermute x7, starting transfers between devices, swap_core(): return lax.ppermute(value, 'tile', [(i, i ^ 1) for i in range(tiles)])  1.39 us
  transfers between devices with their start and end apart: 15, of which 7 were waited for; matrix products, arithmetic and copies ran while one was open for 5% of the time, Pallas kernels for 17%

profile of v7, /device:TPU:0, one launch (start us, length us, event | category | flops | bytes accessed | tf_op | source)
XLA Modules:
  0.0 46.7 jit_solution(8565007073339560054)
XLA Ops:
  0.6 1.0 %shard_map.85.ref = bf16[72,1024]{1,0:T(8,128)(2,1)S(1)} custom-call(bf16[64,1024]{1,0:T(8,128)(2,1)} %bitcast.3, s32[1,1024]{1,0:T(1,128)} %slot_hbm.1, s32[1,1024]{1,0:T(1,128)} %voxel_hbm.1), custom_call_target="tpu_custom_call" | custom-call | tf_op jit(solution)/shard_map/pallas_call | solution.py:45
  1.6 5.1 %collective-permute-start = (bf16[72,1024]{1,0:T(8,128)(2,1)S(1)}, bf16[72,1024]{1,0:T(8,128)(2,1)S(1)}, u32[]{:S(2)}, u32[]{:S(2)}) collective-permute-start(bf16[72,1024]{1,0:T(8,128)(2,1)S(1)} %shard_map.85.ref), channel_id=1, source_target_pairs={{0,6},{1,7},{2,4},{3,5},{4,2},{5,3},{6,0},{7,1},{8,14},{9,15},{10,... | collective-permute-start | bytes 442376 | tf_op jit(solution)/shard_map/ppermute | solution.py:62
  6.7 0.0 collective-permute-start.2
  6.7 1.5 %reshape.12.cot_ref = bf16[128,256]{1,0:T(8,128)(2,1)} reshape(bf16[1,2,16,4,256]{4,3,2,1,0:T(4,128)(2,1)} %param.11) | data formatting | bytes 131072 | tf_op jit(solution)/shard_map/reshape | solution.py:408
  8.2 1.4 %shard_map.86 = (bf16[9,256,256]{2,1,0:T(8,128)(2,1)S(1)}, bf16[4,256,256]{2,1,0:T(8,128)(2,1)S(1)}, bf16[128,256]{1,0:T(8,128)(2,1)S(1)}) custom-call(bf16[1728,128]{1,0:T(8,128)(2,1)} %conv_ref.1, bf16[1024,256]{1,0:T(8,128)(2,1)} %down_ref.1, bf16[128,256]{1,0:T(8,128)(2,1)} %reshape.12.cot_ref), custom_call_target="tpu_custom_call" | custom-call | tf_op jit(solution)/shard_map/pallas_call | solution.py:45
  9.6 1.8 %collective-permute-done.ref = bf16[72,1024]{1,0:T(8,128)(2,1)S(1)} collective-permute-done((bf16[72,1024]{1,0:T(8,128)(2,1)S(1)}, bf16[72,1024]{1,0:T(8,128)(2,1)S(1)}, u32[]{:S(2)}, u32[]{:S(2)}) %collective-permute-start) | collective-permute-done | bytes 147488 | tf_op jit(solution)/shard_map/ppermute | solution.py:62
  11.4 2.0 %collective-permute-start.1 = (bf16[72,1024]{1,0:T(8,128)(2,1)S(1)}, bf16[72,1024]{1,0:T(8,128)(2,1)S(1)}, u32[]{:S(2)}, u32[]{:S(2)}) collective-permute-start(bf16[72,1024]{1,0:T(8,128)(2,1)S(1)} %collective-permute-done.ref), channel_id=1, source_target_pairs={{0,2},{1,3},{2,0},{3,1},{4,6},{5,7},{6,4},{7,5},{8,10},{9,11},{10,... | collective-permute-start | bytes 442376 | tf_op jit(solution)/shard_map/ppermute | solution.py:62
  13.4 0.7 %shard_map.87 = (f32[768,256]{1,0:T(8,128)S(1)}, f32[64,32]{1,0:T(8,128)S(1)}) custom-call(bf16[72,1024]{1,0:T(8,128)(2,1)S(1)} %collective-permute-done.ref), custom_call_target="tpu_custom_call" | custom-call | tf_op jit(solution)/shard_map/pallas_call | solution.py:45
  14.1 2.5 %collective-permute-start.3 = (bf16[128,256]{1,0:T(8,128)(2,1)S(1)}, bf16[128,256]{1,0:T(8,128)(2,1)S(1)}, u32[]{:S(2)}, u32[]{:S(2)}) collective-permute-start(bf16[128,256]{1,0:T(8,128)(2,1)S(1)} %get-tuple-element.83.own_ref), channel_id=1, source_target_pairs={{0,6},{1,7},{2,4},{3,5},{4,2},{5,3},{6,0},{7,1},{8,14},{9,15},{10,... | collective-permute-start | bytes 196616 | tf_op jit(solution)/shard_map/ppermute | solution.py:62
  16.6 0.7 %shard_map.88 = (f32[768,256]{1,0:T(8,128)S(1)}, f32[64,32]{1,0:T(8,128)S(1)}) custom-call(bf16[72,1024]{1,0:T(8,128)(2,1)S(1)} %shard_map.85.ref), custom_call_target="tpu_custom_call" | custom-call | tf_op jit(solution)/shard_map/pallas_call | solution.py:45
  17.3 0.6 %collective-permute-start.7 = (bf16[72,1024]{1,0:T(8,128)(2,1)S(1)}, bf16[72,1024]{1,0:T(8,128)(2,1)S(1)}, u32[]{:S(2)}, u32[]{:S(2)}) collective-permute-start(bf16[72,1024]{1,0:T(8,128)(2,1)S(1)} %collective-permute-done.ref), channel_id=1, source_target_pairs={{0,1},{1,0},{2,3},{3,2},{4,5},{5,4},{6,7},{7,6},{8,9},{9,8},{10,11... | collective-permute-start | bytes 442376 | tf_op jit(solution)/shard_map/ppermute | solution.py:57
  17.9 0.0 collective-permute-done.2.ref
  17.9 0.7 %shard_map.89 = (f32[768,256]{1,0:T(8,128)S(1)}, f32[64,32]{1,0:T(8,128)S(1)}) custom-call(f32[768,256]{1,0:T(8,128)S(1)} %get-tuple-element.75.old_grid_ref, f32[64,32]{1,0:T(8,128)S(1)} %get-tuple-element.76.old_counts_ref, bf16[72,1024]{1,0:T(8,128)(2,1)S(1)} %collective-permute-done.2.ref), custom_call_target="tpu_custom_call" | custom-call | tf_op jit(solution)/shard_map/pallas_call | solution.py:45
  18.6 0.1 collective-permute-start.5
  18.6 1.8 %collective-permute-done.3.got_ref = bf16[128,256]{1,0:T(8,128)(2,1)S(1)} collective-permute-done((bf16[128,256]{1,0:T(8,128)(2,1)S(1)}, bf16[128,256]{1,0:T(8,128)(2,1)S(1)}, u32[]{:S(2)}, u32[]{:S(2)}) %collective-permute-start.3) | collective-permute-done | bytes 65568 | tf_op jit(solution)/shard_map/ppermute | solution.py:62
  20.4 0.0 collective-permute-done.1.ref
  20.4 0.0 collective-permute-start.6
  20.4 0.7 %shard_map.92 = (f32[768,256]{1,0:T(8,128)S(1)}, f32[64,32]{1,0:T(8,128)S(1)}) custom-call(f32[768,256]{1,0:T(8,128)S(1)} %get-tuple-element.92.old_grid_ref, f32[64,32]{1,0:T(8,128)S(1)} %get-tuple-element.93.old_counts_ref, bf16[72,1024]{1,0:T(8,128)(2,1)S(1)} %collective-permute-done.1.ref), custom_call_target="tpu_custom_call" | custom-call | tf_op jit(solution)/shard_map/pallas_call | solution.py:45
  21.1 0.0 collective-permute-done.4.ref
  21.1 0.7 %shard_map.90 = (f32[768,256]{1,0:T(8,128)S(1)}, f32[64,32]{1,0:T(8,128)S(1)}) custom-call(bf16[72,1024]{1,0:T(8,128)(2,1)S(1)} %collective-permute-done.4.ref), custom_call_target="tpu_custom_call" | custom-call | tf_op jit(solution)/shard_map/pallas_call | solution.py:45
  21.8 0.0 collective-permute-done.7.ref
  21.8 0.7 %shard_map.93 = (f32[768,256]{1,0:T(8,128)S(1)}, f32[64,32]{1,0:T(8,128)S(1)}) custom-call(bf16[72,1024]{1,0:T(8,128)(2,1)S(1)} %collective-permute-done.7.ref), custom_call_target="tpu_custom_call" | custom-call | tf_op jit(solution)/shard_map/pallas_call | solution.py:45
  22.5 0.0 collective-permute-done.5.ref
  22.5 0.7 %shard_map.91 = (f32[768,256]{1,0:T(8,128)S(1)}, f32[64,32]{1,0:T(8,128)S(1)}) custom-call(f32[768,256]{1,0:T(8,128)S(1)} %get-tuple-element.86.old_grid_ref, f32[64,32]{1,0:T(8,128)S(1)} %get-tuple-element.87.old_counts_ref, bf16[72,1024]{1,0:T(8,128)(2,1)S(1)} %collective-permute-done.5.ref), custom_call_target="tpu_custom_call" | custom-call | tf_op jit(solution)/shard_map/pallas_call | solution.py:45
  23.1 0.0 collective-permute-done.6.ref
  23.1 0.7 %shard_map.94 = (f32[768,256]{1,0:T(8,128)S(1)}, f32[64,32]{1,0:T(8,128)S(1)}) custom-call(f32[768,256]{1,0:T(8,128)S(1)} %get-tuple-element.99.old_grid_ref, f32[64,32]{1,0:T(8,128)S(1)} %get-tuple-element.100.old_counts_ref, bf16[72,1024]{1,0:T(8,128)(2,1)S(1)} %collective-permute-done.6.ref), custom_call_target="tpu_custom_call" | custom-call | tf_op jit(solution)/shard_map/pallas_call | solution.py:45
  23.8 2.0 %shard_map.95 = (bf16[4,256,256]{2,1,0:T(8,128)(2,1)S(1)}, f32[4,256,256]{2,1,0:T(8,128)S(1)}, bf16[2,6,10,16,256]{4,3,2,1,0:T(8,128)(2,1)S(1)}) custom-call(f32[768,256]{1,0:T(8,128)S(1)} %get-tuple-element.84.grid0, f32[64,32]{1,0:T(8,128)S(1)} %get-tuple-element.85.counts0, f32[768,256]{1,0:T(8,128)S(1)} %get-tuple-element.89.grid1, ...), custom_call_target="tpu_custom_call" | custom-call | tf_op jit(solution)/shard_map/pallas_call | solution.py:45
  25.8 0.5 %shard_map.96 = (bf16[2,4,10,16,256]{4,3,2,1,0:T(8,128)(2,1)S(1)}, f32[4,256,128]{2,1,0:T(8,128)S(1)}, bf16[4,256,128]{2,1,0:T(8,128)(2,1)S(1)}) custom-call(bf16[4,256,256]{2,1,0:T(8,128)(2,1)S(1)} %get-tuple-element.105.act_ref, f32[4,256,256]{2,1,0:T(8,128)S(1)} %get-tuple-element.106.slope_ref, bf16[128,256]{1,0:T(8,128)(2,1)S(1)} %get-tuple-element.83.own_ref, ...), custom_call_target="tpu_custom_call" | custom-call | tf_op jit(solution)/shard_map/pallas_call | solution.py:45
  26.3 0.6 %collective-permute-start.8 = (bf16[4,256,128]{2,1,0:T(8,128)(2,1)S(1)}, bf16[4,256,128]{2,1,0:T(8,128)(2,1)S(1)}, u32[]{:S(2)}, u32[]{:S(2)}) collective-permute-start(bf16[4,256,128]{2,1,0:T(8,128)(2,1)S(1)} %get-tuple-element.110), channel_id=1, source_target_pairs={{0,1},{1,0},{2,3},{3,2},{4,5},{5,4},{6,7},{7,6},{8,9},{9,8},{10,11... | collective-permute-start | bytes 786440 | tf_op jit(solution)/shard_map/ppermute | solution.py:57
  26.9 1.4 %shard_map.97 = (f32[4,224,128]{2,1,0:T(8,128)S(1)}, bf16[4,224,128]{2,1,0:T(8,128)(2,1)S(1)}) custom-call(bf16[2,6,10,16,256]{4,3,2,1,0:T(8,128)(2,1)S(1)} %get-tuple-element.111.es_ref, bf16[2,4,10,16,256]{4,3,2,1,0:T(8,128)(2,1)S(1)} %get-tuple-element.112.pg_ref), custom_call_target="tpu_custom_call" | custom-call | tf_op jit(solution)/shard_map/pallas_call | solution.py:45
  28.3 0.0 collective-permute-done.8.got_ref
  28.3 0.1 collective-permute-start.9
  28.4 1.5 %collective-permute-done.9.got_conv_ref = bf16[4,224,128]{2,1,0:T(8,128)(2,1)S(1)} collective-permute-done((bf16[4,224,128]{2,1,0:T(8,128)(2,1)S(1)}, bf16[4,224,128]{2,1,0:T(8,128)(2,1)S(1)}, u32[]{:S(2)}, u32[]{:S(2)}) %collective-permute-start.9) | collective-permute-done | bytes 229408 | tf_op jit(solution)/shard_map/ppermute | solution.py:57
  29.9 0.1 shard_map.98
  30.0 1.6 %collective-permute-start.10 = (bf16[480,128]{1,0:T(8,128)(2,1)S(1)}, bf16[480,128]{1,0:T(8,128)(2,1)S(1)}, u32[]{:S(2)}, u32[]{:S(2)}) collective-permute-start(bf16[480,128]{1,0:T(8,128)(2,1)S(1)} %get-tuple-element.119), channel_id=1, source_target_pairs={{0,8},{8,0},{16,24},{24,16},{1,9},{9,1},{17,25},{25,17},{2,10},{10... | collective-permute-start | bytes 368648 | tf_op jit(solution)/shard_map/ppermute | solution.py:66
  31.5 1.5 %collective-permute-start.11 = (bf16[480,128]{1,0:T(8,128)(2,1)S(1)}, bf16[480,128]{1,0:T(8,128)(2,1)S(1)}, u32[]{:S(2)}, u32[]{:S(2)}) collective-permute-start(bf16[480,128]{1,0:T(8,128)(2,1)S(1)} %get-tuple-element.120), channel_id=1, source_target_pairs={{0,16},{8,24},{16,0},{24,8},{1,17},{9,25},{17,1},{25,9},{2,18},{10... | collective-permute-start | bytes 368648 | tf_op jit(solution)/shard_map/ppermute | solution.py:66
  33.1 0.5 %collective-permute-start.12 = (bf16[480,128]{1,0:T(8,128)(2,1)S(1)}, bf16[480,128]{1,0:T(8,128)(2,1)S(1)}, u32[]{:S(2)}, u32[]{:S(2)}) collective-permute-start(bf16[480,128]{1,0:T(8,128)(2,1)S(1)} %get-tuple-element.121), channel_id=1, source_target_pairs={{0,24},{8,16},{16,8},{24,0},{1,25},{9,17},{17,9},{25,1},{2,26},{10... | collective-permute-start | bytes 368648 | tf_op jit(solution)/shard_map/ppermute | solution.py:66
  33.5 0.4 shard_map.99
  33.9 0.7 %reshape.13 = bf16[1,2,16,4,256]{4,3,2,1,0:T(4,128)(2,1)} reshape(bf16[128,256]{1,0:T(8,128)(2,1)S(1)} %shard_map.99) | data formatting | bytes 131072 | tf_op jit(solution)/shard_map/reshape | solution.py:480
  34.6 1.0 %collective-permute-done.10.refs_1_ = bf16[480,128]{1,0:T(8,128)(2,1)S(1)} collective-permute-done((bf16[480,128]{1,0:T(8,128)(2,1)S(1)}, bf16[480,128]{1,0:T(8,128)(2,1)S(1)}, u32[]{:S(2)}, u32[]{:S(2)}) %collective-permute-start.10) | collective-permute-done | bytes 122912 | tf_op jit(solution)/shard_map/ppermute | solution.py:66
  35.6 3.7 %collective-permute-done.11.refs_2_ = bf16[480,128]{1,0:T(8,128)(2,1)S(1)} collective-permute-done((bf16[480,128]{1,0:T(8,128)(2,1)S(1)}, bf16[480,128]{1,0:T(8,128)(2,1)S(1)}, u32[]{:S(2)}, u32[]{:S(2)}) %collective-permute-start.11) | collective-permute-done | bytes 122912 | tf_op jit(solution)/shard_map/ppermute | solution.py:66
  39.3 0.0 collective-permute-done.12.refs_3_
  39.3 0.1 shard_map.100.refs_0_
  39.3 0.1 collective-permute-start.13
  39.4 4.9 %collective-permute-done.13.refs_1_ = bf16[480,128]{1,0:T(8,128)(2,1)S(1)} collective-permute-done((bf16[480,128]{1,0:T(8,128)(2,1)S(1)}, bf16[480,128]{1,0:T(8,128)(2,1)S(1)}, u32[]{:S(2)}, u32[]{:S(2)}) %collective-permute-start.13) | collective-permute-done | bytes 122912 | tf_op jit(solution)/shard_map/ppermute | solution.py:62
  44.3 0.1 collective-permute-start.14
  44.4 1.5 %collective-permute-done.14.got_ref = f32[480,128]{1,0:T(8,128)S(1)} collective-permute-done((f32[480,128]{1,0:T(8,128)S(1)}, f32[480,128]{1,0:T(8,128)S(1)}, u32[]{:S(2)}, u32[]{:S(2)}) %collective-permute-start.14) | collective-permute-done | bytes 245792 | tf_op jit(solution)/shard_map/ppermute | solution.py:57
  45.9 0.8 %shard_map.102 = (f32[432,128]{1,0:T(8,128)}, f32[256,256]{1,0:T(8,128)}) custom-call(f32[480,128]{1,0:T(8,128)S(1)} %shard_map.101.own_ref, f32[480,128]{1,0:T(8,128)S(1)} %collective-permute-done.14.got_ref), custom_call_target="tpu_custom_call" | custom-call | tf_op jit(solution)/shard_map/pallas_call | solution.py:45
  (2 shorter events, 0.0 us)
Async XLA Ops:
  1.6 9.8 %collective-permute-start = (bf16[72,1024]{1,0:T(8,128)(2,1)S(1)}, bf16[72,1024]{1,0:T(8,128)(2,1)S(1)}, u32[]{:S(2)}, u32[]{:S(2)}) collective-permute-start(bf16[72,1024]{1,0:T(8,128)(2,1)S(1)} %shard_map.85.ref), channel_id=1, source_target_pairs={{0,6},{1,7},{2,4},{3,5},{4,2},{5,3},{6,0},{7,1},{8,14},{9,15},{10,... | collective-permute-start | bytes 442376 | tf_op jit(solution)/shard_map/ppermute | solution.py:62
  6.7 11.2 %collective-permute-start.2 = (bf16[72,1024]{1,0:T(8,128)(2,1)S(1)}, bf16[72,1024]{1,0:T(8,128)(2,1)S(1)}, u32[]{:S(2)}, u32[]{:S(2)}) collective-permute-start(bf16[72,1024]{1,0:T(8,128)(2,1)S(1)} %shard_map.85.ref), channel_id=1, source_target_pairs={{0,2},{1,3},{2,0},{3,1},{4,6},{5,7},{6,4},{7,5},{8,10},{9,11},{10,... | collective-permute-start | bytes 442376 | tf_op jit(solution)/shard_map/ppermute | solution.py:62
  11.4 9.0 %collective-permute-start.1 = (bf16[72,1024]{1,0:T(8,128)(2,1)S(1)}, bf16[72,1024]{1,0:T(8,128)(2,1)S(1)}, u32[]{:S(2)}, u32[]{:S(2)}) collective-permute-start(bf16[72,1024]{1,0:T(8,128)(2,1)S(1)} %collective-permute-done.ref), channel_id=1, source_target_pairs={{0,2},{1,3},{2,0},{3,1},{4,6},{5,7},{6,4},{7,5},{8,10},{9,11},{10,... | collective-permute-start | bytes 442376 | tf_op jit(solution)/shard_map/ppermute | solution.py:62
  14.1 6.3 %collective-permute-start.3 = (bf16[128,256]{1,0:T(8,128)(2,1)S(1)}, bf16[128,256]{1,0:T(8,128)(2,1)S(1)}, u32[]{:S(2)}, u32[]{:S(2)}) collective-permute-start(bf16[128,256]{1,0:T(8,128)(2,1)S(1)} %get-tuple-element.83.own_ref), channel_id=1, source_target_pairs={{0,6},{1,7},{2,4},{3,5},{4,2},{5,3},{6,0},{7,1},{8,14},{9,15},{10,... | collective-permute-start | bytes 196616 | tf_op jit(solution)/shard_map/ppermute | solution.py:62
  16.6 4.5 %collective-permute-start.4 = (bf16[72,1024]{1,0:T(8,128)(2,1)S(1)}, bf16[72,1024]{1,0:T(8,128)(2,1)S(1)}, u32[]{:S(2)}, u32[]{:S(2)}) collective-permute-start(bf16[72,1024]{1,0:T(8,128)(2,1)S(1)} %shard_map.85.ref), channel_id=1, source_target_pairs={{0,1},{1,0},{2,3},{3,2},{4,5},{5,4},{6,7},{7,6},{8,9},{9,8},{10,11... | collective-permute-start | bytes 442376 | tf_op jit(solution)/shard_map/ppermute | solution.py:57
  17.3 4.5 %collective-permute-start.7 = (bf16[72,1024]{1,0:T(8,128)(2,1)S(1)}, bf16[72,1024]{1,0:T(8,128)(2,1)S(1)}, u32[]{:S(2)}, u32[]{:S(2)}) collective-permute-start(bf16[72,1024]{1,0:T(8,128)(2,1)S(1)} %collective-permute-done.ref), channel_id=1, source_target_pairs={{0,1},{1,0},{2,3},{3,2},{4,5},{5,4},{6,7},{7,6},{8,9},{9,8},{10,11... | collective-permute-start | bytes 442376 | tf_op jit(solution)/shard_map/ppermute | solution.py:57
  18.6 3.9 %collective-permute-start.5 = (bf16[72,1024]{1,0:T(8,128)(2,1)S(1)}, bf16[72,1024]{1,0:T(8,128)(2,1)S(1)}, u32[]{:S(2)}, u32[]{:S(2)}) collective-permute-start(bf16[72,1024]{1,0:T(8,128)(2,1)S(1)} %collective-permute-done.2.ref), channel_id=1, source_target_pairs={{0,1},{1,0},{2,3},{3,2},{4,5},{5,4},{6,7},{7,6},{8,9},{9,8},{10,11... | collective-permute-start | bytes 442376 | tf_op jit(solution)/shard_map/ppermute | solution.py:57
  20.4 2.7 %collective-permute-start.6 = (bf16[72,1024]{1,0:T(8,128)(2,1)S(1)}, bf16[72,1024]{1,0:T(8,128)(2,1)S(1)}, u32[]{:S(2)}, u32[]{:S(2)}) collective-permute-start(bf16[72,1024]{1,0:T(8,128)(2,1)S(1)} %collective-permute-done.1.ref), channel_id=1, source_target_pairs={{0,1},{1,0},{2,3},{3,2},{4,5},{5,4},{6,7},{7,6},{8,9},{9,8},{10,11... | collective-permute-start | bytes 442376 | tf_op jit(solution)/shard_map/ppermute | solution.py:57
  26.3 2.0 %collective-permute-start.8 = (bf16[4,256,128]{2,1,0:T(8,128)(2,1)S(1)}, bf16[4,256,128]{2,1,0:T(8,128)(2,1)S(1)}, u32[]{:S(2)}, u32[]{:S(2)}) collective-permute-start(bf16[4,256,128]{2,1,0:T(8,128)(2,1)S(1)} %get-tuple-element.110), channel_id=1, source_target_pairs={{0,1},{1,0},{2,3},{3,2},{4,5},{5,4},{6,7},{7,6},{8,9},{9,8},{10,11... | collective-permute-start | bytes 786440 | tf_op jit(solution)/shard_map/ppermute | solution.py:57
  28.3 1.6 %collective-permute-start.9 = (bf16[4,224,128]{2,1,0:T(8,128)(2,1)S(1)}, bf16[4,224,128]{2,1,0:T(8,128)(2,1)S(1)}, u32[]{:S(2)}, u32[]{:S(2)}) collective-permute-start(bf16[4,224,128]{2,1,0:T(8,128)(2,1)S(1)} %get-tuple-element.117), channel_id=1, source_target_pairs={{0,1},{1,0},{2,3},{3,2},{4,5},{5,4},{6,7},{7,6},{8,9},{9,8},{10,11... | collective-permute-start | bytes 688136 | tf_op jit(solution)/shard_map/ppermute | solution.py:57
  30.0 5.6 %collective-permute-start.10 = (bf16[480,128]{1,0:T(8,128)(2,1)S(1)}, bf16[480,128]{1,0:T(8,128)(2,1)S(1)}, u32[]{:S(2)}, u32[]{:S(2)}) collective-permute-start(bf16[480,128]{1,0:T(8,128)(2,1)S(1)} %get-tuple-element.119), channel_id=1, source_target_pairs={{0,8},{8,0},{16,24},{24,16},{1,9},{9,1},{17,25},{25,17},{2,10},{10... | collective-permute-start | bytes 368648 | tf_op jit(solution)/shard_map/ppermute | solution.py:66
  31.5 7.7 %collective-permute-start.11 = (bf16[480,128]{1,0:T(8,128)(2,1)S(1)}, bf16[480,128]{1,0:T(8,128)(2,1)S(1)}, u32[]{:S(2)}, u32[]{:S(2)}) collective-permute-start(bf16[480,128]{1,0:T(8,128)(2,1)S(1)} %get-tuple-element.120), channel_id=1, source_target_pairs={{0,16},{8,24},{16,0},{24,8},{1,17},{9,25},{17,1},{25,9},{2,18},{10... | collective-permute-start | bytes 368648 | tf_op jit(solution)/shard_map/ppermute | solution.py:66
  33.1 6.2 %collective-permute-start.12 = (bf16[480,128]{1,0:T(8,128)(2,1)S(1)}, bf16[480,128]{1,0:T(8,128)(2,1)S(1)}, u32[]{:S(2)}, u32[]{:S(2)}) collective-permute-start(bf16[480,128]{1,0:T(8,128)(2,1)S(1)} %get-tuple-element.121), channel_id=1, source_target_pairs={{0,24},{8,16},{16,8},{24,0},{1,25},{9,17},{17,9},{25,1},{2,26},{10... | collective-permute-start | bytes 368648 | tf_op jit(solution)/shard_map/ppermute | solution.py:66
  39.3 4.9 %collective-permute-start.13 = (bf16[480,128]{1,0:T(8,128)(2,1)S(1)}, bf16[480,128]{1,0:T(8,128)(2,1)S(1)}, u32[]{:S(2)}, u32[]{:S(2)}) collective-permute-start(bf16[480,128]{1,0:T(8,128)(2,1)S(1)} %shard_map.100.refs_0_), channel_id=1, source_target_pairs={{0,2},{1,3},{2,0},{3,1},{4,6},{5,7},{6,4},{7,5},{8,10},{9,11},{10,... | collective-permute-start | bytes 368648 | tf_op jit(solution)/shard_map/ppermute | solution.py:62
  44.3 1.6 %collective-permute-start.14 = (f32[480,128]{1,0:T(8,128)S(1)}, f32[480,128]{1,0:T(8,128)S(1)}, u32[]{:S(2)}, u32[]{:S(2)}) collective-permute-start(f32[480,128]{1,0:T(8,128)S(1)} %shard_map.101.own_ref), channel_id=1, source_target_pairs={{0,1},{1,0},{2,3},{3,2},{4,5},{5,4},{6,7},{7,6},{8,9},{9,8},{10,11... | collective-permute-start | bytes 737288 | tf_op jit(solution)/shard_map/ppermute | solution.py:57

commit v8 on v7

--- a/solution.py
+++ b/solution.py
@@ -180,9 +180,14 @@
     counts_ref[...] = old_counts_ref[...] + counts
 
 
-def stack_kernel(*refs):
-    for i, ref in enumerate(refs[:-1]):
-        refs[-1][i] = ref[...]
+def late_points_kernel(
+    old_grid_ref, old_counts_ref, across_ref, coded_ref, beside_ref, beyond_ref,
+    far_ref, far_counts_ref, own_ref, own_counts_ref, swap_ref, swap_counts_ref,
+):
+    first_points_kernel(None, coded_ref, own_ref, own_counts_ref)
+    first_points_kernel(None, beyond_ref, swap_ref, swap_counts_ref)
+    more_points_kernel(None, own_ref, own_counts_ref, beside_ref, own_ref, own_counts_ref)
+    more_points_kernel(None, old_grid_ref, old_counts_ref, across_ref, far_ref, far_counts_ref)
 
 
 def add_grids_kernel(*refs):
@@ -417,11 +422,10 @@
     own = add(own, beside)
     beside, own = lax.optimization_barrier((beside, own))
     beside_swap = swap_core(beside, tiles)
-    across, own, far, cot_got = lax.optimization_barrier((across, own, far, cot_got))
+    across, own, far = lax.optimization_barrier((across, own, far))
     across_swap = swap_core(across, tiles)
-    far = add(far, across)
-    own_swap = add(add(None, coded_swap), beside_swap)
-    far_swap = add(None, beyond_swap)
+    late = call(late_points_kernel, sums * 3, pinned=6)(*far, across, coded_swap, beside_swap, beyond_swap)
+    far, own_swap, far_swap = late[:2], late[2:4], late[4:]
     across_swap, far = lax.optimization_barrier((across_swap, far))
     far_swap = add(far_swap, across_swap)
     grids = [own, own_swap, far, far_swap]

time: 46.9 us -> 46.1 us (0.983)
  waiting for transfers between devices: 16.1 us -> 15.1 us
  starting transfers between devices: 14.7 us -> 15.6 us
  Pallas kernels: 13 us -> 12.3 us
    ppermute x5, waiting for transfers between devices: 8.46 us -> 7.52 us  [send_column(): return lax.ppermute(value, 'tile', pairs)]
    ppermute x5, starting transfers between devices: 9.73 us -> 10.6 us  [send_column(): return lax.ppermute(value, 'tile', pairs)]
    pallas_call x18 -> x15, Pallas kernels: 13 us -> 12.3 us  [run(): return kernel(*held, *far)]
  transfers between devices with their start and end apart: 15 -> 15, of which waited for: 7 -> 7; matrix products, arithmetic and copies ran while one was open for 5% -> 5% of each run, Pallas kernels for 17% -> 22%
where the time goes in v8:
time: 46.1 us; the launch traced here: 45.9 us
  starting transfers between devices  15.6 us (34%)
  waiting for transfers between devices  15.1 us (33%)
  Pallas kernels  12.3 us (27%)
  local copies, waits for them, and re-layouts  2.14 us (5%)
  between operations  0.79 us (2%)
    pallas_call x15, Pallas kernels, run(): return kernel(*held, *far)  12.3 us
    ppermute x5, starting transfers between devices, send_column(): return lax.ppermute(value, 'tile', pairs)  10.6 us
    ppermute x5, waiting for transfers between devices, send_column(): return lax.ppermute(value, 'tile', pairs)  7.52 us
    ppermute x3, waiting for transfers between devices, send_sample(): lax.ppermute(value, 'sample', [(i, target(i, k, samples)) for i in range(...  4.82 us
    ppermute x3, starting transfers between devices, send_sample(): lax.ppermute(value, 'sample', [(i, target(i, k, samples)) for i in range(...  3.55 us
    ppermute x7, waiting for transfers between devices, swap_core(): return lax.ppermute(value, 'tile', [(i, i ^ 1) for i in range(tiles)])  2.72 us
    reshape x1, local copies, waits for them, and re-layouts, local(): cotangent.reshape(128, C2)  1.49 us
    ppermute x7, starting transfers between devices, swap_core(): return lax.ppermute(value, 'tile', [(i, i ^ 1) for i in range(tiles)])  1.41 us
  transfers between devices with their start and end apart: 15, of which 7 were waited for; matrix products, arithmetic and copies ran while one was open for 5% of the time, Pallas kernels for 22%

profile of v8, /device:TPU:0, one launch (start us, length us, event | category | flops | bytes accessed | tf_op | source)
XLA Modules:
  0.0 45.9 jit_solution(6821861110663081797)
XLA Ops:
  0.6 1.0 %shard_map.85.ref = bf16[72,1024]{1,0:T(8,128)(2,1)S(1)} custom-call(bf16[64,1024]{1,0:T(8,128)(2,1)} %bitcast.3, s32[1,1024]{1,0:T(1,128)} %slot_hbm.1, s32[1,1024]{1,0:T(1,128)} %voxel_hbm.1), custom_call_target="tpu_custom_call" | custom-call | tf_op jit(solution)/shard_map/pallas_call | solution.py:45
  1.6 5.1 %collective-permute-start = (bf16[72,1024]{1,0:T(8,128)(2,1)S(1)}, bf16[72,1024]{1,0:T(8,128)(2,1)S(1)}, u32[]{:S(2)}, u32[]{:S(2)}) collective-permute-start(bf16[72,1024]{1,0:T(8,128)(2,1)S(1)} %shard_map.85.ref), channel_id=1, source_target_pairs={{0,6},{1,7},{2,4},{3,5},{4,2},{5,3},{6,0},{7,1},{8,14},{9,15},{10,... | collective-permute-start | bytes 442376 | tf_op jit(solution)/shard_map/ppermute | solution.py:62
  6.7 0.0 collective-permute-start.2
  6.7 1.5 %reshape.12.cot_ref = bf16[128,256]{1,0:T(8,128)(2,1)} reshape(bf16[1,2,16,4,256]{4,3,2,1,0:T(4,128)(2,1)} %param.11) | data formatting | bytes 131072 | tf_op jit(solution)/shard_map/reshape | solution.py:413
  8.2 1.4 %shard_map.86 = (bf16[9,256,256]{2,1,0:T(8,128)(2,1)S(1)}, bf16[4,256,256]{2,1,0:T(8,128)(2,1)S(1)}, bf16[128,256]{1,0:T(8,128)(2,1)S(1)}) custom-call(bf16[1728,128]{1,0:T(8,128)(2,1)} %conv_ref.1, bf16[1024,256]{1,0:T(8,128)(2,1)} %down_ref.1, bf16[128,256]{1,0:T(8,128)(2,1)} %reshape.12.cot_ref), custom_call_target="tpu_custom_call" | custom-call | tf_op jit(solution)/shard_map/pallas_call | solution.py:45
  9.6 1.8 %collective-permute-done.ref = bf16[72,1024]{1,0:T(8,128)(2,1)S(1)} collective-permute-done((bf16[72,1024]{1,0:T(8,128)(2,1)S(1)}, bf16[72,1024]{1,0:T(8,128)(2,1)S(1)}, u32[]{:S(2)}, u32[]{:S(2)}) %collective-permute-start) | collective-permute-done | bytes 147488 | tf_op jit(solution)/shard_map/ppermute | solution.py:62
  11.4 2.0 %collective-permute-start.1 = (bf16[72,1024]{1,0:T(8,128)(2,1)S(1)}, bf16[72,1024]{1,0:T(8,128)(2,1)S(1)}, u32[]{:S(2)}, u32[]{:S(2)}) collective-permute-start(bf16[72,1024]{1,0:T(8,128)(2,1)S(1)} %collective-permute-done.ref), channel_id=1, source_target_pairs={{0,2},{1,3},{2,0},{3,1},{4,6},{5,7},{6,4},{7,5},{8,10},{9,11},{10,... | collective-permute-start | bytes 442376 | tf_op jit(solution)/shard_map/ppermute | solution.py:62
  13.4 0.7 %shard_map.87 = (f32[768,256]{1,0:T(8,128)S(1)}, f32[64,32]{1,0:T(8,128)S(1)}) custom-call(bf16[72,1024]{1,0:T(8,128)(2,1)S(1)} %collective-permute-done.ref), custom_call_target="tpu_custom_call" | custom-call | tf_op jit(solution)/shard_map/pallas_call | solution.py:45
  14.1 0.7 %shard_map.88 = (f32[768,256]{1,0:T(8,128)S(1)}, f32[64,32]{1,0:T(8,128)S(1)}) custom-call(bf16[72,1024]{1,0:T(8,128)(2,1)S(1)} %shard_map.85.ref), custom_call_target="tpu_custom_call" | custom-call | tf_op jit(solution)/shard_map/pallas_call | solution.py:45
  14.8 0.1 collective-permute-start.3
  14.8 0.0 collective-permute-done.2.ref
  14.9 0.7 %shard_map.89 = (f32[768,256]{1,0:T(8,128)S(1)}, f32[64,32]{1,0:T(8,128)S(1)}) custom-call(f32[768,256]{1,0:T(8,128)S(1)} %get-tuple-element.72.old_grid_ref, f32[64,32]{1,0:T(8,128)S(1)} %get-tuple-element.73.old_counts_ref, bf16[72,1024]{1,0:T(8,128)(2,1)S(1)} %collective-permute-done.2.ref), custom_call_target="tpu_custom_call" | custom-call | tf_op jit(solution)/shard_map/pallas_call | solution.py:45
  15.5 0.6 %collective-permute-start.4 = (bf16[72,1024]{1,0:T(8,128)(2,1)S(1)}, bf16[72,1024]{1,0:T(8,128)(2,1)S(1)}, u32[]{:S(2)}, u32[]{:S(2)}) collective-permute-start(bf16[72,1024]{1,0:T(8,128)(2,1)S(1)} %collective-permute-done.2.ref), channel_id=1, source_target_pairs={{0,1},{1,0},{2,3},{3,2},{4,5},{5,4},{6,7},{7,6},{8,9},{9,8},{10,11... | collective-permute-start | bytes 442376 | tf_op jit(solution)/shard_map/ppermute | solution.py:57
  16.1 0.1 collective-permute-start.5
  16.2 0.8 %collective-permute-done.1.across_ref = bf16[72,1024]{1,0:T(8,128)(2,1)S(1)} collective-permute-done((bf16[72,1024]{1,0:T(8,128)(2,1)S(1)}, bf16[72,1024]{1,0:T(8,128)(2,1)S(1)}, u32[]{:S(2)}, u32[]{:S(2)}) %collective-permute-start.1) | collective-permute-done | bytes 147488 | tf_op jit(solution)/shard_map/ppermute | solution.py:62
  17.0 0.0 collective-permute-start.6
  17.0 3.4 %collective-permute-start.7 = (bf16[128,256]{1,0:T(8,128)(2,1)S(1)}, bf16[128,256]{1,0:T(8,128)(2,1)S(1)}, u32[]{:S(2)}, u32[]{:S(2)}) collective-permute-start(bf16[128,256]{1,0:T(8,128)(2,1)S(1)} %get-tuple-element.101.own_ref), channel_id=1, source_target_pairs={{0,6},{1,7},{2,4},{3,5},{4,2},{5,3},{6,0},{7,1},{8,14},{9,15},{10,... | collective-permute-start | bytes 196616 | tf_op jit(solution)/shard_map/ppermute | solution.py:62
  20.4 0.0 collective-permute-done.4.beside_ref
  20.4 0.0 collective-permute-done.3.coded_ref
  20.4 0.0 collective-permute-done.5.beyond_ref
  20.4 2.0 %shard_map.90 = (f32[768,256]{1,0:T(8,128)S(1)}, f32[64,32]{1,0:T(8,128)S(1)}, f32[768,256]{1,0:T(8,128)S(1)}, f32[64,32]{1,0:T(8,128)S(1)}, f32[768,256]{1,0:T(8,128)S(1)}, /*index=5*/f32[64,32]{1,0:T(8,128)S(1)}) custom-call(f32[768,256]{1,0:T(8,128)S(1)} %get-tuple-element.82.old_grid_ref, f32[64,32]{1,0:T(8,128)S(1)} %get-tuple-element.83.old_counts_ref, ...), custom_call_target="tpu_custom_call" | custom-call | tf_op jit(solution)/shard_map/pallas_call | solution.py:45
  22.4 0.0 collective-permute-done.6.ref
  22.5 0.7 %shard_map.91 = (f32[768,256]{1,0:T(8,128)S(1)}, f32[64,32]{1,0:T(8,128)S(1)}) custom-call(f32[768,256]{1,0:T(8,128)S(1)} %get-tuple-element.93.old_grid_ref, f32[64,32]{1,0:T(8,128)S(1)} %get-tuple-element.94.old_counts_ref, bf16[72,1024]{1,0:T(8,128)(2,1)S(1)} %collective-permute-done.6.ref), custom_call_target="tpu_custom_call" | custom-call | tf_op jit(solution)/shard_map/pallas_call | solution.py:45
  23.1 2.0 %shard_map.92 = (bf16[4,256,256]{2,1,0:T(8,128)(2,1)S(1)}, f32[4,256,256]{2,1,0:T(8,128)S(1)}, bf16[2,6,10,16,256]{4,3,2,1,0:T(8,128)(2,1)S(1)}) custom-call(f32[768,256]{1,0:T(8,128)S(1)} %get-tuple-element.80.grid0, f32[64,32]{1,0:T(8,128)S(1)} %get-tuple-element.81.counts0, f32[768,256]{1,0:T(8,128)S(1)} %get-tuple-element.87.grid1, ...), custom_call_target="tpu_custom_call" | custom-call | tf_op jit(solution)/shard_map/pallas_call | solution.py:45
  25.2 0.0 collective-permute-done.7.got_ref
  25.2 0.5 %shard_map.93 = (bf16[2,4,10,16,256]{4,3,2,1,0:T(8,128)(2,1)S(1)}, f32[4,256,128]{2,1,0:T(8,128)S(1)}, bf16[4,256,128]{2,1,0:T(8,128)(2,1)S(1)}) custom-call(bf16[4,256,256]{2,1,0:T(8,128)(2,1)S(1)} %get-tuple-element.99.act_ref, f32[4,256,256]{2,1,0:T(8,128)S(1)} %get-tuple-element.100.slope_ref, bf16[128,256]{1,0:T(8,128)(2,1)S(1)} %get-tuple-element.101.own_ref, ...), custom_call_target="tpu_custom_call" | custom-call | tf_op jit(solution)/shard_map/pallas_call | solution.py:45
  25.6 0.3 collective-permute-start.8
  25.9 1.4 %shard_map.94 = (f32[4,224,128]{2,1,0:T(8,128)S(1)}, bf16[4,224,128]{2,1,0:T(8,128)(2,1)S(1)}) custom-call(bf16[2,6,10,16,256]{4,3,2,1,0:T(8,128)(2,1)S(1)} %get-tuple-element.105.es_ref, bf16[2,4,10,16,256]{4,3,2,1,0:T(8,128)(2,1)S(1)} %get-tuple-element.106.pg_ref), custom_call_target="tpu_custom_call" | custom-call | tf_op jit(solution)/shard_map/pallas_call | solution.py:45
  27.4 0.0 collective-permute-done.8.got_ref
  27.4 0.3 collective-permute-start.9
  27.7 1.2 %collective-permute-done.9.got_conv_ref = bf16[4,224,128]{2,1,0:T(8,128)(2,1)S(1)} collective-permute-done((bf16[4,224,128]{2,1,0:T(8,128)(2,1)S(1)}, bf16[4,224,128]{2,1,0:T(8,128)(2,1)S(1)}, u32[]{:S(2)}, u32[]{:S(2)}) %collective-permute-start.9) | collective-permute-done | bytes 229408 | tf_op jit(solution)/shard_map/ppermute | solution.py:57
  28.9 0.1 shard_map.95
  29.0 1.6 %collective-permute-start.10 = (bf16[480,128]{1,0:T(8,128)(2,1)S(1)}, bf16[480,128]{1,0:T(8,128)(2,1)S(1)}, u32[]{:S(2)}, u32[]{:S(2)}) collective-permute-start(bf16[480,128]{1,0:T(8,128)(2,1)S(1)} %get-tuple-element.113), channel_id=1, source_target_pairs={{0,8},{8,0},{16,24},{24,16},{1,9},{9,1},{17,25},{25,17},{2,10},{10... | collective-permute-start | bytes 368648 | tf_op jit(solution)/shard_map/ppermute | solution.py:66
  30.6 1.5 %collective-permute-start.11 = (bf16[480,128]{1,0:T(8,128)(2,1)S(1)}, bf16[480,128]{1,0:T(8,128)(2,1)S(1)}, u32[]{:S(2)}, u32[]{:S(2)}) collective-permute-start(bf16[480,128]{1,0:T(8,128)(2,1)S(1)} %get-tuple-element.114), channel_id=1, source_target_pairs={{0,16},{8,24},{16,0},{24,8},{1,17},{9,25},{17,1},{25,9},{2,18},{10... | collective-permute-start | bytes 368648 | tf_op jit(solution)/shard_map/ppermute | solution.py:66
  32.1 0.5 %collective-permute-start.12 = (bf16[480,128]{1,0:T(8,128)(2,1)S(1)}, bf16[480,128]{1,0:T(8,128)(2,1)S(1)}, u32[]{:S(2)}, u32[]{:S(2)}) collective-permute-start(bf16[480,128]{1,0:T(8,128)(2,1)S(1)} %get-tuple-element.115), channel_id=1, source_target_pairs={{0,24},{8,16},{16,8},{24,0},{1,25},{9,17},{17,9},{25,1},{2,26},{10... | collective-permute-start | bytes 368648 | tf_op jit(solution)/shard_map/ppermute | solution.py:66
  32.6 0.4 shard_map.96
  33.0 0.7 %reshape.13 = bf16[1,2,16,4,256]{4,3,2,1,0:T(4,128)(2,1)} reshape(bf16[128,256]{1,0:T(8,128)(2,1)S(1)} %shard_map.96) | data formatting | bytes 131072 | tf_op jit(solution)/shard_map/reshape | solution.py:484
  33.6 1.1 %collective-permute-done.10.refs_1_ = bf16[480,128]{1,0:T(8,128)(2,1)S(1)} collective-permute-done((bf16[480,128]{1,0:T(8,128)(2,1)S(1)}, bf16[480,128]{1,0:T(8,128)(2,1)S(1)}, u32[]{:S(2)}, u32[]{:S(2)}) %collective-permute-start.10) | collective-permute-done | bytes 122912 | tf_op jit(solution)/shard_map/ppermute | solution.py:66
  34.8 3.7 %collective-permute-done.11.refs_2_ = bf16[480,128]{1,0:T(8,128)(2,1)S(1)} collective-permute-done((bf16[480,128]{1,0:T(8,128)(2,1)S(1)}, bf16[480,128]{1,0:T(8,128)(2,1)S(1)}, u32[]{:S(2)}, u32[]{:S(2)}) %collective-permute-start.11) | collective-permute-done | bytes 122912 | tf_op jit(solution)/shard_map/ppermute | solution.py:66
  38.5 0.0 collective-permute-done.12.refs_3_
  38.5 0.1 shard_map.97.refs_0_
  38.5 0.1 collective-permute-start.13
  38.6 4.9 %collective-permute-done.13.refs_1_ = bf16[480,128]{1,0:T(8,128)(2,1)S(1)} collective-permute-done((bf16[480,128]{1,0:T(8,128)(2,1)S(1)}, bf16[480,128]{1,0:T(8,128)(2,1)S(1)}, u32[]{:S(2)}, u32[]{:S(2)}) %collective-permute-start.13) | collective-permute-done | bytes 122912 | tf_op jit(solution)/shard_map/ppermute | solution.py:62
  43.5 0.1 collective-permute-start.14
  43.6 1.5 %collective-permute-done.14.got_ref = f32[480,128]{1,0:T(8,128)S(1)} collective-permute-done((f32[480,128]{1,0:T(8,128)S(1)}, f32[480,128]{1,0:T(8,128)S(1)}, u32[]{:S(2)}, u32[]{:S(2)}) %collective-permute-start.14) | collective-permute-done | bytes 245792 | tf_op jit(solution)/shard_map/ppermute | solution.py:57
  45.1 0.8 %shard_map.99 = (f32[432,128]{1,0:T(8,128)}, f32[256,256]{1,0:T(8,128)}) custom-call(f32[480,128]{1,0:T(8,128)S(1)} %shard_map.98.own_ref, f32[480,128]{1,0:T(8,128)S(1)} %collective-permute-done.14.got_ref), custom_call_target="tpu_custom_call" | custom-call | tf_op jit(solution)/shard_map/pallas_call | solution.py:45
  (1 shorter events, 0.0 us)
Async XLA Ops:
  1.6 9.8 %collective-permute-start = (bf16[72,1024]{1,0:T(8,128)(2,1)S(1)}, bf16[72,1024]{1,0:T(8,128)(2,1)S(1)}, u32[]{:S(2)}, u32[]{:S(2)}) collective-permute-start(bf16[72,1024]{1,0:T(8,128)(2,1)S(1)} %shard_map.85.ref), channel_id=1, source_target_pairs={{0,6},{1,7},{2,4},{3,5},{4,2},{5,3},{6,0},{7,1},{8,14},{9,15},{10,... | collective-permute-start | bytes 442376 | tf_op jit(solution)/shard_map/ppermute | solution.py:62
  6.7 8.1 %collective-permute-start.2 = (bf16[72,1024]{1,0:T(8,128)(2,1)S(1)}, bf16[72,1024]{1,0:T(8,128)(2,1)S(1)}, u32[]{:S(2)}, u32[]{:S(2)}) collective-permute-start(bf16[72,1024]{1,0:T(8,128)(2,1)S(1)} %shard_map.85.ref), channel_id=1, source_target_pairs={{0,2},{1,3},{2,0},{3,1},{4,6},{5,7},{6,4},{7,5},{8,10},{9,11},{10,... | collective-permute-start | bytes 442376 | tf_op jit(solution)/shard_map/ppermute | solution.py:62
  11.4 5.5 %collective-permute-start.1 = (bf16[72,1024]{1,0:T(8,128)(2,1)S(1)}, bf16[72,1024]{1,0:T(8,128)(2,1)S(1)}, u32[]{:S(2)}, u32[]{:S(2)}) collective-permute-start(bf16[72,1024]{1,0:T(8,128)(2,1)S(1)} %collective-permute-done.ref), channel_id=1, source_target_pairs={{0,2},{1,3},{2,0},{3,1},{4,6},{5,7},{6,4},{7,5},{8,10},{9,11},{10,... | collective-permute-start | bytes 442376 | tf_op jit(solution)/shard_map/ppermute | solution.py:62
  14.8 5.6 %collective-permute-start.3 = (bf16[72,1024]{1,0:T(8,128)(2,1)S(1)}, bf16[72,1024]{1,0:T(8,128)(2,1)S(1)}, u32[]{:S(2)}, u32[]{:S(2)}) collective-permute-start(bf16[72,1024]{1,0:T(8,128)(2,1)S(1)} %shard_map.85.ref), channel_id=1, source_target_pairs={{0,1},{1,0},{2,3},{3,2},{4,5},{5,4},{6,7},{7,6},{8,9},{9,8},{10,11... | collective-permute-start | bytes 442376 | tf_op jit(solution)/shard_map/ppermute | solution.py:57
  15.5 4.9 %collective-permute-start.4 = (bf16[72,1024]{1,0:T(8,128)(2,1)S(1)}, bf16[72,1024]{1,0:T(8,128)(2,1)S(1)}, u32[]{:S(2)}, u32[]{:S(2)}) collective-permute-start(bf16[72,1024]{1,0:T(8,128)(2,1)S(1)} %collective-permute-done.2.ref), channel_id=1, source_target_pairs={{0,1},{1,0},{2,3},{3,2},{4,5},{5,4},{6,7},{7,6},{8,9},{9,8},{10,11... | collective-permute-start | bytes 442376 | tf_op jit(solution)/shard_map/ppermute | solution.py:57
  16.1 4.3 %collective-permute-start.5 = (bf16[72,1024]{1,0:T(8,128)(2,1)S(1)}, bf16[72,1024]{1,0:T(8,128)(2,1)S(1)}, u32[]{:S(2)}, u32[]{:S(2)}) collective-permute-start(bf16[72,1024]{1,0:T(8,128)(2,1)S(1)} %collective-permute-done.ref), channel_id=1, source_target_pairs={{0,1},{1,0},{2,3},{3,2},{4,5},{5,4},{6,7},{7,6},{8,9},{9,8},{10,11... | collective-permute-start | bytes 442376 | tf_op jit(solution)/shard_map/ppermute | solution.py:57
  17.0 5.5 %collective-permute-start.6 = (bf16[72,1024]{1,0:T(8,128)(2,1)S(1)}, bf16[72,1024]{1,0:T(8,128)(2,1)S(1)}, u32[]{:S(2)}, u32[]{:S(2)}) collective-permute-start(bf16[72,1024]{1,0:T(8,128)(2,1)S(1)} %collective-permute-done.1.across_ref), channel_id=1, source_target_pairs={{0,1},{1,0},{2,3},{3,2},{4,5},{5,4},{6,7},{7,6},{8,9},{9,8},{10,11... | collective-permute-start | bytes 442376 | tf_op jit(solution)/shard_map/ppermute | solution.py:57
  17.0 8.2 %collective-permute-start.7 = (bf16[128,256]{1,0:T(8,128)(2,1)S(1)}, bf16[128,256]{1,0:T(8,128)(2,1)S(1)}, u32[]{:S(2)}, u32[]{:S(2)}) collective-permute-start(bf16[128,256]{1,0:T(8,128)(2,1)S(1)} %get-tuple-element.101.own_ref), channel_id=1, source_target_pairs={{0,6},{1,7},{2,4},{3,5},{4,2},{5,3},{6,0},{7,1},{8,14},{9,15},{10,... | collective-permute-start | bytes 196616 | tf_op jit(solution)/shard_map/ppermute | solution.py:62
  25.6 1.7 %collective-permute-start.8 = (bf16[4,256,128]{2,1,0:T(8,128)(2,1)S(1)}, bf16[4,256,128]{2,1,0:T(8,128)(2,1)S(1)}, u32[]{:S(2)}, u32[]{:S(2)}) collective-permute-start(bf16[4,256,128]{2,1,0:T(8,128)(2,1)S(1)} %get-tuple-element.104), channel_id=1, source_target_pairs={{0,1},{1,0},{2,3},{3,2},{4,5},{5,4},{6,7},{7,6},{8,9},{9,8},{10,11... | collective-permute-start | bytes 786440 | tf_op jit(solution)/shard_map/ppermute | solution.py:57
  27.4 1.6 %collective-permute-start.9 = (bf16[4,224,128]{2,1,0:T(8,128)(2,1)S(1)}, bf16[4,224,128]{2,1,0:T(8,128)(2,1)S(1)}, u32[]{:S(2)}, u32[]{:S(2)}) collective-permute-start(bf16[4,224,128]{2,1,0:T(8,128)(2,1)S(1)} %get-tuple-element.111), channel_id=1, source_target_pairs={{0,1},{1,0},{2,3},{3,2},{4,5},{5,4},{6,7},{7,6},{8,9},{9,8},{10,11... | collective-permute-start | bytes 688136 | tf_op jit(solution)/shard_map/ppermute | solution.py:57
  29.0 5.7 %collective-permute-start.10 = (bf16[480,128]{1,0:T(8,128)(2,1)S(1)}, bf16[480,128]{1,0:T(8,128)(2,1)S(1)}, u32[]{:S(2)}, u32[]{:S(2)}) collective-permute-start(bf16[480,128]{1,0:T(8,128)(2,1)S(1)} %get-tuple-element.113), channel_id=1, source_target_pairs={{0,8},{8,0},{16,24},{24,16},{1,9},{9,1},{17,25},{25,17},{2,10},{10... | collective-permute-start | bytes 368648 | tf_op jit(solution)/shard_map/ppermute | solution.py:66
  30.6 7.9 %collective-permute-start.11 = (bf16[480,128]{1,0:T(8,128)(2,1)S(1)}, bf16[480,128]{1,0:T(8,128)(2,1)S(1)}, u32[]{:S(2)}, u32[]{:S(2)}) collective-permute-start(bf16[480,128]{1,0:T(8,128)(2,1)S(1)} %get-tuple-element.114), channel_id=1, source_target_pairs={{0,16},{8,24},{16,0},{24,8},{1,17},{9,25},{17,1},{25,9},{2,18},{10... | collective-permute-start | bytes 368648 | tf_op jit(solution)/shard_map/ppermute | solution.py:66
  32.1 6.4 %collective-permute-start.12 = (bf16[480,128]{1,0:T(8,128)(2,1)S(1)}, bf16[480,128]{1,0:T(8,128)(2,1)S(1)}, u32[]{:S(2)}, u32[]{:S(2)}) collective-permute-start(bf16[480,128]{1,0:T(8,128)(2,1)S(1)} %get-tuple-element.115), channel_id=1, source_target_pairs={{0,24},{8,16},{16,8},{24,0},{1,25},{9,17},{17,9},{25,1},{2,26},{10... | collective-permute-start | bytes 368648 | tf_op jit(solution)/shard_map/ppermute | solution.py:66
  38.5 4.9 %collective-permute-start.13 = (bf16[480,128]{1,0:T(8,128)(2,1)S(1)}, bf16[480,128]{1,0:T(8,128)(2,1)S(1)}, u32[]{:S(2)}, u32[]{:S(2)}) collective-permute-start(bf16[480,128]{1,0:T(8,128)(2,1)S(1)} %shard_map.97.refs_0_), channel_id=1, source_target_pairs={{0,2},{1,3},{2,0},{3,1},{4,6},{5,7},{6,4},{7,5},{8,10},{9,11},{10,... | collective-permute-start | bytes 368648 | tf_op jit(solution)/shard_map/ppermute | solution.py:62
  43.5 1.6 %collective-permute-start.14 = (f32[480,128]{1,0:T(8,128)S(1)}, f32[480,128]{1,0:T(8,128)S(1)}, u32[]{:S(2)}, u32[]{:S(2)}) collective-permute-start(f32[480,128]{1,0:T(8,128)S(1)} %shard_map.98.own_ref), channel_id=1, source_target_pairs={{0,1},{1,0},{2,3},{3,2},{4,5},{5,4},{6,7},{7,6},{8,9},{9,8},{10,11... | collective-permute-start | bytes 737288 | tf_op jit(solution)/shard_map/ppermute | solution.py:57

commit v9 on v8

--- a/solution.py
+++ b/solution.py
@@ -107,7 +107,9 @@
     return ((here >> 6) * 64 + (here & 3) * 16 + ((here >> 2) & 15) == there).astype(F32).astype(BF16)
 
 
-def weights_kernel(conv_ref, down_ref, cot_ref, taps_ref, pairs_ref, turned_ref):
+def weights_kernel(
+    conv_ref, down_ref, cot_ref, taps_ref, pairs_ref, turned_ref, pick_ref, line_ref, expand_ref
+):
     zero_tap = jnp.zeros((CIN, C1), BF16)
 
     def tap(dx, dy, dz):
@@ -132,6 +134,14 @@
             pairs_ref[ox * 2 + oz] = jnp.concatenate(
                 [down_ref[first : first + C1, :], down_ref[second : second + C1, :]], axis=0
             )
+    full = 2 * SX * LAYER
+    row_plane = lax.broadcasted_iota(I32, (full, 64), 0) >> 4
+    pick_ref[...] = (row_plane == lax.broadcasted_iota(I32, (full, 64), 1)).astype(F32).astype(BF16)
+    row_line = lax.broadcasted_iota(I32, (full, 32), 0) & 15
+    line_ref[...] = (row_line == (lax.broadcasted_iota(I32, (full, 32), 1) >> 1)).astype(F32).astype(BF16)
+    expand_ref[...] = (
+        (lax.broadcasted_iota(I32, (32, 256), 0) & 1) == (lax.broadcasted_iota(I32, (32, 256), 1) >> 7)
+    ).astype(F32).astype(BF16)
     turned_ref[...] = lax.dot_general(turn_matrix(), cot_ref[...], TN, preferred_element_type=F32).astype(BF16)
 
 
@@ -203,6 +213,7 @@
 
 def scene_kernel(
     grid0, counts0, grid1, counts1, grid2, counts2, grid3, counts3, taps_ref,
+    pick_ref, line_ref, expand_ref,
     act_ref, slope_ref, es_ref,
 ):
     counts = counts0[...] + counts1[...] + counts2[...] + counts3[...]
@@ -226,15 +237,9 @@
 
     full = 2 * SX * LAYER
     flags = (counts > 0.5).astype(F32).astype(BF16)
-    row_plane = lax.broadcasted_iota(I32, (full, 64), 0) >> 4
-    pick = (row_plane == lax.broadcasted_iota(I32, (full, 64), 1)).astype(F32).astype(BF16)
-    lines = jnp.dot(pick, flags, preferred_element_type=F32)
-    row_line = lax.broadcasted_iota(I32, (full, 32), 0) & 15
-    lines = jnp.where(row_line == (lax.broadcasted_iota(I32, (full, 32), 1) >> 1), lines, 0.0).astype(BF16)
-    expand = (
-        (lax.broadcasted_iota(I32, (32, 256), 0) & 1) == (lax.broadcasted_iota(I32, (32, 256), 1) >> 7)
-    ).astype(F32).astype(BF16)
-    active = jnp.dot(lines, expand, preferred_element_type=F32) > 0.5
+    lines = jnp.dot(pick_ref[...], flags, preferred_element_type=F32)
+    lines = lines.astype(BF16) * line_ref[...]
+    active = jnp.dot(lines, expand_ref[...], preferred_element_type=F32) > 0.5
 
     part = jnp.concatenate(
         [
@@ -406,9 +411,16 @@
 
     beyond = send_column(coded, lambda i: i ^ FAR, tiles)
     beside = send_column(coded, lambda i: i ^ 1, tiles)
-    taps, pairs, cot = call(
+    taps, pairs, cot, *masks = call(
         weights_kernel,
-        (shape((9, 4 * CIN, 2 * C1), BF16), shape((4, 2 * C1, C2), BF16), shape((128, C2), BF16)),
+        (
+            shape((9, 4 * CIN, 2 * C1), BF16),
+            shape((4, 2 * C1, C2), BF16),
+            shape((128, C2), BF16),
+            shape((2 * SX * LAYER, 64), BF16),
+            shape((2 * SX * LAYER, 32), BF16),
+            shape((32, 2 * C1), BF16),
+        ),
         loose=3,
     )(conv_weight, down_weight, cotangent.reshape(128, C2))
     beyond, taps, pairs, cot, coded = lax.optimization_barrier((beyond, taps, pairs, cot, coded))
@@ -453,8 +465,8 @@
             shape((4, 256, 2 * C1), F32),
             shape((2, SX + 2, SZ + 2, 16, 4 * CIN), BF16),
         ),
-        pinned=9,
-    )(*grids[0], *grids[1], *grids[2], *grids[3], taps)
+        pinned=12,
+    )(*grids[0], *grids[1], *grids[2], *grids[3], taps, *masks)
     pg, mine, other = call(
         functools.partial(down_grad_kernel, samples),
         (

time: 46.1 us -> 46 us (level)
  no operation moved by 1% of the time
where the time goes in v9:
time: 46 us; the launch traced here: 45.8 us
  starting transfers between devices  15.6 us (34%)
  waiting for transfers between devices  14.8 us (32%)
  Pallas kernels  12.4 us (27%)
  local copies, waits for them, and re-layouts  2.14 us (5%)
  between operations  0.79 us (2%)
    pallas_call x15, Pallas kernels, run(): return kernel(*held, *far)  12.4 us
    ppermute x5, starting transfers between devices, send_column(): return lax.ppermute(value, 'tile', pairs)  10.6 us
    ppermute x5, waiting for transfers between devices, send_column(): return lax.ppermute(value, 'tile', pairs)  7.28 us
    ppermute x3, waiting for transfers between devices, send_sample(): lax.ppermute(value, 'sample', [(i, target(i, k, samples)) for i in range(...  4.81 us
    ppermute x3, starting transfers between devices, send_sample(): lax.ppermute(value, 'sample', [(i, target(i, k, samples)) for i in range(...  3.55 us
    ppermute x7, waiting for transfers between devices, swap_core(): return lax.ppermute(value, 'tile', [(i, i ^ 1) for i in range(tiles)])  2.72 us
    reshape x1, local copies, waits for them, and re-layouts, local(): cotangent.reshape(128, C2)  1.49 us
    ppermute x7, starting transfers between devices, swap_core(): return lax.ppermute(value, 'tile', [(i, i ^ 1) for i in range(tiles)])  1.41 us
  transfers between devices with their start and end apart: 15, of which 7 were waited for; matrix products, arithmetic and copies ran while one was open for 5% of the time, Pallas kernels for 22%

profile of v9, /device:TPU:0, one launch (start us, length us, event | category | flops | bytes accessed | tf_op | source)
XLA Modules:
  0.0 45.8 jit_solution(10190297682834767045)
XLA Ops:
  0.6 1.0 %shard_map.85.ref = bf16[72,1024]{1,0:T(8,128)(2,1)S(1)} custom-call(bf16[64,1024]{1,0:T(8,128)(2,1)} %bitcast.3, s32[1,1024]{1,0:T(1,128)} %slot_hbm.1, s32[1,1024]{1,0:T(1,128)} %voxel_hbm.1), custom_call_target="tpu_custom_call" | custom-call | tf_op jit(solution)/shard_map/pallas_call | solution.py:45
  1.6 5.1 %collective-permute-start = (bf16[72,1024]{1,0:T(8,128)(2,1)S(1)}, bf16[72,1024]{1,0:T(8,128)(2,1)S(1)}, u32[]{:S(2)}, u32[]{:S(2)}) collective-permute-start(bf16[72,1024]{1,0:T(8,128)(2,1)S(1)} %shard_map.85.ref), channel_id=1, source_target_pairs={{0,6},{1,7},{2,4},{3,5},{4,2},{5,3},{6,0},{7,1},{8,14},{9,15},{10,... | collective-permute-start | bytes 442376 | tf_op jit(solution)/shard_map/ppermute | solution.py:62
  6.7 0.0 collective-permute-start.2
  6.7 1.5 %reshape.12.cot_ref = bf16[128,256]{1,0:T(8,128)(2,1)} reshape(bf16[1,2,16,4,256]{4,3,2,1,0:T(4,128)(2,1)} %param.11) | data formatting | bytes 131072 | tf_op jit(solution)/shard_map/reshape | solution.py:425
  8.2 1.6 %shard_map.86 = (bf16[9,256,256]{2,1,0:T(8,128)(2,1)S(1)}, bf16[4,256,256]{2,1,0:T(8,128)(2,1)S(1)}, bf16[128,256]{1,0:T(8,128)(2,1)S(1)}, bf16[1024,64]{1,0:T(8...) custom-call(bf16[1728,128]{1,0:T(8,128)(2,1)} %conv_ref.1, bf16[1024,256]{1,0:T(8,128)(2,1)} %down_ref.1, ...), custom_call_target="tpu_custom_call" | custom-call | tf_op jit(solution)/shard_map/pallas_call | solution.py:45
  9.9 1.6 %collective-permute-done.ref = bf16[72,1024]{1,0:T(8,128)(2,1)S(1)} collective-permute-done((bf16[72,1024]{1,0:T(8,128)(2,1)S(1)}, bf16[72,1024]{1,0:T(8,128)(2,1)S(1)}, u32[]{:S(2)}, u32[]{:S(2)}) %collective-permute-start) | collective-permute-done | bytes 147488 | tf_op jit(solution)/shard_map/ppermute | solution.py:62
  11.4 2.0 %collective-permute-start.1 = (bf16[72,1024]{1,0:T(8,128)(2,1)S(1)}, bf16[72,1024]{1,0:T(8,128)(2,1)S(1)}, u32[]{:S(2)}, u32[]{:S(2)}) collective-permute-start(bf16[72,1024]{1,0:T(8,128)(2,1)S(1)} %collective-permute-done.ref), channel_id=1, source_target_pairs={{0,2},{1,3},{2,0},{3,1},{4,6},{5,7},{6,4},{7,5},{8,10},{9,11},{10,... | collective-permute-start | bytes 442376 | tf_op jit(solution)/shard_map/ppermute | solution.py:62
  13.4 0.7 %shard_map.87 = (f32[768,256]{1,0:T(8,128)S(1)}, f32[64,32]{1,0:T(8,128)S(1)}) custom-call(bf16[72,1024]{1,0:T(8,128)(2,1)S(1)} %collective-permute-done.ref), custom_call_target="tpu_custom_call" | custom-call | tf_op jit(solution)/shard_map/pallas_call | solution.py:45
  14.1 0.7 %shard_map.88 = (f32[768,256]{1,0:T(8,128)S(1)}, f32[64,32]{1,0:T(8,128)S(1)}) custom-call(bf16[72,1024]{1,0:T(8,128)(2,1)S(1)} %shard_map.85.ref), custom_call_target="tpu_custom_call" | custom-call | tf_op jit(solution)/shard_map/pallas_call | solution.py:45
  14.8 0.1 collective-permute-start.3
  14.8 0.0 collective-permute-done.2.ref
  14.9 0.7 %shard_map.89 = (f32[768,256]{1,0:T(8,128)S(1)}, f32[64,32]{1,0:T(8,128)S(1)}) custom-call(f32[768,256]{1,0:T(8,128)S(1)} %get-tuple-element.75.old_grid_ref, f32[64,32]{1,0:T(8,128)S(1)} %get-tuple-element.76.old_counts_ref, bf16[72,1024]{1,0:T(8,128)(2,1)S(1)} %collective-permute-done.2.ref), custom_call_target="tpu_custom_call" | custom-call | tf_op jit(solution)/shard_map/pallas_call | solution.py:45
  15.5 0.6 %collective-permute-start.4 = (bf16[72,1024]{1,0:T(8,128)(2,1)S(1)}, bf16[72,1024]{1,0:T(8,128)(2,1)S(1)}, u32[]{:S(2)}, u32[]{:S(2)}) collective-permute-start(bf16[72,1024]{1,0:T(8,128)(2,1)S(1)} %collective-permute-done.2.ref), channel_id=1, source_target_pairs={{0,1},{1,0},{2,3},{3,2},{4,5},{5,4},{6,7},{7,6},{8,9},{9,8},{10,11... | collective-permute-start | bytes 442376 | tf_op jit(solution)/shard_map/ppermute | solution.py:57
  16.1 0.1 collective-permute-start.5
  16.2 0.8 %collective-permute-done.1.across_ref = bf16[72,1024]{1,0:T(8,128)(2,1)S(1)} collective-permute-done((bf16[72,1024]{1,0:T(8,128)(2,1)S(1)}, bf16[72,1024]{1,0:T(8,128)(2,1)S(1)}, u32[]{:S(2)}, u32[]{:S(2)}) %collective-permute-start.1) | collective-permute-done | bytes 147488 | tf_op jit(solution)/shard_map/ppermute | solution.py:62
  17.0 0.0 collective-permute-start.6
  17.0 3.4 %collective-permute-start.7 = (bf16[128,256]{1,0:T(8,128)(2,1)S(1)}, bf16[128,256]{1,0:T(8,128)(2,1)S(1)}, u32[]{:S(2)}, u32[]{:S(2)}) collective-permute-start(bf16[128,256]{1,0:T(8,128)(2,1)S(1)} %get-tuple-element.107.own_ref), channel_id=1, source_target_pairs={{0,6},{1,7},{2,4},{3,5},{4,2},{5,3},{6,0},{7,1},{8,14},{9,15},{10,... | collective-permute-start | bytes 196616 | tf_op jit(solution)/shard_map/ppermute | solution.py:62
  20.4 0.0 collective-permute-done.4.beside_ref
  20.4 0.0 collective-permute-done.3.coded_ref
  20.4 0.0 collective-permute-done.5.beyond_ref
  20.4 2.0 %shard_map.90 = (f32[768,256]{1,0:T(8,128)S(1)}, f32[64,32]{1,0:T(8,128)S(1)}, f32[768,256]{1,0:T(8,128)S(1)}, f32[64,32]{1,0:T(8,128)S(1)}, f32[768,256]{1,0:T(8,128)S(1)}, /*index=5*/f32[64,32]{1,0:T(8,128)S(1)}) custom-call(f32[768,256]{1,0:T(8,128)S(1)} %get-tuple-element.85.old_grid_ref, f32[64,32]{1,0:T(8,128)S(1)} %get-tuple-element.86.old_counts_ref, ...), custom_call_target="tpu_custom_call" | custom-call | tf_op jit(solution)/shard_map/pallas_call | solution.py:45
  22.4 0.0 collective-permute-done.6.ref
  22.5 0.7 %shard_map.91 = (f32[768,256]{1,0:T(8,128)S(1)}, f32[64,32]{1,0:T(8,128)S(1)}) custom-call(f32[768,256]{1,0:T(8,128)S(1)} %get-tuple-element.96.old_grid_ref, f32[64,32]{1,0:T(8,128)S(1)} %get-tuple-element.97.old_counts_ref, bf16[72,1024]{1,0:T(8,128)(2,1)S(1)} %collective-permute-done.6.ref), custom_call_target="tpu_custom_call" | custom-call | tf_op jit(solution)/shard_map/pallas_call | solution.py:45
  23.1 1.9 %shard_map.92 = (bf16[4,256,256]{2,1,0:T(8,128)(2,1)S(1)}, f32[4,256,256]{2,1,0:T(8,128)S(1)}, bf16[2,6,10,16,256]{4,3,2,1,0:T(8,128)(2,1)S(1)}) custom-call(f32[768,256]{1,0:T(8,128)S(1)} %get-tuple-element.83.grid0, f32[64,32]{1,0:T(8,128)S(1)} %get-tuple-element.84.counts0, f32[768,256]{1,0:T(8,128)S(1)} %get-tuple-element.90.grid1, ...), custom_call_target="tpu_custom_call" | custom-call | tf_op jit(solution)/shard_map/pallas_call | solution.py:45
  25.0 0.0 collective-permute-done.7.got_ref
  25.0 0.5 %shard_map.93 = (bf16[2,4,10,16,256]{4,3,2,1,0:T(8,128)(2,1)S(1)}, f32[4,256,128]{2,1,0:T(8,128)S(1)}, bf16[4,256,128]{2,1,0:T(8,128)(2,1)S(1)}) custom-call(bf16[4,256,256]{2,1,0:T(8,128)(2,1)S(1)} %get-tuple-element.105.act_ref, f32[4,256,256]{2,1,0:T(8,128)S(1)} %get-tuple-element.106.slope_ref, bf16[128,256]{1,0:T(8,128)(2,1)S(1)} %get-tuple-element.107.own_ref, ...), custom_call_target="tpu_custom_call" | custom-call | tf_op jit(solution)/shard_map/pallas_call | solution.py:45
  25.5 0.3 collective-permute-start.8
  25.8 1.4 %shard_map.94 = (f32[4,224,128]{2,1,0:T(8,128)S(1)}, bf16[4,224,128]{2,1,0:T(8,128)(2,1)S(1)}) custom-call(bf16[2,6,10,16,256]{4,3,2,1,0:T(8,128)(2,1)S(1)} %get-tuple-element.111.es_ref, bf16[2,4,10,16,256]{4,3,2,1,0:T(8,128)(2,1)S(1)} %get-tuple-element.112.pg_ref), custom_call_target="tpu_custom_call" | custom-call | tf_op jit(solution)/shard_map/pallas_call | solution.py:45
  27.2 0.0 collective-permute-done.8.got_ref
  27.3 0.3 collective-permute-start.9
  27.6 1.2 %collective-permute-done.9.got_conv_ref = bf16[4,224,128]{2,1,0:T(8,128)(2,1)S(1)} collective-permute-done((bf16[4,224,128]{2,1,0:T(8,128)(2,1)S(1)}, bf16[4,224,128]{2,1,0:T(8,128)(2,1)S(1)}, u32[]{:S(2)}, u32[]{:S(2)}) %collective-permute-start.9) | collective-permute-done | bytes 229408 | tf_op jit(solution)/shard_map/ppermute | solution.py:57
  28.8 0.1 shard_map.95
  28.9 1.6 %collective-permute-start.10 = (bf16[480,128]{1,0:T(8,128)(2,1)S(1)}, bf16[480,128]{1,0:T(8,128)(2,1)S(1)}, u32[]{:S(2)}, u32[]{:S(2)}) collective-permute-start(bf16[480,128]{1,0:T(8,128)(2,1)S(1)} %get-tuple-element.119), channel_id=1, source_target_pairs={{0,8},{8,0},{16,24},{24,16},{1,9},{9,1},{17,25},{25,17},{2,10},{10... | collective-permute-start | bytes 368648 | tf_op jit(solution)/shard_map/ppermute | solution.py:66
  30.5 1.5 %collective-permute-start.11 = (bf16[480,128]{1,0:T(8,128)(2,1)S(1)}, bf16[480,128]{1,0:T(8,128)(2,1)S(1)}, u32[]{:S(2)}, u32[]{:S(2)}) collective-permute-start(bf16[480,128]{1,0:T(8,128)(2,1)S(1)} %get-tuple-element.120), channel_id=1, source_target_pairs={{0,16},{8,24},{16,0},{24,8},{1,17},{9,25},{17,1},{25,9},{2,18},{10... | collective-permute-start | bytes 368648 | tf_op jit(solution)/shard_map/ppermute | solution.py:66
  32.0 0.5 %collective-permute-start.12 = (bf16[480,128]{1,0:T(8,128)(2,1)S(1)}, bf16[480,128]{1,0:T(8,128)(2,1)S(1)}, u32[]{:S(2)}, u32[]{:S(2)}) collective-permute-start(bf16[480,128]{1,0:T(8,128)(2,1)S(1)} %get-tuple-element.121), channel_id=1, source_target_pairs={{0,24},{8,16},{16,8},{24,0},{1,25},{9,17},{17,9},{25,1},{2,26},{10... | collective-permute-start | bytes 368648 | tf_op jit(solution)/shard_map/ppermute | solution.py:66
  32.5 0.4 shard_map.96
  32.9 0.7 %reshape.13 = bf16[1,2,16,4,256]{4,3,2,1,0:T(4,128)(2,1)} reshape(bf16[128,256]{1,0:T(8,128)(2,1)S(1)} %shard_map.96) | data formatting | bytes 131072 | tf_op jit(solution)/shard_map/reshape | solution.py:496
  33.5 1.1 %collective-permute-done.10.refs_1_ = bf16[480,128]{1,0:T(8,128)(2,1)S(1)} collective-permute-done((bf16[480,128]{1,0:T(8,128)(2,1)S(1)}, bf16[480,128]{1,0:T(8,128)(2,1)S(1)}, u32[]{:S(2)}, u32[]{:S(2)}) %collective-permute-start.10) | collective-permute-done | bytes 122912 | tf_op jit(solution)/shard_map/ppermute | solution.py:66
  34.6 3.7 %collective-permute-done.11.refs_2_ = bf16[480,128]{1,0:T(8,128)(2,1)S(1)} collective-permute-done((bf16[480,128]{1,0:T(8,128)(2,1)S(1)}, bf16[480,128]{1,0:T(8,128)(2,1)S(1)}, u32[]{:S(2)}, u32[]{:S(2)}) %collective-permute-start.11) | collective-permute-done | bytes 122912 | tf_op jit(solution)/shard_map/ppermute | solution.py:66
  38.3 0.0 collective-permute-done.12.refs_3_
  38.3 0.1 shard_map.97.refs_0_
  38.4 0.1 collective-permute-start.13
  38.5 4.9 %collective-permute-done.13.refs_1_ = bf16[480,128]{1,0:T(8,128)(2,1)S(1)} collective-permute-done((bf16[480,128]{1,0:T(8,128)(2,1)S(1)}, bf16[480,128]{1,0:T(8,128)(2,1)S(1)}, u32[]{:S(2)}, u32[]{:S(2)}) %collective-permute-start.13) | collective-permute-done | bytes 122912 | tf_op jit(solution)/shard_map/ppermute | solution.py:62
  43.4 0.1 collective-permute-start.14
  43.5 1.5 %collective-permute-done.14.got_ref = f32[480,128]{1,0:T(8,128)S(1)} collective-permute-done((f32[480,128]{1,0:T(8,128)S(1)}, f32[480,128]{1,0:T(8,128)S(1)}, u32[]{:S(2)}, u32[]{:S(2)}) %collective-permute-start.14) | collective-permute-done | bytes 245792 | tf_op jit(solution)/shard_map/ppermute | solution.py:57
  44.9 0.8 %shard_map.99 = (f32[432,128]{1,0:T(8,128)}, f32[256,256]{1,0:T(8,128)}) custom-call(f32[480,128]{1,0:T(8,128)S(1)} %shard_map.98.own_ref, f32[480,128]{1,0:T(8,128)S(1)} %collective-permute-done.14.got_ref), custom_call_target="tpu_custom_call" | custom-call | tf_op jit(solution)/shard_map/pallas_call | solution.py:45
  (1 shorter events, 0.0 us)
Async XLA Ops:
  1.6 9.8 %collective-permute-start = (bf16[72,1024]{1,0:T(8,128)(2,1)S(1)}, bf16[72,1024]{1,0:T(8,128)(2,1)S(1)}, u32[]{:S(2)}, u32[]{:S(2)}) collective-permute-start(bf16[72,1024]{1,0:T(8,128)(2,1)S(1)} %shard_map.85.ref), channel_id=1, source_target_pairs={{0,6},{1,7},{2,4},{3,5},{4,2},{5,3},{6,0},{7,1},{8,14},{9,15},{10,... | collective-permute-start | bytes 442376 | tf_op jit(solution)/shard_map/ppermute | solution.py:62
  6.7 8.1 %collective-permute-start.2 = (bf16[72,1024]{1,0:T(8,128)(2,1)S(1)}, bf16[72,1024]{1,0:T(8,128)(2,1)S(1)}, u32[]{:S(2)}, u32[]{:S(2)}) collective-permute-start(bf16[72,1024]{1,0:T(8,128)(2,1)S(1)} %shard_map.85.ref), channel_id=1, source_target_pairs={{0,2},{1,3},{2,0},{3,1},{4,6},{5,7},{6,4},{7,5},{8,10},{9,11},{10,... | collective-permute-start | bytes 442376 | tf_op jit(solution)/shard_map/ppermute | solution.py:62
  11.4 5.5 %collective-permute-start.1 = (bf16[72,1024]{1,0:T(8,128)(2,1)S(1)}, bf16[72,1024]{1,0:T(8,128)(2,1)S(1)}, u32[]{:S(2)}, u32[]{:S(2)}) collective-permute-start(bf16[72,1024]{1,0:T(8,128)(2,1)S(1)} %collective-permute-done.ref), channel_id=1, source_target_pairs={{0,2},{1,3},{2,0},{3,1},{4,6},{5,7},{6,4},{7,5},{8,10},{9,11},{10,... | collective-permute-start | bytes 442376 | tf_op jit(solution)/shard_map/ppermute | solution.py:62
  14.8 5.6 %collective-permute-start.3 = (bf16[72,1024]{1,0:T(8,128)(2,1)S(1)}, bf16[72,1024]{1,0:T(8,128)(2,1)S(1)}, u32[]{:S(2)}, u32[]{:S(2)}) collective-permute-start(bf16[72,1024]{1,0:T(8,128)(2,1)S(1)} %shard_map.85.ref), channel_id=1, source_target_pairs={{0,1},{1,0},{2,3},{3,2},{4,5},{5,4},{6,7},{7,6},{8,9},{9,8},{10,11... | collective-permute-start | bytes 442376 | tf_op jit(solution)/shard_map/ppermute | solution.py:57
  15.5 4.9 %collective-permute-start.4 = (bf16[72,1024]{1,0:T(8,128)(2,1)S(1)}, bf16[72,1024]{1,0:T(8,128)(2,1)S(1)}, u32[]{:S(2)}, u32[]{:S(2)}) collective-permute-start(bf16[72,1024]{1,0:T(8,128)(2,1)S(1)} %collective-permute-done.2.ref), channel_id=1, source_target_pairs={{0,1},{1,0},{2,3},{3,2},{4,5},{5,4},{6,7},{7,6},{8,9},{9,8},{10,11... | collective-permute-start | bytes 442376 | tf_op jit(solution)/shard_map/ppermute | solution.py:57
  16.1 4.3 %collective-permute-start.5 = (bf16[72,1024]{1,0:T(8,128)(2,1)S(1)}, bf16[72,1024]{1,0:T(8,128)(2,1)S(1)}, u32[]{:S(2)}, u32[]{:S(2)}) collective-permute-start(bf16[72,1024]{1,0:T(8,128)(2,1)S(1)} %collective-permute-done.ref), channel_id=1, source_target_pairs={{0,1},{1,0},{2,3},{3,2},{4,5},{5,4},{6,7},{7,6},{8,9},{9,8},{10,11... | collective-permute-start | bytes 442376 | tf_op jit(solution)/shard_map/ppermute | solution.py:57
  17.0 5.5 %collective-permute-start.6 = (bf16[72,1024]{1,0:T(8,128)(2,1)S(1)}, bf16[72,1024]{1,0:T(8,128)(2,1)S(1)}, u32[]{:S(2)}, u32[]{:S(2)}) collective-permute-start(bf16[72,1024]{1,0:T(8,128)(2,1)S(1)} %collective-permute-done.1.across_ref), channel_id=1, source_target_pairs={{0,1},{1,0},{2,3},{3,2},{4,5},{5,4},{6,7},{7,6},{8,9},{9,8},{10,11... | collective-permute-start | bytes 442376 | tf_op jit(solution)/shard_map/ppermute | solution.py:57
  17.0 8.0 %collective-permute-start.7 = (bf16[128,256]{1,0:T(8,128)(2,1)S(1)}, bf16[128,256]{1,0:T(8,128)(2,1)S(1)}, u32[]{:S(2)}, u32[]{:S(2)}) collective-permute-start(bf16[128,256]{1,0:T(8,128)(2,1)S(1)} %get-tuple-element.107.own_ref), channel_id=1, source_target_pairs={{0,6},{1,7},{2,4},{3,5},{4,2},{5,3},{6,0},{7,1},{8,14},{9,15},{10,... | collective-permute-start | bytes 196616 | tf_op jit(solution)/shard_map/ppermute | solution.py:62
  25.5 1.7 %collective-permute-start.8 = (bf16[4,256,128]{2,1,0:T(8,128)(2,1)S(1)}, bf16[4,256,128]{2,1,0:T(8,128)(2,1)S(1)}, u32[]{:S(2)}, u32[]{:S(2)}) collective-permute-start(bf16[4,256,128]{2,1,0:T(8,128)(2,1)S(1)} %get-tuple-element.110), channel_id=1, source_target_pairs={{0,1},{1,0},{2,3},{3,2},{4,5},{5,4},{6,7},{7,6},{8,9},{9,8},{10,11... | collective-permute-start | bytes 786440 | tf_op jit(solution)/shard_map/ppermute | solution.py:57
  27.3 1.6 %collective-permute-start.9 = (bf16[4,224,128]{2,1,0:T(8,128)(2,1)S(1)}, bf16[4,224,128]{2,1,0:T(8,128)(2,1)S(1)}, u32[]{:S(2)}, u32[]{:S(2)}) collective-permute-start(bf16[4,224,128]{2,1,0:T(8,128)(2,1)S(1)} %get-tuple-element.117), channel_id=1, source_target_pairs={{0,1},{1,0},{2,3},{3,2},{4,5},{5,4},{6,7},{7,6},{8,9},{9,8},{10,11... | collective-permute-start | bytes 688136 | tf_op jit(solution)/shard_map/ppermute | solution.py:57
  28.9 5.7 %collective-permute-start.10 = (bf16[480,128]{1,0:T(8,128)(2,1)S(1)}, bf16[480,128]{1,0:T(8,128)(2,1)S(1)}, u32[]{:S(2)}, u32[]{:S(2)}) collective-permute-start(bf16[480,128]{1,0:T(8,128)(2,1)S(1)} %get-tuple-element.119), channel_id=1, source_target_pairs={{0,8},{8,0},{16,24},{24,16},{1,9},{9,1},{17,25},{25,17},{2,10},{10... | collective-permute-start | bytes 368648 | tf_op jit(solution)/shard_map/ppermute | solution.py:66
  30.5 7.9 %collective-permute-start.11 = (bf16[480,128]{1,0:T(8,128)(2,1)S(1)}, bf16[480,128]{1,0:T(8,128)(2,1)S(1)}, u32[]{:S(2)}, u32[]{:S(2)}) collective-permute-start(bf16[480,128]{1,0:T(8,128)(2,1)S(1)} %get-tuple-element.120), channel_id=1, source_target_pairs={{0,16},{8,24},{16,0},{24,8},{1,17},{9,25},{17,1},{25,9},{2,18},{10... | collective-permute-start | bytes 368648 | tf_op jit(solution)/shard_map/ppermute | solution.py:66
  32.0 6.3 %collective-permute-start.12 = (bf16[480,128]{1,0:T(8,128)(2,1)S(1)}, bf16[480,128]{1,0:T(8,128)(2,1)S(1)}, u32[]{:S(2)}, u32[]{:S(2)}) collective-permute-start(bf16[480,128]{1,0:T(8,128)(2,1)S(1)} %get-tuple-element.121), channel_id=1, source_target_pairs={{0,24},{8,16},{16,8},{24,0},{1,25},{9,17},{17,9},{25,1},{2,26},{10... | collective-permute-start | bytes 368648 | tf_op jit(solution)/shard_map/ppermute | solution.py:66
  38.4 4.9 %collective-permute-start.13 = (bf16[480,128]{1,0:T(8,128)(2,1)S(1)}, bf16[480,128]{1,0:T(8,128)(2,1)S(1)}, u32[]{:S(2)}, u32[]{:S(2)}) collective-permute-start(bf16[480,128]{1,0:T(8,128)(2,1)S(1)} %shard_map.97.refs_0_), channel_id=1, source_target_pairs={{0,2},{1,3},{2,0},{3,1},{4,6},{5,7},{6,4},{7,5},{8,10},{9,11},{10,... | collective-permute-start | bytes 368648 | tf_op jit(solution)/shard_map/ppermute | solution.py:62
  43.4 1.6 %collective-permute-start.14 = (f32[480,128]{1,0:T(8,128)S(1)}, f32[480,128]{1,0:T(8,128)S(1)}, u32[]{:S(2)}, u32[]{:S(2)}) collective-permute-start(f32[480,128]{1,0:T(8,128)S(1)} %shard_map.98.own_ref), channel_id=1, source_target_pairs={{0,1},{1,0},{2,3},{3,2},{4,5},{5,4},{6,7},{7,6},{8,9},{9,8},{10,11... | collective-permute-start | bytes 737288 | tf_op jit(solution)/shard_map/ppermute | solution.py:57

commit v10 on v9

--- a/solution.py
+++ b/solution.py
@@ -27,14 +27,15 @@
 VMEM_LIMIT = 24 * 1024 * 1024
 
 
-def call(body, outs, scratch=(), pinned=0, loose=0, raw=0):
+def call(body, outs, scratch=(), pinned=0, loose=0, raw=0, out_space=pltpu.VMEM):
     single = not isinstance(outs, (list, tuple))
     vmem = pl.BlockSpec(memory_space=pltpu.VMEM)
+    result = pl.BlockSpec(memory_space=out_space)
     kernel = pl.pallas_call(
         body,
         out_shape=outs,
         in_specs=[vmem] * (pinned + loose) + [pl.BlockSpec(memory_space=pltpu.HBM)] * raw,
-        out_specs=vmem if single else [vmem] * len(outs),
+        out_specs=result if single else [result] * len(outs),
         scratch_shapes=list(scratch),
         compiler_params=pltpu.CompilerParams(vmem_limit_bytes=VMEM_LIMIT),
     )
@@ -366,17 +367,34 @@
     out_ref[...] = total
 
 
-def finish_kernel(down_rows, own_ref, got_ref, conv_ref, down_ref):
-    low = (lax.axis_index("tile") & 1) == 0
-    own = own_ref[...]
-    got = got_ref[...]
-    first = jnp.where(low, own, got)
-    second = jnp.where(low, got, own)
-    half_rows = first.shape[0] - down_rows
-    down_ref[:, 0:128] = first[:down_rows]
-    down_ref[:, 128:256] = second[:down_rows]
-    conv_ref[0:half_rows, :] = first[down_rows:]
-    conv_ref[half_rows:, :] = second[down_rows : down_rows + conv_ref.shape[0] - half_rows]
+def finish_kernel(down_rows, own_ref, got_ref, conv_hbm, down_hbm, sems):
+    half_rows = own_ref.shape[0] - down_rows
+    rest = conv_hbm.shape[0] - half_rows
+    core = lax.axis_index("tile") & 1
+
+    def leave(first, second):
+        copies = [
+            pltpu.make_async_copy(first.at[:down_rows], down_hbm.at[:, 0:128], sems.at[0]),
+            pltpu.make_async_copy(second.at[:down_rows], down_hbm.at[:, 128:256], sems.at[1]),
+            pltpu.make_async_copy(
+                first.at[down_rows : down_rows + half_rows], conv_hbm.at[0:half_rows], sems.at[2]
+            ),
+            pltpu.make_async_copy(
+                second.at[down_rows : down_rows + rest], conv_hbm.at[half_rows : half_rows + rest], sems.at[3]
+            ),
+        ]
+        for copy in copies:
+            copy.start()
+        for copy in copies:
+            copy.wait()
+
+    @pl.when(core == 0)
+    def _():
+        leave(own_ref, got_ref)
+
+    @pl.when(core == 1)
+    def _():
+        leave(got_ref, own_ref)
 
 
 def local(points, slot, voxel, conv_weight, down_weight, cotangent):
@@ -509,7 +527,9 @@
     conv_grad, down_grad = call(
         functools.partial(finish_kernel, down_rows),
         (hbm((conv_rows, C1), F32), hbm((down_rows, C2), F32)),
+        scratch=(pltpu.SemaphoreType.DMA((4,)),),
         pinned=2,
+        out_space=pltpu.HBM,
     )(total, swap_core(total, tiles))
     return (down, conv_grad, down_grad)
 

time: 46 us -> 46 us (level)
  no operation moved by 1% of the time
where the time goes in v10:
time: 46 us; the launch traced here: 45.8 us
  starting transfers between devices  15.6 us (34%)
  waiting for transfers between devices  14.8 us (32%)
  Pallas kernels  12.4 us (27%)
  local copies, waits for them, and re-layouts  2.14 us (5%)
  between operations  0.79 us (2%)
    pallas_call x15, Pallas kernels, run(): return kernel(*held, *far)  12.4 us
    ppermute x5, starting transfers between devices, send_column(): return lax.ppermute(value, 'tile', pairs)  10.6 us
    ppermute x5, waiting for transfers between devices, send_column(): return lax.ppermute(value, 'tile', pairs)  7.28 us
    ppermute x3, waiting for transfers between devices, send_sample(): lax.ppermute(value, 'sample', [(i, target(i, k, samples)) for i in range(...  4.81 us
    ppermute x3, starting transfers between devices, send_sample(): lax.ppermute(value, 'sample', [(i, target(i, k, samples)) for i in range(...  3.55 us
    ppermute x7, waiting for transfers between devices, swap_core(): return lax.ppermute(value, 'tile', [(i, i ^ 1) for i in range(tiles)])  2.72 us
    reshape x1, local copies, waits for them, and re-layouts, local(): cotangent.reshape(128, C2)  1.49 us
    ppermute x7, starting transfers between devices, swap_core(): return lax.ppermute(value, 'tile', [(i, i ^ 1) for i in range(tiles)])  1.41 us
  transfers between devices with their start and end apart: 15, of which 7 were waited for; matrix products, arithmetic and copies ran while one was open for 5% of the time, Pallas kernels for 22%

profile of v10, /device:TPU:0, one launch (start us, length us, event | category | flops | bytes accessed | tf_op | source)
XLA Modules:
  0.0 45.8 jit_solution(6008891715136882976)
XLA Ops:
  0.6 1.0 %shard_map.85.ref = bf16[72,1024]{1,0:T(8,128)(2,1)S(1)} custom-call(bf16[64,1024]{1,0:T(8,128)(2,1)} %bitcast.3, s32[1,1024]{1,0:T(1,128)} %slot_hbm.1, s32[1,1024]{1,0:T(1,128)} %voxel_hbm.1), custom_call_target="tpu_custom_call" | custom-call | tf_op jit(solution)/shard_map/pallas_call | solution.py:46
  1.6 5.1 %collective-permute-start = (bf16[72,1024]{1,0:T(8,128)(2,1)S(1)}, bf16[72,1024]{1,0:T(8,128)(2,1)S(1)}, u32[]{:S(2)}, u32[]{:S(2)}) collective-permute-start(bf16[72,1024]{1,0:T(8,128)(2,1)S(1)} %shard_map.85.ref), channel_id=1, source_target_pairs={{0,6},{1,7},{2,4},{3,5},{4,2},{5,3},{6,0},{7,1},{8,14},{9,15},{10,... | collective-permute-start | bytes 442376 | tf_op jit(solution)/shard_map/ppermute | solution.py:63
  6.7 0.0 collective-permute-start.2
  6.7 1.5 %reshape.12.cot_ref = bf16[128,256]{1,0:T(8,128)(2,1)} reshape(bf16[1,2,16,4,256]{4,3,2,1,0:T(4,128)(2,1)} %param.11) | data formatting | bytes 131072 | tf_op jit(solution)/shard_map/reshape | solution.py:443
  8.2 1.6 %shard_map.86 = (bf16[9,256,256]{2,1,0:T(8,128)(2,1)S(1)}, bf16[4,256,256]{2,1,0:T(8,128)(2,1)S(1)}, bf16[128,256]{1,0:T(8,128)(2,1)S(1)}, bf16[1024,64]{1,0:T(8...) custom-call(bf16[1728,128]{1,0:T(8,128)(2,1)} %conv_ref.1, bf16[1024,256]{1,0:T(8,128)(2,1)} %down_ref.1, ...), custom_call_target="tpu_custom_call" | custom-call | tf_op jit(solution)/shard_map/pallas_call | solution.py:46
  9.9 1.6 %collective-permute-done.ref = bf16[72,1024]{1,0:T(8,128)(2,1)S(1)} collective-permute-done((bf16[72,1024]{1,0:T(8,128)(2,1)S(1)}, bf16[72,1024]{1,0:T(8,128)(2,1)S(1)}, u32[]{:S(2)}, u32[]{:S(2)}) %collective-permute-start) | collective-permute-done | bytes 147488 | tf_op jit(solution)/shard_map/ppermute | solution.py:63
  11.4 2.0 %collective-permute-start.1 = (bf16[72,1024]{1,0:T(8,128)(2,1)S(1)}, bf16[72,1024]{1,0:T(8,128)(2,1)S(1)}, u32[]{:S(2)}, u32[]{:S(2)}) collective-permute-start(bf16[72,1024]{1,0:T(8,128)(2,1)S(1)} %collective-permute-done.ref), channel_id=1, source_target_pairs={{0,2},{1,3},{2,0},{3,1},{4,6},{5,7},{6,4},{7,5},{8,10},{9,11},{10,... | collective-permute-start | bytes 442376 | tf_op jit(solution)/shard_map/ppermute | solution.py:63
  13.4 0.7 %shard_map.87 = (f32[768,256]{1,0:T(8,128)S(1)}, f32[64,32]{1,0:T(8,128)S(1)}) custom-call(bf16[72,1024]{1,0:T(8,128)(2,1)S(1)} %collective-permute-done.ref), custom_call_target="tpu_custom_call" | custom-call | tf_op jit(solution)/shard_map/pallas_call | solution.py:46
  14.1 0.7 %shard_map.88 = (f32[768,256]{1,0:T(8,128)S(1)}, f32[64,32]{1,0:T(8,128)S(1)}) custom-call(bf16[72,1024]{1,0:T(8,128)(2,1)S(1)} %shard_map.85.ref), custom_call_target="tpu_custom_call" | custom-call | tf_op jit(solution)/shard_map/pallas_call | solution.py:46
  14.8 0.1 collective-permute-start.3
  14.8 0.0 collective-permute-done.2.ref
  14.9 0.7 %shard_map.89 = (f32[768,256]{1,0:T(8,128)S(1)}, f32[64,32]{1,0:T(8,128)S(1)}) custom-call(f32[768,256]{1,0:T(8,128)S(1)} %get-tuple-element.75.old_grid_ref, f32[64,32]{1,0:T(8,128)S(1)} %get-tuple-element.76.old_counts_ref, bf16[72,1024]{1,0:T(8,128)(2,1)S(1)} %collective-permute-done.2.ref), custom_call_target="tpu_custom_call" | custom-call | tf_op jit(solution)/shard_map/pallas_call | solution.py:46
  15.5 0.6 %collective-permute-start.4 = (bf16[72,1024]{1,0:T(8,128)(2,1)S(1)}, bf16[72,1024]{1,0:T(8,128)(2,1)S(1)}, u32[]{:S(2)}, u32[]{:S(2)}) collective-permute-start(bf16[72,1024]{1,0:T(8,128)(2,1)S(1)} %collective-permute-done.2.ref), channel_id=1, source_target_pairs={{0,1},{1,0},{2,3},{3,2},{4,5},{5,4},{6,7},{7,6},{8,9},{9,8},{10,11... | collective-permute-start | bytes 442376 | tf_op jit(solution)/shard_map/ppermute | solution.py:58
  16.1 0.1 collective-permute-start.5
  16.2 0.8 %collective-permute-done.1.across_ref = bf16[72,1024]{1,0:T(8,128)(2,1)S(1)} collective-permute-done((bf16[72,1024]{1,0:T(8,128)(2,1)S(1)}, bf16[72,1024]{1,0:T(8,128)(2,1)S(1)}, u32[]{:S(2)}, u32[]{:S(2)}) %collective-permute-start.1) | collective-permute-done | bytes 147488 | tf_op jit(solution)/shard_map/ppermute | solution.py:63
  17.0 0.0 collective-permute-start.6
  17.0 3.4 %collective-permute-start.7 = (bf16[128,256]{1,0:T(8,128)(2,1)S(1)}, bf16[128,256]{1,0:T(8,128)(2,1)S(1)}, u32[]{:S(2)}, u32[]{:S(2)}) collective-permute-start(bf16[128,256]{1,0:T(8,128)(2,1)S(1)} %get-tuple-element.107.own_ref), channel_id=1, source_target_pairs={{0,6},{1,7},{2,4},{3,5},{4,2},{5,3},{6,0},{7,1},{8,14},{9,15},{10,... | collective-permute-start | bytes 196616 | tf_op jit(solution)/shard_map/ppermute | solution.py:63
  20.4 0.0 collective-permute-done.4.beside_ref
  20.4 0.0 collective-permute-done.3.coded_ref
  20.4 0.0 collective-permute-done.5.beyond_ref
  20.4 2.0 %shard_map.90 = (f32[768,256]{1,0:T(8,128)S(1)}, f32[64,32]{1,0:T(8,128)S(1)}, f32[768,256]{1,0:T(8,128)S(1)}, f32[64,32]{1,0:T(8,128)S(1)}, f32[768,256]{1,0:T(8,128)S(1)}, /*index=5*/f32[64,32]{1,0:T(8,128)S(1)}) custom-call(f32[768,256]{1,0:T(8,128)S(1)} %get-tuple-element.85.old_grid_ref, f32[64,32]{1,0:T(8,128)S(1)} %get-tuple-element.86.old_counts_ref, ...), custom_call_target="tpu_custom_call" | custom-call | tf_op jit(solution)/shard_map/pallas_call | solution.py:46
  22.4 0.0 collective-permute-done.6.ref
  22.5 0.7 %shard_map.91 = (f32[768,256]{1,0:T(8,128)S(1)}, f32[64,32]{1,0:T(8,128)S(1)}) custom-call(f32[768,256]{1,0:T(8,128)S(1)} %get-tuple-element.96.old_grid_ref, f32[64,32]{1,0:T(8,128)S(1)} %get-tuple-element.97.old_counts_ref, bf16[72,1024]{1,0:T(8,128)(2,1)S(1)} %collective-permute-done.6.ref), custom_call_target="tpu_custom_call" | custom-call | tf_op jit(solution)/shard_map/pallas_call | solution.py:46
  23.1 1.9 %shard_map.92 = (bf16[4,256,256]{2,1,0:T(8,128)(2,1)S(1)}, f32[4,256,256]{2,1,0:T(8,128)S(1)}, bf16[2,6,10,16,256]{4,3,2,1,0:T(8,128)(2,1)S(1)}) custom-call(f32[768,256]{1,0:T(8,128)S(1)} %get-tuple-element.83.grid0, f32[64,32]{1,0:T(8,128)S(1)} %get-tuple-element.84.counts0, f32[768,256]{1,0:T(8,128)S(1)} %get-tuple-element.90.grid1, ...), custom_call_target="tpu_custom_call" | custom-call | tf_op jit(solution)/shard_map/pallas_call | solution.py:46
  25.0 0.0 collective-permute-done.7.got_ref
  25.0 0.5 %shard_map.93 = (bf16[2,4,10,16,256]{4,3,2,1,0:T(8,128)(2,1)S(1)}, f32[4,256,128]{2,1,0:T(8,128)S(1)}, bf16[4,256,128]{2,1,0:T(8,128)(2,1)S(1)}) custom-call(bf16[4,256,256]{2,1,0:T(8,128)(2,1)S(1)} %get-tuple-element.105.act_ref, f32[4,256,256]{2,1,0:T(8,128)S(1)} %get-tuple-element.106.slope_ref, bf16[128,256]{1,0:T(8,128)(2,1)S(1)} %get-tuple-element.107.own_ref, ...), custom_call_target="tpu_custom_call" | custom-call | tf_op jit(solution)/shard_map/pallas_call | solution.py:46
  25.5 0.3 collective-permute-start.8
  25.8 1.4 %shard_map.94 = (f32[4,224,128]{2,1,0:T(8,128)S(1)}, bf16[4,224,128]{2,1,0:T(8,128)(2,1)S(1)}) custom-call(bf16[2,6,10,16,256]{4,3,2,1,0:T(8,128)(2,1)S(1)} %get-tuple-element.111.es_ref, bf16[2,4,10,16,256]{4,3,2,1,0:T(8,128)(2,1)S(1)} %get-tuple-element.112.pg_ref), custom_call_target="tpu_custom_call" | custom-call | tf_op jit(solution)/shard_map/pallas_call | solution.py:46
  27.2 0.0 collective-permute-done.8.got_ref
  27.3 0.3 collective-permute-start.9
  27.6 1.2 %collective-permute-done.9.got_conv_ref = bf16[4,224,128]{2,1,0:T(8,128)(2,1)S(1)} collective-permute-done((bf16[4,224,128]{2,1,0:T(8,128)(2,1)S(1)}, bf16[4,224,128]{2,1,0:T(8,128)(2,1)S(1)}, u32[]{:S(2)}, u32[]{:S(2)}) %collective-permute-start.9) | collective-permute-done | bytes 229408 | tf_op jit(solution)/shard_map/ppermute | solution.py:58
  28.8 0.1 shard_map.95
  28.9 1.6 %collective-permute-start.10 = (bf16[480,128]{1,0:T(8,128)(2,1)S(1)}, bf16[480,128]{1,0:T(8,128)(2,1)S(1)}, u32[]{:S(2)}, u32[]{:S(2)}) collective-permute-start(bf16[480,128]{1,0:T(8,128)(2,1)S(1)} %get-tuple-element.119), channel_id=1, source_target_pairs={{0,8},{8,0},{16,24},{24,16},{1,9},{9,1},{17,25},{25,17},{2,10},{10... | collective-permute-start | bytes 368648 | tf_op jit(solution)/shard_map/ppermute | solution.py:67
  30.5 1.5 %collective-permute-start.11 = (bf16[480,128]{1,0:T(8,128)(2,1)S(1)}, bf16[480,128]{1,0:T(8,128)(2,1)S(1)}, u32[]{:S(2)}, u32[]{:S(2)}) collective-permute-start(bf16[480,128]{1,0:T(8,128)(2,1)S(1)} %get-tuple-element.120), channel_id=1, source_target_pairs={{0,16},{8,24},{16,0},{24,8},{1,17},{9,25},{17,1},{25,9},{2,18},{10... | collective-permute-start | bytes 368648 | tf_op jit(solution)/shard_map/ppermute | solution.py:67
  32.0 0.5 %collective-permute-start.12 = (bf16[480,128]{1,0:T(8,128)(2,1)S(1)}, bf16[480,128]{1,0:T(8,128)(2,1)S(1)}, u32[]{:S(2)}, u32[]{:S(2)}) collective-permute-start(bf16[480,128]{1,0:T(8,128)(2,1)S(1)} %get-tuple-element.121), channel_id=1, source_target_pairs={{0,24},{8,16},{16,8},{24,0},{1,25},{9,17},{17,9},{25,1},{2,26},{10... | collective-permute-start | bytes 368648 | tf_op jit(solution)/shard_map/ppermute | solution.py:67
  32.5 0.4 shard_map.96
  32.9 0.7 %reshape.13 = bf16[1,2,16,4,256]{4,3,2,1,0:T(4,128)(2,1)} reshape(bf16[128,256]{1,0:T(8,128)(2,1)S(1)} %shard_map.96) | data formatting | bytes 131072 | tf_op jit(solution)/shard_map/reshape | solution.py:514
  33.5 1.1 %collective-permute-done.10.refs_1_ = bf16[480,128]{1,0:T(8,128)(2,1)S(1)} collective-permute-done((bf16[480,128]{1,0:T(8,128)(2,1)S(1)}, bf16[480,128]{1,0:T(8,128)(2,1)S(1)}, u32[]{:S(2)}, u32[]{:S(2)}) %collective-permute-start.10) | collective-permute-done | bytes 122912 | tf_op jit(solution)/shard_map/ppermute | solution.py:67
  34.6 3.7 %collective-permute-done.11.refs_2_ = bf16[480,128]{1,0:T(8,128)(2,1)S(1)} collective-permute-done((bf16[480,128]{1,0:T(8,128)(2,1)S(1)}, bf16[480,128]{1,0:T(8,128)(2,1)S(1)}, u32[]{:S(2)}, u32[]{:S(2)}) %collective-permute-start.11) | collective-permute-done | bytes 122912 | tf_op jit(solution)/shard_map/ppermute | solution.py:67
  38.3 0.0 collective-permute-done.12.refs_3_
  38.3 0.1 shard_map.97.refs_0_
  38.4 0.1 collective-permute-start.13
  38.5 4.9 %collective-permute-done.13.refs_1_ = bf16[480,128]{1,0:T(8,128)(2,1)S(1)} collective-permute-done((bf16[480,128]{1,0:T(8,128)(2,1)S(1)}, bf16[480,128]{1,0:T(8,128)(2,1)S(1)}, u32[]{:S(2)}, u32[]{:S(2)}) %collective-permute-start.13) | collective-permute-done | bytes 122912 | tf_op jit(solution)/shard_map/ppermute | solution.py:63
  43.4 0.1 collective-permute-start.14
  43.5 1.5 %collective-permute-done.14.got_ref = f32[480,128]{1,0:T(8,128)S(1)} collective-permute-done((f32[480,128]{1,0:T(8,128)S(1)}, f32[480,128]{1,0:T(8,128)S(1)}, u32[]{:S(2)}, u32[]{:S(2)}) %collective-permute-start.14) | collective-permute-done | bytes 245792 | tf_op jit(solution)/shard_map/ppermute | solution.py:58
  44.9 0.8 %shard_map.99 = (f32[432,128]{1,0:T(8,128)}, f32[256,256]{1,0:T(8,128)}) custom-call(f32[480,128]{1,0:T(8,128)S(1)} %shard_map.98.own_ref, f32[480,128]{1,0:T(8,128)S(1)} %collective-permute-done.14.got_ref), custom_call_target="tpu_custom_call" | custom-call | tf_op jit(solution)/shard_map/pallas_call | solution.py:46
  (1 shorter events, 0.0 us)
Async XLA Ops:
  1.6 9.8 %collective-permute-start = (bf16[72,1024]{1,0:T(8,128)(2,1)S(1)}, bf16[72,1024]{1,0:T(8,128)(2,1)S(1)}, u32[]{:S(2)}, u32[]{:S(2)}) collective-permute-start(bf16[72,1024]{1,0:T(8,128)(2,1)S(1)} %shard_map.85.ref), channel_id=1, source_target_pairs={{0,6},{1,7},{2,4},{3,5},{4,2},{5,3},{6,0},{7,1},{8,14},{9,15},{10,... | collective-permute-start | bytes 442376 | tf_op jit(solution)/shard_map/ppermute | solution.py:63
  6.7 8.1 %collective-permute-start.2 = (bf16[72,1024]{1,0:T(8,128)(2,1)S(1)}, bf16[72,1024]{1,0:T(8,128)(2,1)S(1)}, u32[]{:S(2)}, u32[]{:S(2)}) collective-permute-start(bf16[72,1024]{1,0:T(8,128)(2,1)S(1)} %shard_map.85.ref), channel_id=1, source_target_pairs={{0,2},{1,3},{2,0},{3,1},{4,6},{5,7},{6,4},{7,5},{8,10},{9,11},{10,... | collective-permute-start | bytes 442376 | tf_op jit(solution)/shard_map/ppermute | solution.py:63
  11.4 5.5 %collective-permute-start.1 = (bf16[72,1024]{1,0:T(8,128)(2,1)S(1)}, bf16[72,1024]{1,0:T(8,128)(2,1)S(1)}, u32[]{:S(2)}, u32[]{:S(2)}) collective-permute-start(bf16[72,1024]{1,0:T(8,128)(2,1)S(1)} %collective-permute-done.ref), channel_id=1, source_target_pairs={{0,2},{1,3},{2,0},{3,1},{4,6},{5,7},{6,4},{7,5},{8,10},{9,11},{10,... | collective-permute-start | bytes 442376 | tf_op jit(solution)/shard_map/ppermute | solution.py:63
  14.8 5.6 %collective-permute-start.3 = (bf16[72,1024]{1,0:T(8,128)(2,1)S(1)}, bf16[72,1024]{1,0:T(8,128)(2,1)S(1)}, u32[]{:S(2)}, u32[]{:S(2)}) collective-permute-start(bf16[72,1024]{1,0:T(8,128)(2,1)S(1)} %shard_map.85.ref), channel_id=1, source_target_pairs={{0,1},{1,0},{2,3},{3,2},{4,5},{5,4},{6,7},{7,6},{8,9},{9,8},{10,11... | collective-permute-start | bytes 442376 | tf_op jit(solution)/shard_map/ppermute | solution.py:58
  15.5 4.9 %collective-permute-start.4 = (bf16[72,1024]{1,0:T(8,128)(2,1)S(1)}, bf16[72,1024]{1,0:T(8,128)(2,1)S(1)}, u32[]{:S(2)}, u32[]{:S(2)}) collective-permute-start(bf16[72,1024]{1,0:T(8,128)(2,1)S(1)} %collective-permute-done.2.ref), channel_id=1, source_target_pairs={{0,1},{1,0},{2,3},{3,2},{4,5},{5,4},{6,7},{7,6},{8,9},{9,8},{10,11... | collective-permute-start | bytes 442376 | tf_op jit(solution)/shard_map/ppermute | solution.py:58
  16.1 4.3 %collective-permute-start.5 = (bf16[72,1024]{1,0:T(8,128)(2,1)S(1)}, bf16[72,1024]{1,0:T(8,128)(2,1)S(1)}, u32[]{:S(2)}, u32[]{:S(2)}) collective-permute-start(bf16[72,1024]{1,0:T(8,128)(2,1)S(1)} %collective-permute-done.ref), channel_id=1, source_target_pairs={{0,1},{1,0},{2,3},{3,2},{4,5},{5,4},{6,7},{7,6},{8,9},{9,8},{10,11... | collective-permute-start | bytes 442376 | tf_op jit(solution)/shard_map/ppermute | solution.py:58
  17.0 5.5 %collective-permute-start.6 = (bf16[72,1024]{1,0:T(8,128)(2,1)S(1)}, bf16[72,1024]{1,0:T(8,128)(2,1)S(1)}, u32[]{:S(2)}, u32[]{:S(2)}) collective-permute-start(bf16[72,1024]{1,0:T(8,128)(2,1)S(1)} %collective-permute-done.1.across_ref), channel_id=1, source_target_pairs={{0,1},{1,0},{2,3},{3,2},{4,5},{5,4},{6,7},{7,6},{8,9},{9,8},{10,11... | collective-permute-start | bytes 442376 | tf_op jit(solution)/shard_map/ppermute | solution.py:58
  17.0 8.0 %collective-permute-start.7 = (bf16[128,256]{1,0:T(8,128)(2,1)S(1)}, bf16[128,256]{1,0:T(8,128)(2,1)S(1)}, u32[]{:S(2)}, u32[]{:S(2)}) collective-permute-start(bf16[128,256]{1,0:T(8,128)(2,1)S(1)} %get-tuple-element.107.own_ref), channel_id=1, source_target_pairs={{0,6},{1,7},{2,4},{3,5},{4,2},{5,3},{6,0},{7,1},{8,14},{9,15},{10,... | collective-permute-start | bytes 196616 | tf_op jit(solution)/shard_map/ppermute | solution.py:63
  25.5 1.7 %collective-permute-start.8 = (bf16[4,256,128]{2,1,0:T(8,128)(2,1)S(1)}, bf16[4,256,128]{2,1,0:T(8,128)(2,1)S(1)}, u32[]{:S(2)}, u32[]{:S(2)}) collective-permute-start(bf16[4,256,128]{2,1,0:T(8,128)(2,1)S(1)} %get-tuple-element.110), channel_id=1, source_target_pairs={{0,1},{1,0},{2,3},{3,2},{4,5},{5,4},{6,7},{7,6},{8,9},{9,8},{10,11... | collective-permute-start | bytes 786440 | tf_op jit(solution)/shard_map/ppermute | solution.py:58
  27.3 1.6 %collective-permute-start.9 = (bf16[4,224,128]{2,1,0:T(8,128)(2,1)S(1)}, bf16[4,224,128]{2,1,0:T(8,128)(2,1)S(1)}, u32[]{:S(2)}, u32[]{:S(2)}) collective-permute-start(bf16[4,224,128]{2,1,0:T(8,128)(2,1)S(1)} %get-tuple-element.117), channel_id=1, source_target_pairs={{0,1},{1,0},{2,3},{3,2},{4,5},{5,4},{6,7},{7,6},{8,9},{9,8},{10,11... | collective-permute-start | bytes 688136 | tf_op jit(solution)/shard_map/ppermute | solution.py:58
  28.9 5.7 %collective-permute-start.10 = (bf16[480,128]{1,0:T(8,128)(2,1)S(1)}, bf16[480,128]{1,0:T(8,128)(2,1)S(1)}, u32[]{:S(2)}, u32[]{:S(2)}) collective-permute-start(bf16[480,128]{1,0:T(8,128)(2,1)S(1)} %get-tuple-element.119), channel_id=1, source_target_pairs={{0,8},{8,0},{16,24},{24,16},{1,9},{9,1},{17,25},{25,17},{2,10},{10... | collective-permute-start | bytes 368648 | tf_op jit(solution)/shard_map/ppermute | solution.py:67
  30.5 7.9 %collective-permute-start.11 = (bf16[480,128]{1,0:T(8,128)(2,1)S(1)}, bf16[480,128]{1,0:T(8,128)(2,1)S(1)}, u32[]{:S(2)}, u32[]{:S(2)}) collective-permute-start(bf16[480,128]{1,0:T(8,128)(2,1)S(1)} %get-tuple-element.120), channel_id=1, source_target_pairs={{0,16},{8,24},{16,0},{24,8},{1,17},{9,25},{17,1},{25,9},{2,18},{10... | collective-permute-start | bytes 368648 | tf_op jit(solution)/shard_map/ppermute | solution.py:67
  32.0 6.3 %collective-permute-start.12 = (bf16[480,128]{1,0:T(8,128)(2,1)S(1)}, bf16[480,128]{1,0:T(8,128)(2,1)S(1)}, u32[]{:S(2)}, u32[]{:S(2)}) collective-permute-start(bf16[480,128]{1,0:T(8,128)(2,1)S(1)} %get-tuple-element.121), channel_id=1, source_target_pairs={{0,24},{8,16},{16,8},{24,0},{1,25},{9,17},{17,9},{25,1},{2,26},{10... | collective-permute-start | bytes 368648 | tf_op jit(solution)/shard_map/ppermute | solution.py:67
  38.4 4.9 %collective-permute-start.13 = (bf16[480,128]{1,0:T(8,128)(2,1)S(1)}, bf16[480,128]{1,0:T(8,128)(2,1)S(1)}, u32[]{:S(2)}, u32[]{:S(2)}) collective-permute-start(bf16[480,128]{1,0:T(8,128)(2,1)S(1)} %shard_map.97.refs_0_), channel_id=1, source_target_pairs={{0,2},{1,3},{2,0},{3,1},{4,6},{5,7},{6,4},{7,5},{8,10},{9,11},{10,... | collective-permute-start | bytes 368648 | tf_op jit(solution)/shard_map/ppermute | solution.py:63
  43.4 1.6 %collective-permute-start.14 = (f32[480,128]{1,0:T(8,128)S(1)}, f32[480,128]{1,0:T(8,128)S(1)}, u32[]{:S(2)}, u32[]{:S(2)}) collective-permute-start(f32[480,128]{1,0:T(8,128)S(1)} %shard_map.98.own_ref), channel_id=1, source_target_pairs={{0,1},{1,0},{2,3},{3,2},{4,5},{5,4},{6,7},{7,6},{8,9},{9,8},{10,11... | collective-permute-start | bytes 737288 | tf_op jit(solution)/shard_map/ppermute | solution.py:58
